TPU v7x, 128 devices: a whole 4x4x4 slice. The times are simulated.
128 devices in a mesh: row: 8 (over x, core), col: 16 (over z, y).
Axes of the slice: x: 4, y: 4, z: 4, core: 2. Of those that a mesh axis runs over, the one named last changes fastest.
Arguments:
- tile_feats: bfloat16 [128, 128, 32, 192], P(('row', 'col')), may hold values from -6 to 6
- tile_cell: int32 [128, 128, 32], P(('row', 'col')), may hold values from 0 to 4095, as said below
- tile_mask: int32 [128, 128, 32], P(('row', 'col')), may hold values 0 or 1
- tile_count: int32 [128, 128], P(('row', 'col')), may hold values from 0 to 32, as said below
- background: bfloat16 [192], replicated, may hold values from -6 to 6
- norm_gain: float32 [192], replicated, may hold values from 0.1 to 1.9
- in_x: bfloat16 [192, 384], replicated, may hold values from -0.4375 to 0.4375
- in_z: bfloat16 [192, 384], replicated, may hold values from -0.4375 to 0.4375
- conv_w: float32 [3, 3, 384], replicated, may hold values from -2 to 2
- conv_bias: float32 [384], replicated, may hold values from -3 to 3
- x_proj: bfloat16 [384, 128], replicated, may hold values from -0.15625 to 0.15625
- skip_gain: float32 [384], replicated, may hold values from 0.5 to 1.5
- decay_rate: float32 [4, 6, 256, 2048], P(None, None, 'row', 'col'), may hold values from 0 to 1
- out_gain: float32 [384], replicated, may hold values from 0.1 to 1.9
- out_w: bfloat16 [384, 192], replicated, may hold values from -0.3125 to 0.3125
- mlp_gain: float32 [192], replicated, may hold values from 0.1 to 1.9
- ff_in: bfloat16 [192, 768], replicated, may hold values from -0.4375 to 0.4375
- ff_out: bfloat16 [768, 192], replicated, may hold values from -0.21875 to 0.21875
Outputs:
- block_out: bfloat16 [256, 2048, 192], P('row', 'col')
Inputs may be any that keep to these rules, and one draw needn't show every extreme that they name: `tile_cell`: cells of the owner's block of 32 x 128 cells, numbered row by row; the live slots sent to one owner by all loaders name distinct cells. `tile_count`: the live slots from a loader to an owner are its first ones; some owner receives 32 from every loader.
All inputs are finite; a program needn't handle non-finite values. No bound on the sum of `tile_mask` on one device may be relied on, other than what follows from the above.
Results may differ from a plain program's by a relative error of at most 0.015.
Values may be sent and summed in bfloat16 or wider, within the bound.
No kernel may reach another device: no remote copies, remote signals or barrier semaphores. Data moves between devices by JAX's collectives and lax.ppermute only.
A program may use at most 384 MiB of HBM per device.

v0:
```python
import jax
import jax.numpy as jnp
from jax import lax
from jax.sharding import PartitionSpec as P


def prefix(shard, axis, combine, identity, reverse):
    peers, index = (lax.axis_size(axis), lax.axis_index(axis))
    everything = jax.tree.map(
        lambda part, kind: lax.all_gather(part.astype(kind), axis),
        shard,
        (jnp.bfloat16, jnp.bfloat16),
    )
    start = jax.tree.map(
        lambda part, zero: jnp.broadcast_to(jnp.asarray(zero, part.dtype), part.shape),
        shard,
        identity,
    )

    def hop(k, before):
        at = peers - 1 - k if reverse else k
        reached = at > index if reverse else at < index
        new = combine(
            before, jax.tree.map(lambda part, own: part[at].astype(own.dtype), everything, shard)
        )
        return jax.tree.map(lambda a, b: jnp.where(reached, a, b), new, before)

    return lax.fori_loop(0, peers, hop, start)


def padded_2(block, sides, width):
    for axis, dim in sides:
        count = lax.axis_size(axis)
        forward = [(i, i + 1) for i in range(count - 1)]
        backward = [(target, source) for source, target in forward]
        low = lax.ppermute(
            lax.slice_in_dim(block, block.shape[dim] - width, None, axis=dim), axis, forward
        )
        high = lax.ppermute(lax.slice_in_dim(block, 0, width, axis=dim), axis, backward)
        block = jnp.concatenate([low, block, high], axis=dim)
    return block


def rms_scale(values, gains):
    return values * lax.rsqrt(jnp.mean(values * values, axis=-1, keepdims=True) + 1e-06) * gains


def block_parts(x_vals, b_coef, c_coef, rates):
    cumulative = jnp.cumsum(rates, axis=2)
    weight = jnp.sqrt(-jnp.expm1(-2.0 * rates))
    scaled = x_vals.astype(jnp.float32) * jnp.swapaxes(weight, 1, 2)[..., None]
    scores = jnp.einsum("stn,sun->stu", c_coef, b_coef, preferred_element_type=jnp.float32)
    length = rates.shape[2]
    causal = lax.broadcasted_iota(jnp.int32, (length, length), 0) >= lax.broadcasted_iota(
        jnp.int32, (length, length), 1
    )
    log_gap = cumulative[:, :, :, None] - cumulative[:, :, None, :]
    mixing = jnp.where(causal, jnp.exp(-jnp.maximum(log_gap, 0.0)), 0.0) * scores[:, None]
    inner_part = jnp.einsum("shtu,suhp->sthp", mixing, scaled, precision=lax.Precision.HIGHEST)
    to_end = jnp.exp(cumulative - cumulative[:, :, -1:])
    weighted = scaled * jnp.swapaxes(to_end, 1, 2)[..., None]
    final_state = jnp.einsum(
        "suhp,sun->shpn", weighted, b_coef.astype(jnp.float32), precision=lax.Precision.HIGHEST
    )
    total_decay = jnp.exp(-cumulative[:, :, -1])
    return (inner_part, final_state, total_decay, cumulative)


def blocked_parts(x_vals, b_coef, c_coef, rates):
    sequences = x_vals.shape[0]
    groups = sequences // 16

    def grouped(array):
        return array.reshape((groups, 16) + array.shape[1:])

    def ungrouped(array):
        return array.reshape((sequences,) + array.shape[2:])

    parts = lax.map(
        lambda block_args: block_parts(*block_args),
        (grouped(x_vals), grouped(b_coef), grouped(c_coef), grouped(rates)),
    )
    return tuple((ungrouped(array) for array in parts))


def carry_part(c_coef, cumulative, entering):
    reached = jnp.einsum(
        "stn,shpn->sthp", c_coef.astype(jnp.float32), entering, precision=lax.Precision.HIGHEST
    )
    return reached * jnp.swapaxes(jnp.exp(-cumulative), 1, 2)[..., None]


def pass_carry(direction, total_decay, final_state):

    def combine(earlier, latter):
        return (earlier[0] * latter[0], latter[0][..., None, None] * earlier[1] + latter[1])

    neutral = (jnp.ones_like(total_decay), jnp.zeros_like(final_state))
    if direction == 0:
        passed = prefix((total_decay, final_state), "col", combine, neutral, False)
    elif direction == 1:
        passed = prefix((total_decay, final_state), "col", combine, neutral, True)
    elif direction == 2:
        passed = prefix((total_decay, final_state), "row", combine, neutral, False)
    else:
        passed = prefix((total_decay, final_state), "row", combine, neutral, True)
    return passed[1]


def orient(direction, scan_in, coeffs, rate_all):
    rows_n, cols_n, width = scan_in.shape
    head_count = rate_all.shape[1]
    state_size = coeffs.shape[2] // 8
    x_vals = scan_in.reshape(rows_n, cols_n, head_count, width // head_count)
    b_coef = coeffs[:, :, 2 * direction * state_size : (2 * direction + 1) * state_size]
    c_coef = coeffs[:, :, (2 * direction + 1) * state_size : (2 * direction + 2) * state_size]
    rates = rate_all[direction]
    if direction >= 2:
        x_vals = jnp.swapaxes(x_vals, 0, 1)
        b_coef = jnp.swapaxes(b_coef, 0, 1)
        c_coef = jnp.swapaxes(c_coef, 0, 1)
        rates = jnp.transpose(rates, (2, 0, 1))
    else:
        rates = jnp.transpose(rates, (1, 0, 2))
    if direction % 2 == 1:
        x_vals = jnp.flip(x_vals, 1)
        b_coef = jnp.flip(b_coef, 1)
        c_coef = jnp.flip(c_coef, 1)
        rates = jnp.flip(rates, 2)
    return (x_vals, b_coef, c_coef, rates)


def restore(direction, result, rows_n, cols_n):
    if direction % 2 == 1:
        result = jnp.flip(result, 1)
    if direction >= 2:
        result = jnp.swapaxes(result, 0, 1)
    return result.reshape(rows_n, cols_n, -1)


def sharded_direction(direction, scan_in, coeffs, decay_rate):
    rows_n, cols_n = (scan_in.shape[0], scan_in.shape[1])
    x_vals, b_coef, c_coef, rates = orient(direction, scan_in, coeffs, decay_rate)
    inner_part, final_state, total_decay, cumulative = blocked_parts(x_vals, b_coef, c_coef, rates)
    entering = pass_carry(direction, total_decay, final_state)
    result = inner_part + carry_part(c_coef, cumulative, entering)
    return restore(direction, result, rows_n, cols_n)


def local(
    tile_feats,
    tile_cell,
    tile_mask,
    tile_count,
    background,
    norm_gain,
    in_x,
    in_z,
    conv_w,
    conv_bias,
    x_proj,
    skip_gain,
    decay_rate,
    out_gain,
    out_w,
    mlp_gain,
    ff_in,
    ff_out,
):
    rows_n, cols_n = (decay_rate.shape[2], decay_rate.shape[3])
    channels = tile_feats.shape[3]
    slots = tile_feats.shape[2]
    width = in_x.shape[1]
    values = jnp.where(tile_mask[..., None] == 1, tile_feats, background)
    slot_live = jnp.arange(slots, dtype=jnp.int32)[None, None, :] < tile_count[:, :, None]
    marked = jnp.where(slot_live, tile_cell, rows_n * cols_n)
    got_values, got_cells = (
        lax.all_to_all(values, ("row", "col"), split_axis=1, concat_axis=0, tiled=True),
        lax.all_to_all(marked, ("row", "col"), split_axis=1, concat_axis=0, tiled=True),
    )
    tile_grid = (
        jnp.zeros((rows_n * cols_n + 1, channels), jnp.bfloat16)
        .at[got_cells.reshape(-1)]
        .set(got_values.reshape(-1, channels))
    )
    tile_grid = tile_grid[:-1].reshape(rows_n, cols_n, channels)
    normed = rms_scale(tile_grid.astype(jnp.float32), norm_gain).astype(jnp.bfloat16)
    inner_x = jnp.dot(normed, in_x, preferred_element_type=jnp.float32).astype(jnp.bfloat16)
    padded = padded_2(inner_x, (("row", 0), ("col", 1)), 1)
    gate_out = jnp.dot(normed, in_z, preferred_element_type=jnp.float32).astype(jnp.bfloat16)
    summed_conv = jnp.zeros((rows_n, cols_n, width), jnp.float32) + conv_bias
    for shift_row in range(3):
        for shift_col in range(3):
            summed_conv = (
                summed_conv
                + padded[shift_row : shift_row + rows_n, shift_col : shift_col + cols_n].astype(
                    jnp.float32
                )
                * conv_w[shift_row, shift_col]
            )
    scan_in = jax.nn.silu(summed_conv).astype(jnp.bfloat16)
    coeffs = jnp.dot(scan_in, x_proj, preferred_element_type=jnp.float32).astype(jnp.bfloat16)
    summed = skip_gain * scan_in.astype(jnp.float32)
    for direction in range(2):
        summed = summed + sharded_direction(direction, scan_in, coeffs, decay_rate)
    for direction in range(2, 4):
        summed = summed + sharded_direction(direction, scan_in, coeffs, decay_rate)
    gated_out = (rms_scale(summed, out_gain) * jax.nn.silu(gate_out.astype(jnp.float32))).astype(
        jnp.bfloat16
    )
    middle = (
        jnp.dot(gated_out, out_w, preferred_element_type=jnp.float32)
        + tile_grid.astype(jnp.float32)
    ).astype(jnp.bfloat16)
    normed_mid = rms_scale(middle.astype(jnp.float32), mlp_gain).astype(jnp.bfloat16)
    hidden = jax.nn.gelu(
        jnp.dot(normed_mid, ff_in, preferred_element_type=jnp.float32), approximate=False
    ).astype(jnp.bfloat16)
    return (
        jnp.dot(hidden, ff_out, preferred_element_type=jnp.float32) + middle.astype(jnp.float32)
    ).astype(jnp.bfloat16)


def solution(mesh):
    placed = (
        P(("row", "col"), None, None, None),
        P(("row", "col"), None, None),
        P(("row", "col"), None, None),
        P(("row", "col"), None),
        P(),
        P(),
        P(),
        P(),
        P(),
        P(),
        P(),
        P(),
        P(None, None, "row", "col"),
        P(),
        P(),
        P(),
        P(),
        P(),
    )
    return jax.shard_map(
        local, mesh=mesh, in_specs=placed, out_specs=P("row", "col", None), check_vma=False
    )
```

profile of v0, /device:TPU:1, one launch (start us, length us, event | category | flops | bytes accessed | tf_op | source)
XLA Modules:
  0.0 1034.8 jit_solution(5283740344307057812)
XLA Ops:
  8.0 11.5 %all-to-all-start = ((s32[1,128,32]{2,0,1:T(1,128)}), s32[1,128,32]{2,0,1:T(1,128)S(1)}, u32[]{:S(2)}, u32[]{:S(2)}) async-start(s32[1,128,32]{2,0,1:T(1,128)} %copy.251), calls=%async_computation | async-start | bytes 131072 | tf_op jit(solution)/shard_map/all_to_all | solution.py:179
  29.2 6.6 all-to-all-start.1
  37.4 27.8 %all-to-all-done.1 = bf16[1,128,32,192]{3,2,0,1:T(8,128)(2,1)S(1)} async-done(((bf16[1,128,32,192]{3,2,0,1:T(8,128)(2,1)}), bf16[1,128,32,192]{3,2,0,1:T(8,128)(2,1)S(1)}, u32[]{:S(2)}, u32[]{:S(2)}) %all-to-all-start.1) | async-done | bytes 1572896 | tf_op jit(solution)/shard_map/all_to_all | solution.py:178
  66.5 18.8 %scatter_custom_fusion = bf16[4097,192]{1,0:T(8,128)(2,1)S(1)} fusion(s32[4096]{0:T(1024)S(1)} %bitcast.475, bf16[4096,192]{1,0:T(8,128)(2,1)} %bitcast.458, bf16[]{:T(256)} %constant.284.clone.1), kind=kCustom, calls=%fused_computation.250 | custom fusion | bytes 1573760 | tf_op jit(solution)/shard_map/scatter | solution.py:184
  116.6 11.9 %multiply_convert_fusion = bf16[32,128,384]{2,1,0:T(8,128)(2,1)} fusion(bf16[32,128,384]{2,1,0:T(8,128)(2,1)S(1)} %convolution_convert_fusion, bf16[34,129,384]{2,1,0:T(8,128)(2,1)S(1)} %get-tuple-element.1102, bf16[1,128,384]{2,1,0:T(8,128)(2,1)S(1)} %collective-permute-done.1, bf16[34,129,384]{2,1,0:T(8,128)(2,1)S(1)} %get-tuple-element.1101, ...), kind=kLoop, calls=%fused_computation.221 | loop fusion | flops 53477376 | bytes 25377792 | tf_op jit(solution)/shard_map/convert_element_type | solution.py:201
  137.1 5.5 rev.38
  151.1 55.9 %while.125 = (s32[]{:T(128)}, f32[2,16,128,6,64]{2,4,3,1,0:T(8,128)}, bf16[2,16,6,64,16]{3,4,2,1,0:T(8,128)(2,1)}, bf16[2,16,6]{1,0,2:T(2,128)(2,1)S(1)}, f32[2,...) while((s32[]{:T(128)}, ...), condition=%wide.region_9.10_spmd, body=%wide.region_7.9_spmd.sunk | while | flops 1380753536 | bytes 26335036 | solution.py:79
  158.0 15.3 %bitcast_dynamic-update-slice_fusion.18 = f32[2,16,128,6,64]{2,4,3,1,0:T(8,128)} fusion(f32[2,16,128,6,64]{2,4,3,1,0:T(8,128)} %get-tuple-element.1632, s32[]{:T(128)S(6)} %copy.424, f32[16,128,128]{2,1,0:T(8,128)} %fusion.307, f32[16,6,128]{2,1,0:T(8,128)S(1)} %copy.350, pred[128,128]{1,0:T(8,128)(4,1)S(1)} %iota_compare_fusion.10, ...), kind=kOutput, calls=%fused_computation.65.clone.1 | convolution fusion | flops 1217396736 | bytes 5981184 | tf_op jit(solution)/shard_map/while/body/eval_jaxpr/shtu,suhp->sthp/dot_general | solution.py:59
  185.9 15.3 %bitcast_dynamic-update-slice_fusion.18 = f32[2,16,128,6,64]{2,4,3,1,0:T(8,128)} fusion(f32[2,16,128,6,64]{2,4,3,1,0:T(8,128)} %get-tuple-element.1632, s32[]{:T(128)S(6)} %copy.424, f32[16,128,128]{2,1,0:T(8,128)} %fusion.307, f32[16,6,128]{2,1,0:T(8,128)S(1)} %copy.350, pred[128,128]{1,0:T(8,128)(4,1)S(1)} %iota_compare_fusion.10, ...), kind=kOutput, calls=%fused_computation.65.clone.1 | convolution fusion | flops 1217396736 | bytes 5981184 | tf_op jit(solution)/shard_map/while/body/eval_jaxpr/shtu,suhp->sthp/dot_general | solution.py:59
  212.2 56.8 %while.124 = (s32[]{:T(128)}, f32[2,16,128,6,64]{2,4,3,1,0:T(8,128)}, bf16[2,16,6,64,16]{3,4,2,1,0:T(8,128)(2,1)}, bf16[2,16,6]{1,0,2:T(2,128)(2,1)S(1)}, f32[2,...) while((s32[]{:T(128)}, ...), condition=%wide.region_4.5_spmd, body=%wide.region_2.4_spmd.sunk | while | flops 1380753536 | bytes 10606313 | solution.py:79
  219.3 15.7 %bitcast_dynamic-update-slice_fusion.16 = f32[2,16,128,6,64]{2,4,3,1,0:T(8,128)} fusion(f32[2,16,128,6,64]{2,4,3,1,0:T(8,128)} %get-tuple-element.1695, s32[]{:T(128)S(6)} %copy.445, f32[16,128,128]{2,1,0:T(8,128)} %fusion.300, f32[16,6,128]{2,1,0:T(8,128)S(1)} %copy.347, pred[128,128]{1,0:T(8,128)(4,1)S(1)} %iota_compare_fusion.9, ...), kind=kOutput, calls=%fused_computation.22.clone.1 | convolution fusion | flops 1217396736 | bytes 5981184 | tf_op jit(solution)/shard_map/while/body/eval_jaxpr/shtu,suhp->sthp/dot_general | solution.py:59
  235.3 4.6 fusion.301
  247.5 15.6 %bitcast_dynamic-update-slice_fusion.16 = f32[2,16,128,6,64]{2,4,3,1,0:T(8,128)} fusion(f32[2,16,128,6,64]{2,4,3,1,0:T(8,128)} %get-tuple-element.1695, s32[]{:T(128)S(6)} %copy.445, f32[16,128,128]{2,1,0:T(8,128)} %fusion.300, f32[16,6,128]{2,1,0:T(8,128)S(1)} %copy.347, pred[128,128]{1,0:T(8,128)(4,1)S(1)} %iota_compare_fusion.9, ...), kind=kOutput, calls=%fused_computation.22.clone.1 | convolution fusion | flops 1217396736 | bytes 5981184 | tf_op jit(solution)/shard_map/while/body/eval_jaxpr/shtu,suhp->sthp/dot_general | solution.py:59
  277.6 10.2 copy.281
  292.1 6.0 broadcast.199.clone
  299.5 113.1 %while.127 = (s32[]{:T(128)}, f32[8,16,32,6,64]{4,2,3,1,0:T(8,128)}, bf16[8,16,6,64,16]{3,4,2,1,0:T(8,128)(2,1)S(1)}, bf16[8,16,6]{1,0,2:T(8,128)(2,1)S(1)}, f32...) while((s32[]{:T(128)}, f32[8,16,32,6,64]{4,2,3,1,0:T(8,128)}, ...), condition=%wide.region_19.20_spmd, body=%wide.region_17.19_spmd.sunk | while | flops 115350624 | bytes 5016269 | solution.py:79
  305.6 4.6 bitcast_dynamic-update-slice_fusion.22
  319.8 4.6 bitcast_dynamic-update-slice_fusion.22
  348.1 4.6 bitcast_dynamic-update-slice_fusion.22
  362.2 4.6 bitcast_dynamic-update-slice_fusion.22
  376.4 4.6 bitcast_dynamic-update-slice_fusion.22
  390.6 4.6 bitcast_dynamic-update-slice_fusion.22
  412.7 4.9 copy.286
  419.5 5.5 copy.294
  424.9 10.4 %copy.269 = bf16[128,32,6,64]{3,1,2,0:T(8,128)(2,1)} copy(bf16[128,32,6,64]{0,3,2,1:T(8,128)(2,1)} %bitcast.443) | data formatting | bytes 6291456 | tf_op jit(solution)/shard_map/transpose | solution.py:119
  446.2 6.1 broadcast.199.clone.1
  455.4 118.2 %while.126 = (s32[]{:T(128)}, f32[8,16,32,6,64]{4,2,3,1,0:T(8,128)}, bf16[8,16,6,64,16]{3,4,2,1,0:T(8,128)(2,1)}, bf16[8,16,6]{1,0,2:T(8,128)(2,1)S(1)}, f32[8,1...) while((s32[]{:T(128)}, f32[8,16,32,6,64]{4,2,3,1,0:T(8,128)}, ...), condition=%wide.region_14.15_spmd, body=%wide.region_12.14_spmd.sunk | while | flops 115350624 | bytes 4909773 | solution.py:79
  491.1 4.6 bitcast_dynamic-update-slice_fusion.20
  535.4 4.6 bitcast_dynamic-update-slice_fusion.20
  550.2 4.6 bitcast_dynamic-update-slice_fusion.20
  578.6 6.5 copy.274
  588.3 19.3 %all_gather.34 = bf16[16,32,6]{1,2,0:T(8,128)(2,1)S(1)} all-gather(bf16[1,32,6]{1,2,0:T(8,128)(2,1)S(1)} %convert_element_type.343), channel_id=1, replica_groups=mesh['row'=8,'col'=16] {'col'}, dimensions={0}, use_global_device_ids=true | all-gather | bytes 6528 | tf_op jit(solution)/shard_map/all_gather | solution.py:10
  607.6 15.8 %all_gather.32 = bf16[16,32,6]{1,2,0:T(8,128)(2,1)S(1)} all-gather(bf16[1,32,6]{1,2,0:T(8,128)(2,1)S(1)} %convert_element_type.339), channel_id=1, replica_groups=mesh['row'=8,'col'=16] {'col'}, dimensions={0}, use_global_device_ids=true | all-gather | bytes 6528 | tf_op jit(solution)/shard_map/all_gather | solution.py:10
  623.4 25.1 %all_gather.38 = bf16[8,128,6]{1,2,0:T(8,128)(2,1)} all-gather(bf16[1,128,6]{1,2,0:T(8,128)(2,1)} %convert_element_type.351), channel_id=1, replica_groups=mesh['row'=8,'col'=16] {'row'}, dimensions={0}, use_global_device_ids=true | all-gather | bytes 13824 | tf_op jit(solution)/shard_map/all_gather | solution.py:10
  648.5 11.6 %all_gather.36 = bf16[8,128,6]{1,2,0:T(8,128)(2,1)S(1)} all-gather(bf16[1,128,6]{1,2,0:T(8,128)(2,1)} %convert_element_type.347), channel_id=1, replica_groups=mesh['row'=8,'col'=16] {'row'}, dimensions={0}, use_global_device_ids=true | all-gather | bytes 13824 | tf_op jit(solution)/shard_map/all_gather | solution.py:10
  660.1 53.3 %while.129 = (s32[]{:T(128)}, f32[32,6,64,16]{2,3,1,0:T(8,128)}, s32[]{:T(128)}, bf16[16,32,6]{1,2,0:T(8,128)(2,1)S(1)}, bf16[16,32,6,64,16]{3,4,2,1,0:T(8,128)(...) while((s32[]{:T(128)}, f32[32,6,64,16]{2,3,1,0:T(8,128)}, s32[]{:T(128)}, ...), condition=%wide.region_11.12_spmd.clone, body=%wide.region_10.11_spmd.clone.sunk | while | flops 983240 | bytes 1969711 | solution.py:28
  713.4 9.3 bitcast_add_fusion.2
  722.7 10.2 rev.42
  732.9 6.7 copy.268
  739.6 51.6 %while.128 = (s32[]{:T(128)}, f32[32,6,64,16]{2,3,1,0:T(8,128)}, s32[]{:T(128)}, bf16[16,32,6]{1,2,0:T(8,128)(2,1)S(1)}, bf16[16,32,6,64,16]{3,4,2,1,0:T(8,128)(2,1)}, /*index=5*/s32[]{:T(128)}, s32[]{:T(128)}) while((s32[]{:T(128)}, f32[32,6,64,16]{2,3,1,0:T(8,128)}, s32[]{:T(128)}, bf16[16,32,6]{1,2,0:T(8,128)(2,1)S(1)}, ...), condition=%wide.region_6.7_spmd.clone, body=%wide.region_5.6_spmd.clone.sunk | while | flops 983236 | bytes 1969649 | solution.py:28
  791.2 9.3 bitcast_add_fusion.3
  800.5 6.6 copy.262
  807.1 41.9 %while.131 = (s32[]{:T(128)}, f32[128,6,64,16]{0,3,2,1:T(8,128)}, s32[]{:T(128)}, bf16[8,128,6]{1,2,0:T(8,128)(2,1)}, bf16[8,128,6,64,16]{1,4,3,2,0:T(8,128)(2,1...) while((s32[]{:T(128)}, f32[128,6,64,16]{0,3,2,1:T(8,128)}, s32[]{:T(128)}, ...), condition=%wide.region_21.22_spmd.clone, body=%wide.region_20.21_spmd.clone.sunk | while | flops 3932936 | bytes 7872175 | solution.py:28
  812.1 4.7 fusion.326
  817.5 4.7 fusion.326
  822.8 4.7 fusion.326
  828.2 4.7 fusion.326
  833.5 4.7 fusion.326
  838.8 4.7 fusion.326
  844.2 4.8 fusion.326
  849.0 7.5 copy.288
  856.5 16.0 %bitcast_add_fusion = f32[128,32,6,64]{3,1,2,0:T(8,128)} fusion(f32[8,16,32,6,64]{4,2,3,1,0:T(8,128)} %get-tuple-element.672, f32[128,32,6]{1,2,0:T(8,128)} %copy.290, bf16[128,32,16,1]{1,2,3,0:T(8,128)(2,1)} %copy.303, f32[128,6,64,16]{2,3,1,0:T(8,128)} %copy.288), kind=kOutput, calls=%fused_computation.196 | convolution fusion | flops 305135616 | bytes 15958016 | tf_op jit(solution)/shard_map/stn,shpn->sthp/dot_general | solution.py:87
  872.5 17.3 %rev.47 = f32[128,32,6,64]{3,1,2,0:T(8,128)} reverse(f32[128,32,6,64]{3,1,2,0:T(8,128)} %bitcast_add_fusion), dimensions={1} | reverse | bytes 12582912 | tf_op jit(solution)/shard_map/jit(_flip)/rev | solution.py:135
  889.7 11.7 %copy.291 = f32[32,128,6,64]{1,3,2,0:T(8,128)} copy(f32[32,128,6,64]{3,0,2,1:T(8,128)} %bitcast.439) | data formatting | bytes 12582912 | tf_op jit(solution)/shard_map/transpose | solution.py:137
  901.5 6.6 copy.292
  908.0 27.1 %while.130 = (s32[]{:T(128)}, f32[128,6,64,16]{0,3,2,1:T(8,128)S(1)}, s32[]{:T(128)}, bf16[8,128,6]{1,2,0:T(8,128)(2,1)S(1)}, bf16[8,128,6,64,16]{1,4,3,2,0:T(8,128)(2,1)}, /*index=5*/s32[]{:T(128)}, s32[]{:T(128)}) while((s32[]{:T(128)}, f32[128,6,64,16]{0,3,2,1:T(8,128)S(1)}, s32[]{:T(128)}, ...), condition=%wide.region_16.17_spmd.clone, body=%wide.region_15.16_spmd.clone.sunk | while | flops 3932932 | bytes 7872113 | solution.py:28
  935.2 6.2 copy.276
  941.3 16.1 %fusion.184 = f32[32,128,6,64]{3,0,2,1:T(8,128)} fusion(f32[128,32,6]{1,2,0:T(8,128)} %copy.278, bf16[128,32,16,1]{1,2,3,0:T(8,128)(2,1)} %copy.302, f32[128,6,64,16]{2,3,1,0:T(8,128)} %copy.276, f32[8,16,32,6,64]{4,2,3,1,0:T(8,128)} %get-tuple-element.667), kind=kOutput, calls=%fused_computation.227 | convolution fusion | flops 305135616 | bytes 15958016 | tf_op jit(solution)/shard_map/stn,shpn->sthp/dot_general | solution.py:87
  957.4 11.3 %copy.279 = f32[32,128,6,64]{1,3,2,0:T(8,128)} copy(f32[32,128,6,64]{3,0,2,1:T(8,128)} %fusion.184) | data formatting | bytes 12582912 | tf_op jit(solution)/shard_map/transpose | solution.py:137
  968.8 6.7 copy.280
  975.5 11.9 %multiply_reduce_fusion = (f32[32,128]{1,0:T(8,128)S(1)}, f32[32,128,384]{2,1,0:T(8,128)}) fusion(f32[32,128,384]{2,1,0:T(8,128)} %copy.292, f32[32,128,384]{2,1,0:T(8,128)} %copy.280, f32[32,128,384]{2,1,0:T(8,128)} %copy.268, f32[32,128,384]{2,1,0:T(8,128)} %copy.262, bf16[32,128,384]{2,1,0:T(8,128)(2,1)S(1)} %copy-done.2, f32[384]{0:T(512)S(1)} %copy-done.23), kind=kLoop, calls=%fused_computation.219 | loop fusion | flops 12578816 | bytes 34620928 | tf_op jit(solution)/shard_map/reduce_sum | solution.py:45
  987.4 6.6 fusion.185
  994.0 4.9 convert_reduce_fusion.1
  998.9 29.1 %fusion.188 = bf16[32,128,192]{1,2,0:T(8,128)(2,1)} fusion(bf16[32,128,192]{1,2,0:T(8,128)(2,1)S(1)} %get-tuple-element.1121, f32[32,128,768]{2,1,0:T(8,128)S(1)} %get-tuple-element.1122, u32[128,768]{1,0:T(8,128)S(1)} %get-tuple-element.969, u32[128,768]{1,0:T(8,128)S(1)} %get-tuple-element.968, bf16[768,192]{0,1:T(8,128)(2,1)S(1)} %copy-done.25), kind=kOutput, calls=%fused_computation.234 | convolution fusion | flops 1424228352 | bytes 16809984 | tf_op jit(solution)/shard_map/dot_general | solution.py:220
  (580 shorter events, 481.1 us)
Async XLA Ops:
  6.5 987.4 %copy-start = (bf16[192,768]{1,0:T(8,128)(2,1)S(1)}, bf16[192,768]{1,0:T(8,128)(2,1)}, u32[]{:S(2)}) copy-start(bf16[192,768]{1,0:T(8,128)(2,1)} %param.50) | copy-start | bytes 884740
  8.0 21.2 %all-to-all-start = ((s32[1,128,32]{2,0,1:T(1,128)}), s32[1,128,32]{2,0,1:T(1,128)S(1)}, u32[]{:S(2)}, u32[]{:S(2)}) async-start(s32[1,128,32]{2,0,1:T(1,128)} %copy.251), calls=%async_computation | async-start | bytes 131072 | tf_op jit(solution)/shard_map/all_to_all | solution.py:179
  29.2 35.9 %all-to-all-start.1 = ((bf16[1,128,32,192]{3,2,0,1:T(8,128)(2,1)}), bf16[1,128,32,192]{3,2,0,1:T(8,128)(2,1)S(1)}, u32[]{:S(2)}, u32[]{:S(2)}) async-start(bf16[1,128,32,192]{3,2,0,1:T(8,128)(2,1)} %broadcast_select_fusion), calls=%async_computation.1 | async-start | bytes 4194304 | tf_op jit(solution)/shard_map/all_to_all | solution.py:178
  35.9 624.3 %all-gather.7.cloned.1.call-start = ((), (), s32[]{:S(2)}) async-start(), calls=%async_computation.3 | async-start | bytes 13369344 | tf_op jit(solution)/shard_map/all_gather | solution.py:10
  65.1 1.4 copy-start.8
  87.6 4.6 copy-start.24
  92.1 9.8 copy-start.13
  92.2 17.6 %copy-start.17 = (f32[3,3,384]{2,1,0:T(4,128)S(1)}, f32[3,3,384]{2,1,0:T(4,128)}, u32[]{:S(2)}) copy-start(f32[3,3,384]{2,1,0:T(4,128)} %param.42) | copy-start | bytes 41476
  92.6 1.2 copy-start.3
  96.1 6.7 collective-permute-start.1
  99.5 4.1 collective-permute-start
  103.6 0.6 copy-start.11
  105.0 7.1 collective-permute-start.2
  108.3 5.3 collective-permute-start.3
  112.0 4.5 copy-start.12
  112.0 4.5 copy-start.18
  112.0 4.5 copy-start.19
  112.0 4.5 copy-start.20
  112.0 4.5 copy-start.21
  112.0 4.5 copy-start.22
  128.5 3.5 copy-start.15
  135.1 1.0 copy-start.4
  158.0 15.6 %copy-start.5 = (bf16[2,16,128,6,64]{2,4,3,1,0:T(8,128)(2,1)S(1)}, bf16[2,16,128,6,64]{2,4,3,1,0:T(8,128)(2,1)}, u32[]{:S(2)}) copy-start(bf16[2,16,128,6,64]{2,4,3,1,0:T(8,128)(2,1)} %get-tuple-element.1648) | copy-start | bytes 9437188 | tf_op jit(solution)/shard_map/while
  158.0 15.6 %copy-start.6 = (bf16[2,16,6,64,16]{3,4,2,1,0:T(8,128)(2,1)S(1)}, bf16[2,16,6,64,16]{3,4,2,1,0:T(8,128)(2,1)}, u32[]{:S(2)}) copy-start(bf16[2,16,6,64,16]{3,4,2,1,0:T(8,128)(2,1)} %get-tuple-element.1633) | copy-start | bytes 1179652 | tf_op jit(solution)/shard_map/while
  158.0 15.6 %copy-start.10 = (bf16[2,16,128,16]{2,3,1,0:T(8,128)(2,1)S(1)}, bf16[2,16,128,16]{2,3,1,0:T(8,128)(2,1)}, u32[]{:S(2)}) copy-start(bf16[2,16,128,16]{2,3,1,0:T(8,128)(2,1)} %get-tuple-element.1651) | copy-start | bytes 393220 | tf_op jit(solution)/shard_map/while
  177.4 0.9 copy-start.7
  185.9 15.6 %copy-start.5 = (bf16[2,16,128,6,64]{2,4,3,1,0:T(8,128)(2,1)S(1)}, bf16[2,16,128,6,64]{2,4,3,1,0:T(8,128)(2,1)}, u32[]{:S(2)}) copy-start(bf16[2,16,128,6,64]{2,4,3,1,0:T(8,128)(2,1)} %get-tuple-element.1648) | copy-start | bytes 9437188 | tf_op jit(solution)/shard_map/while
  185.9 15.6 %copy-start.6 = (bf16[2,16,6,64,16]{3,4,2,1,0:T(8,128)(2,1)S(1)}, bf16[2,16,6,64,16]{3,4,2,1,0:T(8,128)(2,1)}, u32[]{:S(2)}) copy-start(bf16[2,16,6,64,16]{3,4,2,1,0:T(8,128)(2,1)} %get-tuple-element.1633) | copy-start | bytes 1179652 | tf_op jit(solution)/shard_map/while
  185.9 15.6 %copy-start.10 = (bf16[2,16,128,16]{2,3,1,0:T(8,128)(2,1)S(1)}, bf16[2,16,128,16]{2,3,1,0:T(8,128)(2,1)}, u32[]{:S(2)}) copy-start(bf16[2,16,128,16]{2,3,1,0:T(8,128)(2,1)} %get-tuple-element.1651) | copy-start | bytes 393220 | tf_op jit(solution)/shard_map/while
  205.4 0.9 copy-start.7
  207.0 532.6 %all-gather.5.cloned.1.call-start = ((), (), s32[]{:S(2)}) async-start(), calls=%async_computation.2 | async-start | bytes 13369344 | tf_op jit(solution)/shard_map/all_gather | solution.py:10
  219.3 16.0 %copy-start.9 = (bf16[2,16,128,16]{2,3,1,0:T(8,128)(2,1)S(1)}, bf16[2,16,128,16]{2,3,1,0:T(8,128)(2,1)}, u32[]{:S(2)}) copy-start(bf16[2,16,128,16]{2,3,1,0:T(8,128)(2,1)} %get-tuple-element.1714) | copy-start | bytes 393220 | tf_op jit(solution)/shard_map/while
  247.5 15.9 %copy-start.9 = (bf16[2,16,128,16]{2,3,1,0:T(8,128)(2,1)S(1)}, bf16[2,16,128,16]{2,3,1,0:T(8,128)(2,1)}, u32[]{:S(2)}) copy-start(bf16[2,16,128,16]{2,3,1,0:T(8,128)(2,1)} %get-tuple-element.1714) | copy-start | bytes 393220 | tf_op jit(solution)/shard_map/while
  269.0 18.8 %copy-start.1 = (bf16[2,16,128,6,64]{2,4,3,1,0:T(8,128)(2,1)}, bf16[2,16,128,6,64]{2,4,3,1,0:T(8,128)(2,1)S(1)}, u32[]{:S(2)}) copy-start(bf16[2,16,128,6,64]{2,4,3,1,0:T(8,128)(2,1)S(1)} %get-tuple-element.1743) | copy-start | bytes 9437188
  269.0 18.8 %copy-start.16 = (bf16[2,16,6]{1,0,2:T(2,128)(2,1)}, bf16[2,16,6]{1,0,2:T(2,128)(2,1)S(1)}, u32[]{:S(2)}) copy-start(bf16[2,16,6]{1,0,2:T(2,128)(2,1)S(1)} %get-tuple-element.658) | copy-start | bytes 1156
  269.0 538.0 %all-gather.11.cloned.1.call-start = ((), (), s32[]{:S(2)}) async-start(), calls=%async_computation.5 | async-start | bytes 14155776 | tf_op jit(solution)/shard_map/all_gather | solution.py:10
  417.6 490.5 %all-gather.9.cloned.1.call-start = ((), (), s32[]{:S(2)}) async-start(), calls=%async_computation.4 | async-start | bytes 14155776 | tf_op jit(solution)/shard_map/all_gather | solution.py:10
  573.6 11.5 %copy-start.14 = (f32[2,16,6,128]{3,1,0,2:T(8,128)S(1)}, f32[2,16,6,128]{3,1,0,2:T(8,128)}, u32[]{:S(2)}) copy-start(f32[2,16,6,128]{3,1,0,2:T(8,128)} %get-tuple-element.666) | copy-start | bytes 294916
  968.8 6.7 copy-start.2
  968.8 6.7 copy-start.23
  975.5 11.9 %copy-start.26 = (f32[384]{0:T(512)S(1)}, f32[384]{0:T(512)}, u32[]{:S(2)}) copy-start(f32[384]{0:T(512)} %param.47) | copy-start | bytes 4612
  987.3 6.6 copy-start.27
  994.0 5.0 copy-start.25
Sparse Core Ops, SparseCore 0:
  207.2 92.2 all-gather.6
  301.6 89.6 all-gather.4
  417.7 69.7 all-gather.10
  660.2 65.5 all-gather.8
where the time goes:
time: 1050 us; the launch traced here: 1030 us
  matrix products  331 us (32%)
  other arithmetic  301 us (29%)
  local copies, waits for them, and re-layouts  253 us (24%)
  blocking collectives  71.8 us (7%)
  waiting for transfers between devices  33.3 us (3%)
  starting transfers between devices  28.9 us (3%)
  between operations  13.9 us (1%)
    select_n x48, other arithmetic, hop(): return jax.tree.map(lambda a, b: jnp.where(reached, a, b), new, before)  165 us
    dot_general x20, matrix products, block_parts(): jnp.einsum('shtu,suhp->sthp', mixing, scaled, precision=lax.Precision.HIG...  135 us
    all_gather x4, blocking collectives, prefix(): lax.all_gather(part.astype(kind), axis)  71.8 us
    dot_general x20, matrix products, block_parts(): jnp.einsum('suhp,sun->shpn', weighted, b_coef.astype(jnp.float32), precis...  61.8 us
    another operation x20, other arithmetic, block_parts(): cumulative = jnp.cumsum(rates, axis=2)  58.1 us
    dot_general x4, matrix products, carry_part(): jnp.einsum('stn,shpn->sthp', c_coef.astype(jnp.float32), entering, precis...  50.7 us
    dot_general x20, matrix products, block_parts(): jnp.einsum('stn,sun->stu', c_coef, b_coef, preferred_element_type=jnp.flo...  37.7 us
    dot_general x1, matrix products, local(): jnp.dot(hidden, ff_out, preferred_element_type=jnp.float32)  29.1 us
  transfers between devices with their start and end apart: 10, of which 4 were waited for; matrix products, arithmetic and copies ran while one was open for 62% of the time, Pallas kernels for 0%

commit v1 on v0

v1 whole, which is shorter than its diff:
```python
import functools
import jax
import jax.numpy as jnp
from jax import lax
from jax.experimental import pallas as pl
from jax.experimental.pallas import tpu as pltpu
from jax.sharding import PartitionSpec as P

F32 = jnp.float32
BF16 = jnp.bfloat16
LANES = 128
SUB = 8
VMEM_BYTES = 58 * 1024 * 1024


def whole():
    return pl.BlockSpec(memory_space=pltpu.VMEM)


def call(body, outs, ins, scratch=(), name=None):
    return pl.pallas_call(
        body,
        out_shape=outs,
        in_specs=ins,
        out_specs=jax.tree.map(lambda _: whole(), outs),
        scratch_shapes=list(scratch),
        compiler_params=pltpu.CompilerParams(vmem_limit_bytes=VMEM_BYTES),
        name=name,
    )


def dot(a, b):
    return jnp.dot(a, b, preferred_element_type=F32)


def dot_nt(a, b):
    return lax.dot_general(a, b, (((1,), (1,)), ((), ())), preferred_element_type=F32)


def dot_tn(a, b):
    return lax.dot_general(a, b, (((0,), (0,)), ((), ())), preferred_element_type=F32)


def rms_scale(values, gains):
    return values * lax.rsqrt(jnp.mean(values * values, axis=-1, keepdims=True) + 1e-06) * gains


def two_parts(values):
    high = lax.reduce_precision(values, 8, 7)
    return high.astype(BF16), (values - high).astype(BF16)


def factor_rows(values):
    high, low = two_parts(values)
    heads = values.shape[1]
    both = jnp.concatenate([high, low], axis=1)
    return jnp.pad(both, ((0, 0), (0, 16 - 2 * heads), (0, 0), (0, 0)))


def row_layout(parts):
    return jnp.transpose(parts, (0, 2, 1, 3))


def col_layout(parts):
    k, m, r, c = parts.shape
    parts = parts.reshape(k, m, r, c // SUB, SUB)
    return jnp.transpose(parts, (0, 3, 1, 2, 4)).reshape(k, c // SUB, m, r * SUB)


def decay_factors(decay):
    rows_n, cols_n = decay.shape[2:]
    upto_c = jnp.triu(jnp.ones((cols_n, cols_n), F32))
    upto_r = jnp.triu(jnp.ones((rows_n, rows_n), F32))
    exact = lax.Precision.HIGHEST
    cum = jnp.stack(
        [
            jnp.einsum("hru,ut->hrt", decay[0], upto_c, precision=exact),
            jnp.einsum("hru,ut->hrt", decay[1], upto_c.T, precision=exact),
            jnp.einsum("huc,ut->htc", decay[2], upto_r, precision=exact),
            jnp.einsum("huc,ut->htc", decay[3], upto_r.T, precision=exact),
        ]
    )
    total_row = jnp.sum(decay[:2], axis=3)
    total_col = jnp.sum(decay[2:], axis=2)
    mid = 0.5 * jnp.concatenate(
        [
            jnp.broadcast_to(total_row[..., None], decay[:2].shape),
            jnp.broadcast_to(total_col[:, :, None, :], decay[2:].shape),
        ]
    )
    weight = jnp.sqrt(-jnp.expm1(-2.0 * decay))
    into = factor_rows(weight * jnp.exp(cum - mid))
    out = factor_rows(jnp.exp(mid - cum))
    return (
        row_layout(into[:2]),
        row_layout(out[:2]),
        col_layout(into[2:]),
        col_layout(out[2:]),
        total_row,
        total_col,
    )


def place_body(cells, got, gain, in_x, grid_out, inner_out, left_out, right_out, src, dst):
    slots = got.shape[0]
    channels = grid_out.shape[1]
    cells_n = grid_out.shape[0]
    cols_n = cells_n // left_out.shape[0]

    def fill(i, carry):
        at = pl.ds(pl.multiple_of(i * 256, 256), 256)
        dst[at, :] = jnp.zeros((256, dst.shape[1]), F32)
        return carry

    lax.fori_loop(0, cells_n // 256, fill, 0)

    def widen(i, carry):
        at = pl.ds(pl.multiple_of(i * 256, 256), 256)
        src[at, :] = got[at, :].astype(F32)
        return carry

    lax.fori_loop(0, slots // 256, widen, 0)

    def place(i, carry):
        base = i * 16
        for j in range(16):
            cell = cells[base + j]
            dst[pl.ds(cell, 1), :] = src[pl.ds(base + j, 1), :]
        return carry

    lax.fori_loop(0, slots // 16, place, 0)

    def project(r, carry):
        at = pl.ds(pl.multiple_of(r * cols_n, cols_n), cols_n)
        tiles = dst[at, :channels]
        grid_out[at, :] = tiles.astype(BF16)
        normed = rms_scale(tiles, gain[...]).astype(BF16)
        inner = dot(normed, in_x[...]).astype(BF16)
        inner_out[at, :] = inner
        wide = inner.astype(F32)
        left_out[pl.ds(r, 1), :] = wide[:1]
        right_out[pl.ds(r, 1), :] = wide[cols_n - 1 :]
        return carry

    lax.fori_loop(0, cells_n // cols_n, project, 0)


def place(cells, got, gain, in_x, rows_n, cols_n, channels):
    cells_n = rows_n * cols_n
    width = in_x.shape[1]
    outs = (
        jax.ShapeDtypeStruct((cells_n, channels), BF16),
        jax.ShapeDtypeStruct((cells_n, width), BF16),
        jax.ShapeDtypeStruct((rows_n, width), F32),
        jax.ShapeDtypeStruct((rows_n, width), F32),
    )
    return call(
        place_body,
        outs,
        [pl.BlockSpec(memory_space=pltpu.SMEM), whole(), whole(), whole()],
        [
            pltpu.VMEM(got.shape, F32),
            pltpu.VMEM((cells_n + SUB, got.shape[1]), F32),
        ],
        name="place_norm_project",
    )(cells, got, gain, in_x)


def gate_body(grid, gain, in_z, gate_out, *, block):
    def step(i, carry):
        at = pl.ds(pl.multiple_of(i * block, block), block)
        normed = rms_scale(grid[at, :].astype(F32), gain[...]).astype(BF16)
        gate = dot(normed, in_z[...]).astype(BF16).astype(F32)
        gate_out[at, :] = (gate / (1.0 + jnp.exp(-gate))).astype(BF16)
        return carry

    lax.fori_loop(0, grid.shape[0] // block, step, 0)


def gate(grid, gain, in_z):
    return call(
        functools.partial(gate_body, block=128),
        jax.ShapeDtypeStruct((grid.shape[0], in_z.shape[1]), BF16),
        [whole()] * 3,
        name="gate",
    )(grid, gain, in_z)


def spread(parts, heads_map):
    return dot_tn(parts, heads_map)


def own_column(shape, row_mod, col_mod):
    rows = lax.broadcasted_iota(jnp.int32, shape, 0)
    cols = lax.broadcasted_iota(jnp.int32, shape, 1)
    return (rows & (row_mod - 1)) == (cols & (col_mod - 1))


def conv_body(
    inner, above, below, left, right, conv_w, conv_bias, x_proj, into_row, into_col, heads_map, pick_b,
    x_out, coef_out, state_row, state_col,
    padded, x_wide, coef_wide, left_sum, right_sum,
):
    rows_n, cols_n, width = inner.shape
    state_size = state_row.shape[2]
    padded[0] = above[...]
    padded[rows_n + 1] = below[...]

    def move(r, carry):
        padded[r + 1] = inner[r]
        return carry

    lax.fori_loop(0, rows_n, move, 0)
    for edge, column, sums in ((left, 0, left_sum), (right, 2, right_sum)):
        total = jnp.zeros((rows_n, 1, width), F32)
        for i in range(3):
            total = total + edge[i : i + rows_n] * conv_w[3 * i + column : 3 * i + column + 1, :][None]
        sums[...] = total
    first = lax.broadcasted_iota(jnp.int32, (cols_n, LANES), 0) == 0
    last = lax.broadcasted_iota(jnp.int32, (cols_n, LANES), 0) == cols_n - 1

    def row_step(r, carry):
        for part in range(width // LANES):
            lanes = slice(part * LANES, (part + 1) * LANES)
            rows = [padded[r + i, :, lanes].astype(F32) for i in range(3)]
            sums = []
            for j in range(3):
                total = rows[0] * conv_w[j : j + 1, lanes]
                total = total + rows[1] * conv_w[3 + j : 4 + j, lanes]
                sums.append(total + rows[2] * conv_w[6 + j : 7 + j, lanes])
            from_left = jnp.where(first, left_sum[r, :, lanes], pltpu.roll(sums[0], 1, 0))
            from_right = jnp.where(
                last, right_sum[r, :, lanes], pltpu.roll(sums[2], cols_n - 1, 0)
            )
            value = conv_bias[:, lanes] + from_left + sums[1] + from_right
            scanned = (value / (1.0 + jnp.exp(-value))).astype(BF16)
            x_out[r, :, lanes] = scanned
            x_wide[r, :, lanes] = scanned.astype(F32)
        coef = dot(x_out[r], x_proj[...]).astype(BF16)
        coef_out[r] = coef
        coef_wide[r] = coef.astype(F32)
        flipped = coef.T
        for k in range(2):
            scaled = (x_wide[r] * spread(into_row[k, r], heads_map[...])).astype(BF16)
            b_part = flipped[2 * k * state_size : (2 * k + 1) * state_size, :]
            state_row[r, k] = dot(b_part, scaled).astype(BF16)
        return carry

    lax.fori_loop(0, rows_n, row_step, 0)
    size = rows_n * SUB
    own = own_column((LANES, size), SUB, SUB)

    def col_step(g, carry):
        at = pl.ds(pl.multiple_of(g * SUB, SUB), SUB)
        x_group = x_wide[:, at, :].reshape(size, width)
        coef = coef_wide[:, at, :].reshape(size, LANES).astype(BF16)
        for k in range(2):
            scaled = (x_group * spread(into_col[k, g], heads_map[...])).astype(BF16)
            b_part = jnp.where(own, dot_nt(pick_b[k], coef), 0.0).astype(BF16)
            state_col[g, k] = dot(b_part, scaled).astype(BF16)
        return carry

    lax.fori_loop(0, cols_n // SUB, col_step, 0)


def conv_and_states(inner, above, below, left, right, conv_w, conv_bias, x_proj, into_row, into_col, heads_map, pick_b, state_size):
    rows_n, cols_n, width = inner.shape
    outs = (
        jax.ShapeDtypeStruct((rows_n, cols_n, width), BF16),
        jax.ShapeDtypeStruct((rows_n, cols_n, LANES), BF16),
        jax.ShapeDtypeStruct((rows_n, 2, state_size, width), BF16),
        jax.ShapeDtypeStruct((cols_n // SUB, 2, SUB * state_size, width), BF16),
    )
    return call(
        conv_body,
        outs,
        [whole()] * 12,
        [
            pltpu.VMEM((rows_n + 2, cols_n, width), BF16),
            pltpu.VMEM((rows_n, cols_n, width), F32),
            pltpu.VMEM((rows_n, cols_n, LANES), F32),
            pltpu.VMEM((rows_n, 1, width), F32),
            pltpu.VMEM((rows_n, 1, width), F32),
        ],
        name="conv_states",
    )(inner, above, below, left, right, conv_w, conv_bias, x_proj, into_row, into_col, heads_map, pick_b)


def inner_body(
    x_in, coef_in, into_row, out_row, into_col, out_col, heads_map, skip, total_out, x_wide, coef_wide, acc
):
    rows_n, cols_n, width = x_in.shape
    state_size = LANES // 8
    lane = lax.broadcasted_iota(jnp.int32, (1, LANES), 1)
    t_row = lax.broadcasted_iota(jnp.int32, (cols_n, cols_n), 0)
    u_row = lax.broadcasted_iota(jnp.int32, (cols_n, cols_n), 1)
    row_masks = (t_row >= u_row, t_row <= u_row)

    def c_at_b(wide, k):
        rolled = pltpu.roll(wide, LANES - state_size, 1)
        return jnp.where((lane // state_size) == 2 * k, rolled, 0.0).astype(BF16)

    def row_step(r, carry):
        x_row = x_in[r].astype(F32)
        x_wide[r] = x_row
        coef = coef_in[r]
        wide = coef.astype(F32)
        coef_wide[r] = wide
        total = x_row * skip[...]
        for k in range(2):
            scores = dot_nt(c_at_b(wide, k), coef)
            mixing = jnp.where(row_masks[k], scores, 0.0).astype(BF16)
            scaled = (x_row * spread(into_row[k, r], heads_map[...])).astype(BF16)
            total = total + dot(mixing, scaled) * spread(out_row[k, r], heads_map[...])
        acc[r] = total
        return carry

    lax.fori_loop(0, rows_n, row_step, 0)
    size = rows_n * SUB
    t_col = lax.broadcasted_iota(jnp.int32, (size, size), 0)
    u_col = lax.broadcasted_iota(jnp.int32, (size, size), 1)
    same = (t_col & (SUB - 1)) == (u_col & (SUB - 1))
    col_masks = (same & (t_col >= u_col), same & (t_col <= u_col))

    def col_step(g, carry):
        at = pl.ds(pl.multiple_of(g * SUB, SUB), SUB)
        x_group = x_wide[:, at, :].reshape(size, width)
        wide = coef_wide[:, at, :].reshape(size, LANES)
        coef = wide.astype(BF16)
        total = acc[:, at, :].reshape(size, width)
        for k in range(2):
            scores = dot_nt(c_at_b(wide, k + 2), coef)
            mixing = jnp.where(col_masks[k], scores, 0.0).astype(BF16)
            scaled = (x_group * spread(into_col[k, g], heads_map[...])).astype(BF16)
            total = total + dot(mixing, scaled) * spread(out_col[k, g], heads_map[...])
        acc[:, at, :] = total.reshape(rows_n, SUB, width)
        return carry

    lax.fori_loop(0, cols_n // SUB, col_step, 0)

    def emit(r, carry):
        total_out[r] = acc[r].astype(total_out.dtype)
        return carry

    lax.fori_loop(0, rows_n, emit, 0)


def inner_scans(x_in, coef_in, into_row, out_row, into_col, out_col, heads_map, skip):
    return call(
        inner_body,
        jax.ShapeDtypeStruct(x_in.shape, BF16),
        [whole()] * 8,
        [
            pltpu.VMEM(x_in.shape, F32),
            pltpu.VMEM(coef_in.shape, F32),
            pltpu.VMEM(x_in.shape, F32),
        ],
        name="inner_scans",
    )(x_in, coef_in, into_row, out_row, into_col, out_col, heads_map, skip)


def chain_body(states, half, decay, entering):
    peers, units = states.shape[0], states.shape[1]
    deep = states.shape[3]
    lines = half.shape[3]
    width = states.shape[4]
    for k in range(2):
        order = range(peers) if k == 0 else range(peers - 1, -1, -1)
        for unit in range(units):
            for part in range(width // LANES):
                lanes = slice(part * LANES, (part + 1) * LANES)
                before = jnp.zeros((deep, LANES), F32)
                for at in order:
                    scale = half[at, k, unit, :, lanes]
                    keep = decay[at, k, unit, :, lanes]
                    own = states[at, unit, k, :, lanes].astype(F32)
                    if lines > 1:
                        shape = (deep // lines, lines, LANES)
                        scale, keep = scale[None], keep[None]
                        before, own = before.reshape(shape), own.reshape(shape)
                    entering[at, unit, k, :, lanes] = (scale * before).reshape(deep, LANES).astype(BF16)
                    before = (keep * before + scale * own).reshape(deep, LANES)


def chain(states, half, decay):
    return call(
        chain_body, jax.ShapeDtypeStruct(states.shape, BF16), [whole()] * 3, name="chain"
    )(states, half, decay)


def line_factors(total, axis, width, unit_lines):
    peers, index = lax.axis_size(axis), lax.axis_index(axis)
    k, heads, lines = total.shape
    mine = lines // peers
    everyone = lax.all_gather(total, axis)
    ours = lax.dynamic_slice_in_dim(everyone, index * mine, mine, axis=3)
    ours = jnp.transpose(ours, (0, 1, 3, 2)).reshape(peers, k, mine // unit_lines, unit_lines, heads)
    ours = jnp.repeat(ours, width // heads, axis=-1)
    return jnp.exp(-0.5 * ours), jnp.exp(-ours)


def pass_states(states, factors, axis):
    peers = lax.axis_size(axis)
    got = lax.all_to_all(states, axis, split_axis=0, concat_axis=0, tiled=True)
    split = got.reshape((peers, got.shape[0] // peers) + got.shape[1:])
    entering = chain(split, *factors).reshape(states.shape)
    return lax.all_to_all(entering, axis, split_axis=0, concat_axis=0, tiled=True)


def finish_body(
    total, coef_in, enter_row, enter_col, out_row, out_col, heads_map, pick_c, gate_in, grid, out_gain, out_w,
    mlp_gain, ff_in, ff_out, block_out, coef_wide, acc,
):
    rows_n, cols_n, width = total.shape
    state_size = enter_row.shape[2]

    def row_step(r, carry):
        coef = coef_in[r]
        wide = coef.astype(F32)
        coef_wide[r] = wide
        value = total[r].astype(F32)
        for k in range(2):
            c_part = coef[:, (2 * k + 1) * state_size : (2 * k + 2) * state_size]
            value = value + dot(c_part, enter_row[r, k]) * spread(out_row[k, r], heads_map[...])
        acc[r] = value
        return carry

    lax.fori_loop(0, rows_n, row_step, 0)
    size = rows_n * SUB
    own = own_column((size, LANES), SUB, SUB)

    def col_step(g, carry):
        at = pl.ds(pl.multiple_of(g * SUB, SUB), SUB)
        coef = coef_wide[:, at, :].reshape(size, LANES).astype(BF16)
        value = acc[:, at, :].reshape(size, width)
        for k in range(2):
            c_part = jnp.where(own, dot(coef, pick_c[k]), 0.0).astype(BF16)
            value = value + dot(c_part, enter_col[g, k]) * spread(out_col[k, g], heads_map[...])
        acc[:, at, :] = value.reshape(rows_n, SUB, width)
        return carry

    lax.fori_loop(0, cols_n // SUB, col_step, 0)

    def last(r, carry):
        at = pl.ds(pl.multiple_of(r * cols_n, cols_n), cols_n)
        gated = (rms_scale(acc[r], out_gain[...]) * gate_in[at, :].astype(F32)).astype(BF16)
        middle = (dot(gated, out_w[...]) + grid[at, :].astype(F32)).astype(BF16)
        wide = middle.astype(F32)
        normed = rms_scale(wide, mlp_gain[...]).astype(BF16)
        hidden = dot(normed, ff_in[...])
        hidden = (hidden * (0.5 + 0.5 * lax.erf(hidden * (0.5**0.5)))).astype(BF16)
        block_out[r] = (dot(hidden, ff_out[...]) + wide).astype(BF16)
        return carry

    lax.fori_loop(0, rows_n, last, 0)


def finish(total, coef, *rest, channels):
    rows_n, cols_n, width = total.shape
    return call(
        finish_body,
        jax.ShapeDtypeStruct((rows_n, cols_n, channels), BF16),
        [whole()] * 15,
        [pltpu.VMEM(coef.shape, F32), pltpu.VMEM(total.shape, F32)],
        name="finish",
    )(total, coef, *rest)


def shifted(block, axis, up):
    count = lax.axis_size(axis)
    pairs = [(i, i + 1) if up else (i + 1, i) for i in range(count - 1)]
    return lax.ppermute(block, axis, pairs)


def local(
    tile_feats, tile_cell, tile_mask, tile_count, background, norm_gain, in_x, in_z, conv_w, conv_bias, x_proj,
    skip_gain, decay_rate, out_gain, out_w, mlp_gain, ff_in, ff_out,
):
    heads, rows_n, cols_n = decay_rate.shape[1:]
    owners, slots, channels = tile_feats.shape[1:]
    width = in_x.shape[1]
    state_size = x_proj.shape[1] // 8
    cells_n = rows_n * cols_n

    values = jnp.where(tile_mask[0][..., None] == 1, tile_feats[0], background)
    live = jnp.arange(slots, dtype=jnp.int32)[None, :] < tile_count[0][:, None]
    marked = jnp.where(live, tile_cell[0], cells_n)
    where = jnp.stack([marked // 64, marked % 64], axis=-1).astype(BF16)
    where = jnp.pad(where, ((0, 0), (0, 0), (0, 62)))
    sent = jnp.concatenate([values, where], axis=-1)
    got = lax.all_to_all(sent, ("row", "col"), split_axis=0, concat_axis=0, tiled=True)
    got = got.reshape(owners * slots, sent.shape[2])
    cells = got[:, channels].astype(jnp.int32) * 64 + got[:, channels + 1].astype(jnp.int32)

    into_row, out_row, into_col, out_col, total_row, total_col = decay_factors(decay_rate)
    row_factors = line_factors(total_row, "col", width, 1)
    col_factors = line_factors(total_col, "row", width, SUB)
    head_of = jnp.arange(width, dtype=jnp.int32) // (width // heads)
    part_of = jnp.arange(16, dtype=jnp.int32)
    heads_map = (
        ((part_of % heads)[:, None] == head_of[None, :]) & (part_of < 2 * heads)[:, None]
    ).astype(BF16)
    lane = jnp.arange(LANES, dtype=jnp.int32)
    picks = [
        (lane[:, None] == (m * state_size + lane // SUB)[None, :]).astype(BF16) for m in range(4, 8)
    ]
    pick_b = jnp.stack([picks[0].T, picks[2].T])
    pick_c = jnp.stack([picks[1], picks[3]])

    grid, inner, left_edge, right_edge = place(
        cells, got, norm_gain[None], in_x, rows_n, cols_n, channels
    )
    from_left = shifted(right_edge, "col", True).astype(BF16)
    from_right = shifted(left_edge, "col", False).astype(BF16)
    top = jnp.concatenate([inner[:cols_n], from_left[:1], from_right[:1]])
    bottom = jnp.concatenate([inner[cells_n - cols_n :], from_left[rows_n - 1 :], from_right[rows_n - 1 :]])
    above = shifted(bottom, "row", True)
    below = shifted(top, "row", False)
    gated = gate(grid, norm_gain[None], in_z)
    left = jnp.concatenate([above[cols_n : cols_n + 1], from_left, below[cols_n : cols_n + 1]])[:, None].astype(F32)
    right = jnp.concatenate([above[cols_n + 1 :], from_right, below[cols_n + 1 :]])[:, None].astype(F32)

    x_in, coef, state_row, state_col = conv_and_states(
        inner.reshape(rows_n, cols_n, width), above[:cols_n], below[:cols_n], left, right,
        conv_w.reshape(9, width), conv_bias[None], x_proj, into_row, into_col, heads_map, pick_b, state_size,
    )
    enter_col = pass_states(state_col, col_factors, "row")
    enter_row = pass_states(state_row, row_factors, "col")
    total = inner_scans(x_in, coef, into_row, out_row, into_col, out_col, heads_map, skip_gain[None])
    return finish(
        total, coef, enter_row, enter_col, out_row, out_col, heads_map, pick_c, gated, grid, out_gain[None], out_w,
        mlp_gain[None], ff_in, ff_out, channels=channels,
    )


def solution(mesh):
    spread_all = (
        P(("row", "col"), None, None, None),
        P(("row", "col"), None, None),
        P(("row", "col"), None, None),
        P(("row", "col"), None),
    )
    placed = spread_all + (P(),) * 8 + (P(None, None, "row", "col"),) + (P(),) * 5
    return jax.shard_map(
        local, mesh=mesh, in_specs=placed, out_specs=P("row", "col", None), check_vma=False
    )
```

time: 1050 us -> 350 us (0.33); the launches traced: 1030 us -> 349 us
  matrix products: 331 us -> 1.3 us
  other arithmetic: 301 us -> 12.6 us
  local copies, waits for them, and re-layouts: 253 us -> 46.7 us
  Pallas kernels: 0 us -> 170 us
  blocking collectives: 71.8 us -> 51.3 us
  between operations: 13.9 us -> 0.42 us
    dot_general x69 -> x4, matrix products: 331 us -> 1.3 us  [the longest x1 0.36 us: decay_factors(): jnp.einsum('huc,ut->htc', decay[2], upto_r, precision=exact)]
    pallas_call x0 -> x7, Pallas kernels: none -> 170 us  [the longest x1 47.5 us: finish(): call(finish_body, jax.ShapeDtypeStruct((rows_n, cols_n, channels), BF16),...]
    select_n x51 -> x3, other arithmetic: 168 us -> 0.83 us  [the longest x1 0.81 us: local(): values = jnp.where(tile_mask[0][..., None] == 1, tile_feats[0], background)]
    rev x15 -> x0, local copies, waits for them, and re-layouts: 62.8 us -> none  [the longest x2 27.5 us: restore(): result = jnp.flip(result, 1)]
    another operation x20 -> x4, other arithmetic: 58.1 us -> 2.03 us  [block_parts(): cumulative = jnp.cumsum(rates, axis=2)]
    all_gather x4 -> x2, blocking collectives: 71.8 us -> 30.7 us  [line_factors(): everyone = lax.all_gather(total, axis)]
    transpose x30 -> x2, local copies, waits for them, and re-layouts: 43.9 us -> 6.7 us  [col_layout(): jnp.transpose(parts, (0, 3, 1, 2, 4)).reshape(k, c // SUB, m, r * SUB)]
    transpose x20 -> x0, other arithmetic: 28.4 us -> none  [block_parts(): scaled = x_vals.astype(jnp.float32) * jnp.swapaxes(weight, 1, 2)[..., None]]
  transfers between devices with their start and end apart: 10 -> 8, of which waited for: 4 -> 5; matrix products, arithmetic and copies ran while one was open for 62% -> 12% of each run, Pallas kernels for 0% -> 17%
where the time goes in v1:
time: 350 us; the launch traced here: 349 us
  Pallas kernels  170 us (49%)
  blocking collectives  51.3 us (15%)
  local copies, waits for them, and re-layouts  46.7 us (13%)
  starting transfers between devices  35 us (10%)
  waiting for transfers between devices  31.8 us (9%)
  other arithmetic  12.6 us (4%)
    pallas_call x1, Pallas kernels, finish(): call(finish_body, jax.ShapeDtypeStruct((rows_n, cols_n, channels), BF16),...  47.5 us
    pallas_call x1, Pallas kernels, inner_scans(): call(inner_body, jax.ShapeDtypeStruct(x_in.shape, BF16), [whole()] * 8, [...  38 us
    pallas_call x1, Pallas kernels, conv_and_states(): call(conv_body, outs, [whole()] * 12, [pltpu.VMEM((rows_n + 2, cols_n, wi...  37.9 us
    all_gather x2, blocking collectives, line_factors(): everyone = lax.all_gather(total, axis)  30.7 us
    pallas_call x1, Pallas kernels, place(): call(place_body, outs, [pl.BlockSpec(memory_space=pltpu.SMEM), whole(), w...  26.5 us
    all_to_all x1, blocking collectives, pass_states(): got = lax.all_to_all(states, axis, split_axis=0, concat_axis=0, tiled=True)  20.5 us
    all_to_all x1, waiting for transfers between devices, local(): lax.all_to_all(sent, ('row', 'col'), split_axis=0, concat_axis=0, tiled=T...  16 us
    pallas_call x1, Pallas kernels, gate(): call(functools.partial(gate_body, block=128), jax.ShapeDtypeStruct((grid....  12.5 us
  transfers between devices with their start and end apart: 8, of which 5 were waited for; matrix products, arithmetic and copies ran while one was open for 12% of the time, Pallas kernels for 17%

profile of v1, /device:TPU:1, one launch (start us, length us, event | category | flops | bytes accessed | tf_op | source)
XLA Modules:
  0.0 348.7 jit_solution(10043749456364091354)
XLA Ops:
  0.0 0.7 fusion.40
  0.8 1.7 copy.161
  2.5 3.3 copy.122
  5.9 0.8 bitcast_select_fusion
  6.8 2.1 fusion.1
  8.8 11.5 %all-to-all-start = ((bf16[128,32,256]{2,1,0:T(8,128)(2,1)}), bf16[128,32,256]{2,1,0:T(8,128)(2,1)S(1)}, u32[]{:S(2)}, u32[]{:S(2)}) async-start(bf16[128,32,256]{2,1,0:T(8,128)(2,1)} %fusion.1), calls=%async_computation | async-start | bytes 4194304 | tf_op jit(solution)/shard_map/all_to_all | solution.py:491
  22.4 0.6 reduce-precision_convert_fusion
  23.1 1.3 fusion.8
  24.3 0.7 fusion.68
  25.6 2.8 copy.134
  28.4 2.5 copy.135.into_col
  30.9 0.6 reshape.510.conv_w
  31.5 0.6 broadcast_in_dim.86.conv_bias
  32.3 0.6 add_convert_fusion.pick_b
  33.0 0.7 and_convert_fusion.heads_map
  33.6 16.0 %all-to-all-done = bf16[128,32,256]{2,1,0:T(8,128)(2,1)S(1)} async-done(((bf16[128,32,256]{2,1,0:T(8,128)(2,1)}), bf16[128,32,256]{2,1,0:T(8,128)(2,1)S(1)}, u32[]{:S(2)}, u32[]{:S(2)}) %all-to-all-start) | async-done | bytes 2097184 | tf_op jit(solution)/shard_map/all_to_all | solution.py:491
  49.6 2.0 add_reduce_fusion.cells
  51.7 26.5 %place_norm_project.1 = (bf16[4096,192]{1,0:T(8,128)(2,1)}, bf16[4096,384]{1,0:T(8,128)(2,1)}, f32[32,384]{1,0:T(8,128)}, f32[32,384]{1,0:T(8,128)}) custom-call(s32[4096]{0:T(1024)} %add_reduce_fusion.cells, bf16[4096,256]{1,0:T(8,128)(2,1)} %bitcast.115, f32[1,192]{1,0:T(1,128)} %bitcast.135, bf16[192,384]{1,0:T(8,128)(2,1)} %in_x.1), custom_call_target="tpu_custom_call" | custom-call | tf_op jit(solution)/shard_map/place_norm_project/pallas_call | solution.py:157
  78.1 0.8 convert.13
  78.9 3.0 collective-permute-start
  82.0 1.0 fusion.66
  82.9 0.8 convert.12
  83.7 1.3 collective-permute-start.1
  85.1 3.2 collective-permute-done.1
  88.3 4.1 %collective-permute-start.3 = (bf16[130,384]{1,0:T(8,128)(2,1)S(1)}, bf16[130,384]{1,0:T(8,128)(2,1)S(1)}, u32[]{:S(2)}, u32[]{:S(2)}) collective-permute-start(bf16[130,384]{1,0:T(8,128)(2,1)S(1)} %pad_maximum_fusion.2), channel_id=1, source_target_pairs={{16,0},{32,16},{48,32},{64,48},{80,64},{96,80},{112,96},{17,1},{33... | collective-permute-start | bytes 299528 | tf_op jit(solution)/shard_map/ppermute | solution.py:472
  92.4 2.5 collective-permute-start.2
  95.3 1.3 collective-permute-done.2
  96.6 0.8 maximum_convert_fusion
  97.4 0.6 slice.103.below
  98.1 0.7 slice.100.above
  98.7 37.9 %conv_states.1 = (bf16[32,128,384]{2,1,0:T(8,128)(2,1)}, bf16[32,128,128]{2,1,0:T(8,128)(2,1)}, bf16[32,2,16,384]{3,2,1,0:T(8,128)(2,1)}, bf16[16,2,128,384]{3,2,1,0:T(8,128)(2,1)}) custom-call(bf16[32,128,384]{2,1,0:T(8,128)(2,1)} %bitcast.122, bf16[128,384]{1,0:T(8,128)(2,1)} %slice.100.above, bf16[128,384]{1,0:T(8,128)(2,1)} %slice.103.below, ...), custom_call_target="tpu_custom_call" | custom-call | tf_op jit(solution)/shard_map/conv_states/pallas_call | solution.py:274
  136.6 20.5 %all_to_all.25 = bf16[32,2,16,384]{3,2,1,0:T(8,128)(2,1)} all-to-all(bf16[32,2,16,384]{3,2,1,0:T(8,128)(2,1)} %get-tuple-element.18), channel_id=1, replica_groups=mesh['row'=8,'col'=16] {'col'}, dimensions={0} | all-to-all | bytes 1572864 | tf_op jit(solution)/shard_map/all_to_all | solution.py:404
  157.2 4.7 %all-to-all-start.3 = ((bf16[16,2,128,384]{3,2,1,0:T(8,128)(2,1)}), bf16[16,2,128,384]{3,2,1,0:T(8,128)(2,1)S(1)}, u32[]{:S(2)}, u32[]{:S(2)}) async-start(bf16[16,2,128,384]{3,2,1,0:T(8,128)(2,1)} %get-tuple-element.19), calls=%async_computation.3 | async-start | bytes 6291456 | tf_op jit(solution)/shard_map/all_to_all | solution.py:404
  161.8 17.3 %all-gather = f32[32,6,32]{2,1,0:T(8,128)S(1)} all-gather(f32[2,6,32]{2,1,0:T(8,128)S(1)} %get-tuple-element.21), channel_id=2, replica_groups=mesh['row'=8,'col'=16] {'col'}, dimensions={0}, use_global_device_ids=true | all-gather | bytes 26112 | tf_op jit(solution)/shard_map/all_gather | solution.py:395
  179.2 0.9 copy.140
  180.1 0.9 broadcast_in_dim.94
  181.0 0.7 exp.42
  181.8 1.6 copy.142.half
  183.4 0.9 copy.141
  184.3 0.9 broadcast_in_dim.95
  185.3 0.7 copy.143.decay
  186.0 2.4 chain.2
  188.4 11.0 %all-to-all-done.3 = bf16[16,2,128,384]{3,2,1,0:T(8,128)(2,1)S(1)} async-done(((bf16[16,2,128,384]{3,2,1,0:T(8,128)(2,1)}), bf16[16,2,128,384]{3,2,1,0:T(8,128)(2,1)S(1)}, u32[]{:S(2)}, u32[]{:S(2)}) %all-to-all-start.3) | async-done | bytes 3145760 | tf_op jit(solution)/shard_map/all_to_all | solution.py:404
  199.4 4.3 %all-to-all-start.2 = ((bf16[32,2,16,384]{3,2,1,0:T(8,128)(2,1)}), bf16[32,2,16,384]{3,2,1,0:T(8,128)(2,1)}, u32[]{:S(2)}, u32[]{:S(2)}) async-start(bf16[32,2,16,384]{3,2,1,0:T(8,128)(2,1)} %bitcast.123), calls=%async_computation.2 | async-start | bytes 1572864 | tf_op jit(solution)/shard_map/all_to_all | solution.py:407
  203.7 13.4 %all-gather.1 = f32[16,6,128]{2,1,0:T(8,128)S(1)} all-gather(f32[2,6,128]{2,1,0:T(8,128)S(1)} %get-tuple-element.22), channel_id=3, replica_groups=mesh['row'=8,'col'=16] {'row'}, dimensions={0}, use_global_device_ids=true | all-gather | bytes 55296 | tf_op jit(solution)/shard_map/all_gather | solution.py:395
  217.5 1.3 broadcast_in_dim.96
  218.8 2.2 exp.49.half
  221.5 1.0 exp.53.decay
  222.5 4.8 %chain.3 = bf16[8,2,2,128,384]{4,3,2,1,0:T(8,128)(2,1)} custom-call(bf16[8,2,2,128,384]{4,3,2,1,0:T(8,128)(2,1)} %bitcast.116, f32[8,2,2,8,384]{4,3,2,1,0:T(8,128)} %exp.49.half, f32[8,2,2,8,384]{4,3,2,1,0:T(8,128)} %exp.53.decay), custom_call_target="tpu_custom_call" | custom-call | tf_op jit(solution)/shard_map/chain/pallas_call | solution.py:386
  227.3 3.7 %all-to-all-start.4 = ((bf16[16,2,128,384]{3,2,1,0:T(8,128)(2,1)}), bf16[16,2,128,384]{3,2,1,0:T(8,128)(2,1)S(1)}, u32[]{:S(2)}, u32[]{:S(2)}) async-start(bf16[16,2,128,384]{3,2,1,0:T(8,128)(2,1)} %bitcast.117), calls=%async_computation.4 | async-start | bytes 6291456 | tf_op jit(solution)/shard_map/all_to_all | solution.py:407
  231.1 1.8 fusion.67
  232.8 1.4 copy.136
  234.2 3.9 %copy.137 = bf16[2,16,16,32,8]{2,4,3,1,0:T(8,128)(2,1)} copy(bf16[2,16,16,32,8]{3,4,1,2,0:T(8,128)(2,1)} %bitcast.121) | data formatting | bytes 524288 | tf_op jit(solution)/shard_map/transpose | solution.py:67
  238.2 2.5 copy.139.out_col
  240.7 0.6 broadcast_in_dim.93.skip
  241.3 0.9 copy.151.ff_out
  242.2 1.7 copy.150.out_w
  243.9 0.6 broadcast_in_dim.98.out_gain
  244.5 0.6 add_convert_fusion.1.pick_c
  245.2 12.5 %gate.1.gate_in = bf16[4096,384]{1,0:T(8,128)(2,1)} custom-call(bf16[4096,192]{1,0:T(8,128)(2,1)} %get-tuple-element.20.grid, f32[1,192]{1,0:T(1,128)} %bitcast.136, bf16[192,384]{1,0:T(8,128)(2,1)} %in_z.1), custom_call_target="tpu_custom_call" | custom-call | tf_op jit(solution)/shard_map/gate/pallas_call | solution.py:181
  257.7 38.0 %inner_scans.1.total = bf16[32,128,384]{2,1,0:T(8,128)(2,1)} custom-call(bf16[32,128,384]{2,1,0:T(8,128)(2,1)} %get-tuple-element.16.x_in, bf16[32,128,128]{2,1,0:T(8,128)(2,1)} %get-tuple-element.17.coef_in, bf16[2,32,16,128]{3,2,1,0:T(8,128)(2,1)} %get-tuple-element.34.into_row, bf16[2,32,16,128]{3,2,1,0:T(8,128)(2,1)} %get-tuple-element.32.out_row, ...), custom_call_target="tpu_custom_call" | custom-call | tf_op jit(solution)/shard_map/inner_scans/pallas_call | solution.py:349
  295.7 1.6 copy-done.2
  297.3 47.5 %finish.1 = bf16[32,128,192]{2,1,0:T(8,128)(2,1)} custom-call(bf16[32,128,384]{2,1,0:T(8,128)(2,1)} %inner_scans.1.total, bf16[32,128,128]{2,1,0:T(8,128)(2,1)} %get-tuple-element.17.coef_in, bf16[32,2,16,384]{3,2,1,0:T(8,128)(2,1)} %all-to-all-done.2.enter_row, bf16[16,2,128,384]{3,2,1,0:T(8,128)(2,1)} %copy-done.2, ...), custom_call_target="tpu_custom_call" | custom-call | tf_op jit(solution)/shard_map/finish/pallas_call | solution.py:460
  344.8 3.9 %copy.152 = bf16[32,128,192]{1,2,0:T(8,128)(2,1)} copy(bf16[32,128,192]{2,1,0:T(8,128)(2,1)} %finish.1) | data formatting | bytes 3145728 | tf_op jit(solution)/shard_map/finish/pallas_call | solution.py:460
  (68 shorter events, 4.4 us)
Async XLA Ops:
  2.5 3.3 copy-start.6
  2.5 3.5 copy-start.10
  8.8 11.5 %copy-start.3 = (f32[4,6,32,128]{3,2,1,0:T(8,128)S(1)}, f32[4,6,32,128]{3,2,1,0:T(8,128)}, u32[]{:S(2)}) copy-start(f32[4,6,32,128]{3,2,1,0:T(8,128)} %param.30) | copy-start | bytes 1179652
  8.8 40.8 %all-to-all-start = ((bf16[128,32,256]{2,1,0:T(8,128)(2,1)}), bf16[128,32,256]{2,1,0:T(8,128)(2,1)S(1)}, u32[]{:S(2)}, u32[]{:S(2)}) async-start(bf16[128,32,256]{2,1,0:T(8,128)(2,1)} %fusion.1), calls=%async_computation | async-start | bytes 4194304 | tf_op jit(solution)/shard_map/all_to_all | solution.py:491
  25.6 5.3 %copy-start.5 = (f32[3,3,384]{2,1,0:T(4,128)S(1)}, f32[3,3,384]{2,1,0:T(4,128)}, u32[]{:S(2)}) copy-start(f32[3,3,384]{2,1,0:T(4,128)} %param.26) | copy-start | bytes 41476
  25.6 5.9 %copy-start.7 = (f32[384]{0:T(512)S(1)}, f32[384]{0:T(512)}, u32[]{:S(2)}) copy-start(f32[384]{0:T(512)} %param.27) | copy-start | bytes 4612
  49.6 2.0 copy-start
  78.9 6.1 %collective-permute-start = (bf16[32,384]{1,0:T(8,128)(2,1)S(1)}, bf16[32,384]{1,0:T(8,128)(2,1)S(1)}, u32[]{:S(2)}, u32[]{:S(2)}) collective-permute-start(bf16[32,384]{1,0:T(8,128)(2,1)S(1)} %convert.13), channel_id=1, source_target_pairs={{0,1},{1,2},{2,3},{3,4},{4,5},{5,6},{6,7},{7,8},{8,9},{9,10},{10,1... | collective-permute-start | bytes 73736 | tf_op jit(solution)/shard_map/ppermute | solution.py:472
  83.7 4.6 %collective-permute-start.1 = (bf16[32,384]{1,0:T(8,128)(2,1)S(1)}, bf16[32,384]{1,0:T(8,128)(2,1)S(1)}, u32[]{:S(2)}, u32[]{:S(2)}) collective-permute-start(bf16[32,384]{1,0:T(8,128)(2,1)S(1)} %convert.12), channel_id=1, source_target_pairs={{1,0},{2,1},{3,2},{4,3},{5,4},{6,5},{7,6},{8,7},{9,8},{10,9},{11,1... | collective-permute-start | bytes 73736 | tf_op jit(solution)/shard_map/ppermute | solution.py:472
  88.3 7.0 %collective-permute-start.3 = (bf16[130,384]{1,0:T(8,128)(2,1)S(1)}, bf16[130,384]{1,0:T(8,128)(2,1)S(1)}, u32[]{:S(2)}, u32[]{:S(2)}) collective-permute-start(bf16[130,384]{1,0:T(8,128)(2,1)S(1)} %pad_maximum_fusion.2), channel_id=1, source_target_pairs={{16,0},{32,16},{48,32},{64,48},{80,64},{96,80},{112,96},{17,1},{33... | collective-permute-start | bytes 299528 | tf_op jit(solution)/shard_map/ppermute | solution.py:472
  92.4 4.2 %collective-permute-start.2 = (bf16[130,384]{1,0:T(8,128)(2,1)S(1)}, bf16[130,384]{1,0:T(8,128)(2,1)S(1)}, u32[]{:S(2)}, u32[]{:S(2)}) collective-permute-start(bf16[130,384]{1,0:T(8,128)(2,1)S(1)} %pad_maximum_fusion.1), channel_id=1, source_target_pairs={{0,16},{16,32},{32,48},{48,64},{64,80},{80,96},{96,112},{1,17},{17... | collective-permute-start | bytes 299528 | tf_op jit(solution)/shard_map/ppermute | solution.py:472
  157.2 42.2 %all-to-all-start.3 = ((bf16[16,2,128,384]{3,2,1,0:T(8,128)(2,1)}), bf16[16,2,128,384]{3,2,1,0:T(8,128)(2,1)S(1)}, u32[]{:S(2)}, u32[]{:S(2)}) async-start(bf16[16,2,128,384]{3,2,1,0:T(8,128)(2,1)} %get-tuple-element.19), calls=%async_computation.3 | async-start | bytes 6291456 | tf_op jit(solution)/shard_map/all_to_all | solution.py:404
  199.4 21.6 %copy-start.1 = (bf16[16,2,128,384]{3,2,1,0:T(8,128)(2,1)}, bf16[16,2,128,384]{3,2,1,0:T(8,128)(2,1)S(1)}, u32[]{:S(2)}) copy-start(bf16[16,2,128,384]{3,2,1,0:T(8,128)(2,1)S(1)} %all-to-all-done.3) | copy-start | bytes 9437188
  199.4 27.9 %all-to-all-start.2 = ((bf16[32,2,16,384]{3,2,1,0:T(8,128)(2,1)}), bf16[32,2,16,384]{3,2,1,0:T(8,128)(2,1)}, u32[]{:S(2)}, u32[]{:S(2)}) async-start(bf16[32,2,16,384]{3,2,1,0:T(8,128)(2,1)} %bitcast.123), calls=%async_computation.2 | async-start | bytes 1572864 | tf_op jit(solution)/shard_map/all_to_all | solution.py:407
  227.3 68.4 %all-to-all-start.4 = ((bf16[16,2,128,384]{3,2,1,0:T(8,128)(2,1)}), bf16[16,2,128,384]{3,2,1,0:T(8,128)(2,1)S(1)}, u32[]{:S(2)}, u32[]{:S(2)}) async-start(bf16[16,2,128,384]{3,2,1,0:T(8,128)(2,1)} %bitcast.117), calls=%async_computation.4 | async-start | bytes 6291456 | tf_op jit(solution)/shard_map/all_to_all | solution.py:407
  234.2 6.4 %copy-start.8 = (f32[384]{0:T(512)S(1)}, f32[384]{0:T(512)}, u32[]{:S(2)}) copy-start(f32[384]{0:T(512)} %param.29) | copy-start | bytes 4612
  234.2 7.0 %copy-start.4 = (bf16[768,192]{0,1:T(8,128)(2,1)S(1)}, bf16[768,192]{0,1:T(8,128)(2,1)}, u32[]{:S(2)}) copy-start(bf16[768,192]{0,1:T(8,128)(2,1)} %param.35) | copy-start | bytes 884740
  238.2 5.8 %copy-start.9 = (f32[384]{0:T(512)S(1)}, f32[384]{0:T(512)}, u32[]{:S(2)}) copy-start(f32[384]{0:T(512)} %param.31) | copy-start | bytes 4612
  295.7 1.6 copy-start.2

commit v2 on v1

--- a/solution.py
+++ b/solution.py
@@ -8,6 +8,8 @@
 
 F32 = jnp.float32
 BF16 = jnp.bfloat16
+BLOCK = 1024
+UNROLL = 4
 LANES = 128
 SUB = 8
 VMEM_BYTES = 58 * 1024 * 1024
@@ -27,6 +29,15 @@
         compiler_params=pltpu.CompilerParams(vmem_limit_bytes=VMEM_BYTES),
         name=name,
     )
+
+
+def loop(count, step, unroll=1):
+    def body(i, carry):
+        for j in range(unroll):
+            step(i * unroll + j)
+        return carry
+
+    lax.fori_loop(0, count // unroll, body, 0)
 
 
 def dot(a, b):
@@ -142,7 +153,7 @@
         right_out[pl.ds(r, 1), :] = wide[cols_n - 1 :]
         return carry
 
-    lax.fori_loop(0, cells_n // cols_n, project, 0)
+    loop(cells_n // cols_n, lambda r: project(r, 0), UNROLL)
 
 
 def place(cells, got, gain, in_x, rows_n, cols_n, channels):
@@ -179,7 +190,7 @@
 
 def gate(grid, gain, in_z):
     return call(
-        functools.partial(gate_body, block=128),
+        functools.partial(gate_body, block=BLOCK),
         jax.ShapeDtypeStruct((grid.shape[0], in_z.shape[1]), BF16),
         [whole()] * 3,
         name="gate",
@@ -246,7 +257,7 @@
             state_row[r, k] = dot(b_part, scaled).astype(BF16)
         return carry
 
-    lax.fori_loop(0, rows_n, row_step, 0)
+    loop(rows_n, lambda r: row_step(r, 0), UNROLL)
     size = rows_n * SUB
     own = own_column((LANES, size), SUB, SUB)
 
@@ -260,7 +271,7 @@
             state_col[g, k] = dot(b_part, scaled).astype(BF16)
         return carry
 
-    lax.fori_loop(0, cols_n // SUB, col_step, 0)
+    loop(cols_n // SUB, lambda g: col_step(g, 0), UNROLL)
 
 
 def conv_and_states(inner, above, below, left, right, conv_w, conv_bias, x_proj, into_row, into_col, heads_map, pick_b, state_size):
@@ -286,77 +297,87 @@
     )(inner, above, below, left, right, conv_w, conv_bias, x_proj, into_row, into_col, heads_map, pick_b)
 
 
-def inner_body(
-    x_in, coef_in, into_row, out_row, into_col, out_col, heads_map, skip, total_out, x_wide, coef_wide, acc
-):
-    rows_n, cols_n, width = x_in.shape
+def c_at_b(wide, k):
     state_size = LANES // 8
     lane = lax.broadcasted_iota(jnp.int32, (1, LANES), 1)
+    rolled = pltpu.roll(wide, LANES - state_size, 1)
+    return jnp.where((lane // state_size) == 2 * k, rolled, 0.0).astype(BF16)
+
+
+def inner_row_body(x_in, coef_in, into_row, out_row, heads_map, skip, total_out):
+    rows_n, cols_n, width = x_in.shape
     t_row = lax.broadcasted_iota(jnp.int32, (cols_n, cols_n), 0)
     u_row = lax.broadcasted_iota(jnp.int32, (cols_n, cols_n), 1)
-    row_masks = (t_row >= u_row, t_row <= u_row)
-
-    def c_at_b(wide, k):
-        rolled = pltpu.roll(wide, LANES - state_size, 1)
-        return jnp.where((lane // state_size) == 2 * k, rolled, 0.0).astype(BF16)
-
-    def row_step(r, carry):
+    masks = (t_row >= u_row, t_row <= u_row)
+
+    def row_step(r):
         x_row = x_in[r].astype(F32)
-        x_wide[r] = x_row
         coef = coef_in[r]
         wide = coef.astype(F32)
-        coef_wide[r] = wide
         total = x_row * skip[...]
         for k in range(2):
             scores = dot_nt(c_at_b(wide, k), coef)
-            mixing = jnp.where(row_masks[k], scores, 0.0).astype(BF16)
+            mixing = jnp.where(masks[k], scores, 0.0).astype(BF16)
             scaled = (x_row * spread(into_row[k, r], heads_map[...])).astype(BF16)
             total = total + dot(mixing, scaled) * spread(out_row[k, r], heads_map[...])
-        acc[r] = total
-        return carry
-
-    lax.fori_loop(0, rows_n, row_step, 0)
+        total_out[r] = total.astype(BF16)
+
+    loop(rows_n, row_step, UNROLL)
+
+
+def inner_row(x_in, coef_in, into_row, out_row, heads_map, skip):
+    return call(
+        inner_row_body, jax.ShapeDtypeStruct(x_in.shape, BF16), [whole()] * 6, name="inner_row"
+    )(x_in, coef_in, into_row, out_row, heads_map, skip)
+
+
+def inner_col_body(x_in, coef_in, into_col, out_col, heads_map, total_out, x_wide, coef_wide, acc):
+    rows_n, cols_n, width = x_in.shape
+
+    def widen(r):
+        x_wide[r] = x_in[r].astype(F32)
+        coef_wide[r] = coef_in[r].astype(F32)
+
+    loop(rows_n, widen, UNROLL)
     size = rows_n * SUB
     t_col = lax.broadcasted_iota(jnp.int32, (size, size), 0)
     u_col = lax.broadcasted_iota(jnp.int32, (size, size), 1)
     same = (t_col & (SUB - 1)) == (u_col & (SUB - 1))
-    col_masks = (same & (t_col >= u_col), same & (t_col <= u_col))
-
-    def col_step(g, carry):
+    masks = (same & (t_col >= u_col), same & (t_col <= u_col))
+
+    def col_step(g):
         at = pl.ds(pl.multiple_of(g * SUB, SUB), SUB)
         x_group = x_wide[:, at, :].reshape(size, width)
         wide = coef_wide[:, at, :].reshape(size, LANES)
         coef = wide.astype(BF16)
-        total = acc[:, at, :].reshape(size, width)
+        total = jnp.zeros((size, width), F32)
         for k in range(2):
             scores = dot_nt(c_at_b(wide, k + 2), coef)
-            mixing = jnp.where(col_masks[k], scores, 0.0).astype(BF16)
+            mixing = jnp.where(masks[k], scores, 0.0).astype(BF16)
             scaled = (x_group * spread(into_col[k, g], heads_map[...])).astype(BF16)
             total = total + dot(mixing, scaled) * spread(out_col[k, g], heads_map[...])
         acc[:, at, :] = total.reshape(rows_n, SUB, width)
-        return carry
-
-    lax.fori_loop(0, cols_n // SUB, col_step, 0)
-
-    def emit(r, carry):
-        total_out[r] = acc[r].astype(total_out.dtype)
-        return carry
-
-    lax.fori_loop(0, rows_n, emit, 0)
-
-
-def inner_scans(x_in, coef_in, into_row, out_row, into_col, out_col, heads_map, skip):
-    return call(
-        inner_body,
+
+    loop(cols_n // SUB, col_step, UNROLL)
+
+    def emit(r):
+        total_out[r] = acc[r].astype(BF16)
+
+    loop(rows_n, emit, UNROLL)
+
+
+def inner_col(x_in, coef_in, into_col, out_col, heads_map):
+    return call(
+        inner_col_body,
         jax.ShapeDtypeStruct(x_in.shape, BF16),
-        [whole()] * 8,
+        [whole()] * 5,
         [
             pltpu.VMEM(x_in.shape, F32),
             pltpu.VMEM(coef_in.shape, F32),
             pltpu.VMEM(x_in.shape, F32),
         ],
-        name="inner_scans",
-    )(x_in, coef_in, into_row, out_row, into_col, out_col, heads_map, skip)
+        name="inner_col",
+    )(x_in, coef_in, into_col, out_col, heads_map)
 
 
 def chain_body(states, half, decay, entering):
@@ -399,33 +420,37 @@
     return jnp.exp(-0.5 * ours), jnp.exp(-ours)
 
 
-def pass_states(states, factors, axis):
+def to_chain(states, axis):
     peers = lax.axis_size(axis)
     got = lax.all_to_all(states, axis, split_axis=0, concat_axis=0, tiled=True)
-    split = got.reshape((peers, got.shape[0] // peers) + got.shape[1:])
-    entering = chain(split, *factors).reshape(states.shape)
+    return got.reshape((peers, got.shape[0] // peers) + got.shape[1:])
+
+
+def from_chain(split, factors, axis):
+    entering = chain(split, *factors)
+    entering = entering.reshape((-1,) + entering.shape[2:])
     return lax.all_to_all(entering, axis, split_axis=0, concat_axis=0, tiled=True)
 
 
 def finish_body(
-    total, coef_in, enter_row, enter_col, out_row, out_col, heads_map, pick_c, gate_in, grid, out_gain, out_w,
+    total_row, total_col, coef_in, enter_row, enter_col, out_row, out_col, heads_map, pick_c, gate_in, grid, out_gain, out_w,
     mlp_gain, ff_in, ff_out, block_out, coef_wide, acc,
 ):
-    rows_n, cols_n, width = total.shape
+    rows_n, cols_n, width = total_row.shape
     state_size = enter_row.shape[2]
 
     def row_step(r, carry):
         coef = coef_in[r]
         wide = coef.astype(F32)
         coef_wide[r] = wide
-        value = total[r].astype(F32)
+        value = total_row[r].astype(F32) + total_col[r].astype(F32)
         for k in range(2):
             c_part = coef[:, (2 * k + 1) * state_size : (2 * k + 2) * state_size]
             value = value + dot(c_part, enter_row[r, k]) * spread(out_row[k, r], heads_map[...])
         acc[r] = value
         return carry
 
-    lax.fori_loop(0, rows_n, row_step, 0)
+    loop(rows_n, lambda r: row_step(r, 0), UNROLL)
     size = rows_n * SUB
     own = own_column((size, LANES), SUB, SUB)
 
@@ -439,7 +464,7 @@
         acc[:, at, :] = value.reshape(rows_n, SUB, width)
         return carry
 
-    lax.fori_loop(0, cols_n // SUB, col_step, 0)
+    loop(cols_n // SUB, lambda g: col_step(g, 0), UNROLL)
 
     def last(r, carry):
         at = pl.ds(pl.multiple_of(r * cols_n, cols_n), cols_n)
@@ -452,18 +477,18 @@
         block_out[r] = (dot(hidden, ff_out[...]) + wide).astype(BF16)
         return carry
 
-    lax.fori_loop(0, rows_n, last, 0)
-
-
-def finish(total, coef, *rest, channels):
+    loop(rows_n, lambda r: last(r, 0), UNROLL)
+
+
+def finish(total, total_col, coef, *rest, channels):
     rows_n, cols_n, width = total.shape
     return call(
         finish_body,
         jax.ShapeDtypeStruct((rows_n, cols_n, channels), BF16),
-        [whole()] * 15,
+        [whole()] * 16,
         [pltpu.VMEM(coef.shape, F32), pltpu.VMEM(total.shape, F32)],
         name="finish",
-    )(total, coef, *rest)
+    )(total, total_col, coef, *rest)
 
 
 def shifted(block, axis, up):
@@ -489,9 +514,6 @@
     where = jnp.pad(where, ((0, 0), (0, 0), (0, 62)))
     sent = jnp.concatenate([values, where], axis=-1)
     got = lax.all_to_all(sent, ("row", "col"), split_axis=0, concat_axis=0, tiled=True)
-    got = got.reshape(owners * slots, sent.shape[2])
-    cells = got[:, channels].astype(jnp.int32) * 64 + got[:, channels + 1].astype(jnp.int32)
-
     into_row, out_row, into_col, out_col, total_row, total_col = decay_factors(decay_rate)
     row_factors = line_factors(total_row, "col", width, 1)
     col_factors = line_factors(total_col, "row", width, SUB)
@@ -507,6 +529,12 @@
     pick_b = jnp.stack([picks[0].T, picks[2].T])
     pick_c = jnp.stack([picks[1], picks[3]])
 
+    got = got.reshape(owners * slots, sent.shape[2])
+    ready = (into_row, out_row, into_col, out_col, row_factors, col_factors, heads_map, pick_b, pick_c)
+    got, ready = lax.optimization_barrier((got, ready))
+    into_row, out_row, into_col, out_col, row_factors, col_factors, heads_map, pick_b, pick_c = ready
+    cells = got[:, channels].astype(jnp.int32) * 64 + got[:, channels + 1].astype(jnp.int32)
+
     grid, inner, left_edge, right_edge = place(
         cells, got, norm_gain[None], in_x, rows_n, cols_n, channels
     )
@@ -516,7 +544,6 @@
     bottom = jnp.concatenate([inner[cells_n - cols_n :], from_left[rows_n - 1 :], from_right[rows_n - 1 :]])
     above = shifted(bottom, "row", True)
     below = shifted(top, "row", False)
-    gated = gate(grid, norm_gain[None], in_z)
     left = jnp.concatenate([above[cols_n : cols_n + 1], from_left, below[cols_n : cols_n + 1]])[:, None].astype(F32)
     right = jnp.concatenate([above[cols_n + 1 :], from_right, below[cols_n + 1 :]])[:, None].astype(F32)
 
@@ -524,11 +551,16 @@
         inner.reshape(rows_n, cols_n, width), above[:cols_n], below[:cols_n], left, right,
         conv_w.reshape(9, width), conv_bias[None], x_proj, into_row, into_col, heads_map, pick_b, state_size,
     )
-    enter_col = pass_states(state_col, col_factors, "row")
-    enter_row = pass_states(state_row, row_factors, "col")
-    total = inner_scans(x_in, coef, into_row, out_row, into_col, out_col, heads_map, skip_gain[None])
+    split_col = to_chain(state_col, "row")
+    split_row = to_chain(state_row, "col")
+    gated = gate(grid, norm_gain[None], in_z)
+    total = inner_row(x_in, coef, into_row, out_row, heads_map, skip_gain[None])
+    split_col, split_row, gated, total = lax.optimization_barrier((split_col, split_row, gated, total))
+    enter_col = from_chain(split_col, col_factors, "row")
+    enter_row = from_chain(split_row, row_factors, "col")
+    total_col = inner_col(x_in, coef, into_col, out_col, heads_map)
     return finish(
-        total, coef, enter_row, enter_col, out_row, out_col, heads_map, pick_c, gated, grid, out_gain[None], out_w,
+        total, total_col, coef, enter_row, enter_col, out_row, out_col, heads_map, pick_c, gated, grid, out_gain[None], out_w,
         mlp_gain[None], ff_in, ff_out, channels=channels,
     )
 

time: 350 us -> 336 us (0.960)
  Pallas kernels: 170 us -> 136 us
  blocking collectives: 51.3 us -> 74.9 us
  local copies, waits for them, and re-layouts: 46.7 us -> 37.1 us
  waiting for transfers between devices: 31.8 us -> 35.6 us
    all_gather x2, blocking collectives: 30.7 us -> 54.6 us  [line_factors(): everyone = lax.all_gather(total, axis)]
    all_to_all x3, waiting for transfers between devices: 11 us -> 34 us  [the longest x2 24 us: from_chain(): lax.all_to_all(entering, axis, split_axis=0, concat_axis=0, tiled=True)]
    all_to_all x1, waiting for transfers between devices: 16 us -> 0.01 us  [local(): lax.all_to_all(sent, ('row', 'col'), split_axis=0, concat_axis=0, tiled=T...]
    pallas_call x1, Pallas kernels: 47.5 us -> 34.3 us  [finish(): call(finish_body, jax.ShapeDtypeStruct((rows_n, cols_n, channels), BF16),...]
    pallas_call x2 -> x3, Pallas kernels: 50.5 us -> 41.8 us  [the longest x1 19.1 us: inner_row(): call(inner_row_body, jax.ShapeDtypeStruct(x_in.shape, BF16), [whole()] *...]
    pallas_call x1, Pallas kernels: 37.9 us -> 30.5 us  [conv_and_states(): call(conv_body, outs, [whole()] * 12, [pltpu.VMEM((rows_n + 2, cols_n, wi...]
    optimization_barrier x0 -> x4, local copies, waits for them, and re-layouts: none -> 6.49 us  [local(): got, ready = lax.optimization_barrier((got, ready))]
    exp x10 -> x8, local copies, waits for them, and re-layouts: 8.63 us -> 3.16 us  [line_factors(): return (jnp.exp(-0.5 * ours), jnp.exp(-ours))]
  transfers between devices with their start and end apart: 8 -> 8, of which waited for: 5 -> 5; matrix products, arithmetic and copies ran while one was open for 12% -> 9% of each run, Pallas kernels for 17% -> 14%
where the time goes in v2:
time: 336 us; the launch traced here: 335 us
  Pallas kernels  136 us (40%)
  blocking collectives  74.9 us (22%)
  local copies, waits for them, and re-layouts  37.1 us (11%)
  starting transfers between devices  36.8 us (11%)
  waiting for transfers between devices  35.6 us (11%)
  other arithmetic  13 us (4%)
    all_gather x2, blocking collectives, line_factors(): everyone = lax.all_gather(total, axis)  54.6 us
    pallas_call x1, Pallas kernels, finish(): call(finish_body, jax.ShapeDtypeStruct((rows_n, cols_n, channels), BF16),...  34.3 us
    pallas_call x1, Pallas kernels, conv_and_states(): call(conv_body, outs, [whole()] * 12, [pltpu.VMEM((rows_n + 2, cols_n, wi...  30.5 us
    all_to_all x2, waiting for transfers between devices, from_chain(): lax.all_to_all(entering, axis, split_axis=0, concat_axis=0, tiled=True)  24 us
    pallas_call x1, Pallas kernels, place(): call(place_body, outs, [pl.BlockSpec(memory_space=pltpu.SMEM), whole(), w...  21.5 us
    all_to_all x1, blocking collectives, to_chain(): got = lax.all_to_all(states, axis, split_axis=0, concat_axis=0, tiled=True)  20.4 us
    pallas_call x1, Pallas kernels, inner_row(): call(inner_row_body, jax.ShapeDtypeStruct(x_in.shape, BF16), [whole()] *...  19.1 us
    pallas_call x1, Pallas kernels, inner_col(): call(inner_col_body, jax.ShapeDtypeStruct(x_in.shape, BF16), [whole()] *...  16.2 us
  transfers between devices with their start and end apart: 8, of which 5 were waited for; matrix products, arithmetic and copies ran while one was open for 9% of the time, Pallas kernels for 14%

profile of v2, /device:TPU:1, one launch (start us, length us, event | category | flops | bytes accessed | tf_op | source)
XLA Modules:
  0.0 335.1 jit_solution(6424463115843889115)
XLA Ops:
  0.0 0.7 fusion.40
  0.8 1.7 copy.161
  2.5 3.3 copy.122
  5.9 0.8 bitcast_select_fusion
  6.8 2.0 fusion.1
  8.8 11.5 %all-to-all-start = ((bf16[128,32,256]{2,1,0:T(8,128)(2,1)}), bf16[128,32,256]{2,1,0:T(8,128)(2,1)S(1)}, u32[]{:S(2)}, u32[]{:S(2)}) async-start(bf16[128,32,256]{2,1,0:T(8,128)(2,1)} %fusion.1), calls=%async_computation | async-start | bytes 4194304 | tf_op jit(solution)/shard_map/all_to_all | solution.py:516
  20.8 0.4 fusion.20
  21.1 0.3 fusion.22
  21.9 34.4 %all-gather = f32[32,6,32]{2,1,0:T(8,128)S(1)} all-gather(f32[2,6,32]{2,1,0:T(8,128)S(1)} %get-tuple-element.53), channel_id=2, replica_groups=mesh['row'=8,'col'=16] {'col'}, dimensions={0}, use_global_device_ids=true | all-gather | bytes 26112 | tf_op jit(solution)/shard_map/all_gather | solution.py:416
  56.8 0.6 reduce-precision_convert_fusion
  57.5 0.4 fusion.8
  57.9 0.7 fusion.68
  58.7 0.8 fusion.67
  59.5 0.8 exponential_bitcast_fusion
  60.3 0.5 copy.131
  60.8 2.8 copy.132
  63.6 0.5 copy.133
  64.1 2.8 copy.134
  67.9 20.1 %all-gather.1 = f32[16,6,128]{2,1,0:T(8,128)S(1)} all-gather(f32[2,6,128]{2,1,0:T(8,128)S(1)} %get-tuple-element.54), channel_id=3, replica_groups=mesh['row'=8,'col'=16] {'row'}, dimensions={0}, use_global_device_ids=true | all-gather | bytes 55296 | tf_op jit(solution)/shard_map/all_gather | solution.py:416
  88.7 1.0 exp.79.half
  90.2 1.0 exp.83.decay
  91.2 0.6 reshape.514.conv_w
  91.9 0.6 broadcast_in_dim.96.conv_bias
  92.7 0.6 add_convert_fusion.pick_b
  93.3 0.6 add_convert_fusion.1.pick_c
  94.0 0.7 and_convert_fusion.heads_map
  94.6 2.0 add_reduce_fusion.cells
  96.7 21.5 %place_norm_project.1 = (bf16[4096,192]{1,0:T(8,128)(2,1)}, bf16[4096,384]{1,0:T(8,128)(2,1)}, f32[32,384]{1,0:T(8,128)}, f32[32,384]{1,0:T(8,128)}) custom-call(s32[4096]{0:T(1024)} %add_reduce_fusion.cells, bf16[4096,256]{1,0:T(8,128)(2,1)} %bitcast.115, f32[1,192]{1,0:T(1,128)} %bitcast.135, bf16[192,384]{1,0:T(8,128)(2,1)} %in_x.1), custom_call_target="tpu_custom_call" | custom-call | tf_op jit(solution)/shard_map/place_norm_project/pallas_call | solution.py:168
  118.1 0.8 convert.12
  119.0 1.3 collective-permute-start.1
  120.2 0.8 convert.13
  121.0 4.0 %collective-permute-start = (bf16[32,384]{1,0:T(8,128)(2,1)S(1)}, bf16[32,384]{1,0:T(8,128)(2,1)S(1)}, u32[]{:S(2)}, u32[]{:S(2)}) collective-permute-start(bf16[32,384]{1,0:T(8,128)(2,1)S(1)} %convert.13), channel_id=1, source_target_pairs={{0,1},{1,2},{2,3},{3,4},{4,5},{5,6},{6,7},{7,8},{8,9},{9,10},{10,1... | collective-permute-start | bytes 73736 | tf_op jit(solution)/shard_map/ppermute | solution.py:497
  125.0 1.0 fusion.66
  126.0 2.5 copy.144.into_col
  128.6 2.7 collective-permute-start.3
  131.3 2.9 collective-permute-start.2
  134.6 1.3 collective-permute-done.2
  135.9 0.7 maximum_convert_fusion.left
  136.6 0.7 maximum_convert_fusion.1.right
  137.3 0.6 slice.102.above
  137.9 0.6 slice.105.below
  138.6 30.5 %conv_states.1 = (bf16[32,128,384]{2,1,0:T(8,128)(2,1)}, bf16[32,128,128]{2,1,0:T(8,128)(2,1)}, bf16[32,2,16,384]{3,2,1,0:T(8,128)(2,1)}, bf16[16,2,128,384]{3,2,1,0:T(8,128)(2,1)}) custom-call(bf16[32,128,384]{2,1,0:T(8,128)(2,1)} %bitcast.122, bf16[128,384]{1,0:T(8,128)(2,1)} %slice.102.above, bf16[128,384]{1,0:T(8,128)(2,1)} %slice.105.below, ...), custom_call_target="tpu_custom_call" | custom-call | tf_op jit(solution)/shard_map/conv_states/pallas_call | solution.py:285
  169.0 20.4 %all_to_all.25 = bf16[32,2,16,384]{3,2,1,0:T(8,128)(2,1)} all-to-all(bf16[32,2,16,384]{3,2,1,0:T(8,128)(2,1)} %get-tuple-element.38), channel_id=1, replica_groups=mesh['row'=8,'col'=16] {'col'}, dimensions={0} | all-to-all | bytes 1572864 | tf_op jit(solution)/shard_map/all_to_all | solution.py:425
  189.4 4.1 %all-to-all-start.1 = ((bf16[16,2,128,384]{3,2,1,0:T(8,128)(2,1)}), bf16[16,2,128,384]{3,2,1,0:T(8,128)(2,1)S(1)}, u32[]{:S(2)}, u32[]{:S(2)}) async-start(bf16[16,2,128,384]{3,2,1,0:T(8,128)(2,1)} %get-tuple-element.37), calls=%async_computation.1 | async-start | bytes 6291456 | tf_op jit(solution)/shard_map/all_to_all | solution.py:425
  193.5 0.5 broadcast_in_dim.97.skip
  194.0 0.7 copy.147.half
  194.8 0.7 copy.148.decay
  195.5 6.5 %gate.1.gate_in = bf16[4096,384]{1,0:T(8,128)(2,1)} custom-call(bf16[4096,192]{1,0:T(8,128)(2,1)} %get-tuple-element.39.grid, f32[1,192]{1,0:T(1,128)} %bitcast.136, bf16[192,384]{1,0:T(8,128)(2,1)} %in_z.1), custom_call_target="tpu_custom_call" | custom-call | tf_op jit(solution)/shard_map/gate/pallas_call | solution.py:192
  202.0 19.1 %inner_row.1.total_row = bf16[32,128,384]{2,1,0:T(8,128)(2,1)} custom-call(bf16[32,128,384]{2,1,0:T(8,128)(2,1)} %get-tuple-element.40.x_in, bf16[32,128,128]{2,1,0:T(8,128)(2,1)} %get-tuple-element.41.coef_in, bf16[2,32,16,128]{3,2,1,0:T(8,128)(2,1)} %get-tuple-element.33.into_row, bf16[2,32,16,128]{3,2,1,0:T(8,128)(2,1)} %get-tuple-element.42.out_row, ...), custom_call_target="tpu_custom_call" | custom-call | tf_op jit(solution)/shard_map/inner_row/pallas_call | solution.py:329
  221.0 10.0 %all-to-all-done.1 = bf16[16,2,128,384]{3,2,1,0:T(8,128)(2,1)S(1)} async-done(((bf16[16,2,128,384]{3,2,1,0:T(8,128)(2,1)}), bf16[16,2,128,384]{3,2,1,0:T(8,128)(2,1)S(1)}, u32[]{:S(2)}, u32[]{:S(2)}) %all-to-all-start.1) | async-done | bytes 3145760 | tf_op jit(solution)/shard_map/all_to_all | solution.py:425
  231.1 3.1 chain.2
  234.2 4.5 %all-to-all-start.3 = ((bf16[32,2,16,384]{3,2,1,0:T(8,128)(2,1)}), bf16[32,2,16,384]{3,2,1,0:T(8,128)(2,1)}, u32[]{:S(2)}, u32[]{:S(2)}) async-start(bf16[32,2,16,384]{3,2,1,0:T(8,128)(2,1)} %bitcast.124), calls=%async_computation.3 | async-start | bytes 1572864 | tf_op jit(solution)/shard_map/all_to_all | solution.py:432
  238.7 4.7 %chain.3 = bf16[8,2,2,128,384]{4,3,2,1,0:T(8,128)(2,1)} custom-call(bf16[8,2,2,128,384]{4,3,2,1,0:T(8,128)(2,1)} %bitcast.116, f32[8,2,2,8,384]{4,3,2,1,0:T(8,128)} %exp.79.half, f32[8,2,2,8,384]{4,3,2,1,0:T(8,128)} %exp.83.decay), custom_call_target="tpu_custom_call" | custom-call | tf_op jit(solution)/shard_map/chain/pallas_call | solution.py:407
  243.5 8.3 %all-to-all-done.3.enter_row = bf16[32,2,16,384]{3,2,1,0:T(8,128)(2,1)} async-done(((bf16[32,2,16,384]{3,2,1,0:T(8,128)(2,1)}), bf16[32,2,16,384]{3,2,1,0:T(8,128)(2,1)}, u32[]{:S(2)}, u32[]{:S(2)}) %all-to-all-start.3) | async-done | bytes 786464 | tf_op jit(solution)/shard_map/all_to_all | solution.py:432
  251.8 5.8 %all-to-all-start.4 = ((bf16[16,2,128,384]{3,2,1,0:T(8,128)(2,1)}), bf16[16,2,128,384]{3,2,1,0:T(8,128)(2,1)S(1)}, u32[]{:S(2)}, u32[]{:S(2)}) async-start(bf16[16,2,128,384]{3,2,1,0:T(8,128)(2,1)} %bitcast.117), calls=%async_computation.4 | async-start | bytes 6291456 | tf_op jit(solution)/shard_map/all_to_all | solution.py:432
  257.6 0.5 broadcast_in_dim.98.out_gain
  258.2 1.7 copy.150.out_w
  259.9 0.9 copy.151.ff_out
  260.9 2.5 copy.146.out_col
  263.4 16.2 %inner_col.1.total_col = bf16[32,128,384]{2,1,0:T(8,128)(2,1)} custom-call(bf16[32,128,384]{2,1,0:T(8,128)(2,1)} %get-tuple-element.40.x_in, bf16[32,128,128]{2,1,0:T(8,128)(2,1)} %get-tuple-element.41.coef_in, bf16[2,16,16,256]{3,2,1,0:T(8,128)(2,1)} %copy.144.into_col, bf16[2,16,16,256]{3,2,1,0:T(8,128)(2,1)} %copy.146.out_col, ...), custom_call_target="tpu_custom_call" | custom-call | tf_op jit(solution)/shard_map/inner_col/pallas_call | solution.py:370
  279.6 15.6 %all-to-all-done.4.enter_col = bf16[16,2,128,384]{3,2,1,0:T(8,128)(2,1)S(1)} async-done(((bf16[16,2,128,384]{3,2,1,0:T(8,128)(2,1)}), bf16[16,2,128,384]{3,2,1,0:T(8,128)(2,1)S(1)}, u32[]{:S(2)}, u32[]{:S(2)}) %all-to-all-start.4) | async-done | bytes 3145760 | tf_op jit(solution)/shard_map/all_to_all | solution.py:432
  295.2 1.6 copy-done.2
  296.8 34.3 %finish.1 = bf16[32,128,192]{2,1,0:T(8,128)(2,1)} custom-call(bf16[32,128,384]{2,1,0:T(8,128)(2,1)} %inner_row.1.total_row, bf16[32,128,384]{2,1,0:T(8,128)(2,1)} %inner_col.1.total_col, bf16[32,128,128]{2,1,0:T(8,128)(2,1)} %get-tuple-element.41.coef_in, bf16[32,2,16,384]{3,2,1,0:T(8,128)(2,1)} %all-to-all-done.3.enter_row, ...), custom_call_target="tpu_custom_call" | custom-call | tf_op jit(solution)/shard_map/finish/pallas_call | solution.py:485
  331.2 3.9 %copy.152 = bf16[32,128,192]{1,2,0:T(8,128)(2,1)} copy(bf16[32,128,192]{2,1,0:T(8,128)(2,1)} %finish.1) | data formatting | bytes 3145728 | tf_op jit(solution)/shard_map/finish/pallas_call | solution.py:485
  (74 shorter events, 4.3 us)
Async XLA Ops:
  2.5 3.3 copy-start.8
  2.5 3.5 %copy-start.12 = (bf16[192]{0:T(256)(128)(2,1)S(1)}, bf16[192]{0:T(256)(128)(2,1)}, u32[]{:S(2)}) copy-start(bf16[192]{0:T(256)(128)(2,1)} %param.22) | copy-start | bytes 1156
  8.8 11.5 %copy-start.3 = (f32[4,6,32,128]{3,2,1,0:T(8,128)S(1)}, f32[4,6,32,128]{3,2,1,0:T(8,128)}, u32[]{:S(2)}) copy-start(f32[4,6,32,128]{3,2,1,0:T(8,128)} %param.30) | copy-start | bytes 1179652
  8.8 85.8 %all-to-all-start = ((bf16[128,32,256]{2,1,0:T(8,128)(2,1)}), bf16[128,32,256]{2,1,0:T(8,128)(2,1)S(1)}, u32[]{:S(2)}, u32[]{:S(2)}) async-start(bf16[128,32,256]{2,1,0:T(8,128)(2,1)} %fusion.1), calls=%async_computation | async-start | bytes 4194304 | tf_op jit(solution)/shard_map/all_to_all | solution.py:516
  60.8 2.8 copy-start.4
  64.0 2.8 copy-start.5
  88.7 2.6 copy-start.7
  88.7 3.2 copy-start.9
  94.6 2.1 copy-start
  119.0 9.6 %collective-permute-start.1 = (bf16[32,384]{1,0:T(8,128)(2,1)S(1)}, bf16[32,384]{1,0:T(8,128)(2,1)S(1)}, u32[]{:S(2)}, u32[]{:S(2)}) collective-permute-start(bf16[32,384]{1,0:T(8,128)(2,1)S(1)} %convert.12), channel_id=1, source_target_pairs={{1,0},{2,1},{3,2},{4,3},{5,4},{6,5},{7,6},{8,7},{9,8},{10,9},{11,1... | collective-permute-start | bytes 73736 | tf_op jit(solution)/shard_map/ppermute | solution.py:497
  121.0 7.5 %collective-permute-start = (bf16[32,384]{1,0:T(8,128)(2,1)S(1)}, bf16[32,384]{1,0:T(8,128)(2,1)S(1)}, u32[]{:S(2)}, u32[]{:S(2)}) collective-permute-start(bf16[32,384]{1,0:T(8,128)(2,1)S(1)} %convert.13), channel_id=1, source_target_pairs={{0,1},{1,2},{2,3},{3,4},{4,5},{5,6},{6,7},{7,8},{8,9},{9,10},{10,1... | collective-permute-start | bytes 73736 | tf_op jit(solution)/shard_map/ppermute | solution.py:497
  128.6 6.0 %collective-permute-start.3 = (bf16[130,384]{1,0:T(8,128)(2,1)S(1)}, bf16[130,384]{1,0:T(8,128)(2,1)S(1)}, u32[]{:S(2)}, u32[]{:S(2)}) collective-permute-start(bf16[130,384]{1,0:T(8,128)(2,1)S(1)} %pad_maximum_fusion.2), channel_id=1, source_target_pairs={{16,0},{32,16},{48,32},{64,48},{80,64},{96,80},{112,96},{17,1},{33... | collective-permute-start | bytes 299528 | tf_op jit(solution)/shard_map/ppermute | solution.py:497
  131.3 4.6 %collective-permute-start.2 = (bf16[130,384]{1,0:T(8,128)(2,1)S(1)}, bf16[130,384]{1,0:T(8,128)(2,1)S(1)}, u32[]{:S(2)}, u32[]{:S(2)}) collective-permute-start(bf16[130,384]{1,0:T(8,128)(2,1)S(1)} %pad_maximum_fusion.1), channel_id=1, source_target_pairs={{0,16},{16,32},{32,48},{48,64},{64,80},{80,96},{96,112},{1,17},{17... | collective-permute-start | bytes 299528 | tf_op jit(solution)/shard_map/ppermute | solution.py:497
  189.4 4.1 %copy-start.10 = (f32[384]{0:T(512)S(1)}, f32[384]{0:T(512)}, u32[]{:S(2)}) copy-start(f32[384]{0:T(512)} %param.29) | copy-start | bytes 4612
  189.4 41.7 %all-to-all-start.1 = ((bf16[16,2,128,384]{3,2,1,0:T(8,128)(2,1)}), bf16[16,2,128,384]{3,2,1,0:T(8,128)(2,1)S(1)}, u32[]{:S(2)}, u32[]{:S(2)}) async-start(bf16[16,2,128,384]{3,2,1,0:T(8,128)(2,1)} %get-tuple-element.37), calls=%async_computation.1 | async-start | bytes 6291456 | tf_op jit(solution)/shard_map/all_to_all | solution.py:425
  231.1 7.6 %copy-start.1 = (bf16[16,2,128,384]{3,2,1,0:T(8,128)(2,1)}, bf16[16,2,128,384]{3,2,1,0:T(8,128)(2,1)S(1)}, u32[]{:S(2)}) copy-start(bf16[16,2,128,384]{3,2,1,0:T(8,128)(2,1)S(1)} %all-to-all-done.1) | copy-start | bytes 9437188
  234.2 17.6 %all-to-all-start.3 = ((bf16[32,2,16,384]{3,2,1,0:T(8,128)(2,1)}), bf16[32,2,16,384]{3,2,1,0:T(8,128)(2,1)}, u32[]{:S(2)}, u32[]{:S(2)}) async-start(bf16[32,2,16,384]{3,2,1,0:T(8,128)(2,1)} %bitcast.124), calls=%async_computation.3 | async-start | bytes 1572864 | tf_op jit(solution)/shard_map/all_to_all | solution.py:432
  251.8 5.9 %copy-start.11 = (f32[384]{0:T(512)S(1)}, f32[384]{0:T(512)}, u32[]{:S(2)}) copy-start(f32[384]{0:T(512)} %param.31) | copy-start | bytes 4612
  251.8 8.1 %copy-start.6 = (bf16[768,192]{0,1:T(8,128)(2,1)S(1)}, bf16[768,192]{0,1:T(8,128)(2,1)}, u32[]{:S(2)}) copy-start(bf16[768,192]{0,1:T(8,128)(2,1)} %param.35) | copy-start | bytes 884740
  251.8 43.4 %all-to-all-start.4 = ((bf16[16,2,128,384]{3,2,1,0:T(8,128)(2,1)}), bf16[16,2,128,384]{3,2,1,0:T(8,128)(2,1)S(1)}, u32[]{:S(2)}, u32[]{:S(2)}) async-start(bf16[16,2,128,384]{3,2,1,0:T(8,128)(2,1)} %bitcast.117), calls=%async_computation.4 | async-start | bytes 6291456 | tf_op jit(solution)/shard_map/all_to_all | solution.py:432
  295.2 1.6 copy-start.2

commit v3 on v2

--- a/solution.py
+++ b/solution.py
@@ -208,12 +208,16 @@
 
 
 def conv_body(
-    inner, above, below, left, right, conv_w, conv_bias, x_proj, into_row, into_col, heads_map, pick_b,
-    x_out, coef_out, state_row, state_col,
+    spot, inner, above, below, left, right, conv_w, conv_bias, x_proj, into_row, into_col, heads_map, pick_b,
+    half_row, half_col, x_out, coef_out, state_row, state_own, state_other,
     padded, x_wide, coef_wide, left_sum, right_sum,
 ):
     rows_n, cols_n, width = inner.shape
-    state_size = state_row.shape[2]
+    state_size = LANES // 8
+    peers, tile_rows = half_row.shape[:2]
+    each = rows_n // peers
+    for q in range(peers):
+        state_row[q, 2 * each * state_size :] = half_row[q]
     padded[0] = above[...]
     padded[rows_n + 1] = below[...]
 
@@ -254,38 +258,48 @@
         for k in range(2):
             scaled = (x_wide[r] * spread(into_row[k, r], heads_map[...])).astype(BF16)
             b_part = flipped[2 * k * state_size : (2 * k + 1) * state_size, :]
-            state_row[r, k] = dot(b_part, scaled).astype(BF16)
+            at = pl.multiple_of((r % each) * 2 * state_size + k * state_size, state_size)
+            state_row[r // each, pl.ds(at, state_size), :] = dot(b_part, scaled).astype(BF16)
         return carry
 
     loop(rows_n, lambda r: row_step(r, 0), UNROLL)
     size = rows_n * SUB
     own = own_column((LANES, size), SUB, SUB)
 
-    def col_step(g, carry):
-        at = pl.ds(pl.multiple_of(g * SUB, SUB), SUB)
-        x_group = x_wide[:, at, :].reshape(size, width)
-        coef = coef_wide[:, at, :].reshape(size, LANES).astype(BF16)
-        for k in range(2):
-            scaled = (x_group * spread(into_col[k, g], heads_map[...])).astype(BF16)
-            b_part = jnp.where(own, dot_nt(pick_b[k], coef), 0.0).astype(BF16)
-            state_col[g, k] = dot(b_part, scaled).astype(BF16)
-        return carry
-
-    loop(cols_n // SUB, lambda g: col_step(g, 0), UNROLL)
-
-
-def conv_and_states(inner, above, below, left, right, conv_w, conv_bias, x_proj, into_row, into_col, heads_map, pick_b, state_size):
+    half = state_own.shape[0]
+    deep = SUB * state_size
+
+    def col_step(j):
+        for states, side in ((state_own, spot[0]), (state_other, 1 - spot[0])):
+            g = side * half + j
+            at = pl.ds(pl.multiple_of(g * SUB, SUB), SUB)
+            x_group = x_wide[:, at, :].reshape(size, width)
+            coef = coef_wide[:, at, :].reshape(size, LANES).astype(BF16)
+            for k in range(2):
+                scaled = (x_group * spread(into_col[k, g], heads_map[...])).astype(BF16)
+                b_part = jnp.where(own, dot_nt(pick_b[k], coef), 0.0).astype(BF16)
+                states[j, k * deep : (k + 1) * deep, :] = dot(b_part, scaled).astype(BF16)
+            states[j, 2 * deep :, :] = half_col[g]
+
+    loop(half, col_step, UNROLL // 2)
+
+
+def conv_and_states(spot, inner, *rest):
     rows_n, cols_n, width = inner.shape
+    half_row, half_col = rest[-2:]
+    peers, tile_rows = half_row.shape[:2]
+    groups, deep = half_col.shape[0] // 2, 2 * SUB * (LANES // 8) + half_col.shape[1]
     outs = (
         jax.ShapeDtypeStruct((rows_n, cols_n, width), BF16),
         jax.ShapeDtypeStruct((rows_n, cols_n, LANES), BF16),
-        jax.ShapeDtypeStruct((rows_n, 2, state_size, width), BF16),
-        jax.ShapeDtypeStruct((cols_n // SUB, 2, SUB * state_size, width), BF16),
+        jax.ShapeDtypeStruct((peers, rows_n // peers * 2 * (LANES // 8) + tile_rows, width), BF16),
+        jax.ShapeDtypeStruct((groups, deep, width), BF16),
+        jax.ShapeDtypeStruct((groups, deep, width), BF16),
     )
     return call(
         conv_body,
         outs,
-        [whole()] * 12,
+        [pl.BlockSpec(memory_space=pltpu.SMEM)] + [whole()] * 14,
         [
             pltpu.VMEM((rows_n + 2, cols_n, width), BF16),
             pltpu.VMEM((rows_n, cols_n, width), F32),
@@ -294,7 +308,7 @@
             pltpu.VMEM((rows_n, 1, width), F32),
         ],
         name="conv_states",
-    )(inner, above, below, left, right, conv_w, conv_bias, x_proj, into_row, into_col, heads_map, pick_b)
+    )(spot, inner, *rest)
 
 
 def c_at_b(wide, k):
@@ -380,64 +394,175 @@
     )(x_in, coef_in, into_col, out_col, heads_map)
 
 
-def chain_body(states, half, decay, entering):
-    peers, units = states.shape[0], states.shape[1]
-    deep = states.shape[3]
-    lines = half.shape[3]
-    width = states.shape[4]
+def half_of(tile, k, heads_map):
+    return dot(tile[:, 16 * k : 16 * k + 16], heads_map)
+
+
+def chain_body(states, heads_map, entering):
+    peers = states.shape[0]
+    state_size = LANES // 8
+    width = states.shape[2]
+    lines = entering.shape[1] // (2 * state_size)
+    top = 2 * lines * state_size
     for k in range(2):
         order = range(peers) if k == 0 else range(peers - 1, -1, -1)
-        for unit in range(units):
-            for part in range(width // LANES):
-                lanes = slice(part * LANES, (part + 1) * LANES)
-                before = jnp.zeros((deep, LANES), F32)
-                for at in order:
-                    scale = half[at, k, unit, :, lanes]
-                    keep = decay[at, k, unit, :, lanes]
-                    own = states[at, unit, k, :, lanes].astype(F32)
-                    if lines > 1:
-                        shape = (deep // lines, lines, LANES)
-                        scale, keep = scale[None], keep[None]
-                        before, own = before.reshape(shape), own.reshape(shape)
-                    entering[at, unit, k, :, lanes] = (scale * before).reshape(deep, LANES).astype(BF16)
-                    before = (keep * before + scale * own).reshape(deep, LANES)
-
-
-def chain(states, half, decay):
-    return call(
-        chain_body, jax.ShapeDtypeStruct(states.shape, BF16), [whole()] * 3, name="chain"
-    )(states, half, decay)
-
-
-def line_factors(total, axis, width, unit_lines):
-    peers, index = lax.axis_size(axis), lax.axis_index(axis)
+        before = [jnp.zeros((state_size, width), F32)] * lines
+        for at in order:
+            scale = half_of(states[at, top:, :LANES], k, heads_map[...])
+            for line in range(lines):
+                rows = slice((2 * line + k) * state_size, (2 * line + k + 1) * state_size)
+                own = scale[line : line + 1]
+                entering[at, rows, :] = (own * before[line]).astype(BF16)
+                before[line] = own * (own * before[line] + states[at, rows, :].astype(F32))
+
+
+def chain(states, heads_map, lines):
+    peers, _, width = states.shape
+    return call(
+        chain_body,
+        jax.ShapeDtypeStruct((peers, lines * 2 * (LANES // 8), width), BF16),
+        [whole()] * 2,
+        name="chain",
+    )(states, heads_map)
+
+
+def pair_halves(upper, lower, j, top, heads_map):
+    low_rows = pltpu.roll(lower[j, top:, :LANES].astype(F32), SUB, 0)
+    first = lax.broadcasted_iota(jnp.int32, low_rows.shape, 0) < SUB
+    tile = jnp.where(first, upper[j, top:, :LANES].astype(F32), low_rows).astype(BF16)
+    halves = []
+    for k in range(2):
+        both = half_of(tile, k, heads_map)
+        halves.append((both[:SUB], both[SUB:]))
+    return tile, halves
+
+
+def lines_of(states, j, k, lines_shape):
+    deep = lines_shape[0] * lines_shape[1]
+    return states[j, k * deep : (k + 1) * deep, :].astype(F32).reshape(lines_shape)
+
+
+def by_core(spot, run, own, got):
+    @pl.when(spot[0] == 0)
+    def _():
+        run(own, got)
+
+    @pl.when(spot[0] != 0)
+    def _():
+        run(got, own)
+
+
+def chip_total_body(spot, own, got, heads_map, *sends):
+    groups, rows, width = own.shape
+    state_size = LANES // 8
+    deep = SUB * state_size
+    shape = (state_size, SUB, width)
+    chips = len(sends) + 1
+
+    def run(upper, lower):
+        def step(j):
+            tile, halves = pair_halves(upper, lower, j, 2 * deep, heads_map[...])
+            (up_2, low_2), (up_3, low_3) = halves
+            down = (low_2 * low_2 * up_2) * lines_of(upper, j, 0, shape) + low_2 * lines_of(lower, j, 0, shape)
+            rise = (up_3 * up_3 * low_3) * lines_of(lower, j, 1, shape) + up_3 * lines_of(upper, j, 1, shape)
+            for shift, send in enumerate(sends, 1):
+                past_end = spot[1] + shift >= chips
+                send[j, :deep, :] = jnp.where(past_end, rise, down).reshape(deep, width).astype(BF16)
+                send[j, deep:, :] = jnp.zeros((rows - 2 * deep, width), BF16)
+                send[j, deep:, :LANES] = tile
+
+        loop(groups, step, 1)
+
+    by_core(spot, run, own, got)
+
+
+def chip_total(spot, own, got, heads_map, chips):
+    groups, rows, width = own.shape
+    send = jax.ShapeDtypeStruct((groups, rows - SUB * (LANES // 8), width), BF16)
+    return call(
+        chip_total_body,
+        (send,) * (chips - 1),
+        [pl.BlockSpec(memory_space=pltpu.SMEM)] + [whole()] * 3,
+        name="chip_total",
+    )(spot, own, got, heads_map)
+
+
+def entering_body(spot, own, got, heads_map, *rest):
+    receipts, (enter_own, enter_other) = rest[:-2], rest[-2:]
+    groups, rows, width = own.shape
+    state_size = LANES // 8
+    deep = SUB * state_size
+    shape = (state_size, SUB, width)
+    chips = len(receipts) + 1
+
+    def run(upper, lower, enter_upper, enter_lower):
+        def step(j):
+            _, halves = pair_halves(upper, lower, j, 2 * deep, heads_map[...])
+            (up_2, low_2), (up_3, low_3) = halves
+            states = [lines_of(receipt, j, 0, shape) for receipt in receipts]
+            keeps = []
+            for k in range(2):
+                keep = []
+                for receipt in receipts:
+                    both = half_of(receipt[j, deep:, :LANES], k, heads_map[...])
+                    chip = both[:SUB] * both[SUB:]
+                    keep.append(chip * chip)
+                keeps.append(keep)
+            down = jnp.zeros(shape, F32)
+            rise = jnp.zeros(shape, F32)
+            keep_2 = jnp.ones((SUB, width), F32)
+            keep_3 = jnp.ones((SUB, width), F32)
+            for away in range(1, chips):
+                above, below = away - 1, chips - away - 1
+                down = down + jnp.where(spot[1] >= away, keep_2, 0.0) * states[above]
+                rise = rise + jnp.where(spot[1] + away < chips, keep_3, 0.0) * states[below]
+                keep_2 = keep_2 * keeps[0][above]
+                keep_3 = keep_3 * keeps[1][below]
+            lower_2 = low_2 * up_2 * (up_2 * down + lines_of(upper, j, 0, shape))
+            upper_3 = up_3 * low_3 * (low_3 * rise + lines_of(lower, j, 1, shape))
+            enter_upper[j, 0] = (up_2 * down).reshape(deep, width).astype(BF16)
+            enter_upper[j, 1] = upper_3.reshape(deep, width).astype(BF16)
+            enter_lower[j, 0] = lower_2.reshape(deep, width).astype(BF16)
+            enter_lower[j, 1] = (low_3 * rise).reshape(deep, width).astype(BF16)
+
+        loop(groups, step, 1)
+
+    @pl.when(spot[0] == 0)
+    def _():
+        run(own, got, enter_own, enter_other)
+
+    @pl.when(spot[0] != 0)
+    def _():
+        run(got, own, enter_other, enter_own)
+
+
+def entering_states(spot, own, got, heads_map, receipts):
+    groups, rows, width = own.shape
+    enter = jax.ShapeDtypeStruct((groups, 2, SUB * (LANES // 8), width), BF16)
+    return call(
+        entering_body,
+        (enter, enter),
+        [pl.BlockSpec(memory_space=pltpu.SMEM)] + [whole()] * (3 + len(receipts)),
+        name="entering",
+    )(spot, own, got, heads_map, *receipts)
+
+
+def half_tiles(total, units):
     k, heads, lines = total.shape
-    mine = lines // peers
-    everyone = lax.all_gather(total, axis)
-    ours = lax.dynamic_slice_in_dim(everyone, index * mine, mine, axis=3)
-    ours = jnp.transpose(ours, (0, 1, 3, 2)).reshape(peers, k, mine // unit_lines, unit_lines, heads)
-    ours = jnp.repeat(ours, width // heads, axis=-1)
-    return jnp.exp(-0.5 * ours), jnp.exp(-ours)
-
-
-def to_chain(states, axis):
-    peers = lax.axis_size(axis)
-    got = lax.all_to_all(states, axis, split_axis=0, concat_axis=0, tiled=True)
-    return got.reshape((peers, got.shape[0] // peers) + got.shape[1:])
-
-
-def from_chain(split, factors, axis):
-    entering = chain(split, *factors)
-    entering = entering.reshape((-1,) + entering.shape[2:])
-    return lax.all_to_all(entering, axis, split_axis=0, concat_axis=0, tiled=True)
+    high, low = two_parts(jnp.exp(-0.5 * total))
+    both = jnp.pad(jnp.concatenate([high, low], axis=1), ((0, 0), (0, 16 - 2 * heads), (0, 0)))
+    both = jnp.transpose(both, (2, 0, 1)).reshape(units, lines // units, k * 16)
+    rows = -(-both.shape[1] // 16) * 16
+    return jnp.pad(both, ((0, 0), (0, rows - both.shape[1]), (0, 0)))
 
 
 def finish_body(
-    total_row, total_col, coef_in, enter_row, enter_col, out_row, out_col, heads_map, pick_c, gate_in, grid, out_gain, out_w,
+    spot, total_row, total_col, coef_in, enter_row, enter_own, enter_other, out_row, out_col, heads_map, pick_c, gate_in, grid, out_gain, out_w,
     mlp_gain, ff_in, ff_out, block_out, coef_wide, acc,
 ):
     rows_n, cols_n, width = total_row.shape
-    state_size = enter_row.shape[2]
+    state_size = LANES // 8
+    half = enter_own.shape[0]
 
     def row_step(r, carry):
         coef = coef_in[r]
@@ -454,17 +579,18 @@
     size = rows_n * SUB
     own = own_column((size, LANES), SUB, SUB)
 
-    def col_step(g, carry):
-        at = pl.ds(pl.multiple_of(g * SUB, SUB), SUB)
-        coef = coef_wide[:, at, :].reshape(size, LANES).astype(BF16)
-        value = acc[:, at, :].reshape(size, width)
-        for k in range(2):
-            c_part = jnp.where(own, dot(coef, pick_c[k]), 0.0).astype(BF16)
-            value = value + dot(c_part, enter_col[g, k]) * spread(out_col[k, g], heads_map[...])
-        acc[:, at, :] = value.reshape(rows_n, SUB, width)
-        return carry
-
-    loop(cols_n // SUB, lambda g: col_step(g, 0), UNROLL)
+    def col_step(j):
+        for enter, side in ((enter_own, spot[0]), (enter_other, 1 - spot[0])):
+            g = side * half + j
+            at = pl.ds(pl.multiple_of(g * SUB, SUB), SUB)
+            coef = coef_wide[:, at, :].reshape(size, LANES).astype(BF16)
+            value = acc[:, at, :].reshape(size, width)
+            for k in range(2):
+                c_part = jnp.where(own, dot(coef, pick_c[k]), 0.0).astype(BF16)
+                value = value + dot(c_part, enter[j, k]) * spread(out_col[k, g], heads_map[...])
+            acc[:, at, :] = value.reshape(rows_n, SUB, width)
+
+    loop(half, col_step, UNROLL // 2)
 
     def last(r, carry):
         at = pl.ds(pl.multiple_of(r * cols_n, cols_n), cols_n)
@@ -480,15 +606,15 @@
     loop(rows_n, lambda r: last(r, 0), UNROLL)
 
 
-def finish(total, total_col, coef, *rest, channels):
+def finish(spot, total, total_col, coef, *rest, channels):
     rows_n, cols_n, width = total.shape
     return call(
         finish_body,
         jax.ShapeDtypeStruct((rows_n, cols_n, channels), BF16),
-        [whole()] * 16,
+        [pl.BlockSpec(memory_space=pltpu.SMEM)] + [whole()] * 17,
         [pltpu.VMEM(coef.shape, F32), pltpu.VMEM(total.shape, F32)],
         name="finish",
-    )(total, total_col, coef, *rest)
+    )(spot, total, total_col, coef, *rest)
 
 
 def shifted(block, axis, up):
@@ -515,8 +641,12 @@
     sent = jnp.concatenate([values, where], axis=-1)
     got = lax.all_to_all(sent, ("row", "col"), split_axis=0, concat_axis=0, tiled=True)
     into_row, out_row, into_col, out_col, total_row, total_col = decay_factors(decay_rate)
-    row_factors = line_factors(total_row, "col", width, 1)
-    col_factors = line_factors(total_col, "row", width, SUB)
+    half_row = half_tiles(total_row, lax.axis_size("col"))
+    half_col = half_tiles(total_col, cols_n // SUB)
+    half_row = jnp.pad(half_row, ((0, 0), (0, 0), (0, width - half_row.shape[2])))
+    half_col = jnp.pad(half_col, ((0, 0), (0, 0), (0, width - half_col.shape[2])))
+    line = lax.axis_index("row")
+    spot = jnp.stack([line % 2, line // 2]).astype(jnp.int32)
     head_of = jnp.arange(width, dtype=jnp.int32) // (width // heads)
     part_of = jnp.arange(16, dtype=jnp.int32)
     heads_map = (
@@ -530,9 +660,9 @@
     pick_c = jnp.stack([picks[1], picks[3]])
 
     got = got.reshape(owners * slots, sent.shape[2])
-    ready = (into_row, out_row, into_col, out_col, row_factors, col_factors, heads_map, pick_b, pick_c)
+    ready = (into_row, out_row, into_col, out_col, half_row, half_col, heads_map, pick_b, pick_c, spot)
     got, ready = lax.optimization_barrier((got, ready))
-    into_row, out_row, into_col, out_col, row_factors, col_factors, heads_map, pick_b, pick_c = ready
+    into_row, out_row, into_col, out_col, half_row, half_col, heads_map, pick_b, pick_c, spot = ready
     cells = got[:, channels].astype(jnp.int32) * 64 + got[:, channels + 1].astype(jnp.int32)
 
     grid, inner, left_edge, right_edge = place(
@@ -547,20 +677,36 @@
     left = jnp.concatenate([above[cols_n : cols_n + 1], from_left, below[cols_n : cols_n + 1]])[:, None].astype(F32)
     right = jnp.concatenate([above[cols_n + 1 :], from_right, below[cols_n + 1 :]])[:, None].astype(F32)
 
-    x_in, coef, state_row, state_col = conv_and_states(
-        inner.reshape(rows_n, cols_n, width), above[:cols_n], below[:cols_n], left, right,
-        conv_w.reshape(9, width), conv_bias[None], x_proj, into_row, into_col, heads_map, pick_b, state_size,
-    )
-    split_col = to_chain(state_col, "row")
-    split_row = to_chain(state_row, "col")
+    x_in, coef, state_row, state_own, state_other = conv_and_states(
+        spot, inner.reshape(rows_n, cols_n, width), above[:cols_n], below[:cols_n], left, right,
+        conv_w.reshape(9, width), conv_bias[None], x_proj, into_row, into_col, heads_map, pick_b, half_row, half_col,
+    )
+    order = lax.optimization_barrier
+    lines, peers = lax.axis_size("row"), lax.axis_size("col")
+    chips = lines // 2
+    twin = [(i, i ^ 1) for i in range(lines)]
+    state_got = lax.ppermute(state_other, "row", twin)
+    split_row = lax.all_to_all(state_row, "col", split_axis=0, concat_axis=0, tiled=True)
     gated = gate(grid, norm_gain[None], in_z)
-    total = inner_row(x_in, coef, into_row, out_row, heads_map, skip_gain[None])
-    split_col, split_row, gated, total = lax.optimization_barrier((split_col, split_row, gated, total))
-    enter_col = from_chain(split_col, col_factors, "row")
-    enter_row = from_chain(split_row, row_factors, "col")
-    total_col = inner_col(x_in, coef, into_col, out_col, heads_map)
+    state_got, gated = order((state_got, gated))
+    sends = chip_total(spot, state_own, state_got, heads_map, chips)
+    receipts = [
+        lax.ppermute(send, "row", [(i, (i + 2 * shift) % lines) for i in range(lines)])
+        for shift, send in enumerate(sends, 1)
+    ]
+    x_row, sends = order((x_in, sends))
+    total = inner_row(x_row, coef, into_row, out_row, heads_map, skip_gain[None])
+    split_row, total = order((split_row, total))
+    passed = chain(split_row, heads_map, rows_n // peers)
+    enter_row = lax.all_to_all(passed, "col", split_axis=0, concat_axis=0, tiled=True)
+    enter_row = enter_row.reshape(rows_n, 2, state_size, width)
+    x_col, passed = order((x_in, passed))
+    total_col = inner_col(x_col, coef, into_col, out_col, heads_map)
+    receipts, total_col, enter_row = order((receipts, total_col, enter_row))
+    enter_own, enter_other = entering_states(spot, state_own, state_got, heads_map, receipts)
+    enter_other = lax.ppermute(enter_other, "row", twin)
     return finish(
-        total, total_col, coef, enter_row, enter_col, out_row, out_col, heads_map, pick_c, gated, grid, out_gain[None], out_w,
+        spot, total, total_col, coef, enter_row, enter_own, enter_other, out_row, out_col, heads_map, pick_c, gated, grid, out_gain[None], out_w,
         mlp_gain[None], ff_in, ff_out, channels=channels,
     )
 

time: 336 us -> 250 us (0.74)
  blocking collectives: 74.9 us -> 0 us
  waiting for transfers between devices: 35.6 us -> 14.3 us
  Pallas kernels: 136 us -> 145 us
  starting transfers between devices: 36.8 us -> 41.8 us
  local copies, waits for them, and re-layouts: 37.1 us -> 33.2 us
    all_gather x2 -> x0, blocking collectives: 54.6 us -> none  [line_factors(): everyone = lax.all_gather(total, axis)]
    all_to_all x3 -> x2, waiting for transfers between devices: 34 us -> 0.01 us  [the longest x1 0.01 us: local(): lax.all_to_all(state_row, 'col', split_axis=0, concat_axis=0, tiled=True)]
    all_to_all x1 -> x0, blocking collectives: 20.4 us -> none  [to_chain(): got = lax.all_to_all(states, axis, split_axis=0, concat_axis=0, tiled=True)]
    all_to_all x1, waiting for transfers between devices: 0.01 us -> 11.9 us  [local(): lax.all_to_all(sent, ('row', 'col'), split_axis=0, concat_axis=0, tiled=T...]
    pallas_call x3 -> x4, Pallas kernels: 38.3 us -> 47.3 us  [the longest x1 31.5 us: conv_and_states(): call(conv_body, outs, [pl.BlockSpec(memory_space=pltpu.SMEM)] + [whole()]...]
    ppermute x0 -> x5, starting transfers between devices: none -> 6.71 us  [the longest x3 5.01 us: local(): lax.ppermute(send, 'row', [(i, (i + 2 * shift) % lines) for i in range(li...]
    all_to_all x3 -> x2, starting transfers between devices: 14.4 us -> 11.7 us  [the longest x1 6.66 us: local(): lax.all_to_all(passed, 'col', split_axis=0, concat_axis=0, tiled=True)]
    unnamed x30 -> x36, local copies, waits for them, and re-layouts: 9.34 us -> 10.1 us
  transfers between devices with their start and end apart: 8 -> 12, of which waited for: 5 -> 4; matrix products, arithmetic and copies ran while one was open for 9% -> 10% of each run, Pallas kernels for 14% -> 20%
where the time goes in v3:
time: 250 us; the launch traced here: 249 us
  Pallas kernels  145 us (58%)
  starting transfers between devices  41.8 us (17%)
  local copies, waits for them, and re-layouts  33.2 us (13%)
  waiting for transfers between devices  14.3 us (6%)
  other arithmetic  12.8 us (5%)
    pallas_call x1, Pallas kernels, finish(): call(finish_body, jax.ShapeDtypeStruct((rows_n, cols_n, channels), BF16),...  34.4 us
    pallas_call x1, Pallas kernels, conv_and_states(): call(conv_body, outs, [pl.BlockSpec(memory_space=pltpu.SMEM)] + [whole()]...  31.5 us
    pallas_call x1, Pallas kernels, place(): call(place_body, outs, [pl.BlockSpec(memory_space=pltpu.SMEM), whole(), w...  21.5 us
    pallas_call x1, Pallas kernels, inner_row(): call(inner_row_body, jax.ShapeDtypeStruct(x_in.shape, BF16), [whole()] *...  19.1 us
    pallas_call x1, Pallas kernels, inner_col(): call(inner_col_body, jax.ShapeDtypeStruct(x_in.shape, BF16), [whole()] *...  16.2 us
    all_to_all x1, waiting for transfers between devices, local(): lax.all_to_all(sent, ('row', 'col'), split_axis=0, concat_axis=0, tiled=T...  11.9 us
    ppermute x4, starting transfers between devices, shifted(): return lax.ppermute(block, axis, pairs)  11.9 us
    all_to_all x1, starting transfers between devices, local(): lax.all_to_all(sent, ('row', 'col'), split_axis=0, concat_axis=0, tiled=T...  11.5 us
  transfers between devices with their start and end apart: 12, of which 4 were waited for; matrix products, arithmetic and copies ran while one was open for 10% of the time, Pallas kernels for 20%

profile of v3, /device:TPU:1, one launch (start us, length us, event | category | flops | bytes accessed | tf_op | source)
XLA Modules:
  0.0 248.8 jit_solution(8792219168664179334)
XLA Ops:
  0.0 0.7 fusion.40
  0.8 1.7 copy.117
  2.5 3.3 %copy.87 = bf16[1,128,32,192]{3,2,1,0:T(8,128)(2,1)S(1)} copy(bf16[1,128,32,192]{1,3,2,0:T(8,128)(2,1)} %param.18) | data formatting | bytes 3145728 | tf_op args[0]
  5.9 0.8 bitcast_select_fusion
  6.8 2.1 fusion.1
  8.8 11.5 %all-to-all-start = ((bf16[128,32,256]{2,1,0:T(8,128)(2,1)}), bf16[128,32,256]{2,1,0:T(8,128)(2,1)S(1)}, u32[]{:S(2)}, u32[]{:S(2)}) async-start(bf16[128,32,256]{2,1,0:T(8,128)(2,1)} %fusion.1), calls=%async_computation | async-start | bytes 4194304 | tf_op jit(solution)/shard_map/all_to_all | solution.py:642
  20.8 0.4 fusion.20
  21.2 0.3 fusion.22
  22.4 0.6 reduce-precision_convert_fusion
  23.1 0.4 fusion.8
  23.6 0.8 fusion.78
  24.3 0.8 fusion.77
  25.2 0.5 copy.96
  25.7 2.8 %copy.97 = bf16[2,16,16,32,8]{2,4,3,1,0:T(8,128)(2,1)} copy(bf16[2,16,16,32,8]{3,4,1,2,0:T(8,128)(2,1)S(1)} %bitcast.105) | data formatting | bytes 524288 | tf_op jit(solution)/shard_map/transpose | solution.py:78
  28.5 0.5 copy.98
  29.0 2.8 %copy.99 = bf16[2,16,16,32,8]{2,4,3,1,0:T(8,128)(2,1)} copy(bf16[2,16,16,32,8]{3,4,1,2,0:T(8,128)(2,1)S(1)} %bitcast.106) | data formatting | bytes 524288 | tf_op jit(solution)/shard_map/transpose | solution.py:78
  32.3 0.7 pad.86.half_row
  33.0 0.7 pad.89.half_col
  33.7 0.6 reshape.456.conv_w
  34.3 0.5 broadcast_in_dim.82.conv_bias
  34.9 0.6 pad_add_fusion.spot
  35.7 0.6 add_convert_fusion.pick_b
  36.4 0.6 add_convert_fusion.1.pick_c
  37.0 0.7 and_convert_fusion.heads_map
  37.7 11.9 %all-to-all-done = bf16[128,32,256]{2,1,0:T(8,128)(2,1)S(1)} async-done(((bf16[128,32,256]{2,1,0:T(8,128)(2,1)}), bf16[128,32,256]{2,1,0:T(8,128)(2,1)S(1)}, u32[]{:S(2)}, u32[]{:S(2)}) %all-to-all-start) | async-done | bytes 2097184 | tf_op jit(solution)/shard_map/all_to_all | solution.py:642
  49.6 2.0 add_reduce_fusion.cells
  51.6 21.5 %place_norm_project.1 = (bf16[4096,192]{1,0:T(8,128)(2,1)}, bf16[4096,384]{1,0:T(8,128)(2,1)}, f32[32,384]{1,0:T(8,128)}, f32[32,384]{1,0:T(8,128)}) custom-call(s32[4096]{0:T(1024)} %add_reduce_fusion.cells, bf16[4096,256]{1,0:T(8,128)(2,1)} %bitcast.102, f32[1,192]{1,0:T(1,128)} %bitcast.115, bf16[192,384]{1,0:T(8,128)(2,1)} %in_x.1), custom_call_target="tpu_custom_call" | custom-call | tf_op jit(solution)/shard_map/place_norm_project/pallas_call | solution.py:168
  73.1 0.8 convert.12
  73.9 1.3 collective-permute-start.1
  75.2 0.8 convert.13
  76.0 4.0 %collective-permute-start = (bf16[32,384]{1,0:T(8,128)(2,1)S(1)}, bf16[32,384]{1,0:T(8,128)(2,1)S(1)}, u32[]{:S(2)}, u32[]{:S(2)}) collective-permute-start(bf16[32,384]{1,0:T(8,128)(2,1)S(1)} %convert.13), channel_id=1, source_target_pairs={{0,1},{1,2},{2,3},{3,4},{4,5},{5,6},{6,7},{7,8},{8,9},{9,10},{10,1... | collective-permute-start | bytes 73736 | tf_op jit(solution)/shard_map/ppermute | solution.py:623
  80.0 1.0 fusion.76
  81.0 2.5 %copy.108.into_col = bf16[2,16,16,256]{3,2,1,0:T(8,128)(2,1)} copy(bf16[2,16,16,256]{2,3,1,0:T(8,128)(2,1)} %bitcast.104) | data formatting | bytes 524288 | tf_op jit(solution)/shard_map/optimization_barrier | solution.py:664
  83.5 4.0 %collective-permute-start.3 = (bf16[130,384]{1,0:T(8,128)(2,1)S(1)}, bf16[130,384]{1,0:T(8,128)(2,1)S(1)}, u32[]{:S(2)}, u32[]{:S(2)}) collective-permute-start(bf16[130,384]{1,0:T(8,128)(2,1)S(1)} %pad_maximum_fusion.2), channel_id=1, source_target_pairs={{16,0},{32,16},{48,32},{64,48},{80,64},{96,80},{112,96},{17,1},{33... | collective-permute-start | bytes 299528 | tf_op jit(solution)/shard_map/ppermute | solution.py:623
  87.6 2.6 %collective-permute-start.2 = (bf16[130,384]{1,0:T(8,128)(2,1)S(1)}, bf16[130,384]{1,0:T(8,128)(2,1)S(1)}, u32[]{:S(2)}, u32[]{:S(2)}) collective-permute-start(bf16[130,384]{1,0:T(8,128)(2,1)S(1)} %pad_maximum_fusion.1), channel_id=1, source_target_pairs={{0,16},{16,32},{32,48},{48,64},{64,80},{80,96},{96,112},{1,17},{17... | collective-permute-start | bytes 299528 | tf_op jit(solution)/shard_map/ppermute | solution.py:623
  90.4 1.3 collective-permute-done.2
  91.7 0.7 maximum_convert_fusion.left
  92.4 0.7 maximum_convert_fusion.1.right
  93.1 0.6 slice.102.above
  93.8 0.6 slice.105.below
  94.4 31.5 %conv_states.1 = (bf16[32,128,384]{2,1,0:T(8,128)(2,1)}, bf16[32,128,128]{2,1,0:T(8,128)(2,1)}, bf16[16,80,384]{2,1,0:T(8,128)(2,1)}, bf16[8,272,384]{2,1,0:T(8,128)(2,1)}, bf16[8,272,384]{2,1,0:T(8,128)(2,1)}) custom-call(s32[2]{0:T(128)} %pad_add_fusion.spot, bf16[32,128,384]{2,1,0:T(8,128)(2,1)} %bitcast.107, bf16[128,384]{1,0:T(8,128)(2,1)} %slice.102.above, ...), custom_call_target="tpu_custom_call" | custom-call | tf_op jit(solution)/shard_map/conv_states/pallas_call | solution.py:299
  125.9 5.0 %all-to-all-start.1 = ((bf16[16,80,384]{2,1,0:T(8,128)(2,1)}), bf16[16,80,384]{2,1,0:T(8,128)(2,1)S(1)}, u32[]{:S(2)}, u32[]{:S(2)}) async-start(bf16[16,80,384]{2,1,0:T(8,128)(2,1)} %get-tuple-element.52), calls=%async_computation.1 | async-start | bytes 1966080 | tf_op jit(solution)/shard_map/all_to_all | solution.py:689
  130.9 6.4 %gate.1.gate_in = bf16[4096,384]{1,0:T(8,128)(2,1)} custom-call(bf16[4096,192]{1,0:T(8,128)(2,1)} %get-tuple-element.56.grid, f32[1,192]{1,0:T(1,128)} %bitcast.116, bf16[192,384]{1,0:T(8,128)(2,1)} %in_z.1), custom_call_target="tpu_custom_call" | custom-call | tf_op jit(solution)/shard_map/gate/pallas_call | solution.py:192
  137.3 1.2 copy-done.2
  138.5 5.6 %chip_total.1 = (bf16[8,144,384]{2,1,0:T(8,128)(2,1)}, bf16[8,144,384]{2,1,0:T(8,128)(2,1)}, bf16[8,144,384]{2,1,0:T(8,128)(2,1)}) custom-call(s32[2]{0:T(128)} %pad_add_fusion.spot, bf16[8,272,384]{2,1,0:T(8,128)(2,1)} %get-tuple-element.54.own, bf16[8,272,384]{2,1,0:T(8,128)(2,1)} %copy-done.2, bf16[16,384]{1,0:T(8,128)(2,1)} %and_convert_fusion.heads_map), custom_call_target="tpu_custom_call" | custom-call | tf_op jit(solution)/shard_map/chip_total/pallas_call | solution.py:482
  144.0 2.5 %collective-permute-start.5 = (bf16[8,144,384]{2,1,0:T(8,128)(2,1)}, bf16[8,144,384]{2,1,0:T(8,128)(2,1)}, u32[]{:S(2)}, u32[]{:S(2)}) collective-permute-start(bf16[8,144,384]{2,1,0:T(8,128)(2,1)} %get-tuple-element.58), channel_id=1, source_target_pairs={{0,32},{16,48},{32,64},{48,80},{64,96},{80,112},{96,0},{112,16},{1... | collective-permute-start | bytes 2654216 | tf_op jit(solution)/shard_map/ppermute | solution.py:694
  146.6 1.9 collective-permute-start.6
  148.4 0.6 collective-permute-start.7
  149.0 0.5 broadcast_in_dim.83.skip
  149.6 19.1 %inner_row.1.total_row = bf16[32,128,384]{2,1,0:T(8,128)(2,1)} custom-call(bf16[32,128,384]{2,1,0:T(8,128)(2,1)} %get-tuple-element.66.x_in, bf16[32,128,128]{2,1,0:T(8,128)(2,1)} %get-tuple-element.62.coef_in, bf16[2,32,16,128]{3,2,1,0:T(8,128)(2,1)} %get-tuple-element.46.into_row, bf16[2,32,16,128]{3,2,1,0:T(8,128)(2,1)} %get-tuple-element.63.out_row, ...), custom_call_target="tpu_custom_call" | custom-call | tf_op jit(solution)/shard_map/inner_row/pallas_call | solution.py:343
  168.7 0.9 copy-done.3
  169.6 2.6 %chain.1 = bf16[16,64,384]{2,1,0:T(8,128)(2,1)} custom-call(bf16[16,80,384]{2,1,0:T(8,128)(2,1)} %copy-done.3, bf16[16,384]{1,0:T(8,128)(2,1)} %and_convert_fusion.heads_map), custom_call_target="tpu_custom_call" | custom-call | tf_op jit(solution)/shard_map/chain/pallas_call | solution.py:421
  172.2 6.7 %all-to-all-start.2 = ((bf16[16,64,384]{2,1,0:T(8,128)(2,1)}), bf16[16,64,384]{2,1,0:T(8,128)(2,1)S(1)}, u32[]{:S(2)}, u32[]{:S(2)}) async-start(bf16[16,64,384]{2,1,0:T(8,128)(2,1)} %chain.1), calls=%async_computation.2 | async-start | bytes 1572864 | tf_op jit(solution)/shard_map/all_to_all | solution.py:701
  178.9 1.4 copy.110.out_col
  180.3 16.2 %inner_col.1.total_col = bf16[32,128,384]{2,1,0:T(8,128)(2,1)} custom-call(bf16[32,128,384]{2,1,0:T(8,128)(2,1)} %get-tuple-element.66.x_in, bf16[32,128,128]{2,1,0:T(8,128)(2,1)} %get-tuple-element.62.coef_in, bf16[2,16,16,256]{3,2,1,0:T(8,128)(2,1)} %copy.108.into_col, bf16[2,16,16,256]{3,2,1,0:T(8,128)(2,1)} %copy.110.out_col, ...), custom_call_target="tpu_custom_call" | custom-call | tf_op jit(solution)/shard_map/inner_col/pallas_call | solution.py:384
  196.6 7.7 %entering.1 = (bf16[8,2,128,384]{3,2,1,0:T(8,128)(2,1)}, bf16[8,2,128,384]{3,2,1,0:T(8,128)(2,1)}) custom-call(s32[2]{0:T(128)} %pad_add_fusion.spot, bf16[8,272,384]{2,1,0:T(8,128)(2,1)} %get-tuple-element.54.own, bf16[8,272,384]{2,1,0:T(8,128)(2,1)} %copy-done.2, bf16[16,384]{1,0:T(8,128)(2,1)} %and_convert_fusion.heads_map, ...), custom_call_target="tpu_custom_call" | custom-call | tf_op jit(solution)/shard_map/entering/pallas_call | solution.py:542
  204.4 1.7 collective-permute-start.8
  206.1 0.5 broadcast_in_dim.84.out_gain
  206.6 0.8 copy.112.out_w
  207.4 0.9 copy.113.ff_out
  208.3 1.0 collective-permute-done.8.enter_other
  209.3 1.1 copy-done.6
  210.5 34.4 %finish.1 = bf16[32,128,192]{2,1,0:T(8,128)(2,1)} custom-call(s32[2]{0:T(128)} %pad_add_fusion.spot, bf16[32,128,384]{2,1,0:T(8,128)(2,1)} %inner_row.1.total_row, bf16[32,128,384]{2,1,0:T(8,128)(2,1)} %inner_col.1.total_col, bf16[32,128,128]{2,1,0:T(8,128)(2,1)} %get-tuple-element.62.coef_in, bf16[32,2,16,384]{3,2,1,0:T(8,128)(2,1)} %bitcast.108, ...), custom_call_target="tpu_custom_call" | custom-call | tf_op jit(solution)/shard_map/finish/pallas_call | solution.py:611
  244.9 3.9 %copy.114 = bf16[32,128,192]{1,2,0:T(8,128)(2,1)} copy(bf16[32,128,192]{2,1,0:T(8,128)(2,1)} %finish.1) | data formatting | bytes 3145728 | tf_op jit(solution)/shard_map/finish/pallas_call | solution.py:611
  (84 shorter events, 2.4 us)
Async XLA Ops:
  2.5 3.3 %copy-start.11 = (s32[1,128,32]{1,2,0:T(8,128)S(1)}, s32[1,128,32]{1,2,0:T(8,128)}, u32[]{:S(2)}) copy-start(s32[1,128,32]{1,2,0:T(8,128)} %param.20) | copy-start | bytes 49156
  2.5 3.5 %copy-start.15 = (bf16[192]{0:T(256)(128)(2,1)S(1)}, bf16[192]{0:T(256)(128)(2,1)}, u32[]{:S(2)}) copy-start(bf16[192]{0:T(256)(128)(2,1)} %param.22) | copy-start | bytes 1156
  8.8 11.5 %copy-start.4 = (f32[4,6,32,128]{3,2,1,0:T(8,128)S(1)}, f32[4,6,32,128]{3,2,1,0:T(8,128)}, u32[]{:S(2)}) copy-start(f32[4,6,32,128]{3,2,1,0:T(8,128)} %param.30) | copy-start | bytes 1179652
  8.8 40.8 %all-to-all-start = ((bf16[128,32,256]{2,1,0:T(8,128)(2,1)}), bf16[128,32,256]{2,1,0:T(8,128)(2,1)S(1)}, u32[]{:S(2)}, u32[]{:S(2)}) async-start(bf16[128,32,256]{2,1,0:T(8,128)(2,1)} %fusion.1), calls=%async_computation | async-start | bytes 4194304 | tf_op jit(solution)/shard_map/all_to_all | solution.py:642
  25.7 2.8 %copy-start.7 = (bf16[2,16,32,128]{3,1,2,0:T(8,128)(2,1)S(1)}, bf16[2,16,32,128]{3,1,2,0:T(8,128)(2,1)}, u32[]{:S(2)}) copy-start(bf16[2,16,32,128]{3,1,2,0:T(8,128)(2,1)} %get-tuple-element.87) | copy-start | bytes 786436
  29.0 4.7 %copy-start.10 = (f32[3,3,384]{2,1,0:T(4,128)S(1)}, f32[3,3,384]{2,1,0:T(4,128)}, u32[]{:S(2)}) copy-start(f32[3,3,384]{2,1,0:T(4,128)} %param.26) | copy-start | bytes 41476
  29.0 5.3 %copy-start.12 = (f32[384]{0:T(512)S(1)}, f32[384]{0:T(512)}, u32[]{:S(2)}) copy-start(f32[384]{0:T(512)} %param.27) | copy-start | bytes 4612
  49.6 2.0 copy-start
  73.9 9.6 %collective-permute-start.1 = (bf16[32,384]{1,0:T(8,128)(2,1)S(1)}, bf16[32,384]{1,0:T(8,128)(2,1)S(1)}, u32[]{:S(2)}, u32[]{:S(2)}) collective-permute-start(bf16[32,384]{1,0:T(8,128)(2,1)S(1)} %convert.12), channel_id=1, source_target_pairs={{1,0},{2,1},{3,2},{4,3},{5,4},{6,5},{7,6},{8,7},{9,8},{10,9},{11,1... | collective-permute-start | bytes 73736 | tf_op jit(solution)/shard_map/ppermute | solution.py:623
  76.0 7.5 %collective-permute-start = (bf16[32,384]{1,0:T(8,128)(2,1)S(1)}, bf16[32,384]{1,0:T(8,128)(2,1)S(1)}, u32[]{:S(2)}, u32[]{:S(2)}) collective-permute-start(bf16[32,384]{1,0:T(8,128)(2,1)S(1)} %convert.13), channel_id=1, source_target_pairs={{0,1},{1,2},{2,3},{3,4},{4,5},{5,6},{6,7},{7,8},{8,9},{9,10},{10,1... | collective-permute-start | bytes 73736 | tf_op jit(solution)/shard_map/ppermute | solution.py:623
  83.5 6.9 %collective-permute-start.3 = (bf16[130,384]{1,0:T(8,128)(2,1)S(1)}, bf16[130,384]{1,0:T(8,128)(2,1)S(1)}, u32[]{:S(2)}, u32[]{:S(2)}) collective-permute-start(bf16[130,384]{1,0:T(8,128)(2,1)S(1)} %pad_maximum_fusion.2), channel_id=1, source_target_pairs={{16,0},{32,16},{48,32},{64,48},{80,64},{96,80},{112,96},{17,1},{33... | collective-permute-start | bytes 299528 | tf_op jit(solution)/shard_map/ppermute | solution.py:623
  87.6 4.1 %collective-permute-start.2 = (bf16[130,384]{1,0:T(8,128)(2,1)S(1)}, bf16[130,384]{1,0:T(8,128)(2,1)S(1)}, u32[]{:S(2)}, u32[]{:S(2)}) collective-permute-start(bf16[130,384]{1,0:T(8,128)(2,1)S(1)} %pad_maximum_fusion.1), channel_id=1, source_target_pairs={{0,16},{16,32},{32,48},{48,64},{64,80},{80,96},{96,112},{1,17},{17... | collective-permute-start | bytes 299528 | tf_op jit(solution)/shard_map/ppermute | solution.py:623
  125.9 11.4 %collective-permute-start.4 = (bf16[8,272,384]{2,1,0:T(8,128)(2,1)}, bf16[8,272,384]{2,1,0:T(8,128)(2,1)S(1)}, u32[]{:S(2)}, u32[]{:S(2)}) collective-permute-start(bf16[8,272,384]{2,1,0:T(8,128)(2,1)} %get-tuple-element.55), channel_id=1, source_target_pairs={{0,16},{16,0},{32,48},{48,32},{64,80},{80,64},{96,112},{112,96},{1... | collective-permute-start | bytes 5013512 | tf_op jit(solution)/shard_map/ppermute | solution.py:688
  125.9 42.8 %all-to-all-start.1 = ((bf16[16,80,384]{2,1,0:T(8,128)(2,1)}), bf16[16,80,384]{2,1,0:T(8,128)(2,1)S(1)}, u32[]{:S(2)}, u32[]{:S(2)}) async-start(bf16[16,80,384]{2,1,0:T(8,128)(2,1)} %get-tuple-element.52), calls=%async_computation.1 | async-start | bytes 1966080 | tf_op jit(solution)/shard_map/all_to_all | solution.py:689
  137.3 11.8 %copy-start.13 = (f32[384]{0:T(512)S(1)}, f32[384]{0:T(512)}, u32[]{:S(2)}) copy-start(f32[384]{0:T(512)} %param.29) | copy-start | bytes 4612
  137.3 1.2 copy-start.2
  144.0 52.5 %collective-permute-start.5 = (bf16[8,144,384]{2,1,0:T(8,128)(2,1)}, bf16[8,144,384]{2,1,0:T(8,128)(2,1)}, u32[]{:S(2)}, u32[]{:S(2)}) collective-permute-start(bf16[8,144,384]{2,1,0:T(8,128)(2,1)} %get-tuple-element.58), channel_id=1, source_target_pairs={{0,32},{16,48},{32,64},{48,80},{64,96},{80,112},{96,0},{112,16},{1... | collective-permute-start | bytes 2654216 | tf_op jit(solution)/shard_map/ppermute | solution.py:694
  146.6 50.0 %collective-permute-start.6 = (bf16[8,144,384]{2,1,0:T(8,128)(2,1)}, bf16[8,144,384]{2,1,0:T(8,128)(2,1)}, u32[]{:S(2)}, u32[]{:S(2)}) collective-permute-start(bf16[8,144,384]{2,1,0:T(8,128)(2,1)} %get-tuple-element.59), channel_id=1, source_target_pairs={{0,64},{16,80},{32,96},{48,112},{64,0},{80,16},{96,32},{112,48},{1... | collective-permute-start | bytes 2654216 | tf_op jit(solution)/shard_map/ppermute | solution.py:694
  148.4 48.2 %collective-permute-start.7 = (bf16[8,144,384]{2,1,0:T(8,128)(2,1)}, bf16[8,144,384]{2,1,0:T(8,128)(2,1)}, u32[]{:S(2)}, u32[]{:S(2)}) collective-permute-start(bf16[8,144,384]{2,1,0:T(8,128)(2,1)} %get-tuple-element.60), channel_id=1, source_target_pairs={{0,96},{16,112},{32,0},{48,16},{64,32},{80,48},{96,64},{112,80},{1... | collective-permute-start | bytes 2654216 | tf_op jit(solution)/shard_map/ppermute | solution.py:694
  168.7 10.2 %copy-start.1 = (bf16[2,16,16,32,8]{2,4,3,1,0:T(8,128)(2,1)S(1)}, bf16[2,16,16,32,8]{2,4,3,1,0:T(8,128)(2,1)}, u32[]{:S(2)}) copy-start(bf16[2,16,16,32,8]{2,4,3,1,0:T(8,128)(2,1)} %copy.99) | copy-start | bytes 786436
  168.7 0.9 copy-start.3
  172.2 24.3 %all-to-all-start.2 = ((bf16[16,64,384]{2,1,0:T(8,128)(2,1)}), bf16[16,64,384]{2,1,0:T(8,128)(2,1)S(1)}, u32[]{:S(2)}, u32[]{:S(2)}) async-start(bf16[16,64,384]{2,1,0:T(8,128)(2,1)} %chain.1), calls=%async_computation.2 | async-start | bytes 1572864 | tf_op jit(solution)/shard_map/all_to_all | solution.py:701
  196.6 7.8 %copy-start.5 = (bf16[16,64,384]{2,1,0:T(8,128)(2,1)}, bf16[16,64,384]{2,1,0:T(8,128)(2,1)S(1)}, u32[]{:S(2)}) copy-start(bf16[16,64,384]{2,1,0:T(8,128)(2,1)S(1)} %all-to-all-done.2) | copy-start | bytes 2359300
  196.6 9.5 %copy-start.14 = (f32[384]{0:T(512)S(1)}, f32[384]{0:T(512)}, u32[]{:S(2)}) copy-start(f32[384]{0:T(512)} %param.31) | copy-start | bytes 4612
  196.6 10.0 %copy-start.9 = (bf16[384,192]{0,1:T(8,128)(2,1)S(1)}, bf16[384,192]{0,1:T(8,128)(2,1)}, u32[]{:S(2)}) copy-start(bf16[384,192]{0,1:T(8,128)(2,1)} %param.32) | copy-start | bytes 442372
  196.6 10.8 %copy-start.8 = (bf16[768,192]{0,1:T(8,128)(2,1)S(1)}, bf16[768,192]{0,1:T(8,128)(2,1)}, u32[]{:S(2)}) copy-start(bf16[768,192]{0,1:T(8,128)(2,1)} %param.35) | copy-start | bytes 884740
  204.4 4.9 %collective-permute-start.8 = (bf16[8,2,128,384]{3,2,1,0:T(8,128)(2,1)}, bf16[8,2,128,384]{3,2,1,0:T(8,128)(2,1)S(1)}, u32[]{:S(2)}, u32[]{:S(2)}) collective-permute-start(bf16[8,2,128,384]{3,2,1,0:T(8,128)(2,1)} %get-tuple-element.74), channel_id=1, source_target_pairs={{0,16},{16,0},{32,48},{48,32},{64,80},{80,64},{96,112},{112,96},{1... | collective-permute-start | bytes 4718600 | tf_op jit(solution)/shard_map/ppermute | solution.py:707
  209.3 1.1 copy-start.6

commit v4 on v3

--- a/solution.py
+++ b/solution.py
@@ -10,18 +10,27 @@
 BF16 = jnp.bfloat16
 BLOCK = 1024
 UNROLL = 4
+TOGETHER = 4
+LAST_UNROLL = 1
 LANES = 128
 SUB = 8
-VMEM_BYTES = 58 * 1024 * 1024
+VMEM_BYTES = 40 * 1024 * 1024
 
 
 def whole():
     return pl.BlockSpec(memory_space=pltpu.VMEM)
 
 
+KERNEL_US = dict(
+    place_norm_project=12, gate=6, conv_states=31, row_scan=20, inner_col=16, chain=3, chip_total=5, entering=6, finish=25
+)
+
+
 def call(body, outs, ins, scratch=(), name=None):
+    work = KERNEL_US[name] * 10**9
     return pl.pallas_call(
         body,
+        cost_estimate=pl.CostEstimate(flops=work, bytes_accessed=work // 400, transcendentals=0),
         out_shape=outs,
         in_specs=ins,
         out_specs=jax.tree.map(lambda _: whole(), outs),
@@ -50,6 +59,11 @@
 
 def dot_tn(a, b):
     return lax.dot_general(a, b, (((0,), (0,)), ((), ())), preferred_element_type=F32)
+
+
+def silu(values):
+    half = 0.5 * values
+    return half + half * jnp.tanh(half)
 
 
 def rms_scale(values, gains):
@@ -112,7 +126,8 @@
     )
 
 
-def place_body(cells, got, gain, in_x, grid_out, inner_out, left_out, right_out, src, dst):
+def place_body(cells, got, gain, in_x, grid_out, inner_out, left_out, right_out, *scratch):
+    src, dst = scratch[:2], scratch[2:]
     slots = got.shape[0]
     channels = grid_out.shape[1]
     cells_n = grid_out.shape[0]
@@ -120,14 +135,16 @@
 
     def fill(i, carry):
         at = pl.ds(pl.multiple_of(i * 256, 256), 256)
-        dst[at, :] = jnp.zeros((256, dst.shape[1]), F32)
+        for part in dst:
+            part[at, :] = jnp.zeros((256, LANES), F32)
         return carry
 
     lax.fori_loop(0, cells_n // 256, fill, 0)
 
     def widen(i, carry):
         at = pl.ds(pl.multiple_of(i * 256, 256), 256)
-        src[at, :] = got[at, :].astype(F32)
+        for m, part in enumerate(src):
+            part[at, :] = got[at, m * LANES : (m + 1) * LANES].astype(F32)
         return carry
 
     lax.fori_loop(0, slots // 256, widen, 0)
@@ -136,14 +153,15 @@
         base = i * 16
         for j in range(16):
             cell = cells[base + j]
-            dst[pl.ds(cell, 1), :] = src[pl.ds(base + j, 1), :]
+            for from_part, to_part in zip(src, dst):
+                to_part[pl.ds(cell, 1), :] = from_part[pl.ds(base + j, 1), :]
         return carry
 
     lax.fori_loop(0, slots // 16, place, 0)
 
     def project(r, carry):
         at = pl.ds(pl.multiple_of(r * cols_n, cols_n), cols_n)
-        tiles = dst[at, :channels]
+        tiles = jnp.concatenate([dst[0][at, :], dst[1][at, : channels - LANES]], axis=1)
         grid_out[at, :] = tiles.astype(BF16)
         normed = rms_scale(tiles, gain[...]).astype(BF16)
         inner = dot(normed, in_x[...]).astype(BF16)
@@ -170,8 +188,10 @@
         outs,
         [pl.BlockSpec(memory_space=pltpu.SMEM), whole(), whole(), whole()],
         [
-            pltpu.VMEM(got.shape, F32),
-            pltpu.VMEM((cells_n + SUB, got.shape[1]), F32),
+            pltpu.VMEM((got.shape[0], LANES), F32),
+            pltpu.VMEM((got.shape[0], LANES), F32),
+            pltpu.VMEM((cells_n + SUB, LANES), F32),
+            pltpu.VMEM((cells_n + SUB, LANES), F32),
         ],
         name="place_norm_project",
     )(cells, got, gain, in_x)
@@ -182,7 +202,7 @@
         at = pl.ds(pl.multiple_of(i * block, block), block)
         normed = rms_scale(grid[at, :].astype(F32), gain[...]).astype(BF16)
         gate = dot(normed, in_z[...]).astype(BF16).astype(F32)
-        gate_out[at, :] = (gate / (1.0 + jnp.exp(-gate))).astype(BF16)
+        gate_out[at, :] = silu(gate).astype(BF16)
         return carry
 
     lax.fori_loop(0, grid.shape[0] // block, step, 0)
@@ -248,7 +268,7 @@
                 last, right_sum[r, :, lanes], pltpu.roll(sums[2], cols_n - 1, 0)
             )
             value = conv_bias[:, lanes] + from_left + sums[1] + from_right
-            scanned = (value / (1.0 + jnp.exp(-value))).astype(BF16)
+            scanned = silu(value).astype(BF16)
             x_out[r, :, lanes] = scanned
             x_wide[r, :, lanes] = scanned.astype(F32)
         coef = dot(x_out[r], x_proj[...]).astype(BF16)
@@ -318,11 +338,13 @@
     return jnp.where((lane // state_size) == 2 * k, rolled, 0.0).astype(BF16)
 
 
-def inner_row_body(x_in, coef_in, into_row, out_row, heads_map, skip, total_out):
+def row_scan_body(x_in, coef_in, enter_row, into_row, out_row, heads_map, skip, total_out):
     rows_n, cols_n, width = x_in.shape
     t_row = lax.broadcasted_iota(jnp.int32, (cols_n, cols_n), 0)
     u_row = lax.broadcasted_iota(jnp.int32, (cols_n, cols_n), 1)
     masks = (t_row >= u_row, t_row <= u_row)
+
+    state_size = LANES // 8
 
     def row_step(r):
         x_row = x_in[r].astype(F32)
@@ -332,17 +354,22 @@
         for k in range(2):
             scores = dot_nt(c_at_b(wide, k), coef)
             mixing = jnp.where(masks[k], scores, 0.0).astype(BF16)
+            c_part = coef[:, (2 * k + 1) * state_size : (2 * k + 2) * state_size]
             scaled = (x_row * spread(into_row[k, r], heads_map[...])).astype(BF16)
-            total = total + dot(mixing, scaled) * spread(out_row[k, r], heads_map[...])
+            both = dot(
+                jnp.concatenate([mixing, c_part], axis=1),
+                jnp.concatenate([scaled, enter_row[r, k]], axis=0),
+            )
+            total = total + both * spread(out_row[k, r], heads_map[...])
         total_out[r] = total.astype(BF16)
 
     loop(rows_n, row_step, UNROLL)
 
 
-def inner_row(x_in, coef_in, into_row, out_row, heads_map, skip):
-    return call(
-        inner_row_body, jax.ShapeDtypeStruct(x_in.shape, BF16), [whole()] * 6, name="inner_row"
-    )(x_in, coef_in, into_row, out_row, heads_map, skip)
+def row_scan(x_in, *rest):
+    return call(
+        row_scan_body, jax.ShapeDtypeStruct(x_in.shape, BF16), [whole()] * 7, name="row_scan"
+    )(x_in, *rest)
 
 
 def inner_col_body(x_in, coef_in, into_col, out_col, heads_map, total_out, x_wide, coef_wide, acc):
@@ -471,7 +498,7 @@
                 send[j, deep:, :] = jnp.zeros((rows - 2 * deep, width), BF16)
                 send[j, deep:, :LANES] = tile
 
-        loop(groups, step, 1)
+        loop(groups, step, 4)
 
     by_core(spot, run, own, got)
 
@@ -525,7 +552,7 @@
             enter_lower[j, 0] = lower_2.reshape(deep, width).astype(BF16)
             enter_lower[j, 1] = (low_3 * rise).reshape(deep, width).astype(BF16)
 
-        loop(groups, step, 1)
+        loop(groups, step, 4)
 
     @pl.when(spot[0] == 0)
     def _():
@@ -557,25 +584,17 @@
 
 
 def finish_body(
-    spot, total_row, total_col, coef_in, enter_row, enter_own, enter_other, out_row, out_col, heads_map, pick_c, gate_in, grid, out_gain, out_w,
-    mlp_gain, ff_in, ff_out, block_out, coef_wide, acc,
+    spot, total_row, total_col, coef_in, enter_own, enter_other, out_col, heads_map, pick_c, gate_in, grid,
+    out_gain, out_w, mlp_gain, ff_in, ff_out, block_out, coef_wide, acc,
 ):
     rows_n, cols_n, width = total_row.shape
-    state_size = LANES // 8
     half = enter_own.shape[0]
 
-    def row_step(r, carry):
-        coef = coef_in[r]
-        wide = coef.astype(F32)
-        coef_wide[r] = wide
-        value = total_row[r].astype(F32) + total_col[r].astype(F32)
-        for k in range(2):
-            c_part = coef[:, (2 * k + 1) * state_size : (2 * k + 2) * state_size]
-            value = value + dot(c_part, enter_row[r, k]) * spread(out_row[k, r], heads_map[...])
-        acc[r] = value
-        return carry
-
-    loop(rows_n, lambda r: row_step(r, 0), UNROLL)
+    def widen(r):
+        coef_wide[r] = coef_in[r].astype(F32)
+        acc[r] = total_row[r].astype(F32) + total_col[r].astype(F32)
+
+    loop(rows_n, widen, UNROLL)
     size = rows_n * SUB
     own = own_column((size, LANES), SUB, SUB)
 
@@ -591,27 +610,30 @@
             acc[:, at, :] = value.reshape(rows_n, SUB, width)
 
     loop(half, col_step, UNROLL // 2)
-
-    def last(r, carry):
-        at = pl.ds(pl.multiple_of(r * cols_n, cols_n), cols_n)
-        gated = (rms_scale(acc[r], out_gain[...]) * gate_in[at, :].astype(F32)).astype(BF16)
-        middle = (dot(gated, out_w[...]) + grid[at, :].astype(F32)).astype(BF16)
+    deep = TOGETHER * cols_n
+
+    def last(i):
+        at = pl.ds(pl.multiple_of(i * deep, deep), deep)
+        value = acc[pl.ds(i * TOGETHER, TOGETHER)].reshape(deep, width)
+        gated = (rms_scale(value, out_gain[...]) * gate_in[at, :].astype(F32)).astype(BF16)
+        middle = (dot_nt(gated, out_w[...]) + grid[at, :].astype(F32)).astype(BF16)
         wide = middle.astype(F32)
         normed = rms_scale(wide, mlp_gain[...]).astype(BF16)
         hidden = dot(normed, ff_in[...])
         hidden = (hidden * (0.5 + 0.5 * lax.erf(hidden * (0.5**0.5)))).astype(BF16)
-        block_out[r] = (dot(hidden, ff_out[...]) + wide).astype(BF16)
-        return carry
-
-    loop(rows_n, lambda r: last(r, 0), UNROLL)
+        result = dot_nt(hidden, ff_out[...]) + wide
+        for j in range(TOGETHER):
+            block_out[i * TOGETHER + j] = result[j * cols_n : (j + 1) * cols_n].T.astype(BF16)
+
+    loop(rows_n // TOGETHER, last, LAST_UNROLL)
 
 
 def finish(spot, total, total_col, coef, *rest, channels):
     rows_n, cols_n, width = total.shape
     return call(
         finish_body,
-        jax.ShapeDtypeStruct((rows_n, cols_n, channels), BF16),
-        [pl.BlockSpec(memory_space=pltpu.SMEM)] + [whole()] * 17,
+        jax.ShapeDtypeStruct((rows_n, channels, cols_n), BF16),
+        [pl.BlockSpec(memory_space=pltpu.SMEM)] + [whole()] * 15,
         [pltpu.VMEM(coef.shape, F32), pltpu.VMEM(total.shape, F32)],
         name="finish",
     )(spot, total, total_col, coef, *rest)
@@ -687,28 +709,29 @@
     twin = [(i, i ^ 1) for i in range(lines)]
     state_got = lax.ppermute(state_other, "row", twin)
     split_row = lax.all_to_all(state_row, "col", split_axis=0, concat_axis=0, tiled=True)
-    gated = gate(grid, norm_gain[None], in_z)
-    state_got, gated = order((state_got, gated))
     sends = chip_total(spot, state_own, state_got, heads_map, chips)
     receipts = [
         lax.ppermute(send, "row", [(i, (i + 2 * shift) % lines) for i in range(lines)])
         for shift, send in enumerate(sends, 1)
     ]
-    x_row, sends = order((x_in, sends))
-    total = inner_row(x_row, coef, into_row, out_row, heads_map, skip_gain[None])
-    split_row, total = order((split_row, total))
+    x_col, sends = order((x_in, sends))
+    total_col = inner_col(x_col, coef, into_col, out_col, heads_map)
+    split_row, total_col = order((split_row, total_col))
     passed = chain(split_row, heads_map, rows_n // peers)
     enter_row = lax.all_to_all(passed, "col", split_axis=0, concat_axis=0, tiled=True)
     enter_row = enter_row.reshape(rows_n, 2, state_size, width)
-    x_col, passed = order((x_in, passed))
-    total_col = inner_col(x_col, coef, into_col, out_col, heads_map)
-    receipts, total_col, enter_row = order((receipts, total_col, enter_row))
+    grid_in, passed = order((grid, passed))
+    gated = gate(grid_in, norm_gain[None], in_z)
+    receipts, gated = order((receipts, gated))
     enter_own, enter_other = entering_states(spot, state_own, state_got, heads_map, receipts)
+    x_row, enter_own, enter_other = order((x_in, enter_own, enter_other))
     enter_other = lax.ppermute(enter_other, "row", twin)
-    return finish(
-        spot, total, total_col, coef, enter_row, enter_own, enter_other, out_row, out_col, heads_map, pick_c, gated, grid, out_gain[None], out_w,
-        mlp_gain[None], ff_in, ff_out, channels=channels,
-    )
+    total = row_scan(x_row, coef, enter_row, into_row, out_row, heads_map, skip_gain[None])
+    block = finish(
+        spot, total, total_col, coef, enter_own, enter_other, out_col, heads_map, pick_c, gated, grid,
+        out_gain[None], out_w.T, mlp_gain[None], ff_in, ff_out.T, channels=channels,
+    )
+    return jnp.swapaxes(block, 1, 2)
 
 
 def solution(mesh):

time: 250 us -> 221 us (0.88)
  Pallas kernels: 145 us -> 101 us
  waiting for transfers between devices: 14.3 us -> 27.5 us
  local copies, waits for them, and re-layouts: 33.2 us -> 41 us
  other arithmetic: 12.8 us -> 6.97 us
    pallas_call x2, Pallas kernels: 53.5 us -> 37.1 us  [the longest x1 21.2 us: finish(): call(finish_body, jax.ShapeDtypeStruct((rows_n, channels, cols_n), BF16),...]
    unnamed x36 -> x72, local copies, waits for them, and re-layouts: 10.1 us -> 25.6 us
    pallas_call x1, Pallas kernels: 21.5 us -> 10.1 us  [place(): call(place_body, outs, [pl.BlockSpec(memory_space=pltpu.SMEM), whole(), w...]
    ppermute x3, waiting for transfers between devices: 0.01 us -> 10.2 us  [local(): lax.ppermute(send, 'row', [(i, (i + 2 * shift) % lines) for i in range(li...]
    pallas_call x1, Pallas kernels: 16.2 us -> 12.3 us  [inner_col(): call(inner_col_body, jax.ShapeDtypeStruct(x_in.shape, BF16), [whole()] *...]
    pallas_call x1 -> x0, local copies, waits for them, and re-layouts: 3.92 us -> none  [finish(): call(finish_body, jax.ShapeDtypeStruct((rows_n, cols_n, channels), BF16),...]
    pallas_call x1, Pallas kernels: 6.38 us -> 2.52 us  [gate(): call(functools.partial(gate_body, block=BLOCK), jax.ShapeDtypeStruct((gri...]
    pallas_call x1, Pallas kernels: 31.5 us -> 27.9 us  [conv_and_states(): call(conv_body, outs, [pl.BlockSpec(memory_space=pltpu.SMEM)] + [whole()]...]
  transfers between devices with their start and end apart: 12 -> 12, of which waited for: 4 -> 5; matrix products, arithmetic and copies ran while one was open for 10% -> 8% of each run, Pallas kernels for 20% -> 19%
where the time goes in v4:
time: 221 us
  Pallas kernels  101 us (46%)
  starting transfers between devices  41.9 us (19%)
  local copies, waits for them, and re-layouts  41 us (19%)
  waiting for transfers between devices  27.5 us (12%)
  other arithmetic  6.97 us (3%)
    pallas_call x1, Pallas kernels, conv_and_states(): call(conv_body, outs, [pl.BlockSpec(memory_space=pltpu.SMEM)] + [whole()]...  27.9 us
    unnamed x72, local copies, waits for them, and re-layouts  25.6 us
    pallas_call x1, Pallas kernels, finish(): call(finish_body, jax.ShapeDtypeStruct((rows_n, channels, cols_n), BF16),...  21.2 us
    pallas_call x1, Pallas kernels, row_scan(): call(row_scan_body, jax.ShapeDtypeStruct(x_in.shape, BF16), [whole()] * 7...  15.8 us
    all_to_all x1, waiting for transfers between devices, local(): lax.all_to_all(sent, ('row', 'col'), split_axis=0, concat_axis=0, tiled=T...  14.5 us
    pallas_call x1, Pallas kernels, inner_col(): call(inner_col_body, jax.ShapeDtypeStruct(x_in.shape, BF16), [whole()] *...  12.3 us
    all_to_all x1, starting transfers between devices, local(): lax.all_to_all(sent, ('row', 'col'), split_axis=0, concat_axis=0, tiled=T...  11.5 us
    ppermute x4, starting transfers between devices, shifted(): return lax.ppermute(block, axis, pairs)  11.2 us
  transfers between devices with their start and end apart: 12, of which 5 were waited for; matrix products, arithmetic and copies ran while one was open for 8% of the time, Pallas kernels for 19%

profile of v4, /device:TPU:1, one launch (start us, length us, event | category | flops | bytes accessed | tf_op | source)
XLA Modules:
  0.0 220.6 jit_solution(16517894400653295217)
XLA Ops:
  0.0 0.7 fusion.40
  0.8 2.6 %copy.105 = bf16[128,32,2]{2,1,0:T(8,128)(2,1)} copy(bf16[128,32,2]{0,1,2:T(8,128)(2,1)S(1)} %pad_maximum_fusion.3) | data formatting | bytes 32768
  3.3 3.3 %copy.78 = bf16[1,128,32,192]{3,2,1,0:T(8,128)(2,1)S(1)} copy(bf16[1,128,32,192]{1,3,2,0:T(8,128)(2,1)} %param.18) | data formatting | bytes 3145728 | tf_op args[0]
  6.7 0.1 copy.77
  6.8 0.8 bitcast_select_fusion
  7.6 0.4 copy-done.27
  8.0 2.1 fusion.1
  10.1 11.5 %all-to-all-start = ((bf16[128,32,256]{2,1,0:T(8,128)(2,1)}), bf16[128,32,256]{2,1,0:T(8,128)(2,1)S(1)}, u32[]{:S(2)}, u32[]{:S(2)}) async-start(bf16[128,32,256]{2,1,0:T(8,128)(2,1)} %fusion.1), calls=%async_computation | async-start | bytes 4194304 | tf_op jit(solution)/shard_map/all_to_all | solution.py:664
  21.6 0.1 slice_reduce_fusion.1
  21.8 0.3 fusion.18
  22.1 0.4 fusion.20
  22.4 0.3 fusion.22
  22.8 0.3 fusion.24
  23.1 0.1 copy.86
  23.5 0.1 broadcast_in_dim.79
  23.7 0.7 reduce-precision_convert_fusion
  24.4 0.4 fusion.8
  24.9 1.4 copy.87
  26.2 3.8 %copy.88 = bf16[2,16,16,32,8]{2,4,3,1,0:T(8,128)(2,1)} copy(bf16[2,16,16,32,8]{3,4,1,2,0:T(8,128)(2,1)} %bitcast.115) | data formatting | bytes 524288 | tf_op jit(solution)/shard_map/transpose | solution.py:92
  30.1 1.4 copy.89
  31.4 3.8 %copy.90 = bf16[2,16,16,32,8]{2,4,3,1,0:T(8,128)(2,1)} copy(bf16[2,16,16,32,8]{3,4,1,2,0:T(8,128)(2,1)} %bitcast.116) | data formatting | bytes 524288 | tf_op jit(solution)/shard_map/transpose | solution.py:92
  35.3 0.1 copy.96
  35.5 0.1 reshape.454
  36.1 0.1 iota_compare_fusion.4
  36.3 14.5 %all-to-all-done = bf16[128,32,256]{2,1,0:T(8,128)(2,1)S(1)} async-done(((bf16[128,32,256]{2,1,0:T(8,128)(2,1)}), bf16[128,32,256]{2,1,0:T(8,128)(2,1)S(1)}, u32[]{:S(2)}, u32[]{:S(2)}) %all-to-all-start) | async-done | bytes 2097184 | tf_op jit(solution)/shard_map/all_to_all | solution.py:664
  50.9 1.4 add_reduce_fusion.cells
  52.3 10.1 %place_norm_project.1 = (bf16[4096,192]{1,0:T(8,128)(2,1)S(1)}, bf16[4096,384]{1,0:T(8,128)(2,1)S(1)}, f32[32,384]{1,0:T(8,128)S(1)}, f32[32,384]{1,0:T(8,128)S(1)}) custom-call(s32[4096]{0:T(1024)S(1)} %add_reduce_fusion.cells, bf16[4096,256]{1,0:T(8,128)(2,1)S(1)} %bitcast.105, f32[1,192]{1,0:T(1,128)S(1)} %bitcast.110, bf16[192,384]{1,0:T(8,128)(2,1)S(1)} %copy-done.4), custom_call_target="tpu_custom_call" | custom-call | flops 12000000000 | bytes 30000000 | tf_op jit(solution)/shard_map/place_norm_project/pallas_call | solution.py:186
  62.4 1.3 copy-done.11
  63.7 3.2 %collective-permute-start = (bf16[32,384]{1,0:T(8,128)(2,1)S(1)}, bf16[32,384]{1,0:T(8,128)(2,1)S(1)}, u32[]{:S(2)}, u32[]{:S(2)}) collective-permute-start(bf16[32,384]{1,0:T(8,128)(2,1)S(1)} %convert.13), channel_id=1, source_target_pairs={{0,1},{1,2},{2,3},{3,4},{4,5},{5,6},{6,7},{7,8},{8,9},{9,10},{10,1... | collective-permute-start | bytes 73736 | tf_op jit(solution)/shard_map/ppermute | solution.py:645
  66.9 1.6 copy-done
  68.5 1.3 collective-permute-start.1
  69.8 1.9 copy.99.into_col
  71.7 1.4 collective-permute-done.1
  73.1 4.1 %collective-permute-start.3 = (bf16[130,384]{1,0:T(8,128)(2,1)S(1)}, bf16[130,384]{1,0:T(8,128)(2,1)S(1)}, u32[]{:S(2)}, u32[]{:S(2)}) collective-permute-start(bf16[130,384]{1,0:T(8,128)(2,1)S(1)} %pad_maximum_fusion.2), channel_id=1, source_target_pairs={{16,0},{32,16},{48,32},{64,48},{80,64},{96,80},{112,96},{17,1},{33... | collective-permute-start | bytes 299528 | tf_op jit(solution)/shard_map/ppermute | solution.py:645
  77.2 2.7 %collective-permute-start.2 = (bf16[130,384]{1,0:T(8,128)(2,1)S(1)}, bf16[130,384]{1,0:T(8,128)(2,1)S(1)}, u32[]{:S(2)}, u32[]{:S(2)}) collective-permute-start(bf16[130,384]{1,0:T(8,128)(2,1)S(1)} %pad_maximum_fusion.1), channel_id=1, source_target_pairs={{0,16},{16,32},{32,48},{48,64},{64,80},{80,96},{96,112},{1,17},{17... | collective-permute-start | bytes 299528 | tf_op jit(solution)/shard_map/ppermute | solution.py:645
  80.0 0.1 collective-permute-done.3
  80.1 1.3 collective-permute-done.2
  81.6 1.9 copy-done.1
  83.5 27.9 %conv_states.1 = (bf16[32,128,384]{2,1,0:T(8,128)(2,1)S(1)}, bf16[32,128,128]{2,1,0:T(8,128)(2,1)S(1)}, bf16[16,80,384]{2,1,0:T(8,128)(2,1)}, bf16[8,272,384]{2,1,0:T(8,128)(2,1)S(1)}, bf16[8,272,384]{2,1,0:T(8,128)(2,1)}) custom-call(s32[2]{0:T(128)S(1)} %pad_add_fusion.spot, bf16[32,128,384]{2,1,0:T(8,128)(2,1)S(1)} %bitcast.107, ...), custom_call_target="tpu_custom_call" | custom-call | flops 31000000512 | bytes 77500000 | tf_op jit(solution)/shard_map/conv_states/pallas_call | solution.py:319
  111.5 1.2 copy-done.14
  112.7 1.6 copy-done.19
  114.3 1.0 copy-done.24
  115.3 1.9 copy.101.out_col
  117.2 6.2 %all-to-all-start.1 = ((bf16[16,80,384]{2,1,0:T(8,128)(2,1)}), bf16[16,80,384]{2,1,0:T(8,128)(2,1)S(1)}, u32[]{:S(2)}, u32[]{:S(2)}) async-start(bf16[16,80,384]{2,1,0:T(8,128)(2,1)} %get-tuple-element.59), calls=%async_computation.1 | async-start | bytes 1966080 | tf_op jit(solution)/shard_map/all_to_all | solution.py:711
  123.5 1.4 copy-done.15
  124.9 4.3 %chip_total.1 = (bf16[8,144,384]{2,1,0:T(8,128)(2,1)}, bf16[8,144,384]{2,1,0:T(8,128)(2,1)}, bf16[8,144,384]{2,1,0:T(8,128)(2,1)}) custom-call(s32[2]{0:T(128)S(1)} %pad_add_fusion.spot, bf16[8,272,384]{2,1,0:T(8,128)(2,1)S(1)} %copy-done.15, bf16[8,272,384]{2,1,0:T(8,128)(2,1)} %collective-permute-done.4.got, bf16[16,384]{1,0:T(8,128)(2,1)S(1)} %and_convert_fusion.heads_map), custom_call_target="tpu_custom_call" | custom-call | flops 5000000000 | bytes 12500000 | tf_op jit(solution)/shard_map/chip_total/pallas_call | solution.py:509
  129.2 2.5 %collective-permute-start.5 = (bf16[8,144,384]{2,1,0:T(8,128)(2,1)}, bf16[8,144,384]{2,1,0:T(8,128)(2,1)}, u32[]{:S(2)}, u32[]{:S(2)}) collective-permute-start(bf16[8,144,384]{2,1,0:T(8,128)(2,1)} %get-tuple-element.55), channel_id=1, source_target_pairs={{0,32},{16,48},{32,64},{48,80},{64,96},{80,112},{96,0},{112,16},{1... | collective-permute-start | bytes 2654216 | tf_op jit(solution)/shard_map/ppermute | solution.py:714
  131.7 2.0 collective-permute-start.6
  133.7 0.7 collective-permute-start.7
  134.5 12.3 %inner_col.1.total_col = bf16[32,128,384]{2,1,0:T(8,128)(2,1)S(1)} custom-call(bf16[32,128,384]{2,1,0:T(8,128)(2,1)S(1)} %copy-done.20, bf16[32,128,128]{2,1,0:T(8,128)(2,1)S(1)} %copy-done.25, bf16[2,16,16,256]{3,2,1,0:T(8,128)(2,1)S(1)} %copy.99.into_col, bf16[2,16,16,256]{3,2,1,0:T(8,128)(2,1)S(1)} %copy.101.out_col, ...), custom_call_target="tpu_custom_call" | custom-call | flops 16000000000 | bytes 40000000 | tf_op jit(solution)/shard_map/inner_col/pallas_call | solution.py:411
  146.8 1.7 copy-done.22
  148.4 1.3 chain.1
  149.8 6.7 %all-to-all-start.2 = ((bf16[16,64,384]{2,1,0:T(8,128)(2,1)}), bf16[16,64,384]{2,1,0:T(8,128)(2,1)S(1)}, u32[]{:S(2)}, u32[]{:S(2)}) async-start(bf16[16,64,384]{2,1,0:T(8,128)(2,1)} %chain.1), calls=%async_computation.2 | async-start | bytes 1572864 | tf_op jit(solution)/shard_map/all_to_all | solution.py:721
  156.4 1.6 copy-done.12
  158.0 2.5 %gate.1.gate_in = bf16[4096,384]{1,0:T(8,128)(2,1)S(1)} custom-call(bf16[4096,192]{1,0:T(8,128)(2,1)S(1)} %copy-done.12, f32[1,192]{1,0:T(1,128)S(1)} %bitcast.111, bf16[192,384]{1,0:T(8,128)(2,1)S(1)} %copy-done.5), custom_call_target="tpu_custom_call" | custom-call | flops 6000000000 | bytes 15000000 | tf_op jit(solution)/shard_map/gate/pallas_call | solution.py:212
  160.6 1.7 copy-done.10
  162.3 10.2 %collective-permute-done.6.rest_1_ = bf16[8,144,384]{2,1,0:T(8,128)(2,1)} collective-permute-done((bf16[8,144,384]{2,1,0:T(8,128)(2,1)}, bf16[8,144,384]{2,1,0:T(8,128)(2,1)}, u32[]{:S(2)}, u32[]{:S(2)}) %collective-permute-start.6) | collective-permute-done | bytes 884768 | tf_op jit(solution)/shard_map/ppermute | solution.py:714
  172.5 5.6 %entering.1 = (bf16[8,2,128,384]{3,2,1,0:T(8,128)(2,1)S(1)}, bf16[8,2,128,384]{3,2,1,0:T(8,128)(2,1)}) custom-call(s32[2]{0:T(128)S(1)} %pad_add_fusion.spot, bf16[8,272,384]{2,1,0:T(8,128)(2,1)S(1)} %copy-done.16, bf16[8,272,384]{2,1,0:T(8,128)(2,1)} %collective-permute-done.4.got, bf16[16,384]{1,0:T(8,128)(2,1)S(1)} %and_convert_fusion.heads_map, ...), custom_call_target="tpu_custom_call" | custom-call | flops 6000000000 | bytes 15000000 | tf_op jit(solution)/shard_map/entering/pallas_call | solution.py:569
  178.1 1.1 copy-done.17
  179.2 1.1 collective-permute-start.8
  180.3 1.9 copy-done.21
  182.2 1.2 copy-done.26
  183.5 15.8 %row_scan.1.total_row = bf16[32,128,384]{2,1,0:T(8,128)(2,1)S(1)} custom-call(bf16[32,128,384]{2,1,0:T(8,128)(2,1)S(1)} %copy-done.21, bf16[32,128,128]{2,1,0:T(8,128)(2,1)S(1)} %copy-done.26, bf16[32,2,16,384]{3,2,1,0:T(8,128)(2,1)S(1)} %bitcast.106, bf16[2,32,16,128]{3,2,1,0:T(8,128)(2,1)S(1)} %get-tuple-element.46.into_row, ...), custom_call_target="tpu_custom_call" | custom-call | flops 20000000000 | bytes 50000000 | tf_op jit(solution)/shard_map/row_scan/pallas_call | solution.py:370
  199.4 21.2 %finish.1 = bf16[32,192,128]{2,1,0:T(8,128)(2,1)} custom-call(s32[2]{0:T(128)S(1)} %pad_add_fusion.spot, bf16[32,128,384]{2,1,0:T(8,128)(2,1)S(1)} %row_scan.1.total_row, bf16[32,128,384]{2,1,0:T(8,128)(2,1)S(1)} %copy-done.23, bf16[32,128,128]{2,1,0:T(8,128)(2,1)S(1)} %copy-done.26, bf16[8,2,128,384]{3,2,1,0:T(8,128)(2,1)S(1)} %copy-done.18, ...), custom_call_target="tpu_custom_call" | custom-call | flops 24999999488 | bytes 62500000 | tf_op jit(solution)/shard_map/finish/pallas_call | solution.py:633
  (119 shorter events, 1.5 us)
Async XLA Ops:
  3.3 3.3 %copy-start.30 = (s32[1,128,32]{1,2,0:T(8,128)S(1)}, s32[1,128,32]{1,2,0:T(8,128)}, u32[]{:S(2)}) copy-start(s32[1,128,32]{1,2,0:T(8,128)} %param.20) | copy-start | bytes 49156
  3.3 3.5 %copy-start.34 = (bf16[192]{0:T(256)(128)(2,1)S(1)}, bf16[192]{0:T(256)(128)(2,1)}, u32[]{:S(2)}) copy-start(bf16[192]{0:T(256)(128)(2,1)} %param.22) | copy-start | bytes 1156
  6.8 1.2 copy-start.27
  10.1 11.5 %copy-start.28 = (f32[4,6,32,128]{3,2,1,0:T(8,128)S(1)}, f32[4,6,32,128]{3,2,1,0:T(8,128)}, u32[]{:S(2)}) copy-start(f32[4,6,32,128]{3,2,1,0:T(8,128)} %param.30) | copy-start | bytes 1179652
  10.1 40.8 %all-to-all-start = ((bf16[128,32,256]{2,1,0:T(8,128)(2,1)}), bf16[128,32,256]{2,1,0:T(8,128)(2,1)S(1)}, u32[]{:S(2)}, u32[]{:S(2)}) async-start(bf16[128,32,256]{2,1,0:T(8,128)(2,1)} %fusion.1), calls=%async_computation | async-start | bytes 4194304 | tf_op jit(solution)/shard_map/all_to_all | solution.py:664
  31.4 4.4 %copy-start.29 = (f32[3,3,384]{2,1,0:T(4,128)S(1)}, f32[3,3,384]{2,1,0:T(4,128)}, u32[]{:S(2)}) copy-start(f32[3,3,384]{2,1,0:T(4,128)} %param.26) | copy-start | bytes 41476
  31.4 4.5 %copy-start.31 = (f32[384]{0:T(512)S(1)}, f32[384]{0:T(512)}, u32[]{:S(2)}) copy-start(f32[384]{0:T(512)} %param.27) | copy-start | bytes 4612
  35.3 17.0 %copy-start.4 = (bf16[192,384]{1,0:T(8,128)(2,1)S(1)}, bf16[192,384]{1,0:T(8,128)(2,1)}, u32[]{:S(2)}) copy-start(bf16[192,384]{1,0:T(8,128)(2,1)} %in_x.1) | copy-start | bytes 442372
  35.3 17.0 %copy-start.8 = (f32[192]{0:T(256)S(1)}, f32[192]{0:T(256)}, u32[]{:S(2)}) copy-start(f32[192]{0:T(256)} %param.23) | copy-start | bytes 2308
  62.4 1.3 copy-start.11
  63.7 17.9 %copy-start.7 = (bf16[384,128]{1,0:T(8,128)(2,1)S(1)}, bf16[384,128]{1,0:T(8,128)(2,1)}, u32[]{:S(2)}) copy-start(bf16[384,128]{1,0:T(8,128)(2,1)} %x_proj.1) | copy-start | bytes 294916
  63.7 8.0 %collective-permute-start = (bf16[32,384]{1,0:T(8,128)(2,1)S(1)}, bf16[32,384]{1,0:T(8,128)(2,1)S(1)}, u32[]{:S(2)}, u32[]{:S(2)}) collective-permute-start(bf16[32,384]{1,0:T(8,128)(2,1)S(1)} %convert.13), channel_id=1, source_target_pairs={{0,1},{1,2},{2,3},{3,4},{4,5},{5,6},{6,7},{7,8},{8,9},{9,10},{10,1... | collective-permute-start | bytes 73736 | tf_op jit(solution)/shard_map/ppermute | solution.py:645
  66.9 1.6 copy-start
  68.5 4.6 %collective-permute-start.1 = (bf16[32,384]{1,0:T(8,128)(2,1)S(1)}, bf16[32,384]{1,0:T(8,128)(2,1)S(1)}, u32[]{:S(2)}, u32[]{:S(2)}) collective-permute-start(bf16[32,384]{1,0:T(8,128)(2,1)S(1)} %convert.12), channel_id=1, source_target_pairs={{1,0},{2,1},{3,2},{4,3},{5,4},{6,5},{7,6},{8,7},{9,8},{10,9},{11,1... | collective-permute-start | bytes 73736 | tf_op jit(solution)/shard_map/ppermute | solution.py:645
  73.1 7.0 %collective-permute-start.3 = (bf16[130,384]{1,0:T(8,128)(2,1)S(1)}, bf16[130,384]{1,0:T(8,128)(2,1)S(1)}, u32[]{:S(2)}, u32[]{:S(2)}) collective-permute-start(bf16[130,384]{1,0:T(8,128)(2,1)S(1)} %pad_maximum_fusion.2), channel_id=1, source_target_pairs={{16,0},{32,16},{48,32},{64,48},{80,64},{96,80},{112,96},{17,1},{33... | collective-permute-start | bytes 299528 | tf_op jit(solution)/shard_map/ppermute | solution.py:645
  77.2 4.2 %collective-permute-start.2 = (bf16[130,384]{1,0:T(8,128)(2,1)S(1)}, bf16[130,384]{1,0:T(8,128)(2,1)S(1)}, u32[]{:S(2)}, u32[]{:S(2)}) collective-permute-start(bf16[130,384]{1,0:T(8,128)(2,1)S(1)} %pad_maximum_fusion.1), channel_id=1, source_target_pairs={{0,16},{16,32},{32,48},{48,64},{64,80},{80,96},{96,112},{1,17},{17... | collective-permute-start | bytes 299528 | tf_op jit(solution)/shard_map/ppermute | solution.py:645
  81.6 1.9 copy-start.1
  83.5 31.8 %copy-start.32 = (f32[384]{0:T(512)S(1)}, f32[384]{0:T(512)}, u32[]{:S(2)}) copy-start(f32[384]{0:T(512)} %param.29) | copy-start | bytes 4612
  83.5 31.8 %copy-start.33 = (f32[384]{0:T(512)S(1)}, f32[384]{0:T(512)}, u32[]{:S(2)}) copy-start(f32[384]{0:T(512)} %param.31) | copy-start | bytes 4612
  111.5 1.2 copy-start.14
  112.7 1.6 copy-start.19
  114.3 1.0 copy-start.24
  115.3 8.1 %collective-permute-start.4 = (bf16[8,272,384]{2,1,0:T(8,128)(2,1)}, bf16[8,272,384]{2,1,0:T(8,128)(2,1)}, u32[]{:S(2)}, u32[]{:S(2)}) collective-permute-start(bf16[8,272,384]{2,1,0:T(8,128)(2,1)} %get-tuple-element.54), channel_id=1, source_target_pairs={{0,16},{16,0},{32,48},{48,32},{64,80},{80,64},{96,112},{112,96},{1... | collective-permute-start | bytes 5013512 | tf_op jit(solution)/shard_map/ppermute | solution.py:710
  117.2 31.2 %all-to-all-start.1 = ((bf16[16,80,384]{2,1,0:T(8,128)(2,1)}), bf16[16,80,384]{2,1,0:T(8,128)(2,1)S(1)}, u32[]{:S(2)}, u32[]{:S(2)}) async-start(bf16[16,80,384]{2,1,0:T(8,128)(2,1)} %get-tuple-element.59), calls=%async_computation.1 | async-start | bytes 1966080 | tf_op jit(solution)/shard_map/all_to_all | solution.py:711
  123.4 1.4 copy-start.15
  124.9 9.6 %copy-start.20 = (bf16[32,128,384]{2,1,0:T(8,128)(2,1)S(1)}, bf16[32,128,384]{2,1,0:T(8,128)(2,1)}, u32[]{:S(2)}) copy-start(bf16[32,128,384]{2,1,0:T(8,128)(2,1)} %copy-done.19) | copy-start | bytes 9437188
  124.9 9.6 %copy-start.25 = (bf16[32,128,128]{2,1,0:T(8,128)(2,1)S(1)}, bf16[32,128,128]{2,1,0:T(8,128)(2,1)}, u32[]{:S(2)}) copy-start(bf16[32,128,128]{2,1,0:T(8,128)(2,1)} %copy-done.24) | copy-start | bytes 3145732
  129.2 33.1 %collective-permute-start.5 = (bf16[8,144,384]{2,1,0:T(8,128)(2,1)}, bf16[8,144,384]{2,1,0:T(8,128)(2,1)}, u32[]{:S(2)}, u32[]{:S(2)}) collective-permute-start(bf16[8,144,384]{2,1,0:T(8,128)(2,1)} %get-tuple-element.55), channel_id=1, source_target_pairs={{0,32},{16,48},{32,64},{48,80},{64,96},{80,112},{96,0},{112,16},{1... | collective-permute-start | bytes 2654216 | tf_op jit(solution)/shard_map/ppermute | solution.py:714
  131.7 40.8 %collective-permute-start.6 = (bf16[8,144,384]{2,1,0:T(8,128)(2,1)}, bf16[8,144,384]{2,1,0:T(8,128)(2,1)}, u32[]{:S(2)}, u32[]{:S(2)}) collective-permute-start(bf16[8,144,384]{2,1,0:T(8,128)(2,1)} %get-tuple-element.56), channel_id=1, source_target_pairs={{0,64},{16,80},{32,96},{48,112},{64,0},{80,16},{96,32},{112,48},{1... | collective-permute-start | bytes 2654216 | tf_op jit(solution)/shard_map/ppermute | solution.py:714
  133.7 38.8 %collective-permute-start.7 = (bf16[8,144,384]{2,1,0:T(8,128)(2,1)}, bf16[8,144,384]{2,1,0:T(8,128)(2,1)}, u32[]{:S(2)}, u32[]{:S(2)}) collective-permute-start(bf16[8,144,384]{2,1,0:T(8,128)(2,1)} %get-tuple-element.57), channel_id=1, source_target_pairs={{0,96},{16,112},{32,0},{48,16},{64,32},{80,48},{96,64},{112,80},{1... | collective-permute-start | bytes 2654216 | tf_op jit(solution)/shard_map/ppermute | solution.py:714
  146.8 1.7 copy-start.22
  148.4 8.0 %copy-start.5 = (bf16[192,384]{1,0:T(8,128)(2,1)S(1)}, bf16[192,384]{1,0:T(8,128)(2,1)}, u32[]{:S(2)}) copy-start(bf16[192,384]{1,0:T(8,128)(2,1)} %in_z.1) | copy-start | bytes 442372
  149.8 30.6 %all-to-all-start.2 = ((bf16[16,64,384]{2,1,0:T(8,128)(2,1)}), bf16[16,64,384]{2,1,0:T(8,128)(2,1)S(1)}, u32[]{:S(2)}, u32[]{:S(2)}) async-start(bf16[16,64,384]{2,1,0:T(8,128)(2,1)} %chain.1), calls=%async_computation.2 | async-start | bytes 1572864 | tf_op jit(solution)/shard_map/all_to_all | solution.py:721
  156.4 1.6 copy-start.12
  158.0 14.5 %copy-start.16 = (bf16[8,272,384]{2,1,0:T(8,128)(2,1)S(1)}, bf16[8,272,384]{2,1,0:T(8,128)(2,1)}, u32[]{:S(2)}) copy-start(bf16[8,272,384]{2,1,0:T(8,128)(2,1)} %copy-done.14) | copy-start | bytes 5013508
  160.6 1.7 copy-start.10
  178.1 1.1 copy-start.17
  179.2 20.1 %collective-permute-start.8 = (bf16[8,2,128,384]{3,2,1,0:T(8,128)(2,1)}, bf16[8,2,128,384]{3,2,1,0:T(8,128)(2,1)}, u32[]{:S(2)}, u32[]{:S(2)}) collective-permute-start(bf16[8,2,128,384]{3,2,1,0:T(8,128)(2,1)} %get-tuple-element.74), channel_id=1, source_target_pairs={{0,16},{16,0},{32,48},{48,32},{64,80},{80,64},{96,112},{112,96},{1... | collective-permute-start | bytes 4718600 | tf_op jit(solution)/shard_map/ppermute | solution.py:728
  180.3 1.9 copy-start.21
  182.2 1.2 copy-start.26
  183.5 15.9 %copy-start.2 = (bf16[192,768]{1,0:T(8,128)(2,1)S(1)}, bf16[192,768]{1,0:T(8,128)(2,1)}, u32[]{:S(2)}) copy-start(bf16[192,768]{1,0:T(8,128)(2,1)} %ff_in.1) | copy-start | bytes 884740
  183.5 15.9 %copy-start.3 = (bf16[768,192]{0,1:T(8,128)(2,1)S(1)}, bf16[768,192]{0,1:T(8,128)(2,1)}, u32[]{:S(2)}) copy-start(bf16[768,192]{0,1:T(8,128)(2,1)} %param.35) | copy-start | bytes 884740
  183.5 15.9 %copy-start.6 = (bf16[384,192]{0,1:T(8,128)(2,1)S(1)}, bf16[384,192]{0,1:T(8,128)(2,1)}, u32[]{:S(2)}) copy-start(bf16[384,192]{0,1:T(8,128)(2,1)} %param.32) | copy-start | bytes 442372
  183.5 15.9 %copy-start.9 = (f32[192]{0:T(256)S(1)}, f32[192]{0:T(256)}, u32[]{:S(2)}) copy-start(f32[192]{0:T(256)} %param.33) | copy-start | bytes 2308
  183.5 15.9 %copy-start.13 = (bf16[4096,192]{1,0:T(8,128)(2,1)S(1)}, bf16[4096,192]{1,0:T(8,128)(2,1)}, u32[]{:S(2)}) copy-start(bf16[4096,192]{1,0:T(8,128)(2,1)} %copy-done.11) | copy-start | bytes 4718596
  183.5 15.9 %copy-start.18 = (bf16[8,2,128,384]{3,2,1,0:T(8,128)(2,1)S(1)}, bf16[8,2,128,384]{3,2,1,0:T(8,128)(2,1)}, u32[]{:S(2)}) copy-start(bf16[8,2,128,384]{3,2,1,0:T(8,128)(2,1)} %copy-done.17) | copy-start | bytes 4718596
  183.5 15.9 %copy-start.23 = (bf16[32,128,384]{2,1,0:T(8,128)(2,1)S(1)}, bf16[32,128,384]{2,1,0:T(8,128)(2,1)}, u32[]{:S(2)}) copy-start(bf16[32,128,384]{2,1,0:T(8,128)(2,1)} %copy-done.22) | copy-start | bytes 9437188

commit v5 on v4

--- a/solution.py
+++ b/solution.py
@@ -3,6 +3,7 @@
 import jax.numpy as jnp
 from jax import lax
 from jax.experimental import pallas as pl
+from jax.experimental.layout import Layout, with_layout_constraint
 from jax.experimental.pallas import tpu as pltpu
 from jax.sharding import PartitionSpec as P
 
@@ -14,7 +15,9 @@
 LAST_UNROLL = 1
 LANES = 128
 SUB = 8
-VMEM_BYTES = 40 * 1024 * 1024
+KERNEL_MIB = dict(
+    place_norm_project=20, gate=10, conv_states=32, row_scan=16, inner_col=28, chain=8, chip_total=10, entering=13, finish=34
+)
 
 
 def whole():
@@ -35,7 +38,7 @@
         in_specs=ins,
         out_specs=jax.tree.map(lambda _: whole(), outs),
         scratch_shapes=list(scratch),
-        compiler_params=pltpu.CompilerParams(vmem_limit_bytes=VMEM_BYTES),
+        compiler_params=pltpu.CompilerParams(vmem_limit_bytes=KERNEL_MIB[name] * 1024 * 1024),
         name=name,
     )
 
@@ -89,7 +92,8 @@
 def col_layout(parts):
     k, m, r, c = parts.shape
     parts = parts.reshape(k, m, r, c // SUB, SUB)
-    return jnp.transpose(parts, (0, 3, 1, 2, 4)).reshape(k, c // SUB, m, r * SUB)
+    parts = jnp.transpose(parts, (0, 3, 1, 2, 4)).reshape(k, c // SUB, m, r * SUB)
+    return with_layout_constraint(parts, Layout(major_to_minor=(0, 1, 2, 3)))
 
 
 def decay_factors(decay):
@@ -655,12 +659,16 @@
     state_size = x_proj.shape[1] // 8
     cells_n = rows_n * cols_n
 
-    values = jnp.where(tile_mask[0][..., None] == 1, tile_feats[0], background)
-    live = jnp.arange(slots, dtype=jnp.int32)[None, :] < tile_count[0][:, None]
-    marked = jnp.where(live, tile_cell[0], cells_n)
-    where = jnp.stack([marked // 64, marked % 64], axis=-1).astype(BF16)
-    where = jnp.pad(where, ((0, 0), (0, 0), (0, 62)))
-    sent = jnp.concatenate([values, where], axis=-1)
+    feats = jnp.transpose(tile_feats[0], (1, 2, 0))
+    values = jnp.where(tile_mask[0].T[:, None, :] == 1, feats, background[None, :, None])
+    live = jnp.arange(slots, dtype=jnp.int32)[:, None] < tile_count
+    marked = jnp.where(live, tile_cell[0].T, cells_n)
+    where = jnp.stack([marked // 64, marked % 64], axis=1).astype(BF16)
+    filler = jnp.zeros((slots, 2 * LANES - channels - 2, owners), BF16)
+    sent = jnp.concatenate([values, where, filler], axis=1)
+    sent = with_layout_constraint(sent, Layout(major_to_minor=(0, 1, 2)))
+    sent = lax.optimization_barrier(sent)
+    sent = jnp.transpose(sent, (2, 0, 1))
     got = lax.all_to_all(sent, ("row", "col"), split_axis=0, concat_axis=0, tiled=True)
     into_row, out_row, into_col, out_col, total_row, total_col = decay_factors(decay_rate)
     half_row = half_tiles(total_row, lax.axis_size("col"))

time: 221 us -> 212 us (0.959)
  waiting for transfers between devices: 27.5 us -> 20.3 us
  local copies, waits for them, and re-layouts: 41 us -> 37.9 us
  other arithmetic: 6.97 us -> 9.54 us
    all_to_all x1, waiting for transfers between devices: 14.5 us -> 5.41 us  [local(): lax.all_to_all(sent, ('row', 'col'), split_axis=0, concat_axis=0, tiled=T...]
    unnamed x72 -> x70, local copies, waits for them, and re-layouts: 25.6 us -> 16.5 us
    optimization_barrier x2 -> x0, local copies, waits for them, and re-layouts: 3.7 us -> none  [local(): got, ready = lax.optimization_barrier((got, ready))]
    reshape x0 -> x2, local copies, waits for them, and re-layouts: none -> 3.69 us  [col_layout(): jnp.transpose(parts, (0, 3, 1, 2, 4)).reshape(k, c // SUB, m, r * SUB)]
    transpose x0 -> x1, local copies, waits for them, and re-layouts: none -> 3.01 us  [local(): sent = jnp.transpose(sent, (2, 0, 1))]
  transfers between devices with their start and end apart: 12 -> 12, of which waited for: 5 -> 5; matrix products, arithmetic and copies ran while one was open for 8% -> 11% of each run, Pallas kernels for 19% -> 20%
where the time goes in v5:
time: 212 us; the launch traced here: 211 us
  Pallas kernels  99.4 us (47%)
  starting transfers between devices  41.8 us (20%)
  local copies, waits for them, and re-layouts  37.9 us (18%)
  waiting for transfers between devices  20.3 us (10%)
  other arithmetic  9.54 us (4%)
    pallas_call x1, Pallas kernels, conv_and_states(): call(conv_body, outs, [pl.BlockSpec(memory_space=pltpu.SMEM)] + [whole()]...  27.9 us
    pallas_call x1, Pallas kernels, finish(): call(finish_body, jax.ShapeDtypeStruct((rows_n, channels, cols_n), BF16),...  20.3 us
    unnamed x70, local copies, waits for them, and re-layouts  16.5 us
    pallas_call x1, Pallas kernels, row_scan(): call(row_scan_body, jax.ShapeDtypeStruct(x_in.shape, BF16), [whole()] * 7...  15.7 us
    pallas_call x1, Pallas kernels, inner_col(): call(inner_col_body, jax.ShapeDtypeStruct(x_in.shape, BF16), [whole()] *...  12.3 us
    all_to_all x1, starting transfers between devices, local(): lax.all_to_all(sent, ('row', 'col'), split_axis=0, concat_axis=0, tiled=T...  11.5 us
    ppermute x4, starting transfers between devices, shifted(): return lax.ppermute(block, axis, pairs)  11.1 us
    ppermute x3, waiting for transfers between devices, local(): lax.ppermute(send, 'row', [(i, (i + 2 * shift) % lines) for i in range(li...  10.3 us
  transfers between devices with their start and end apart: 12, of which 5 were waited for; matrix products, arithmetic and copies ran while one was open for 11% of the time, Pallas kernels for 20%

profile of v5, /device:TPU:1, one launch (start us, length us, event | category | flops | bytes accessed | tf_op | source)
XLA Modules:
  0.0 211.0 jit_solution(18375728986098390502)
XLA Ops:
  0.0 0.7 fusion.63
  0.8 0.7 compare_bitcast_fusion
  1.6 1.6 bitcast_select_fusion
  3.2 0.6 maximum_maximum_fusion
  3.8 3.0 %copy.70 = bf16[128,32,256]{2,1,0:T(8,128)(2,1)} copy(bf16[128,32,256]{0,2,1:T(8,128)(2,1)S(1)} %bitcast.128) | data formatting | bytes 4194304 | tf_op jit(solution)/shard_map/transpose | solution.py:671
  6.8 11.5 %all-to-all-start = ((bf16[128,32,256]{2,1,0:T(8,128)(2,1)}), bf16[128,32,256]{2,1,0:T(8,128)(2,1)S(1)}, u32[]{:S(2)}, u32[]{:S(2)}) async-start(bf16[128,32,256]{2,1,0:T(8,128)(2,1)} %copy.70), calls=%async_computation | async-start | bytes 4194304 | tf_op jit(solution)/shard_map/all_to_all | solution.py:672
  18.4 0.1 slice_reduce_fusion.1
  18.5 0.3 fusion.16
  18.8 0.4 fusion.18
  19.2 0.3 fusion.20
  19.5 0.3 fusion.22
  20.2 0.1 broadcast_in_dim.89
  20.4 0.6 reduce-precision_convert_fusion
  21.1 1.2 fusion.6
  22.4 1.4 copy.78
  23.7 3.8 %copy.79 = bf16[2,16,16,32,8]{2,4,3,1,0:T(8,128)(2,1)} copy(bf16[2,16,16,32,8]{3,4,1,2,0:T(8,128)(2,1)} %bitcast.129) | data formatting | bytes 524288 | tf_op jit(solution)/shard_map/transpose | solution.py:95
  27.5 1.8 copy.80.into_col
  29.4 1.1 fusion.77
  30.4 1.4 copy.81
  31.8 3.8 %copy.82 = bf16[2,16,16,32,8]{2,4,3,1,0:T(8,128)(2,1)} copy(bf16[2,16,16,32,8]{3,4,1,2,0:T(8,128)(2,1)} %bitcast.130) | data formatting | bytes 524288 | tf_op jit(solution)/shard_map/transpose | solution.py:95
  35.6 1.8 copy.83.out_col
  37.5 0.1 copy.89
  38.0 1.3 reshape.313.conv_w
  39.4 0.7 broadcast_in_dim.92.conv_bias
  40.1 0.6 pad_add_fusion.spot
  40.8 0.6 add_convert_fusion.pick_b
  41.4 0.6 add_convert_fusion.1.pick_c
  42.2 5.4 %all-to-all-done = bf16[128,32,256]{2,1,0:T(8,128)(2,1)S(1)} async-done(((bf16[128,32,256]{2,1,0:T(8,128)(2,1)}), bf16[128,32,256]{2,1,0:T(8,128)(2,1)S(1)}, u32[]{:S(2)}, u32[]{:S(2)}) %all-to-all-start) | async-done | bytes 2097184 | tf_op jit(solution)/shard_map/all_to_all | solution.py:672
  47.6 1.4 add_reduce_fusion.cells
  49.0 0.7 copy-done.9
  49.7 10.0 %place_norm_project.1 = (bf16[4096,192]{1,0:T(8,128)(2,1)S(1)}, bf16[4096,384]{1,0:T(8,128)(2,1)S(1)}, f32[32,384]{1,0:T(8,128)S(1)}, f32[32,384]{1,0:T(8,128)S(1)}) custom-call(s32[4096]{0:T(1024)S(1)} %add_reduce_fusion.cells, bf16[4096,256]{1,0:T(8,128)(2,1)S(1)} %bitcast.118, f32[1,192]{1,0:T(1,128)S(1)} %bitcast.123, bf16[192,384]{1,0:T(8,128)(2,1)S(1)} %copy-done.5), custom_call_target="tpu_custom_call" | custom-call | flops 12000000000 | bytes 30000000 | tf_op jit(solution)/shard_map/place_norm_project/pallas_call | solution.py:190
  59.7 1.3 copy-done.16
  61.0 3.0 %collective-permute-start = (bf16[32,384]{1,0:T(8,128)(2,1)S(1)}, bf16[32,384]{1,0:T(8,128)(2,1)S(1)}, u32[]{:S(2)}, u32[]{:S(2)}) collective-permute-start(bf16[32,384]{1,0:T(8,128)(2,1)S(1)} %convert.19), channel_id=1, source_target_pairs={{0,1},{1,2},{2,3},{3,4},{4,5},{5,6},{6,7},{7,8},{8,9},{9,10},{10,1... | collective-permute-start | bytes 73736 | tf_op jit(solution)/shard_map/ppermute | solution.py:649
  64.1 1.3 collective-permute-start.1
  65.4 3.2 %collective-permute-done.1 = bf16[32,384]{1,0:T(8,128)(2,1)S(1)} collective-permute-done((bf16[32,384]{1,0:T(8,128)(2,1)S(1)}, bf16[32,384]{1,0:T(8,128)(2,1)S(1)}, u32[]{:S(2)}, u32[]{:S(2)}) %collective-permute-start.1) | collective-permute-done | bytes 24608 | tf_op jit(solution)/shard_map/ppermute | solution.py:649
  68.7 4.1 %collective-permute-start.3 = (bf16[130,384]{1,0:T(8,128)(2,1)S(1)}, bf16[130,384]{1,0:T(8,128)(2,1)S(1)}, u32[]{:S(2)}, u32[]{:S(2)}) collective-permute-start(bf16[130,384]{1,0:T(8,128)(2,1)S(1)} %pad_maximum_fusion.2), channel_id=1, source_target_pairs={{16,0},{32,16},{48,32},{64,48},{80,64},{96,80},{112,96},{17,1},{33... | collective-permute-start | bytes 299528 | tf_op jit(solution)/shard_map/ppermute | solution.py:649
  72.8 2.6 %collective-permute-start.2 = (bf16[130,384]{1,0:T(8,128)(2,1)S(1)}, bf16[130,384]{1,0:T(8,128)(2,1)S(1)}, u32[]{:S(2)}, u32[]{:S(2)}) collective-permute-start(bf16[130,384]{1,0:T(8,128)(2,1)S(1)} %pad_maximum_fusion.1), channel_id=1, source_target_pairs={{0,16},{16,32},{32,48},{48,64},{64,80},{80,96},{96,112},{1,17},{17... | collective-permute-start | bytes 299528 | tf_op jit(solution)/shard_map/ppermute | solution.py:649
  75.5 0.1 collective-permute-done.3
  75.7 1.3 collective-permute-done.2
  77.2 27.9 %conv_states.1 = (bf16[32,128,384]{2,1,0:T(8,128)(2,1)S(1)}, bf16[32,128,128]{2,1,0:T(8,128)(2,1)S(1)}, bf16[16,80,384]{2,1,0:T(8,128)(2,1)}, bf16[8,272,384]{2,1,0:T(8,128)(2,1)S(1)}, bf16[8,272,384]{2,1,0:T(8,128)(2,1)}) custom-call(s32[2]{0:T(128)S(1)} %copy-done.12, bf16[32,128,384]{2,1,0:T(8,128)(2,1)S(1)} %bitcast.120, ...), custom_call_target="tpu_custom_call" | custom-call | flops 31000000512 | bytes 77500000 | tf_op jit(solution)/shard_map/conv_states/pallas_call | solution.py:323
  105.1 1.2 copy-done.19
  106.4 1.6 copy-done.24
  108.0 1.0 copy-done.29
  109.0 6.2 %all-to-all-start.1 = ((bf16[16,80,384]{2,1,0:T(8,128)(2,1)}), bf16[16,80,384]{2,1,0:T(8,128)(2,1)S(1)}, u32[]{:S(2)}, u32[]{:S(2)}) async-start(bf16[16,80,384]{2,1,0:T(8,128)(2,1)} %get-tuple-element.59), calls=%async_computation.1 | async-start | bytes 1966080 | tf_op jit(solution)/shard_map/all_to_all | solution.py:719
  115.3 1.4 copy-done.20
  116.7 4.3 %chip_total.1 = (bf16[8,144,384]{2,1,0:T(8,128)(2,1)}, bf16[8,144,384]{2,1,0:T(8,128)(2,1)}, bf16[8,144,384]{2,1,0:T(8,128)(2,1)}) custom-call(s32[2]{0:T(128)S(1)} %copy-done.13, bf16[8,272,384]{2,1,0:T(8,128)(2,1)S(1)} %copy-done.20, bf16[8,272,384]{2,1,0:T(8,128)(2,1)} %collective-permute-done.4.got, bf16[16,384]{1,0:T(8,128)(2,1)S(1)} %and_convert_fusion.heads_map), custom_call_target="tpu_custom_call" | custom-call | flops 5000000000 | bytes 12500000 | tf_op jit(solution)/shard_map/chip_total/pallas_call | solution.py:513
  121.0 2.5 %collective-permute-start.5 = (bf16[8,144,384]{2,1,0:T(8,128)(2,1)}, bf16[8,144,384]{2,1,0:T(8,128)(2,1)S(1)}, u32[]{:S(2)}, u32[]{:S(2)}) collective-permute-start(bf16[8,144,384]{2,1,0:T(8,128)(2,1)} %get-tuple-element.55), channel_id=1, source_target_pairs={{0,32},{16,48},{32,64},{48,80},{64,96},{80,112},{96,0},{112,16},{1... | collective-permute-start | bytes 2654216 | tf_op jit(solution)/shard_map/ppermute | solution.py:722
  123.5 2.0 collective-permute-start.6
  125.6 0.7 collective-permute-start.7
  126.3 12.3 %inner_col.1.total_col = bf16[32,128,384]{2,1,0:T(8,128)(2,1)S(1)} custom-call(bf16[32,128,384]{2,1,0:T(8,128)(2,1)S(1)} %copy-done.25, bf16[32,128,128]{2,1,0:T(8,128)(2,1)S(1)} %copy-done.30, bf16[2,16,16,256]{3,2,1,0:T(8,128)(2,1)S(1)} %copy.80.into_col, bf16[2,16,16,256]{3,2,1,0:T(8,128)(2,1)S(1)} %copy.83.out_col, ...), custom_call_target="tpu_custom_call" | custom-call | flops 16000000000 | bytes 40000000 | tf_op jit(solution)/shard_map/inner_col/pallas_call | solution.py:415
  138.6 1.7 copy-done.27
  140.2 1.3 chain.1
  141.5 6.7 %all-to-all-start.2 = ((bf16[16,64,384]{2,1,0:T(8,128)(2,1)}), bf16[16,64,384]{2,1,0:T(8,128)(2,1)S(1)}, u32[]{:S(2)}, u32[]{:S(2)}) async-start(bf16[16,64,384]{2,1,0:T(8,128)(2,1)} %chain.1), calls=%async_computation.2 | async-start | bytes 1572864 | tf_op jit(solution)/shard_map/all_to_all | solution.py:729
  148.2 1.6 copy-done.17
  149.8 2.5 %gate.1.gate_in = bf16[4096,384]{1,0:T(8,128)(2,1)S(1)} custom-call(bf16[4096,192]{1,0:T(8,128)(2,1)S(1)} %copy-done.17, f32[1,192]{1,0:T(1,128)S(1)} %bitcast.124, bf16[192,384]{1,0:T(8,128)(2,1)S(1)} %copy-done.6), custom_call_target="tpu_custom_call" | custom-call | flops 6000000000 | bytes 15000000 | tf_op jit(solution)/shard_map/gate/pallas_call | solution.py:216
  152.3 1.7 copy-done.14
  154.1 10.3 %collective-permute-done.6.rest_1_ = bf16[8,144,384]{2,1,0:T(8,128)(2,1)} collective-permute-done((bf16[8,144,384]{2,1,0:T(8,128)(2,1)}, bf16[8,144,384]{2,1,0:T(8,128)(2,1)}, u32[]{:S(2)}, u32[]{:S(2)}) %collective-permute-start.6) | collective-permute-done | bytes 884768 | tf_op jit(solution)/shard_map/ppermute | solution.py:722
  164.3 5.1 %entering.1 = (bf16[8,2,128,384]{3,2,1,0:T(8,128)(2,1)S(1)}, bf16[8,2,128,384]{3,2,1,0:T(8,128)(2,1)}) custom-call(s32[2]{0:T(128)S(1)} %copy-done.13, bf16[8,272,384]{2,1,0:T(8,128)(2,1)S(1)} %copy-done.21, bf16[8,272,384]{2,1,0:T(8,128)(2,1)} %collective-permute-done.4.got, bf16[16,384]{1,0:T(8,128)(2,1)S(1)} %and_convert_fusion.heads_map, ...), custom_call_target="tpu_custom_call" | custom-call | flops 6000000000 | bytes 15000000 | tf_op jit(solution)/shard_map/entering/pallas_call | solution.py:573
  169.4 1.1 copy-done.22
  170.6 1.1 collective-permute-start.8
  171.7 1.9 copy-done.26
  173.6 1.2 copy-done.31
  174.9 15.7 %row_scan.1.total_row = bf16[32,128,384]{2,1,0:T(8,128)(2,1)S(1)} custom-call(bf16[32,128,384]{2,1,0:T(8,128)(2,1)S(1)} %copy-done.26, bf16[32,128,128]{2,1,0:T(8,128)(2,1)S(1)} %copy-done.31, bf16[32,2,16,384]{3,2,1,0:T(8,128)(2,1)S(1)} %bitcast.119, bf16[2,32,16,128]{3,2,1,0:T(8,128)(2,1)S(1)} %get-tuple-element.46.into_row, ...), custom_call_target="tpu_custom_call" | custom-call | flops 20000000000 | bytes 50000000 | tf_op jit(solution)/shard_map/row_scan/pallas_call | solution.py:374
  190.7 20.3 %finish.1 = bf16[32,192,128]{2,1,0:T(8,128)(2,1)} custom-call(s32[2]{0:T(128)S(1)} %copy-done.13, bf16[32,128,384]{2,1,0:T(8,128)(2,1)S(1)} %row_scan.1.total_row, bf16[32,128,384]{2,1,0:T(8,128)(2,1)S(1)} %copy-done.28, bf16[32,128,128]{2,1,0:T(8,128)(2,1)S(1)} %copy-done.31, bf16[8,2,128,384]{3,2,1,0:T(8,128)(2,1)S(1)} %copy-done.23, ...), custom_call_target="tpu_custom_call" | custom-call | flops 24999999488 | bytes 62500000 | tf_op jit(solution)/shard_map/finish/pallas_call | solution.py:637
  (120 shorter events, 1.7 us)
Async XLA Ops:
  6.8 11.5 %copy-start.32 = (f32[4,6,32,128]{3,2,1,0:T(8,128)S(1)}, f32[4,6,32,128]{3,2,1,0:T(8,128)}, u32[]{:S(2)}) copy-start(f32[4,6,32,128]{3,2,1,0:T(8,128)} %param.30) | copy-start | bytes 1179652
  6.8 40.8 %all-to-all-start = ((bf16[128,32,256]{2,1,0:T(8,128)(2,1)}), bf16[128,32,256]{2,1,0:T(8,128)(2,1)S(1)}, u32[]{:S(2)}, u32[]{:S(2)}) async-start(bf16[128,32,256]{2,1,0:T(8,128)(2,1)} %copy.70), calls=%async_computation | async-start | bytes 4194304 | tf_op jit(solution)/shard_map/all_to_all | solution.py:672
  47.6 1.4 copy-start.5
  49.0 0.7 copy-start.9
  49.7 27.5 %copy-start.1 = (bf16[2,128,128]{2,1,0:T(8,128)(2,1)S(1)}, bf16[2,128,128]{2,1,0:T(8,128)(2,1)}, u32[]{:S(2)}) copy-start(bf16[2,128,128]{2,1,0:T(8,128)(2,1)} %add_convert_fusion.pick_b) | copy-start | bytes 196612
  49.7 27.5 %copy-start.2 = (f32[9,384]{1,0:T(8,128)S(1)}, f32[9,384]{1,0:T(8,128)}, u32[]{:S(2)}) copy-start(f32[9,384]{1,0:T(8,128)} %reshape.313.conv_w) | copy-start | bytes 41476
  49.7 27.5 %copy-start.8 = (bf16[384,128]{1,0:T(8,128)(2,1)S(1)}, bf16[384,128]{1,0:T(8,128)(2,1)}, u32[]{:S(2)}) copy-start(bf16[384,128]{1,0:T(8,128)(2,1)} %x_proj.1) | copy-start | bytes 294916
  49.7 27.5 %copy-start.12 = (s32[2]{0:T(128)S(1)}, s32[2]{0:T(128)}, u32[]{:S(2)}) copy-start(s32[2]{0:T(128)} %pad_add_fusion.spot) | copy-start | bytes 28
  59.7 1.3 copy-start.16
  61.0 4.4 %collective-permute-start = (bf16[32,384]{1,0:T(8,128)(2,1)S(1)}, bf16[32,384]{1,0:T(8,128)(2,1)S(1)}, u32[]{:S(2)}, u32[]{:S(2)}) collective-permute-start(bf16[32,384]{1,0:T(8,128)(2,1)S(1)} %convert.19), channel_id=1, source_target_pairs={{0,1},{1,2},{2,3},{3,4},{4,5},{5,6},{6,7},{7,8},{8,9},{9,10},{10,1... | collective-permute-start | bytes 73736 | tf_op jit(solution)/shard_map/ppermute | solution.py:649
  64.1 4.6 %collective-permute-start.1 = (bf16[32,384]{1,0:T(8,128)(2,1)S(1)}, bf16[32,384]{1,0:T(8,128)(2,1)S(1)}, u32[]{:S(2)}, u32[]{:S(2)}) collective-permute-start(bf16[32,384]{1,0:T(8,128)(2,1)S(1)} %convert.18), channel_id=1, source_target_pairs={{1,0},{2,1},{3,2},{4,3},{5,4},{6,5},{7,6},{8,7},{9,8},{10,9},{11,1... | collective-permute-start | bytes 73736 | tf_op jit(solution)/shard_map/ppermute | solution.py:649
  68.7 7.0 %collective-permute-start.3 = (bf16[130,384]{1,0:T(8,128)(2,1)S(1)}, bf16[130,384]{1,0:T(8,128)(2,1)S(1)}, u32[]{:S(2)}, u32[]{:S(2)}) collective-permute-start(bf16[130,384]{1,0:T(8,128)(2,1)S(1)} %pad_maximum_fusion.2), channel_id=1, source_target_pairs={{16,0},{32,16},{48,32},{64,48},{80,64},{96,80},{112,96},{17,1},{33... | collective-permute-start | bytes 299528 | tf_op jit(solution)/shard_map/ppermute | solution.py:649
  72.8 4.2 %collective-permute-start.2 = (bf16[130,384]{1,0:T(8,128)(2,1)S(1)}, bf16[130,384]{1,0:T(8,128)(2,1)S(1)}, u32[]{:S(2)}, u32[]{:S(2)}) collective-permute-start(bf16[130,384]{1,0:T(8,128)(2,1)S(1)} %pad_maximum_fusion.1), channel_id=1, source_target_pairs={{0,16},{16,32},{32,48},{48,64},{64,80},{80,96},{96,112},{1,17},{17... | collective-permute-start | bytes 299528 | tf_op jit(solution)/shard_map/ppermute | solution.py:649
  77.2 31.8 %copy-start.33 = (f32[384]{0:T(512)S(1)}, f32[384]{0:T(512)}, u32[]{:S(2)}) copy-start(f32[384]{0:T(512)} %param.29) | copy-start | bytes 4612
  77.2 31.8 %copy-start.34 = (f32[384]{0:T(512)S(1)}, f32[384]{0:T(512)}, u32[]{:S(2)}) copy-start(f32[384]{0:T(512)} %param.31) | copy-start | bytes 4612
  77.2 38.0 %copy-start.13 = (s32[2]{0:T(128)S(1)}, s32[2]{0:T(128)}, u32[]{:S(2)}) copy-start(s32[2]{0:T(128)} %pad_add_fusion.spot) | copy-start | bytes 28
  105.1 1.2 copy-start.19
  106.4 1.6 copy-start.24
  108.0 1.0 copy-start.29
  109.0 6.3 %collective-permute-start.4 = (bf16[8,272,384]{2,1,0:T(8,128)(2,1)}, bf16[8,272,384]{2,1,0:T(8,128)(2,1)}, u32[]{:S(2)}, u32[]{:S(2)}) collective-permute-start(bf16[8,272,384]{2,1,0:T(8,128)(2,1)} %get-tuple-element.54), channel_id=1, source_target_pairs={{0,16},{16,0},{32,48},{48,32},{64,80},{80,64},{96,112},{112,96},{1... | collective-permute-start | bytes 5013512 | tf_op jit(solution)/shard_map/ppermute | solution.py:718
  109.0 31.2 %all-to-all-start.1 = ((bf16[16,80,384]{2,1,0:T(8,128)(2,1)}), bf16[16,80,384]{2,1,0:T(8,128)(2,1)S(1)}, u32[]{:S(2)}, u32[]{:S(2)}) async-start(bf16[16,80,384]{2,1,0:T(8,128)(2,1)} %get-tuple-element.59), calls=%async_computation.1 | async-start | bytes 1966080 | tf_op jit(solution)/shard_map/all_to_all | solution.py:719
  115.3 1.4 copy-start.20
  116.7 9.6 %copy-start.25 = (bf16[32,128,384]{2,1,0:T(8,128)(2,1)S(1)}, bf16[32,128,384]{2,1,0:T(8,128)(2,1)}, u32[]{:S(2)}) copy-start(bf16[32,128,384]{2,1,0:T(8,128)(2,1)} %copy-done.24) | copy-start | bytes 9437188
  116.7 9.6 %copy-start.30 = (bf16[32,128,128]{2,1,0:T(8,128)(2,1)S(1)}, bf16[32,128,128]{2,1,0:T(8,128)(2,1)}, u32[]{:S(2)}) copy-start(bf16[32,128,128]{2,1,0:T(8,128)(2,1)} %copy-done.29) | copy-start | bytes 3145732
  121.0 33.0 %collective-permute-start.5 = (bf16[8,144,384]{2,1,0:T(8,128)(2,1)}, bf16[8,144,384]{2,1,0:T(8,128)(2,1)S(1)}, u32[]{:S(2)}, u32[]{:S(2)}) collective-permute-start(bf16[8,144,384]{2,1,0:T(8,128)(2,1)} %get-tuple-element.55), channel_id=1, source_target_pairs={{0,32},{16,48},{32,64},{48,80},{64,96},{80,112},{96,0},{112,16},{1... | collective-permute-start | bytes 2654216 | tf_op jit(solution)/shard_map/ppermute | solution.py:722
  123.5 40.8 %collective-permute-start.6 = (bf16[8,144,384]{2,1,0:T(8,128)(2,1)}, bf16[8,144,384]{2,1,0:T(8,128)(2,1)}, u32[]{:S(2)}, u32[]{:S(2)}) collective-permute-start(bf16[8,144,384]{2,1,0:T(8,128)(2,1)} %get-tuple-element.56), channel_id=1, source_target_pairs={{0,64},{16,80},{32,96},{48,112},{64,0},{80,16},{96,32},{112,48},{1... | collective-permute-start | bytes 2654216 | tf_op jit(solution)/shard_map/ppermute | solution.py:722
  125.6 38.8 %collective-permute-start.7 = (bf16[8,144,384]{2,1,0:T(8,128)(2,1)}, bf16[8,144,384]{2,1,0:T(8,128)(2,1)}, u32[]{:S(2)}, u32[]{:S(2)}) collective-permute-start(bf16[8,144,384]{2,1,0:T(8,128)(2,1)} %get-tuple-element.57), channel_id=1, source_target_pairs={{0,96},{16,112},{32,0},{48,16},{64,32},{80,48},{96,64},{112,80},{1... | collective-permute-start | bytes 2654216 | tf_op jit(solution)/shard_map/ppermute | solution.py:722
  138.6 1.7 copy-start.27
  140.2 7.9 %copy-start.6 = (bf16[192,384]{1,0:T(8,128)(2,1)S(1)}, bf16[192,384]{1,0:T(8,128)(2,1)}, u32[]{:S(2)}) copy-start(bf16[192,384]{1,0:T(8,128)(2,1)} %in_z.1) | copy-start | bytes 442372
  140.2 7.9 %copy-start.10 = (f32[192]{0:T(256)S(1)}, f32[192]{0:T(256)}, u32[]{:S(2)}) copy-start(f32[192]{0:T(256)} %param.23) | copy-start | bytes 2308
  141.5 30.2 %all-to-all-start.2 = ((bf16[16,64,384]{2,1,0:T(8,128)(2,1)}), bf16[16,64,384]{2,1,0:T(8,128)(2,1)S(1)}, u32[]{:S(2)}, u32[]{:S(2)}) async-start(bf16[16,64,384]{2,1,0:T(8,128)(2,1)} %chain.1), calls=%async_computation.2 | async-start | bytes 1572864 | tf_op jit(solution)/shard_map/all_to_all | solution.py:729
  148.2 1.6 copy-start.17
  149.8 14.5 %copy-start.21 = (bf16[8,272,384]{2,1,0:T(8,128)(2,1)S(1)}, bf16[8,272,384]{2,1,0:T(8,128)(2,1)}, u32[]{:S(2)}) copy-start(bf16[8,272,384]{2,1,0:T(8,128)(2,1)} %copy-done.19) | copy-start | bytes 5013508
  152.3 1.7 copy-start.14
  169.4 1.1 copy-start.22
  170.6 20.0 %collective-permute-start.8 = (bf16[8,2,128,384]{3,2,1,0:T(8,128)(2,1)}, bf16[8,2,128,384]{3,2,1,0:T(8,128)(2,1)}, u32[]{:S(2)}, u32[]{:S(2)}) collective-permute-start(bf16[8,2,128,384]{3,2,1,0:T(8,128)(2,1)} %get-tuple-element.74), channel_id=1, source_target_pairs={{0,16},{16,0},{32,48},{48,32},{64,80},{80,64},{96,112},{112,96},{1... | collective-permute-start | bytes 4718600 | tf_op jit(solution)/shard_map/ppermute | solution.py:736
  171.7 1.9 copy-start.26
  173.6 1.2 copy-start.31
  174.8 15.8 %copy-start = (bf16[2,128,128]{2,1,0:T(8,128)(2,1)S(1)}, bf16[2,128,128]{2,1,0:T(8,128)(2,1)}, u32[]{:S(2)}) copy-start(bf16[2,128,128]{2,1,0:T(8,128)(2,1)} %add_convert_fusion.1.pick_c) | copy-start | bytes 196612
  174.8 15.8 %copy-start.3 = (bf16[192,768]{1,0:T(8,128)(2,1)S(1)}, bf16[192,768]{1,0:T(8,128)(2,1)}, u32[]{:S(2)}) copy-start(bf16[192,768]{1,0:T(8,128)(2,1)} %ff_in.1) | copy-start | bytes 884740
  174.8 15.8 %copy-start.4 = (bf16[768,192]{0,1:T(8,128)(2,1)S(1)}, bf16[768,192]{0,1:T(8,128)(2,1)}, u32[]{:S(2)}) copy-start(bf16[768,192]{0,1:T(8,128)(2,1)} %param.35) | copy-start | bytes 884740
  174.8 15.9 %copy-start.7 = (bf16[384,192]{0,1:T(8,128)(2,1)S(1)}, bf16[384,192]{0,1:T(8,128)(2,1)}, u32[]{:S(2)}) copy-start(bf16[384,192]{0,1:T(8,128)(2,1)} %param.32) | copy-start | bytes 442372
  174.8 15.9 %copy-start.11 = (f32[192]{0:T(256)S(1)}, f32[192]{0:T(256)}, u32[]{:S(2)}) copy-start(f32[192]{0:T(256)} %param.33) | copy-start | bytes 2308
  174.8 15.9 %copy-start.15 = (bf16[4096,384]{1,0:T(8,128)(2,1)S(1)}, bf16[4096,384]{1,0:T(8,128)(2,1)}, u32[]{:S(2)}) copy-start(bf16[4096,384]{1,0:T(8,128)(2,1)} %copy-done.14) | copy-start | bytes 9437188
  174.8 15.9 %copy-start.18 = (bf16[4096,192]{1,0:T(8,128)(2,1)S(1)}, bf16[4096,192]{1,0:T(8,128)(2,1)}, u32[]{:S(2)}) copy-start(bf16[4096,192]{1,0:T(8,128)(2,1)} %copy-done.16) | copy-start | bytes 4718596
  174.8 15.9 %copy-start.23 = (bf16[8,2,128,384]{3,2,1,0:T(8,128)(2,1)S(1)}, bf16[8,2,128,384]{3,2,1,0:T(8,128)(2,1)}, u32[]{:S(2)}) copy-start(bf16[8,2,128,384]{3,2,1,0:T(8,128)(2,1)} %copy-done.22) | copy-start | bytes 4718596
  174.8 15.9 %copy-start.28 = (bf16[32,128,384]{2,1,0:T(8,128)(2,1)S(1)}, bf16[32,128,384]{2,1,0:T(8,128)(2,1)}, u32[]{:S(2)}) copy-start(bf16[32,128,384]{2,1,0:T(8,128)(2,1)} %copy-done.27) | copy-start | bytes 9437188

commit v6 on v5

--- a/solution.py
+++ b/solution.py
@@ -29,14 +29,18 @@
 )
 
 
-def call(body, outs, ins, scratch=(), name=None):
+def hbm():
+    return pl.BlockSpec(memory_space=pltpu.HBM)
+
+
+def call(body, outs, ins, scratch=(), name=None, out_specs=None):
     work = KERNEL_US[name] * 10**9
     return pl.pallas_call(
         body,
         cost_estimate=pl.CostEstimate(flops=work, bytes_accessed=work // 400, transcendentals=0),
         out_shape=outs,
         in_specs=ins,
-        out_specs=jax.tree.map(lambda _: whole(), outs),
+        out_specs=out_specs or jax.tree.map(lambda _: whole(), outs),
         scratch_shapes=list(scratch),
         compiler_params=pltpu.CompilerParams(vmem_limit_bytes=KERNEL_MIB[name] * 1024 * 1024),
         name=name,
@@ -233,8 +237,8 @@
 
 def conv_body(
     spot, inner, above, below, left, right, conv_w, conv_bias, x_proj, into_row, into_col, heads_map, pick_b,
-    half_row, half_col, x_out, coef_out, state_row, state_own, state_other,
-    padded, x_wide, coef_wide, left_sum, right_sum,
+    half_row, half_col, x_hbm, coef_hbm, state_row, own_hbm, other_hbm,
+    padded, x_wide, coef_wide, left_sum, right_sum, x_out, coef_out, state_own, state_other, done,
 ):
     rows_n, cols_n, width = inner.shape
     state_size = LANES // 8
@@ -290,11 +294,19 @@
     size = rows_n * SUB
     own = own_column((LANES, size), SUB, SUB)
 
+    copies = [
+        pltpu.make_async_copy(held, out, done.at[m])
+        for m, (held, out) in enumerate(
+            ((x_out, x_hbm), (coef_out, coef_hbm), (state_other, other_hbm), (state_own, own_hbm))
+        )
+    ]
+    copies[0].start()
+    copies[1].start()
     half = state_own.shape[0]
     deep = SUB * state_size
 
-    def col_step(j):
-        for states, side in ((state_own, spot[0]), (state_other, 1 - spot[0])):
+    def column_states(states, side):
+        def col_step(j):
             g = side * half + j
             at = pl.ds(pl.multiple_of(g * SUB, SUB), SUB)
             x_group = x_wide[:, at, :].reshape(size, width)
@@ -305,7 +317,14 @@
                 states[j, k * deep : (k + 1) * deep, :] = dot(b_part, scaled).astype(BF16)
             states[j, 2 * deep :, :] = half_col[g]
 
-    loop(half, col_step, UNROLL // 2)
+        loop(half, col_step, UNROLL)
+
+    column_states(state_other, 1 - spot[0])
+    copies[2].start()
+    column_states(state_own, spot[0])
+    copies[3].start()
+    for copy in copies:
+        copy.wait()
 
 
 def conv_and_states(spot, inner, *rest):
@@ -330,8 +349,14 @@
             pltpu.VMEM((rows_n, cols_n, LANES), F32),
             pltpu.VMEM((rows_n, 1, width), F32),
             pltpu.VMEM((rows_n, 1, width), F32),
+            pltpu.VMEM((rows_n, cols_n, width), BF16),
+            pltpu.VMEM((rows_n, cols_n, LANES), BF16),
+            pltpu.VMEM((groups, deep, width), BF16),
+            pltpu.VMEM((groups, deep, width), BF16),
+            pltpu.SemaphoreType.DMA((4,)),
         ],
         name="conv_states",
+        out_specs=(hbm(), hbm(), whole(), hbm(), hbm()),
     )(spot, inner, *rest)
 
 
@@ -722,19 +747,19 @@
         lax.ppermute(send, "row", [(i, (i + 2 * shift) % lines) for i in range(lines)])
         for shift, send in enumerate(sends, 1)
     ]
-    x_col, sends = order((x_in, sends))
-    total_col = inner_col(x_col, coef, into_col, out_col, heads_map)
-    split_row, total_col = order((split_row, total_col))
+    split_row, sends = order((split_row, sends))
     passed = chain(split_row, heads_map, rows_n // peers)
     enter_row = lax.all_to_all(passed, "col", split_axis=0, concat_axis=0, tiled=True)
     enter_row = enter_row.reshape(rows_n, 2, state_size, width)
-    grid_in, passed = order((grid, passed))
+    x_col, passed = order((x_in, passed))
+    total_col = inner_col(x_col, coef, into_col, out_col, heads_map)
+    grid_in, total_col = order((grid, total_col))
     gated = gate(grid_in, norm_gain[None], in_z)
-    receipts, gated = order((receipts, gated))
+    x_row, gated = order((x_in, gated))
+    total = row_scan(x_row, coef, enter_row, into_row, out_row, heads_map, skip_gain[None])
+    receipts, total = order((receipts, total))
     enter_own, enter_other = entering_states(spot, state_own, state_got, heads_map, receipts)
-    x_row, enter_own, enter_other = order((x_in, enter_own, enter_other))
     enter_other = lax.ppermute(enter_other, "row", twin)
-    total = row_scan(x_row, coef, enter_row, into_row, out_row, heads_map, skip_gain[None])
     block = finish(
         spot, total, total_col, coef, enter_own, enter_other, out_col, heads_map, pick_c, gated, grid,
         out_gain[None], out_w.T, mlp_gain[None], ff_in, ff_out.T, channels=channels,

time: 212 us -> 207 us (0.976)
    ppermute x3, waiting for transfers between devices: 10.3 us -> 0.01 us  [local(): lax.ppermute(send, 'row', [(i, (i + 2 * shift) % lines) for i in range(li...]
    all_to_all x1, waiting for transfers between devices: 0.01 us -> 4.6 us  [local(): lax.all_to_all(state_row, 'col', split_axis=0, concat_axis=0, tiled=True)]
    ppermute x1, waiting for transfers between devices: 0.01 us -> 3.03 us  [local(): enter_other = lax.ppermute(enter_other, 'row', twin)]
    all_to_all x1, starting transfers between devices: 6.65 us -> 4.07 us  [local(): lax.all_to_all(passed, 'col', split_axis=0, concat_axis=0, tiled=True)]
    unnamed x70 -> x68, local copies, waits for them, and re-layouts: 16.5 us -> 16.9 us
  transfers between devices with their start and end apart: 12 -> 12, of which waited for: 5 -> 6; matrix products, arithmetic and copies ran while one was open for 11% -> 11% of each run, Pallas kernels for 20% -> 18%
where the time goes in v6:
time: 207 us; the launch traced here: 206 us
  Pallas kernels  97.7 us (47%)
  starting transfers between devices  40.2 us (19%)
  local copies, waits for them, and re-layouts  37.5 us (18%)
  waiting for transfers between devices  18.4 us (9%)
  other arithmetic  9.57 us (5%)
    pallas_call x1, Pallas kernels, conv_and_states(): call(conv_body, outs, [pl.BlockSpec(memory_space=pltpu.SMEM)] + [whole()]...  28.1 us
    pallas_call x1, Pallas kernels, finish(): call(finish_body, jax.ShapeDtypeStruct((rows_n, channels, cols_n), BF16),...  19.5 us
    unnamed x68, local copies, waits for them, and re-layouts  16.9 us
    pallas_call x1, Pallas kernels, row_scan(): call(row_scan_body, jax.ShapeDtypeStruct(x_in.shape, BF16), [whole()] * 7...  15.7 us
    pallas_call x1, Pallas kernels, inner_col(): call(inner_col_body, jax.ShapeDtypeStruct(x_in.shape, BF16), [whole()] *...  12.3 us
    all_to_all x1, starting transfers between devices, local(): lax.all_to_all(sent, ('row', 'col'), split_axis=0, concat_axis=0, tiled=T...  11.5 us
    ppermute x4, starting transfers between devices, shifted(): return lax.ppermute(block, axis, pairs)  11.1 us
    pallas_call x1, Pallas kernels, place(): call(place_body, outs, [pl.BlockSpec(memory_space=pltpu.SMEM), whole(), w...  10 us
  transfers between devices with their start and end apart: 12, of which 6 were waited for; matrix products, arithmetic and copies ran while one was open for 11% of the time, Pallas kernels for 18%

profile of v6, /device:TPU:1, one launch (start us, length us, event | category | flops | bytes accessed | tf_op | source)
XLA Modules:
  0.0 205.5 jit_solution(233411869350839882)
XLA Ops:
  0.0 0.7 fusion.63
  0.8 0.7 compare_bitcast_fusion
  1.6 1.6 bitcast_select_fusion
  3.2 0.6 maximum_maximum_fusion
  3.8 3.0 %copy.70 = bf16[128,32,256]{2,1,0:T(8,128)(2,1)} copy(bf16[128,32,256]{0,2,1:T(8,128)(2,1)S(1)} %bitcast.128) | data formatting | bytes 4194304 | tf_op jit(solution)/shard_map/transpose | solution.py:696
  6.8 11.5 %all-to-all-start = ((bf16[128,32,256]{2,1,0:T(8,128)(2,1)}), bf16[128,32,256]{2,1,0:T(8,128)(2,1)S(1)}, u32[]{:S(2)}, u32[]{:S(2)}) async-start(bf16[128,32,256]{2,1,0:T(8,128)(2,1)} %copy.70), calls=%async_computation | async-start | bytes 4194304 | tf_op jit(solution)/shard_map/all_to_all | solution.py:697
  18.4 0.1 slice_reduce_fusion.1
  18.5 0.3 fusion.16
  18.8 0.4 fusion.18
  19.2 0.3 fusion.20
  19.5 0.3 fusion.22
  20.2 0.1 broadcast_in_dim.89
  20.4 0.6 reduce-precision_convert_fusion
  21.1 1.2 fusion.6
  22.4 1.4 copy.78
  23.7 3.8 %copy.79 = bf16[2,16,16,32,8]{2,4,3,1,0:T(8,128)(2,1)} copy(bf16[2,16,16,32,8]{3,4,1,2,0:T(8,128)(2,1)} %bitcast.129) | data formatting | bytes 524288 | tf_op jit(solution)/shard_map/transpose | solution.py:99
  27.5 1.8 copy.80.into_col
  29.4 1.1 fusion.77
  30.4 1.4 copy.81
  31.8 3.8 %copy.82 = bf16[2,16,16,32,8]{2,4,3,1,0:T(8,128)(2,1)} copy(bf16[2,16,16,32,8]{3,4,1,2,0:T(8,128)(2,1)} %bitcast.130) | data formatting | bytes 524288 | tf_op jit(solution)/shard_map/transpose | solution.py:99
  35.6 1.9 copy.83.out_col
  37.5 0.1 copy.89
  38.0 1.3 reshape.313.conv_w
  39.4 0.6 pad_add_fusion.spot
  40.1 0.6 add_convert_fusion.pick_b
  40.8 0.6 add_convert_fusion.1.pick_c
  41.5 6.1 %all-to-all-done = bf16[128,32,256]{2,1,0:T(8,128)(2,1)S(1)} async-done(((bf16[128,32,256]{2,1,0:T(8,128)(2,1)}), bf16[128,32,256]{2,1,0:T(8,128)(2,1)S(1)}, u32[]{:S(2)}, u32[]{:S(2)}) %all-to-all-start) | async-done | bytes 2097184 | tf_op jit(solution)/shard_map/all_to_all | solution.py:697
  47.6 1.4 add_reduce_fusion.cells
  49.0 0.7 copy-done.9
  49.7 10.0 %place_norm_project.1 = (bf16[4096,192]{1,0:T(8,128)(2,1)S(1)}, bf16[4096,384]{1,0:T(8,128)(2,1)S(1)}, f32[32,384]{1,0:T(8,128)S(1)}, f32[32,384]{1,0:T(8,128)S(1)}) custom-call(s32[4096]{0:T(1024)S(1)} %add_reduce_fusion.cells, bf16[4096,256]{1,0:T(8,128)(2,1)S(1)} %bitcast.118, f32[1,192]{1,0:T(1,128)S(1)} %bitcast.123, bf16[192,384]{1,0:T(8,128)(2,1)S(1)} %copy-done.5), custom_call_target="tpu_custom_call" | custom-call | flops 12000000000 | bytes 30000000 | tf_op jit(solution)/shard_map/place_norm_project/pallas_call | solution.py:194
  59.8 1.3 copy-done.16
  61.1 3.0 %collective-permute-start = (bf16[32,384]{1,0:T(8,128)(2,1)S(1)}, bf16[32,384]{1,0:T(8,128)(2,1)S(1)}, u32[]{:S(2)}, u32[]{:S(2)}) collective-permute-start(bf16[32,384]{1,0:T(8,128)(2,1)S(1)} %convert.19), channel_id=1, source_target_pairs={{0,1},{1,2},{2,3},{3,4},{4,5},{5,6},{6,7},{7,8},{8,9},{9,10},{10,1... | collective-permute-start | bytes 73736 | tf_op jit(solution)/shard_map/ppermute | solution.py:674
  64.2 1.3 collective-permute-start.1
  65.5 3.2 %collective-permute-done.1 = bf16[32,384]{1,0:T(8,128)(2,1)S(1)} collective-permute-done((bf16[32,384]{1,0:T(8,128)(2,1)S(1)}, bf16[32,384]{1,0:T(8,128)(2,1)S(1)}, u32[]{:S(2)}, u32[]{:S(2)}) %collective-permute-start.1) | collective-permute-done | bytes 24608 | tf_op jit(solution)/shard_map/ppermute | solution.py:674
  68.8 4.1 %collective-permute-start.3 = (bf16[130,384]{1,0:T(8,128)(2,1)S(1)}, bf16[130,384]{1,0:T(8,128)(2,1)S(1)}, u32[]{:S(2)}, u32[]{:S(2)}) collective-permute-start(bf16[130,384]{1,0:T(8,128)(2,1)S(1)} %pad_maximum_fusion.2), channel_id=1, source_target_pairs={{16,0},{32,16},{48,32},{64,48},{80,64},{96,80},{112,96},{17,1},{33... | collective-permute-start | bytes 299528 | tf_op jit(solution)/shard_map/ppermute | solution.py:674
  72.9 2.7 %collective-permute-start.2 = (bf16[130,384]{1,0:T(8,128)(2,1)S(1)}, bf16[130,384]{1,0:T(8,128)(2,1)S(1)}, u32[]{:S(2)}, u32[]{:S(2)}) collective-permute-start(bf16[130,384]{1,0:T(8,128)(2,1)S(1)} %pad_maximum_fusion.1), channel_id=1, source_target_pairs={{0,16},{16,32},{32,48},{48,64},{64,80},{80,96},{96,112},{1,17},{17... | collective-permute-start | bytes 299528 | tf_op jit(solution)/shard_map/ppermute | solution.py:674
  75.6 0.1 collective-permute-done.3
  75.8 1.3 collective-permute-done.2
  77.3 28.1 %conv_states.1 = (bf16[32,128,384]{2,1,0:T(8,128)(2,1)S(1)}, bf16[32,128,128]{2,1,0:T(8,128)(2,1)S(1)}, bf16[16,80,384]{2,1,0:T(8,128)(2,1)}, bf16[8,272,384]{2,1,0:T(8,128)(2,1)S(1)}, bf16[8,272,384]{2,1,0:T(8,128)(2,1)}) custom-call(s32[2]{0:T(128)S(1)} %copy-done.12, bf16[32,128,384]{2,1,0:T(8,128)(2,1)S(1)} %bitcast.120, ...), custom_call_target="tpu_custom_call" | custom-call | flops 31000000512 | bytes 77500000 | tf_op jit(solution)/shard_map/conv_states/pallas_call | solution.py:342
  105.5 1.2 copy-done.19
  106.7 1.6 copy-done.22
  108.3 1.0 copy-done.27
  109.3 6.2 %all-to-all-start.1 = ((bf16[16,80,384]{2,1,0:T(8,128)(2,1)}), bf16[16,80,384]{2,1,0:T(8,128)(2,1)S(1)}, u32[]{:S(2)}, u32[]{:S(2)}) async-start(bf16[16,80,384]{2,1,0:T(8,128)(2,1)} %get-tuple-element.58), calls=%async_computation.1 | async-start | bytes 1966080 | tf_op jit(solution)/shard_map/all_to_all | solution.py:744
  115.6 1.4 copy-done.20
  117.0 4.2 %chip_total.1 = (bf16[8,144,384]{2,1,0:T(8,128)(2,1)}, bf16[8,144,384]{2,1,0:T(8,128)(2,1)}, bf16[8,144,384]{2,1,0:T(8,128)(2,1)}) custom-call(s32[2]{0:T(128)S(1)} %copy-done.13, bf16[8,272,384]{2,1,0:T(8,128)(2,1)S(1)} %copy-done.20, bf16[8,272,384]{2,1,0:T(8,128)(2,1)} %collective-permute-done.4.got, bf16[16,384]{1,0:T(8,128)(2,1)S(1)} %and_convert_fusion.heads_map), custom_call_target="tpu_custom_call" | custom-call | flops 5000000000 | bytes 12500000 | tf_op jit(solution)/shard_map/chip_total/pallas_call | solution.py:538
  121.2 2.5 %collective-permute-start.5 = (bf16[8,144,384]{2,1,0:T(8,128)(2,1)}, bf16[8,144,384]{2,1,0:T(8,128)(2,1)S(1)}, u32[]{:S(2)}, u32[]{:S(2)}) collective-permute-start(bf16[8,144,384]{2,1,0:T(8,128)(2,1)} %get-tuple-element.53), channel_id=1, source_target_pairs={{0,32},{16,48},{32,64},{48,80},{64,96},{80,112},{96,0},{112,16},{1... | collective-permute-start | bytes 2654216 | tf_op jit(solution)/shard_map/ppermute | solution.py:747
  123.7 2.0 collective-permute-start.6
  125.7 0.7 collective-permute-start.7
  126.4 4.6 %all-to-all-done.1.states = bf16[16,80,384]{2,1,0:T(8,128)(2,1)S(1)} async-done(((bf16[16,80,384]{2,1,0:T(8,128)(2,1)}), bf16[16,80,384]{2,1,0:T(8,128)(2,1)S(1)}, u32[]{:S(2)}, u32[]{:S(2)}) %all-to-all-start.1) | async-done | bytes 983072 | tf_op jit(solution)/shard_map/all_to_all | solution.py:744
  131.0 1.3 chain.1
  132.3 4.1 %all-to-all-start.2 = ((bf16[16,64,384]{2,1,0:T(8,128)(2,1)}), bf16[16,64,384]{2,1,0:T(8,128)(2,1)S(1)}, u32[]{:S(2)}, u32[]{:S(2)}) async-start(bf16[16,64,384]{2,1,0:T(8,128)(2,1)} %chain.1), calls=%async_computation.2 | async-start | bytes 1572864 | tf_op jit(solution)/shard_map/all_to_all | solution.py:752
  136.4 1.9 copy-done.23
  138.3 1.2 copy-done.28
  139.5 12.3 %inner_col.1.total_col = bf16[32,128,384]{2,1,0:T(8,128)(2,1)S(1)} custom-call(bf16[32,128,384]{2,1,0:T(8,128)(2,1)S(1)} %copy-done.23, bf16[32,128,128]{2,1,0:T(8,128)(2,1)S(1)} %copy-done.28, bf16[2,16,16,256]{3,2,1,0:T(8,128)(2,1)S(1)} %copy.80.into_col, bf16[2,16,16,256]{3,2,1,0:T(8,128)(2,1)S(1)} %copy.83.out_col, ...), custom_call_target="tpu_custom_call" | custom-call | flops 16000000000 | bytes 40000000 | tf_op jit(solution)/shard_map/inner_col/pallas_call | solution.py:440
  151.8 1.7 copy-done.25
  153.5 2.5 %gate.1.gate_in = bf16[4096,384]{1,0:T(8,128)(2,1)S(1)} custom-call(bf16[4096,192]{1,0:T(8,128)(2,1)S(1)} %copy-done.17, f32[1,192]{1,0:T(1,128)S(1)} %bitcast.124, bf16[192,384]{1,0:T(8,128)(2,1)S(1)} %copy-done.6), custom_call_target="tpu_custom_call" | custom-call | flops 6000000000 | bytes 15000000 | tf_op jit(solution)/shard_map/gate/pallas_call | solution.py:220
  156.0 1.7 copy-done.14
  157.7 1.9 copy-done.24
  159.6 1.2 copy-done.29
  160.8 15.7 %row_scan.1.total_row = bf16[32,128,384]{2,1,0:T(8,128)(2,1)S(1)} custom-call(bf16[32,128,384]{2,1,0:T(8,128)(2,1)S(1)} %copy-done.24, bf16[32,128,128]{2,1,0:T(8,128)(2,1)S(1)} %copy-done.29, bf16[32,2,16,384]{3,2,1,0:T(8,128)(2,1)S(1)} %bitcast.119, bf16[2,32,16,128]{3,2,1,0:T(8,128)(2,1)S(1)} %get-tuple-element.45.into_row, ...), custom_call_target="tpu_custom_call" | custom-call | flops 20000000000 | bytes 50000000 | tf_op jit(solution)/shard_map/row_scan/pallas_call | solution.py:399
  176.7 4.1 %entering.1 = (bf16[8,2,128,384]{3,2,1,0:T(8,128)(2,1)S(1)}, bf16[8,2,128,384]{3,2,1,0:T(8,128)(2,1)S(1)}) custom-call(s32[2]{0:T(128)S(1)} %copy-done.13, bf16[8,272,384]{2,1,0:T(8,128)(2,1)S(1)} %copy-done.21, bf16[8,272,384]{2,1,0:T(8,128)(2,1)} %collective-permute-done.4.got, bf16[16,384]{1,0:T(8,128)(2,1)S(1)} %and_convert_fusion.heads_map, ...), custom_call_target="tpu_custom_call" | custom-call | flops 6000000000 | bytes 15000000 | tf_op jit(solution)/shard_map/entering/pallas_call | solution.py:598
  180.8 2.1 %collective-permute-start.8 = (bf16[8,2,128,384]{3,2,1,0:T(8,128)(2,1)S(1)}, bf16[8,2,128,384]{3,2,1,0:T(8,128)(2,1)S(1)}, u32[]{:S(2)}, u32[]{:S(2)}) collective-permute-start(bf16[8,2,128,384]{3,2,1,0:T(8,128)(2,1)S(1)} %get-tuple-element.72), channel_id=1, source_target_pairs={{0,16},{16,0},{32,48},{48,32},{64,80},{80,64},{96,112},{112,96},{1... | collective-permute-start | bytes 4718600 | tf_op jit(solution)/shard_map/ppermute | solution.py:762
  183.0 3.0 %collective-permute-done.8.enter_other = bf16[8,2,128,384]{3,2,1,0:T(8,128)(2,1)S(1)} collective-permute-done((bf16[8,2,128,384]{3,2,1,0:T(8,128)(2,1)S(1)}, bf16[8,2,128,384]{3,2,1,0:T(8,128)(2,1)S(1)}, u32[]{:S(2)}, u32[]{:S(2)}) %collective-permute-start.8) | collective-permute-done | bytes 1572896 | tf_op jit(solution)/shard_map/ppermute | solution.py:762
  186.1 19.5 %finish.1 = bf16[32,192,128]{2,1,0:T(8,128)(2,1)} custom-call(s32[2]{0:T(128)S(1)} %copy-done.13, bf16[32,128,384]{2,1,0:T(8,128)(2,1)S(1)} %row_scan.1.total_row, bf16[32,128,384]{2,1,0:T(8,128)(2,1)S(1)} %copy-done.26, bf16[32,128,128]{2,1,0:T(8,128)(2,1)S(1)} %copy-done.29, bf16[8,2,128,384]{3,2,1,0:T(8,128)(2,1)S(1)} %get-tuple-element.71.enter_own, ...), custom_call_target="tpu_custom_call" | custom-call | flops 24999999488 | bytes 62500000 | tf_op jit(solution)/shard_map/finish/pallas_call | solution.py:662
  (118 shorter events, 1.7 us)
Async XLA Ops:
  6.8 11.5 %copy-start.30 = (f32[4,6,32,128]{3,2,1,0:T(8,128)S(1)}, f32[4,6,32,128]{3,2,1,0:T(8,128)}, u32[]{:S(2)}) copy-start(f32[4,6,32,128]{3,2,1,0:T(8,128)} %param.30) | copy-start | bytes 1179652
  6.8 40.8 %all-to-all-start = ((bf16[128,32,256]{2,1,0:T(8,128)(2,1)}), bf16[128,32,256]{2,1,0:T(8,128)(2,1)S(1)}, u32[]{:S(2)}, u32[]{:S(2)}) async-start(bf16[128,32,256]{2,1,0:T(8,128)(2,1)} %copy.70), calls=%async_computation | async-start | bytes 4194304 | tf_op jit(solution)/shard_map/all_to_all | solution.py:697
  35.6 3.8 %copy-start.31 = (f32[384]{0:T(512)S(1)}, f32[384]{0:T(512)}, u32[]{:S(2)}) copy-start(f32[384]{0:T(512)} %param.27) | copy-start | bytes 4612
  47.6 1.4 copy-start.5
  49.0 0.7 copy-start.9
  49.7 27.5 %copy-start.1 = (bf16[2,128,128]{2,1,0:T(8,128)(2,1)S(1)}, bf16[2,128,128]{2,1,0:T(8,128)(2,1)}, u32[]{:S(2)}) copy-start(bf16[2,128,128]{2,1,0:T(8,128)(2,1)} %add_convert_fusion.pick_b) | copy-start | bytes 196612
  49.7 27.6 %copy-start.2 = (f32[9,384]{1,0:T(8,128)S(1)}, f32[9,384]{1,0:T(8,128)}, u32[]{:S(2)}) copy-start(f32[9,384]{1,0:T(8,128)} %reshape.313.conv_w) | copy-start | bytes 41476
  49.7 27.6 %copy-start.8 = (bf16[384,128]{1,0:T(8,128)(2,1)S(1)}, bf16[384,128]{1,0:T(8,128)(2,1)}, u32[]{:S(2)}) copy-start(bf16[384,128]{1,0:T(8,128)(2,1)} %x_proj.1) | copy-start | bytes 294916
  49.7 27.6 %copy-start.12 = (s32[2]{0:T(128)S(1)}, s32[2]{0:T(128)}, u32[]{:S(2)}) copy-start(s32[2]{0:T(128)} %pad_add_fusion.spot) | copy-start | bytes 28
  59.8 1.3 copy-start.16
  61.1 4.4 %collective-permute-start = (bf16[32,384]{1,0:T(8,128)(2,1)S(1)}, bf16[32,384]{1,0:T(8,128)(2,1)S(1)}, u32[]{:S(2)}, u32[]{:S(2)}) collective-permute-start(bf16[32,384]{1,0:T(8,128)(2,1)S(1)} %convert.19), channel_id=1, source_target_pairs={{0,1},{1,2},{2,3},{3,4},{4,5},{5,6},{6,7},{7,8},{8,9},{9,10},{10,1... | collective-permute-start | bytes 73736 | tf_op jit(solution)/shard_map/ppermute | solution.py:674
  64.2 4.6 %collective-permute-start.1 = (bf16[32,384]{1,0:T(8,128)(2,1)S(1)}, bf16[32,384]{1,0:T(8,128)(2,1)S(1)}, u32[]{:S(2)}, u32[]{:S(2)}) collective-permute-start(bf16[32,384]{1,0:T(8,128)(2,1)S(1)} %convert.18), channel_id=1, source_target_pairs={{1,0},{2,1},{3,2},{4,3},{5,4},{6,5},{7,6},{8,7},{9,8},{10,9},{11,1... | collective-permute-start | bytes 73736 | tf_op jit(solution)/shard_map/ppermute | solution.py:674
  68.8 7.0 %collective-permute-start.3 = (bf16[130,384]{1,0:T(8,128)(2,1)S(1)}, bf16[130,384]{1,0:T(8,128)(2,1)S(1)}, u32[]{:S(2)}, u32[]{:S(2)}) collective-permute-start(bf16[130,384]{1,0:T(8,128)(2,1)S(1)} %pad_maximum_fusion.2), channel_id=1, source_target_pairs={{16,0},{32,16},{48,32},{64,48},{80,64},{96,80},{112,96},{17,1},{33... | collective-permute-start | bytes 299528 | tf_op jit(solution)/shard_map/ppermute | solution.py:674
  72.9 4.2 %collective-permute-start.2 = (bf16[130,384]{1,0:T(8,128)(2,1)S(1)}, bf16[130,384]{1,0:T(8,128)(2,1)S(1)}, u32[]{:S(2)}, u32[]{:S(2)}) collective-permute-start(bf16[130,384]{1,0:T(8,128)(2,1)S(1)} %pad_maximum_fusion.1), channel_id=1, source_target_pairs={{0,16},{16,32},{32,48},{48,64},{64,80},{80,96},{96,112},{1,17},{17... | collective-permute-start | bytes 299528 | tf_op jit(solution)/shard_map/ppermute | solution.py:674
  77.3 38.2 %copy-start.32 = (f32[384]{0:T(512)S(1)}, f32[384]{0:T(512)}, u32[]{:S(2)}) copy-start(f32[384]{0:T(512)} %param.29) | copy-start | bytes 4612
  77.3 38.3 %copy-start.13 = (s32[2]{0:T(128)S(1)}, s32[2]{0:T(128)}, u32[]{:S(2)}) copy-start(s32[2]{0:T(128)} %pad_add_fusion.spot) | copy-start | bytes 28
  105.5 1.2 copy-start.19
  106.7 1.6 copy-start.22
  108.3 1.0 copy-start.27
  109.3 6.3 %collective-permute-start.4 = (bf16[8,272,384]{2,1,0:T(8,128)(2,1)}, bf16[8,272,384]{2,1,0:T(8,128)(2,1)}, u32[]{:S(2)}, u32[]{:S(2)}) collective-permute-start(bf16[8,272,384]{2,1,0:T(8,128)(2,1)} %get-tuple-element.52), channel_id=1, source_target_pairs={{0,16},{16,0},{32,48},{48,32},{64,80},{80,64},{96,112},{112,96},{1... | collective-permute-start | bytes 5013512 | tf_op jit(solution)/shard_map/ppermute | solution.py:743
  109.3 21.7 %all-to-all-start.1 = ((bf16[16,80,384]{2,1,0:T(8,128)(2,1)}), bf16[16,80,384]{2,1,0:T(8,128)(2,1)S(1)}, u32[]{:S(2)}, u32[]{:S(2)}) async-start(bf16[16,80,384]{2,1,0:T(8,128)(2,1)} %get-tuple-element.58), calls=%async_computation.1 | async-start | bytes 1966080 | tf_op jit(solution)/shard_map/all_to_all | solution.py:744
  115.6 1.4 copy-start.20
  121.2 55.5 %collective-permute-start.5 = (bf16[8,144,384]{2,1,0:T(8,128)(2,1)}, bf16[8,144,384]{2,1,0:T(8,128)(2,1)S(1)}, u32[]{:S(2)}, u32[]{:S(2)}) collective-permute-start(bf16[8,144,384]{2,1,0:T(8,128)(2,1)} %get-tuple-element.53), channel_id=1, source_target_pairs={{0,32},{16,48},{32,64},{48,80},{64,96},{80,112},{96,0},{112,16},{1... | collective-permute-start | bytes 2654216 | tf_op jit(solution)/shard_map/ppermute | solution.py:747
  123.7 53.0 %collective-permute-start.6 = (bf16[8,144,384]{2,1,0:T(8,128)(2,1)}, bf16[8,144,384]{2,1,0:T(8,128)(2,1)}, u32[]{:S(2)}, u32[]{:S(2)}) collective-permute-start(bf16[8,144,384]{2,1,0:T(8,128)(2,1)} %get-tuple-element.54), channel_id=1, source_target_pairs={{0,64},{16,80},{32,96},{48,112},{64,0},{80,16},{96,32},{112,48},{1... | collective-permute-start | bytes 2654216 | tf_op jit(solution)/shard_map/ppermute | solution.py:747
  125.7 51.0 %collective-permute-start.7 = (bf16[8,144,384]{2,1,0:T(8,128)(2,1)}, bf16[8,144,384]{2,1,0:T(8,128)(2,1)}, u32[]{:S(2)}, u32[]{:S(2)}) collective-permute-start(bf16[8,144,384]{2,1,0:T(8,128)(2,1)} %get-tuple-element.55), channel_id=1, source_target_pairs={{0,96},{16,112},{32,0},{48,16},{64,32},{80,48},{96,64},{112,80},{1... | collective-permute-start | bytes 2654216 | tf_op jit(solution)/shard_map/ppermute | solution.py:747
  132.3 25.4 %all-to-all-start.2 = ((bf16[16,64,384]{2,1,0:T(8,128)(2,1)}), bf16[16,64,384]{2,1,0:T(8,128)(2,1)S(1)}, u32[]{:S(2)}, u32[]{:S(2)}) async-start(bf16[16,64,384]{2,1,0:T(8,128)(2,1)} %chain.1), calls=%async_computation.2 | async-start | bytes 1572864 | tf_op jit(solution)/shard_map/all_to_all | solution.py:752
  136.4 1.9 copy-start.23
  138.3 1.2 copy-start.28
  139.5 13.9 %copy-start.6 = (bf16[192,384]{1,0:T(8,128)(2,1)S(1)}, bf16[192,384]{1,0:T(8,128)(2,1)}, u32[]{:S(2)}) copy-start(bf16[192,384]{1,0:T(8,128)(2,1)} %in_z.1) | copy-start | bytes 442372
  139.5 14.0 %copy-start.10 = (f32[192]{0:T(256)S(1)}, f32[192]{0:T(256)}, u32[]{:S(2)}) copy-start(f32[192]{0:T(256)} %param.23) | copy-start | bytes 2308
  139.5 14.0 %copy-start.17 = (bf16[4096,192]{1,0:T(8,128)(2,1)S(1)}, bf16[4096,192]{1,0:T(8,128)(2,1)}, u32[]{:S(2)}) copy-start(bf16[4096,192]{1,0:T(8,128)(2,1)} %copy-done.16) | copy-start | bytes 4718596
  151.8 1.7 copy-start.25
  156.0 1.7 copy-start.14
  157.7 1.9 copy-start.24
  159.6 1.2 copy-start.29
  160.8 15.9 %copy-start.21 = (bf16[8,272,384]{2,1,0:T(8,128)(2,1)S(1)}, bf16[8,272,384]{2,1,0:T(8,128)(2,1)}, u32[]{:S(2)}) copy-start(bf16[8,272,384]{2,1,0:T(8,128)(2,1)} %copy-done.19) | copy-start | bytes 5013508
  176.6 6.4 %copy-start.33 = (f32[384]{0:T(512)S(1)}, f32[384]{0:T(512)}, u32[]{:S(2)}) copy-start(f32[384]{0:T(512)} %param.31) | copy-start | bytes 4612
  176.6 9.4 %copy-start = (bf16[2,128,128]{2,1,0:T(8,128)(2,1)S(1)}, bf16[2,128,128]{2,1,0:T(8,128)(2,1)}, u32[]{:S(2)}) copy-start(bf16[2,128,128]{2,1,0:T(8,128)(2,1)} %add_convert_fusion.1.pick_c) | copy-start | bytes 196612
  176.6 9.4 %copy-start.3 = (bf16[192,768]{1,0:T(8,128)(2,1)S(1)}, bf16[192,768]{1,0:T(8,128)(2,1)}, u32[]{:S(2)}) copy-start(bf16[192,768]{1,0:T(8,128)(2,1)} %ff_in.1) | copy-start | bytes 884740
  176.6 9.4 %copy-start.4 = (bf16[768,192]{0,1:T(8,128)(2,1)S(1)}, bf16[768,192]{0,1:T(8,128)(2,1)}, u32[]{:S(2)}) copy-start(bf16[768,192]{0,1:T(8,128)(2,1)} %param.35) | copy-start | bytes 884740
  176.6 9.4 %copy-start.7 = (bf16[384,192]{0,1:T(8,128)(2,1)S(1)}, bf16[384,192]{0,1:T(8,128)(2,1)}, u32[]{:S(2)}) copy-start(bf16[384,192]{0,1:T(8,128)(2,1)} %param.32) | copy-start | bytes 442372
  176.6 9.4 %copy-start.11 = (f32[192]{0:T(256)S(1)}, f32[192]{0:T(256)}, u32[]{:S(2)}) copy-start(f32[192]{0:T(256)} %param.33) | copy-start | bytes 2308
  176.6 9.4 %copy-start.15 = (bf16[4096,384]{1,0:T(8,128)(2,1)S(1)}, bf16[4096,384]{1,0:T(8,128)(2,1)}, u32[]{:S(2)}) copy-start(bf16[4096,384]{1,0:T(8,128)(2,1)} %copy-done.14) | copy-start | bytes 9437188
  176.6 9.4 %copy-start.18 = (bf16[4096,192]{1,0:T(8,128)(2,1)S(1)}, bf16[4096,192]{1,0:T(8,128)(2,1)}, u32[]{:S(2)}) copy-start(bf16[4096,192]{1,0:T(8,128)(2,1)} %copy-done.16) | copy-start | bytes 4718596
  176.6 9.4 %copy-start.26 = (bf16[32,128,384]{2,1,0:T(8,128)(2,1)S(1)}, bf16[32,128,384]{2,1,0:T(8,128)(2,1)}, u32[]{:S(2)}) copy-start(bf16[32,128,384]{2,1,0:T(8,128)(2,1)} %copy-done.25) | copy-start | bytes 9437188
  180.8 5.2 %collective-permute-start.8 = (bf16[8,2,128,384]{3,2,1,0:T(8,128)(2,1)S(1)}, bf16[8,2,128,384]{3,2,1,0:T(8,128)(2,1)S(1)}, u32[]{:S(2)}, u32[]{:S(2)}) collective-permute-start(bf16[8,2,128,384]{3,2,1,0:T(8,128)(2,1)S(1)} %get-tuple-element.72), channel_id=1, source_target_pairs={{0,16},{16,0},{32,48},{48,32},{64,80},{80,64},{96,112},{112,96},{1... | collective-permute-start | bytes 4718600 | tf_op jit(solution)/shard_map/ppermute | solution.py:762

commit v7 on v6

--- a/solution.py
+++ b/solution.py
@@ -34,7 +34,7 @@
 
 
 def call(body, outs, ins, scratch=(), name=None, out_specs=None):
-    work = KERNEL_US[name] * 10**9
+    work = KERNEL_US[name] * 10**7
     return pl.pallas_call(
         body,
         cost_estimate=pl.CostEstimate(flops=work, bytes_accessed=work // 400, transcendentals=0),
@@ -747,15 +747,15 @@
         lax.ppermute(send, "row", [(i, (i + 2 * shift) % lines) for i in range(lines)])
         for shift, send in enumerate(sends, 1)
     ]
-    split_row, sends = order((split_row, sends))
+    grid_in, sends = order((grid, sends))
+    gated = gate(grid_in, norm_gain[None], in_z)
+    split_row, gated = order((split_row, gated))
     passed = chain(split_row, heads_map, rows_n // peers)
     enter_row = lax.all_to_all(passed, "col", split_axis=0, concat_axis=0, tiled=True)
     enter_row = enter_row.reshape(rows_n, 2, state_size, width)
     x_col, passed = order((x_in, passed))
     total_col = inner_col(x_col, coef, into_col, out_col, heads_map)
-    grid_in, total_col = order((grid, total_col))
-    gated = gate(grid_in, norm_gain[None], in_z)
-    x_row, gated = order((x_in, gated))
+    x_row, total_col = order((x_in, total_col))
     total = row_scan(x_row, coef, enter_row, into_row, out_row, heads_map, skip_gain[None])
     receipts, total = order((receipts, total))
     enter_own, enter_other = entering_states(spot, state_own, state_got, heads_map, receipts)

time: 207 us -> 204 us (0.986)
  local copies, waits for them, and re-layouts: 37.5 us -> 34.9 us
  starting transfers between devices: 40.2 us -> 42.3 us
    all_to_all x1, waiting for transfers between devices: 4.6 us -> 0.27 us  [local(): lax.all_to_all(state_row, 'col', split_axis=0, concat_axis=0, tiled=True)]
    all_to_all x1, waiting for transfers between devices: 6.07 us -> 9.23 us  [local(): lax.all_to_all(sent, ('row', 'col'), split_axis=0, concat_axis=0, tiled=T...]
    all_to_all x1, starting transfers between devices: 4.07 us -> 6.4 us  [local(): lax.all_to_all(passed, 'col', split_axis=0, concat_axis=0, tiled=True)]
    unnamed x68 -> x80, local copies, waits for them, and re-layouts: 16.9 us -> 15.7 us
  transfers between devices with their start and end apart: 12 -> 12, of which waited for: 6 -> 6; matrix products, arithmetic and copies ran while one was open for 11% -> 10% of each run, Pallas kernels for 18% -> 19%
where the time goes in v7:
time: 204 us; the launch traced here: 203 us
  Pallas kernels  98.5 us (48%)
  starting transfers between devices  42.3 us (21%)
  local copies, waits for them, and re-layouts  34.9 us (17%)
  waiting for transfers between devices  17.2 us (8%)
  other arithmetic  7.78 us (4%)
    pallas_call x1, Pallas kernels, conv_and_states(): call(conv_body, outs, [pl.BlockSpec(memory_space=pltpu.SMEM)] + [whole()]...  27.1 us
    pallas_call x1, Pallas kernels, finish(): call(finish_body, jax.ShapeDtypeStruct((rows_n, channels, cols_n), BF16),...  19.4 us
    pallas_call x1, Pallas kernels, row_scan(): call(row_scan_body, jax.ShapeDtypeStruct(x_in.shape, BF16), [whole()] * 7...  17 us
    unnamed x80, local copies, waits for them, and re-layouts  15.7 us
    pallas_call x1, Pallas kernels, inner_col(): call(inner_col_body, jax.ShapeDtypeStruct(x_in.shape, BF16), [whole()] *...  12.3 us
    all_to_all x1, starting transfers between devices, local(): lax.all_to_all(sent, ('row', 'col'), split_axis=0, concat_axis=0, tiled=T...  11.5 us
    ppermute x4, starting transfers between devices, shifted(): return lax.ppermute(block, axis, pairs)  11.1 us
    pallas_call x1, Pallas kernels, place(): call(place_body, outs, [pl.BlockSpec(memory_space=pltpu.SMEM), whole(), w...  9.98 us
  transfers between devices with their start and end apart: 12, of which 6 were waited for; matrix products, arithmetic and copies ran while one was open for 10% of the time, Pallas kernels for 19%

profile of v7, /device:TPU:1, one launch (start us, length us, event | category | flops | bytes accessed | tf_op | source)
XLA Modules:
  0.0 202.9 jit_solution(8832818282224761304)
XLA Ops:
  0.0 0.7 fusion.63
  0.8 0.7 compare_bitcast_fusion
  1.6 1.6 bitcast_select_fusion
  3.2 0.6 maximum_maximum_fusion
  3.8 3.0 %copy.70 = bf16[128,32,256]{2,1,0:T(8,128)(2,1)} copy(bf16[128,32,256]{0,2,1:T(8,128)(2,1)S(1)} %bitcast.127) | data formatting | bytes 4194304 | tf_op jit(solution)/shard_map/transpose | solution.py:696
  6.9 11.5 %all-to-all-start = ((bf16[128,32,256]{2,1,0:T(8,128)(2,1)}), bf16[128,32,256]{2,1,0:T(8,128)(2,1)S(1)}, u32[]{:S(2)}, u32[]{:S(2)}) async-start(bf16[128,32,256]{2,1,0:T(8,128)(2,1)} %copy.70), calls=%async_computation | async-start | bytes 4194304 | tf_op jit(solution)/shard_map/all_to_all | solution.py:697
  18.5 0.3 fusion.16
  18.8 0.4 fusion.18
  19.2 0.3 fusion.20
  19.5 0.3 fusion.22
  20.4 0.6 reduce-precision_convert_fusion
  21.1 1.2 fusion.6
  22.4 0.8 fusion.78
  23.1 0.5 copy.78
  23.6 2.8 %copy.79 = bf16[2,16,16,32,8]{2,4,3,1,0:T(8,128)(2,1)} copy(bf16[2,16,16,32,8]{3,4,1,2,0:T(8,128)(2,1)S(1)} %bitcast.128) | data formatting | bytes 524288 | tf_op jit(solution)/shard_map/transpose | solution.py:99
  26.4 2.6 %copy.80.into_col = bf16[2,16,16,256]{3,2,1,0:T(8,128)(2,1)} copy(bf16[2,16,16,256]{2,3,1,0:T(8,128)(2,1)} %bitcast.125) | data formatting | bytes 524288 | tf_op jit(solution)/shard_map/reshape | solution.py:99
  29.0 0.7 fusion.77
  29.7 0.5 copy.81
  30.2 2.8 %copy.82 = bf16[2,16,16,32,8]{2,4,3,1,0:T(8,128)(2,1)} copy(bf16[2,16,16,32,8]{3,4,1,2,0:T(8,128)(2,1)S(1)} %bitcast.129) | data formatting | bytes 524288 | tf_op jit(solution)/shard_map/transpose | solution.py:99
  33.0 1.9 copy.83.out_col
  34.9 0.1 copy.89
  35.2 0.7 pad.83.half_col
  36.1 0.7 pad.80.half_row
  36.8 0.6 reshape.313.conv_w
  37.4 0.6 broadcast_in_dim.92.conv_bias
  38.4 9.2 %all-to-all-done = bf16[128,32,256]{2,1,0:T(8,128)(2,1)S(1)} async-done(((bf16[128,32,256]{2,1,0:T(8,128)(2,1)}), bf16[128,32,256]{2,1,0:T(8,128)(2,1)S(1)}, u32[]{:S(2)}, u32[]{:S(2)}) %all-to-all-start) | async-done | bytes 2097184 | tf_op jit(solution)/shard_map/all_to_all | solution.py:697
  47.6 1.4 add_reduce_fusion.cells
  49.2 10.0 %place_norm_project.1 = (bf16[4096,192]{1,0:T(8,128)(2,1)S(1)}, bf16[4096,384]{1,0:T(8,128)(2,1)S(1)}, f32[32,384]{1,0:T(8,128)S(1)}, f32[32,384]{1,0:T(8,128)S(1)}) custom-call(s32[4096]{0:T(1024)S(1)} %add_reduce_fusion.cells, bf16[4096,256]{1,0:T(8,128)(2,1)S(1)} %bitcast.118, f32[1,192]{1,0:T(1,128)S(1)} %bitcast.122, bf16[192,384]{1,0:T(8,128)(2,1)S(1)} %copy-done.25), custom_call_target="tpu_custom_call" | custom-call | flops 120000000 | bytes 300000 | tf_op jit(solution)/shard_map/place_norm_project/pallas_call | solution.py:194
  59.2 1.4 copy-done.8
  60.5 3.0 %collective-permute-start = (bf16[32,384]{1,0:T(8,128)(2,1)S(1)}, bf16[32,384]{1,0:T(8,128)(2,1)S(1)}, u32[]{:S(2)}, u32[]{:S(2)}) collective-permute-start(bf16[32,384]{1,0:T(8,128)(2,1)S(1)} %convert.19), channel_id=1, source_target_pairs={{0,1},{1,2},{2,3},{3,4},{4,5},{5,6},{6,7},{7,8},{8,9},{9,10},{10,1... | collective-permute-start | bytes 73736 | tf_op jit(solution)/shard_map/ppermute | solution.py:674
  63.6 1.3 collective-permute-start.1
  64.9 3.2 %collective-permute-done.1 = bf16[32,384]{1,0:T(8,128)(2,1)S(1)} collective-permute-done((bf16[32,384]{1,0:T(8,128)(2,1)S(1)}, bf16[32,384]{1,0:T(8,128)(2,1)S(1)}, u32[]{:S(2)}, u32[]{:S(2)}) %collective-permute-start.1) | collective-permute-done | bytes 24608 | tf_op jit(solution)/shard_map/ppermute | solution.py:674
  68.2 4.1 %collective-permute-start.3 = (bf16[130,384]{1,0:T(8,128)(2,1)S(1)}, bf16[130,384]{1,0:T(8,128)(2,1)S(1)}, u32[]{:S(2)}, u32[]{:S(2)}) collective-permute-start(bf16[130,384]{1,0:T(8,128)(2,1)S(1)} %pad_maximum_fusion.2), channel_id=1, source_target_pairs={{16,0},{32,16},{48,32},{64,48},{80,64},{96,80},{112,96},{17,1},{33... | collective-permute-start | bytes 299528 | tf_op jit(solution)/shard_map/ppermute | solution.py:674
  72.3 2.7 %collective-permute-start.2 = (bf16[130,384]{1,0:T(8,128)(2,1)S(1)}, bf16[130,384]{1,0:T(8,128)(2,1)S(1)}, u32[]{:S(2)}, u32[]{:S(2)}) collective-permute-start(bf16[130,384]{1,0:T(8,128)(2,1)S(1)} %pad_maximum_fusion.1), channel_id=1, source_target_pairs={{0,16},{16,32},{32,48},{48,64},{64,80},{80,96},{96,112},{1,17},{17... | collective-permute-start | bytes 299528 | tf_op jit(solution)/shard_map/ppermute | solution.py:674
  75.1 0.1 collective-permute-done.3
  75.2 1.3 collective-permute-done.2
  76.8 27.1 %conv_states.1 = (bf16[32,128,384]{2,1,0:T(8,128)(2,1)S(1)}, bf16[32,128,128]{2,1,0:T(8,128)(2,1)S(1)}, bf16[16,80,384]{2,1,0:T(8,128)(2,1)S(1)}, bf16[8,272,384]{2,1,0:T(8,128)(2,1)S(1)}, bf16[8,272,384]{2,1,0:T(8,128)(2,1)}) custom-call(s32[2]{0:T(128)S(1)} %pad_add_fusion.spot, bf16[32,128,384]{2,1,0:T(8,128)(2,1)S(1)} %bitcast.119, ...), custom_call_target="tpu_custom_call" | custom-call | flops 310000000 | bytes 775000 | tf_op jit(solution)/shard_map/conv_states/pallas_call | solution.py:342
  103.9 1.0 copy-done.4
  104.9 1.2 copy-done.11
  106.1 0.9 copy-done.20
  107.0 6.4 %all-to-all-start.1 = ((bf16[16,80,384]{2,1,0:T(8,128)(2,1)}), bf16[16,80,384]{2,1,0:T(8,128)(2,1)}, u32[]{:S(2)}, u32[]{:S(2)}) async-start(bf16[16,80,384]{2,1,0:T(8,128)(2,1)} %copy-done.20), calls=%async_computation.1 | async-start | bytes 1966080 | tf_op jit(solution)/shard_map/all_to_all | solution.py:744
  113.5 1.6 copy-done.12
  115.0 4.2 %chip_total.1 = (bf16[8,144,384]{2,1,0:T(8,128)(2,1)}, bf16[8,144,384]{2,1,0:T(8,128)(2,1)}, bf16[8,144,384]{2,1,0:T(8,128)(2,1)}) custom-call(s32[2]{0:T(128)S(1)} %pad_add_fusion.spot, bf16[8,272,384]{2,1,0:T(8,128)(2,1)S(1)} %copy-done.12, bf16[8,272,384]{2,1,0:T(8,128)(2,1)} %collective-permute-done.4.got, bf16[16,384]{1,0:T(8,128)(2,1)S(1)} %and_convert_fusion.heads_map), custom_call_target="tpu_custom_call" | custom-call | flops 50000000 | bytes 125000 | tf_op jit(solution)/shard_map/chip_total/pallas_call | solution.py:538
  119.3 2.5 %collective-permute-start.5 = (bf16[8,144,384]{2,1,0:T(8,128)(2,1)}, bf16[8,144,384]{2,1,0:T(8,128)(2,1)}, u32[]{:S(2)}, u32[]{:S(2)}) collective-permute-start(bf16[8,144,384]{2,1,0:T(8,128)(2,1)} %get-tuple-element.53), channel_id=1, source_target_pairs={{0,32},{16,48},{32,64},{48,80},{64,96},{80,112},{96,0},{112,16},{1... | collective-permute-start | bytes 2654216 | tf_op jit(solution)/shard_map/ppermute | solution.py:747
  121.8 2.0 collective-permute-start.6
  123.8 0.7 collective-permute-start.7
  124.5 2.6 %gate.1.gate_in = bf16[4096,384]{1,0:T(8,128)(2,1)S(1)} custom-call(bf16[4096,192]{1,0:T(8,128)(2,1)S(1)} %copy-done.9, f32[1,192]{1,0:T(1,128)S(1)} %bitcast.123, bf16[192,384]{1,0:T(8,128)(2,1)S(1)} %copy-done.26), custom_call_target="tpu_custom_call" | custom-call | flops 60000000 | bytes 150000 | tf_op jit(solution)/shard_map/gate/pallas_call | solution.py:220
  127.1 1.6 copy-done
  128.7 0.3 all-to-all-done.1.states
  129.0 1.6 chain.1
  130.6 0.9 copy-done.14
  131.5 6.4 %all-to-all-start.2 = ((bf16[16,64,384]{2,1,0:T(8,128)(2,1)}), bf16[16,64,384]{2,1,0:T(8,128)(2,1)}, u32[]{:S(2)}, u32[]{:S(2)}) async-start(bf16[16,64,384]{2,1,0:T(8,128)(2,1)} %copy-done.14), calls=%async_computation.2 | async-start | bytes 1572864 | tf_op jit(solution)/shard_map/all_to_all | solution.py:754
  137.9 1.2 copy-done.5
  139.1 0.9 copy-done.16
  140.1 12.3 %inner_col.1.total_col = bf16[32,128,384]{2,1,0:T(8,128)(2,1)S(1)} custom-call(bf16[32,128,384]{2,1,0:T(8,128)(2,1)S(1)} %get-tuple-element.64.x_in, bf16[32,128,128]{2,1,0:T(8,128)(2,1)S(1)} %copy-done.5, bf16[2,16,16,256]{3,2,1,0:T(8,128)(2,1)S(1)} %copy-done.16, bf16[2,16,16,256]{3,2,1,0:T(8,128)(2,1)S(1)} %copy.83.out_col, ...), custom_call_target="tpu_custom_call" | custom-call | flops 160000000 | bytes 400000 | tf_op jit(solution)/shard_map/inner_col/pallas_call | solution.py:440
  152.4 1.7 copy-done.2
  154.1 1.2 copy-done.6
  155.3 0.9 copy-done.18
  156.2 0.9 copy-done.19
  157.2 17.0 %row_scan.1.total_row = bf16[32,128,384]{2,1,0:T(8,128)(2,1)S(1)} custom-call(bf16[32,128,384]{2,1,0:T(8,128)(2,1)S(1)} %get-tuple-element.64.x_in, bf16[32,128,128]{2,1,0:T(8,128)(2,1)S(1)} %copy-done.6, bf16[32,2,16,384]{3,2,1,0:T(8,128)(2,1)} %bitcast.46.enter_row, bf16[2,32,16,128]{3,2,1,0:T(8,128)(2,1)S(1)} %copy-done.18, ...), custom_call_target="tpu_custom_call" | custom-call | flops 200000000 | bytes 500000 | tf_op jit(solution)/shard_map/row_scan/pallas_call | solution.py:399
  174.3 4.4 %entering.1 = (bf16[8,2,128,384]{3,2,1,0:T(8,128)(2,1)S(1)}, bf16[8,2,128,384]{3,2,1,0:T(8,128)(2,1)S(1)}) custom-call(s32[2]{0:T(128)S(1)} %pad_add_fusion.spot, bf16[8,272,384]{2,1,0:T(8,128)(2,1)S(1)} %copy-done.13, bf16[8,272,384]{2,1,0:T(8,128)(2,1)} %collective-permute-done.4.got, bf16[16,384]{1,0:T(8,128)(2,1)S(1)} %and_convert_fusion.heads_map, ...), custom_call_target="tpu_custom_call" | custom-call | flops 60000000 | bytes 150000 | tf_op jit(solution)/shard_map/entering/pallas_call | solution.py:598
  178.7 1.8 collective-permute-start.8
  180.4 3.0 %collective-permute-done.8.enter_other = bf16[8,2,128,384]{3,2,1,0:T(8,128)(2,1)S(1)} collective-permute-done((bf16[8,2,128,384]{3,2,1,0:T(8,128)(2,1)S(1)}, bf16[8,2,128,384]{3,2,1,0:T(8,128)(2,1)S(1)}, u32[]{:S(2)}, u32[]{:S(2)}) %collective-permute-start.8) | collective-permute-done | bytes 1572896 | tf_op jit(solution)/shard_map/ppermute | solution.py:762
  183.5 19.4 %finish.1 = bf16[32,192,128]{2,1,0:T(8,128)(2,1)} custom-call(s32[2]{0:T(128)S(1)} %pad_add_fusion.spot, bf16[32,128,384]{2,1,0:T(8,128)(2,1)S(1)} %row_scan.1.total_row, bf16[32,128,384]{2,1,0:T(8,128)(2,1)S(1)} %copy-done.3, bf16[32,128,128]{2,1,0:T(8,128)(2,1)S(1)} %copy-done.7, bf16[8,2,128,384]{3,2,1,0:T(8,128)(2,1)S(1)} %get-tuple-element.71.enter_own, ...), custom_call_target="tpu_custom_call" | custom-call | flops 250000000 | bytes 625000 | tf_op jit(solution)/shard_map/finish/pallas_call | solution.py:662
  (130 shorter events, 2.0 us)
Async XLA Ops:
  6.9 11.5 %copy-start.34 = (f32[4,6,32,128]{3,2,1,0:T(8,128)S(1)}, f32[4,6,32,128]{3,2,1,0:T(8,128)}, u32[]{:S(2)}) copy-start(f32[4,6,32,128]{3,2,1,0:T(8,128)} %param.30) | copy-start | bytes 1179652
  6.9 40.8 %all-to-all-start = ((bf16[128,32,256]{2,1,0:T(8,128)(2,1)}), bf16[128,32,256]{2,1,0:T(8,128)(2,1)S(1)}, u32[]{:S(2)}, u32[]{:S(2)}) async-start(bf16[128,32,256]{2,1,0:T(8,128)(2,1)} %copy.70), calls=%async_computation | async-start | bytes 4194304 | tf_op jit(solution)/shard_map/all_to_all | solution.py:697
  26.4 2.6 %copy-start.35 = (bf16[4,16,32,128]{3,1,2,0:T(8,128)(2,1)S(1)}, bf16[4,16,32,128]{3,1,2,0:T(8,128)(2,1)}, u32[]{:S(2)}) copy-start(bf16[4,16,32,128]{3,1,2,0:T(8,128)(2,1)} %get-tuple-element.104) | copy-start | bytes 1572868
  33.0 3.8 %copy-start.36 = (f32[3,3,384]{2,1,0:T(4,128)S(1)}, f32[3,3,384]{2,1,0:T(4,128)}, u32[]{:S(2)}) copy-start(f32[3,3,384]{2,1,0:T(4,128)} %param.26) | copy-start | bytes 41476
  33.0 4.4 %copy-start.37 = (f32[384]{0:T(512)S(1)}, f32[384]{0:T(512)}, u32[]{:S(2)}) copy-start(f32[384]{0:T(512)} %param.27) | copy-start | bytes 4612
  34.9 14.3 %copy-start.25 = (bf16[192,384]{1,0:T(8,128)(2,1)S(1)}, bf16[192,384]{1,0:T(8,128)(2,1)}, u32[]{:S(2)}) copy-start(bf16[192,384]{1,0:T(8,128)(2,1)} %in_x.1) | copy-start | bytes 442372
  34.9 14.3 %copy-start.31 = (f32[192]{0:T(256)S(1)}, f32[192]{0:T(256)}, u32[]{:S(2)}) copy-start(f32[192]{0:T(256)} %param.23) | copy-start | bytes 2308
  49.1 27.6 %copy-start.15 = (bf16[2,16,16,256]{3,2,1,0:T(8,128)(2,1)S(1)}, bf16[2,16,16,256]{3,2,1,0:T(8,128)(2,1)}, u32[]{:S(2)}) copy-start(bf16[2,16,16,256]{3,2,1,0:T(8,128)(2,1)} %copy.80.into_col) | copy-start | bytes 786436
  49.1 27.6 %copy-start.17 = (bf16[2,32,16,128]{3,2,1,0:T(8,128)(2,1)S(1)}, bf16[2,32,16,128]{3,2,1,0:T(8,128)(2,1)}, u32[]{:S(2)}) copy-start(bf16[2,32,16,128]{3,2,1,0:T(8,128)(2,1)} %get-tuple-element.45.into_row) | copy-start | bytes 786436
  49.1 27.6 %copy-start.21 = (bf16[16,16,384]{2,1,0:T(8,128)(2,1)S(1)}, bf16[16,16,384]{2,1,0:T(8,128)(2,1)}, u32[]{:S(2)}) copy-start(bf16[16,16,384]{2,1,0:T(8,128)(2,1)} %pad.83.half_col) | copy-start | bytes 589828
  49.1 27.6 %copy-start.22 = (bf16[16,16,384]{2,1,0:T(8,128)(2,1)S(1)}, bf16[16,16,384]{2,1,0:T(8,128)(2,1)}, u32[]{:S(2)}) copy-start(bf16[16,16,384]{2,1,0:T(8,128)(2,1)} %pad.80.half_row) | copy-start | bytes 589828
  49.1 27.6 %copy-start.28 = (f32[9,384]{1,0:T(8,128)S(1)}, f32[9,384]{1,0:T(8,128)}, u32[]{:S(2)}) copy-start(f32[9,384]{1,0:T(8,128)} %reshape.313.conv_w) | copy-start | bytes 41476
  49.1 27.6 %copy-start.29 = (bf16[384,128]{1,0:T(8,128)(2,1)S(1)}, bf16[384,128]{1,0:T(8,128)(2,1)}, u32[]{:S(2)}) copy-start(bf16[384,128]{1,0:T(8,128)(2,1)} %x_proj.1) | copy-start | bytes 294916
  49.1 27.6 %copy-start.30 = (f32[1,384]{1,0:T(1,128)S(1)}, f32[1,384]{1,0:T(1,128)}, u32[]{:S(2)}) copy-start(f32[1,384]{1,0:T(1,128)} %broadcast_in_dim.92.conv_bias) | copy-start | bytes 4612
  59.1 1.4 copy-start.8
  60.5 4.4 %collective-permute-start = (bf16[32,384]{1,0:T(8,128)(2,1)S(1)}, bf16[32,384]{1,0:T(8,128)(2,1)S(1)}, u32[]{:S(2)}, u32[]{:S(2)}) collective-permute-start(bf16[32,384]{1,0:T(8,128)(2,1)S(1)} %convert.19), channel_id=1, source_target_pairs={{0,1},{1,2},{2,3},{3,4},{4,5},{5,6},{6,7},{7,8},{8,9},{9,10},{10,1... | collective-permute-start | bytes 73736 | tf_op jit(solution)/shard_map/ppermute | solution.py:674
  63.6 4.6 %collective-permute-start.1 = (bf16[32,384]{1,0:T(8,128)(2,1)S(1)}, bf16[32,384]{1,0:T(8,128)(2,1)S(1)}, u32[]{:S(2)}, u32[]{:S(2)}) collective-permute-start(bf16[32,384]{1,0:T(8,128)(2,1)S(1)} %convert.18), channel_id=1, source_target_pairs={{1,0},{2,1},{3,2},{4,3},{5,4},{6,5},{7,6},{8,7},{9,8},{10,9},{11,1... | collective-permute-start | bytes 73736 | tf_op jit(solution)/shard_map/ppermute | solution.py:674
  68.2 7.0 %collective-permute-start.3 = (bf16[130,384]{1,0:T(8,128)(2,1)S(1)}, bf16[130,384]{1,0:T(8,128)(2,1)S(1)}, u32[]{:S(2)}, u32[]{:S(2)}) collective-permute-start(bf16[130,384]{1,0:T(8,128)(2,1)S(1)} %pad_maximum_fusion.2), channel_id=1, source_target_pairs={{16,0},{32,16},{48,32},{64,48},{80,64},{96,80},{112,96},{17,1},{33... | collective-permute-start | bytes 299528 | tf_op jit(solution)/shard_map/ppermute | solution.py:674
  72.3 4.2 %collective-permute-start.2 = (bf16[130,384]{1,0:T(8,128)(2,1)S(1)}, bf16[130,384]{1,0:T(8,128)(2,1)S(1)}, u32[]{:S(2)}, u32[]{:S(2)}) collective-permute-start(bf16[130,384]{1,0:T(8,128)(2,1)S(1)} %pad_maximum_fusion.1), channel_id=1, source_target_pairs={{0,16},{16,32},{32,48},{48,64},{64,80},{80,96},{96,112},{1,17},{17... | collective-permute-start | bytes 299528 | tf_op jit(solution)/shard_map/ppermute | solution.py:674
  103.9 1.0 copy-start.4
  104.9 1.2 copy-start.11
  106.1 0.9 copy-start.20
  107.0 6.4 %collective-permute-start.4 = (bf16[8,272,384]{2,1,0:T(8,128)(2,1)}, bf16[8,272,384]{2,1,0:T(8,128)(2,1)}, u32[]{:S(2)}, u32[]{:S(2)}) collective-permute-start(bf16[8,272,384]{2,1,0:T(8,128)(2,1)} %get-tuple-element.52), channel_id=1, source_target_pairs={{0,16},{16,0},{32,48},{48,32},{64,80},{80,64},{96,112},{112,96},{1... | collective-permute-start | bytes 5013512 | tf_op jit(solution)/shard_map/ppermute | solution.py:743
  107.0 17.5 %copy-start.32 = (f32[192]{0:T(256)S(1)}, f32[192]{0:T(256)}, u32[]{:S(2)}) copy-start(f32[192]{0:T(256)} %param.23) | copy-start | bytes 2308
  107.0 21.9 %all-to-all-start.1 = ((bf16[16,80,384]{2,1,0:T(8,128)(2,1)}), bf16[16,80,384]{2,1,0:T(8,128)(2,1)}, u32[]{:S(2)}, u32[]{:S(2)}) async-start(bf16[16,80,384]{2,1,0:T(8,128)(2,1)} %copy-done.20), calls=%async_computation.1 | async-start | bytes 1966080 | tf_op jit(solution)/shard_map/all_to_all | solution.py:744
  113.4 11.1 %copy-start.9 = (bf16[4096,192]{1,0:T(8,128)(2,1)S(1)}, bf16[4096,192]{1,0:T(8,128)(2,1)}, u32[]{:S(2)}) copy-start(bf16[4096,192]{1,0:T(8,128)(2,1)} %copy-done.8) | copy-start | bytes 4718596
  113.4 1.6 copy-start.12
  115.0 9.5 %copy-start.26 = (bf16[192,384]{1,0:T(8,128)(2,1)S(1)}, bf16[192,384]{1,0:T(8,128)(2,1)}, u32[]{:S(2)}) copy-start(bf16[192,384]{1,0:T(8,128)(2,1)} %in_z.1) | copy-start | bytes 442372
  119.3 55.0 %collective-permute-start.5 = (bf16[8,144,384]{2,1,0:T(8,128)(2,1)}, bf16[8,144,384]{2,1,0:T(8,128)(2,1)}, u32[]{:S(2)}, u32[]{:S(2)}) collective-permute-start(bf16[8,144,384]{2,1,0:T(8,128)(2,1)} %get-tuple-element.53), channel_id=1, source_target_pairs={{0,32},{16,48},{32,64},{48,80},{64,96},{80,112},{96,0},{112,16},{1... | collective-permute-start | bytes 2654216 | tf_op jit(solution)/shard_map/ppermute | solution.py:747
  121.8 52.5 %collective-permute-start.6 = (bf16[8,144,384]{2,1,0:T(8,128)(2,1)}, bf16[8,144,384]{2,1,0:T(8,128)(2,1)}, u32[]{:S(2)}, u32[]{:S(2)}) collective-permute-start(bf16[8,144,384]{2,1,0:T(8,128)(2,1)} %get-tuple-element.54), channel_id=1, source_target_pairs={{0,64},{16,80},{32,96},{48,112},{64,0},{80,16},{96,32},{112,48},{1... | collective-permute-start | bytes 2654216 | tf_op jit(solution)/shard_map/ppermute | solution.py:747
  123.8 50.5 %collective-permute-start.7 = (bf16[8,144,384]{2,1,0:T(8,128)(2,1)}, bf16[8,144,384]{2,1,0:T(8,128)(2,1)}, u32[]{:S(2)}, u32[]{:S(2)}) collective-permute-start(bf16[8,144,384]{2,1,0:T(8,128)(2,1)} %get-tuple-element.55), channel_id=1, source_target_pairs={{0,96},{16,112},{32,0},{48,16},{64,32},{80,48},{96,64},{112,80},{1... | collective-permute-start | bytes 2654216 | tf_op jit(solution)/shard_map/ppermute | solution.py:747
  127.1 1.6 copy-start
  128.7 9.2 %copy-start.38 = (f32[384]{0:T(512)S(1)}, f32[384]{0:T(512)}, u32[]{:S(2)}) copy-start(f32[384]{0:T(512)} %param.29) | copy-start | bytes 4612
  130.5 0.9 copy-start.14
  131.5 22.6 %all-to-all-start.2 = ((bf16[16,64,384]{2,1,0:T(8,128)(2,1)}), bf16[16,64,384]{2,1,0:T(8,128)(2,1)}, u32[]{:S(2)}, u32[]{:S(2)}) async-start(bf16[16,64,384]{2,1,0:T(8,128)(2,1)} %copy-done.14), calls=%async_computation.2 | async-start | bytes 1572864 | tf_op jit(solution)/shard_map/all_to_all | solution.py:754
  137.9 1.2 copy-start.5
  139.1 0.9 copy-start.16
  152.4 1.7 copy-start.2
  154.1 1.2 copy-start.6
  155.3 0.9 copy-start.18
  156.2 0.9 copy-start.19
  157.2 17.1 %copy-start.13 = (bf16[8,272,384]{2,1,0:T(8,128)(2,1)S(1)}, bf16[8,272,384]{2,1,0:T(8,128)(2,1)}, u32[]{:S(2)}) copy-start(bf16[8,272,384]{2,1,0:T(8,128)(2,1)} %copy-done.11) | copy-start | bytes 5013508
  157.2 26.3 %copy-start.3 = (bf16[32,128,384]{2,1,0:T(8,128)(2,1)S(1)}, bf16[32,128,384]{2,1,0:T(8,128)(2,1)}, u32[]{:S(2)}) copy-start(bf16[32,128,384]{2,1,0:T(8,128)(2,1)} %copy-done.2) | copy-start | bytes 9437188
  157.2 26.3 %copy-start.10 = (bf16[4096,192]{1,0:T(8,128)(2,1)S(1)}, bf16[4096,192]{1,0:T(8,128)(2,1)}, u32[]{:S(2)}) copy-start(bf16[4096,192]{1,0:T(8,128)(2,1)} %copy-done.8) | copy-start | bytes 4718596
  174.2 6.3 %copy-start.39 = (f32[384]{0:T(512)S(1)}, f32[384]{0:T(512)}, u32[]{:S(2)}) copy-start(f32[384]{0:T(512)} %param.31) | copy-start | bytes 4612
  174.2 9.3 %copy-start.1 = (bf16[4096,384]{1,0:T(8,128)(2,1)S(1)}, bf16[4096,384]{1,0:T(8,128)(2,1)}, u32[]{:S(2)}) copy-start(bf16[4096,384]{1,0:T(8,128)(2,1)} %copy-done) | copy-start | bytes 9437188
  174.2 9.3 %copy-start.7 = (bf16[32,128,128]{2,1,0:T(8,128)(2,1)S(1)}, bf16[32,128,128]{2,1,0:T(8,128)(2,1)}, u32[]{:S(2)}) copy-start(bf16[32,128,128]{2,1,0:T(8,128)(2,1)} %copy-done.4) | copy-start | bytes 3145732
  174.2 9.3 %copy-start.23 = (bf16[192,768]{1,0:T(8,128)(2,1)S(1)}, bf16[192,768]{1,0:T(8,128)(2,1)}, u32[]{:S(2)}) copy-start(bf16[192,768]{1,0:T(8,128)(2,1)} %ff_in.1) | copy-start | bytes 884740
  174.2 9.3 %copy-start.24 = (bf16[768,192]{0,1:T(8,128)(2,1)S(1)}, bf16[768,192]{0,1:T(8,128)(2,1)}, u32[]{:S(2)}) copy-start(bf16[768,192]{0,1:T(8,128)(2,1)} %param.35) | copy-start | bytes 884740
  174.2 9.3 %copy-start.27 = (bf16[384,192]{0,1:T(8,128)(2,1)S(1)}, bf16[384,192]{0,1:T(8,128)(2,1)}, u32[]{:S(2)}) copy-start(bf16[384,192]{0,1:T(8,128)(2,1)} %param.32) | copy-start | bytes 442372
  174.3 9.3 %copy-start.33 = (f32[192]{0:T(256)S(1)}, f32[192]{0:T(256)}, u32[]{:S(2)}) copy-start(f32[192]{0:T(256)} %param.33) | copy-start | bytes 2308
  178.7 4.8 %collective-permute-start.8 = (bf16[8,2,128,384]{3,2,1,0:T(8,128)(2,1)S(1)}, bf16[8,2,128,384]{3,2,1,0:T(8,128)(2,1)S(1)}, u32[]{:S(2)}, u32[]{:S(2)}) collective-permute-start(bf16[8,2,128,384]{3,2,1,0:T(8,128)(2,1)S(1)} %get-tuple-element.72), channel_id=1, source_target_pairs={{0,16},{16,0},{32,48},{48,32},{64,80},{80,64},{96,112},{112,96},{1... | collective-permute-start | bytes 4718600 | tf_op jit(solution)/shard_map/ppermute | solution.py:762

commit v8 on v7

--- a/solution.py
+++ b/solution.py
@@ -10,7 +10,7 @@
 F32 = jnp.float32
 BF16 = jnp.bfloat16
 BLOCK = 1024
-UNROLL = 4
+UNROLL = 8
 TOGETHER = 4
 LAST_UNROLL = 1
 LANES = 128
@@ -90,14 +90,15 @@
 
 
 def row_layout(parts):
-    return jnp.transpose(parts, (0, 2, 1, 3))
+    k, m, r, c = parts.shape
+    return jnp.transpose(parts, (2, 0, 1, 3)).reshape(r, k * m, c)
 
 
 def col_layout(parts):
     k, m, r, c = parts.shape
     parts = parts.reshape(k, m, r, c // SUB, SUB)
-    parts = jnp.transpose(parts, (0, 3, 1, 2, 4)).reshape(k, c // SUB, m, r * SUB)
-    return with_layout_constraint(parts, Layout(major_to_minor=(0, 1, 2, 3)))
+    parts = jnp.transpose(parts, (3, 0, 1, 2, 4)).reshape(c // SUB, k * m, r * SUB)
+    return with_layout_constraint(parts, Layout(major_to_minor=(0, 1, 2)))
 
 
 def decay_factors(decay):
@@ -226,7 +227,9 @@
 
 
 def spread(parts, heads_map):
-    return dot_tn(parts, heads_map)
+    both = dot_tn(parts, heads_map)
+    width = both.shape[1] // 2
+    return both[:, :width], both[:, width:]
 
 
 def own_column(shape, row_mod, col_mod):
@@ -283,8 +286,9 @@
         coef_out[r] = coef
         coef_wide[r] = coef.astype(F32)
         flipped = coef.T
+        into = spread(into_row[r], heads_map[...])
         for k in range(2):
-            scaled = (x_wide[r] * spread(into_row[k, r], heads_map[...])).astype(BF16)
+            scaled = (x_wide[r] * into[k]).astype(BF16)
             b_part = flipped[2 * k * state_size : (2 * k + 1) * state_size, :]
             at = pl.multiple_of((r % each) * 2 * state_size + k * state_size, state_size)
             state_row[r // each, pl.ds(at, state_size), :] = dot(b_part, scaled).astype(BF16)
@@ -311,8 +315,9 @@
             at = pl.ds(pl.multiple_of(g * SUB, SUB), SUB)
             x_group = x_wide[:, at, :].reshape(size, width)
             coef = coef_wide[:, at, :].reshape(size, LANES).astype(BF16)
+            into = spread(into_col[g], heads_map[...])
             for k in range(2):
-                scaled = (x_group * spread(into_col[k, g], heads_map[...])).astype(BF16)
+                scaled = (x_group * into[k]).astype(BF16)
                 b_part = jnp.where(own, dot_nt(pick_b[k], coef), 0.0).astype(BF16)
                 states[j, k * deep : (k + 1) * deep, :] = dot(b_part, scaled).astype(BF16)
             states[j, 2 * deep :, :] = half_col[g]
@@ -380,16 +385,18 @@
         coef = coef_in[r]
         wide = coef.astype(F32)
         total = x_row * skip[...]
+        into = spread(into_row[r], heads_map[...])
+        out = spread(out_row[r], heads_map[...])
         for k in range(2):
             scores = dot_nt(c_at_b(wide, k), coef)
             mixing = jnp.where(masks[k], scores, 0.0).astype(BF16)
             c_part = coef[:, (2 * k + 1) * state_size : (2 * k + 2) * state_size]
-            scaled = (x_row * spread(into_row[k, r], heads_map[...])).astype(BF16)
+            scaled = (x_row * into[k]).astype(BF16)
             both = dot(
                 jnp.concatenate([mixing, c_part], axis=1),
                 jnp.concatenate([scaled, enter_row[r, k]], axis=0),
             )
-            total = total + both * spread(out_row[k, r], heads_map[...])
+            total = total + both * out[k]
         total_out[r] = total.astype(BF16)
 
     loop(rows_n, row_step, UNROLL)
@@ -421,11 +428,13 @@
         wide = coef_wide[:, at, :].reshape(size, LANES)
         coef = wide.astype(BF16)
         total = jnp.zeros((size, width), F32)
+        into = spread(into_col[g], heads_map[...])
+        out = spread(out_col[g], heads_map[...])
         for k in range(2):
             scores = dot_nt(c_at_b(wide, k + 2), coef)
             mixing = jnp.where(masks[k], scores, 0.0).astype(BF16)
-            scaled = (x_group * spread(into_col[k, g], heads_map[...])).astype(BF16)
-            total = total + dot(mixing, scaled) * spread(out_col[k, g], heads_map[...])
+            scaled = (x_group * into[k]).astype(BF16)
+            total = total + dot(mixing, scaled) * out[k]
         acc[:, at, :] = total.reshape(rows_n, SUB, width)
 
     loop(cols_n // SUB, col_step, UNROLL)
@@ -451,7 +460,7 @@
 
 
 def half_of(tile, k, heads_map):
-    return dot(tile[:, 16 * k : 16 * k + 16], heads_map)
+    return dot(tile[:, 16 * k : 16 * k + 16], heads_map[:16, : heads_map.shape[1] // 2])
 
 
 def chain_body(states, heads_map, entering):
@@ -633,9 +642,11 @@
             at = pl.ds(pl.multiple_of(g * SUB, SUB), SUB)
             coef = coef_wide[:, at, :].reshape(size, LANES).astype(BF16)
             value = acc[:, at, :].reshape(size, width)
+            out = spread(out_col[g], heads_map[...])
+            c_both = dot(coef, pick_c[...])
             for k in range(2):
-                c_part = jnp.where(own, dot(coef, pick_c[k]), 0.0).astype(BF16)
-                value = value + dot(c_part, enter[j, k]) * spread(out_col[k, g], heads_map[...])
+                c_part = jnp.where(own, c_both[:, k * LANES : (k + 1) * LANES], 0.0).astype(BF16)
+                value = value + dot(c_part, enter[j, k]) * out[k]
             acc[:, at, :] = value.reshape(rows_n, SUB, width)
 
     loop(half, col_step, UNROLL // 2)
@@ -702,17 +713,16 @@
     half_col = jnp.pad(half_col, ((0, 0), (0, 0), (0, width - half_col.shape[2])))
     line = lax.axis_index("row")
     spot = jnp.stack([line % 2, line // 2]).astype(jnp.int32)
-    head_of = jnp.arange(width, dtype=jnp.int32) // (width // heads)
-    part_of = jnp.arange(16, dtype=jnp.int32)
-    heads_map = (
-        ((part_of % heads)[:, None] == head_of[None, :]) & (part_of < 2 * heads)[:, None]
-    ).astype(BF16)
+    head_of = jnp.arange(2 * width, dtype=jnp.int32) // (width // heads)
+    part_of = jnp.arange(32, dtype=jnp.int32)
+    head_at = part_of // 16 * heads + part_of % 16 % heads
+    heads_map = ((head_at[:, None] == head_of[None, :]) & (part_of % 16 < 2 * heads)[:, None]).astype(BF16)
     lane = jnp.arange(LANES, dtype=jnp.int32)
     picks = [
         (lane[:, None] == (m * state_size + lane // SUB)[None, :]).astype(BF16) for m in range(4, 8)
     ]
     pick_b = jnp.stack([picks[0].T, picks[2].T])
-    pick_c = jnp.stack([picks[1], picks[3]])
+    pick_c = jnp.concatenate([picks[1], picks[3]], axis=1)
 
     got = got.reshape(owners * slots, sent.shape[2])
     ready = (into_row, out_row, into_col, out_col, half_row, half_col, heads_map, pick_b, pick_c, spot)

time: 204 us -> 202 us (level)
  local copies, waits for them, and re-layouts: 34.9 us -> 47 us
  Pallas kernels: 98.5 us -> 86.7 us
    all_to_all x1, waiting for transfers between devices: 9.23 us -> 0.01 us  [local(): lax.all_to_all(sent, ('row', 'col'), split_axis=0, concat_axis=0, tiled=T...]
    all_to_all x1, waiting for transfers between devices: 0.27 us -> 7.9 us  [local(): lax.all_to_all(state_row, 'col', split_axis=0, concat_axis=0, tiled=True)]
    transpose x2 -> x4, local copies, waits for them, and re-layouts: 5.54 us -> 11.7 us  [the longest x2 8.69 us: col_layout(): jnp.transpose(parts, (3, 0, 1, 2, 4)).reshape(c // SUB, k * m, r * SUB)]
    pallas_call x1, Pallas kernels: 27.1 us -> 22.1 us  [conv_and_states(): call(conv_body, outs, [pl.BlockSpec(memory_space=pltpu.SMEM)] + [whole()]...]
    reshape x2 -> x4, local copies, waits for them, and re-layouts: 4.43 us -> 9.14 us  [col_layout(): jnp.transpose(parts, (3, 0, 1, 2, 4)).reshape(c // SUB, k * m, r * SUB)]
    pallas_call x1, Pallas kernels: 19.4 us -> 17 us  [finish(): call(finish_body, jax.ShapeDtypeStruct((rows_n, channels, cols_n), BF16),...]
    all_to_all x1, starting transfers between devices: 6.39 us -> 8.71 us  [local(): lax.all_to_all(state_row, 'col', split_axis=0, concat_axis=0, tiled=True)]
    slice x2, local copies, waits for them, and re-layouts: 1.23 us -> 3.41 us  [decay_factors(): out[2:]]
  transfers between devices with their start and end apart: 12 -> 12, of which waited for: 6 -> 5; matrix products, arithmetic and copies ran while one was open for 10% -> 15% of each run, Pallas kernels for 19% -> 17%
where the time goes in v8:
time: 202 us; the launch traced here: 201 us
  Pallas kernels  86.7 us (43%)
  local copies, waits for them, and re-layouts  47 us (23%)
  starting transfers between devices  42.3 us (21%)
  waiting for transfers between devices  15.6 us (8%)
  other arithmetic  7.2 us (4%)
    pallas_call x1, Pallas kernels, conv_and_states(): call(conv_body, outs, [pl.BlockSpec(memory_space=pltpu.SMEM)] + [whole()]...  22.1 us
    unnamed x76, local copies, waits for them, and re-layouts  17.6 us
    pallas_call x1, Pallas kernels, finish(): call(finish_body, jax.ShapeDtypeStruct((rows_n, channels, cols_n), BF16),...  17 us
    pallas_call x1, Pallas kernels, row_scan(): call(row_scan_body, jax.ShapeDtypeStruct(x_in.shape, BF16), [whole()] * 7...  16 us
    all_to_all x1, starting transfers between devices, local(): lax.all_to_all(sent, ('row', 'col'), split_axis=0, concat_axis=0, tiled=T...  11.5 us
    ppermute x4, starting transfers between devices, shifted(): return lax.ppermute(block, axis, pairs)  11.4 us
    pallas_call x1, Pallas kernels, inner_col(): call(inner_col_body, jax.ShapeDtypeStruct(x_in.shape, BF16), [whole()] *...  11.4 us
    reshape x4, local copies, waits for them, and re-layouts, col_layout(): jnp.transpose(parts, (3, 0, 1, 2, 4)).reshape(c // SUB, k * m, r * SUB)  9.14 us
  transfers between devices with their start and end apart: 12, of which 5 were waited for; matrix products, arithmetic and copies ran while one was open for 15% of the time, Pallas kernels for 17%

profile of v8, /device:TPU:1, one launch (start us, length us, event | category | flops | bytes accessed | tf_op | source)
XLA Modules:
  0.0 201.0 jit_solution(16271377399368621339)
XLA Ops:
  0.0 0.7 fusion.56
  0.8 0.7 compare_bitcast_fusion
  1.6 1.6 bitcast_select_fusion
  3.2 0.6 maximum_maximum_fusion
  3.8 3.0 %copy.61 = bf16[128,32,256]{2,1,0:T(8,128)(2,1)} copy(bf16[128,32,256]{0,2,1:T(8,128)(2,1)S(1)} %bitcast.128) | data formatting | bytes 4194304 | tf_op jit(solution)/shard_map/transpose | solution.py:707
  6.8 11.5 %all-to-all-start = ((bf16[128,32,256]{2,1,0:T(8,128)(2,1)}), bf16[128,32,256]{2,1,0:T(8,128)(2,1)S(1)}, u32[]{:S(2)}, u32[]{:S(2)}) async-start(bf16[128,32,256]{2,1,0:T(8,128)(2,1)} %copy.61), calls=%async_computation | async-start | bytes 4194304 | tf_op jit(solution)/shard_map/all_to_all | solution.py:708
  18.5 0.3 convolution_bitcast_fusion
  18.8 0.4 convolution_bitcast_fusion.1
  19.2 0.3 convolution_bitcast_fusion.2
  19.5 0.3 convolution_bitcast_fusion.3
  20.0 0.4 reduce-precision_convert_fusion
  20.4 0.9 fusion.4
  21.4 0.8 fusion.73
  22.1 0.5 copy.65
  22.6 4.3 %copy.66 = bf16[16,2,16,32,8]{2,1,4,3,0:T(2,128)(2,1)} copy(bf16[16,2,16,32,8]{3,4,0,2,1:T(8,128)(2,1)S(1)} %bitcast.129) | data formatting | bytes 524288 | tf_op jit(solution)/shard_map/transpose | solution.py:100
  27.0 3.9 %reshape.267 = bf16[16,32,256]{1,2,0:T(8,128)(2,1)S(1)} reshape(bf16[16,2,16,32,8]{2,1,4,3,0:T(2,128)(2,1)} %copy.66) | data formatting | bytes 524288 | tf_op jit(solution)/shard_map/reshape | solution.py:100
  30.8 0.3 copy.67.into_col
  31.2 2.0 fusion.72
  33.2 1.4 copy.68
  34.6 4.3 %copy.69 = bf16[16,2,16,32,8]{2,1,4,3,0:T(2,128)(2,1)} copy(bf16[16,2,16,32,8]{3,4,0,2,1:T(8,128)(2,1)S(1)} %bitcast.130) | data formatting | bytes 524288 | tf_op jit(solution)/shard_map/transpose | solution.py:100
  38.9 3.9 %reshape.269 = bf16[16,32,256]{1,2,0:T(8,128)(2,1)S(1)} reshape(bf16[16,2,16,32,8]{2,1,4,3,0:T(2,128)(2,1)} %copy.69) | data formatting | bytes 524288 | tf_op jit(solution)/shard_map/reshape | solution.py:100
  42.9 1.0 copy.70.out_col
  43.9 1.1 copy.63
  45.0 1.9 copy.64
  46.9 0.1 copy.76
  48.0 1.4 add_reduce_fusion.cells
  49.4 9.0 %place_norm_project.1 = (bf16[4096,192]{1,0:T(8,128)(2,1)S(1)}, bf16[4096,384]{1,0:T(8,128)(2,1)S(1)}, f32[32,384]{1,0:T(8,128)S(1)}, f32[32,384]{1,0:T(8,128)S(1)}) custom-call(s32[4096]{0:T(1024)S(1)} %add_reduce_fusion.cells, bf16[4096,256]{1,0:T(8,128)(2,1)S(1)} %bitcast.118, f32[1,192]{1,0:T(1,128)S(1)} %bitcast.125, bf16[192,384]{1,0:T(8,128)(2,1)S(1)} %copy-done.28), custom_call_target="tpu_custom_call" | custom-call | flops 120000000 | bytes 300000 | tf_op jit(solution)/shard_map/place_norm_project/pallas_call | solution.py:195
  58.4 1.4 copy-done.9
  59.8 3.3 %collective-permute-start = (bf16[32,384]{1,0:T(8,128)(2,1)S(1)}, bf16[32,384]{1,0:T(8,128)(2,1)S(1)}, u32[]{:S(2)}, u32[]{:S(2)}) collective-permute-start(bf16[32,384]{1,0:T(8,128)(2,1)S(1)} %convert.19), channel_id=1, source_target_pairs={{0,1},{1,2},{2,3},{3,4},{4,5},{5,6},{6,7},{7,8},{8,9},{9,10},{10,1... | collective-permute-start | bytes 73736 | tf_op jit(solution)/shard_map/ppermute | solution.py:685
  63.1 1.3 collective-permute-start.1
  64.5 3.2 %collective-permute-done.1 = bf16[32,384]{1,0:T(8,128)(2,1)S(1)} collective-permute-done((bf16[32,384]{1,0:T(8,128)(2,1)S(1)}, bf16[32,384]{1,0:T(8,128)(2,1)S(1)}, u32[]{:S(2)}, u32[]{:S(2)}) %collective-permute-start.1) | collective-permute-done | bytes 24608 | tf_op jit(solution)/shard_map/ppermute | solution.py:685
  67.7 3.7 %collective-permute-start.3 = (bf16[130,384]{1,0:T(8,128)(2,1)S(1)}, bf16[130,384]{1,0:T(8,128)(2,1)S(1)}, u32[]{:S(2)}, u32[]{:S(2)}) collective-permute-start(bf16[130,384]{1,0:T(8,128)(2,1)S(1)} %pad_maximum_fusion.2), channel_id=1, source_target_pairs={{16,0},{32,16},{48,32},{64,48},{80,64},{96,80},{112,96},{17,1},{33... | collective-permute-start | bytes 299528 | tf_op jit(solution)/shard_map/ppermute | solution.py:685
  71.5 3.2 %collective-permute-start.2 = (bf16[130,384]{1,0:T(8,128)(2,1)S(1)}, bf16[130,384]{1,0:T(8,128)(2,1)S(1)}, u32[]{:S(2)}, u32[]{:S(2)}) collective-permute-start(bf16[130,384]{1,0:T(8,128)(2,1)S(1)} %pad_maximum_fusion.1), channel_id=1, source_target_pairs={{0,16},{16,32},{32,48},{48,64},{64,80},{80,96},{96,112},{1,17},{17... | collective-permute-start | bytes 299528 | tf_op jit(solution)/shard_map/ppermute | solution.py:685
  74.7 0.1 collective-permute-done.3
  74.9 1.3 collective-permute-done.2
  76.4 22.1 %conv_states.1 = (bf16[32,128,384]{2,1,0:T(8,128)(2,1)S(1)}, bf16[32,128,128]{2,1,0:T(8,128)(2,1)S(1)}, bf16[16,80,384]{2,1,0:T(8,128)(2,1)S(1)}, bf16[8,272,384]{2,1,0:T(8,128)(2,1)S(1)}, bf16[8,272,384]{2,1,0:T(8,128)(2,1)}) custom-call(s32[2]{0:T(128)S(1)} %pad_add_fusion.spot, bf16[32,128,384]{2,1,0:T(8,128)(2,1)S(1)} %bitcast.119, ...), custom_call_target="tpu_custom_call" | custom-call | flops 310000000 | bytes 775000 | tf_op jit(solution)/shard_map/conv_states/pallas_call | solution.py:347
  98.5 1.6 copy-done.2
  100.1 1.0 copy-done.5
  101.1 1.0 copy-done.24
  102.1 8.7 %all-to-all-start.1 = ((bf16[16,80,384]{2,1,0:T(8,128)(2,1)}), bf16[16,80,384]{2,1,0:T(8,128)(2,1)}, u32[]{:S(2)}, u32[]{:S(2)}) async-start(bf16[16,80,384]{2,1,0:T(8,128)(2,1)} %copy-done.24), calls=%async_computation.1 | async-start | bytes 1966080 | tf_op jit(solution)/shard_map/all_to_all | solution.py:754
  110.8 3.3 %chip_total.1 = (bf16[8,144,384]{2,1,0:T(8,128)(2,1)}, bf16[8,144,384]{2,1,0:T(8,128)(2,1)}, bf16[8,144,384]{2,1,0:T(8,128)(2,1)}) custom-call(s32[2]{0:T(128)S(1)} %pad_add_fusion.spot, bf16[8,272,384]{2,1,0:T(8,128)(2,1)S(1)} %get-tuple-element.51.own, bf16[8,272,384]{2,1,0:T(8,128)(2,1)S(1)} %collective-permute-done.4.got, ...), custom_call_target="tpu_custom_call" | custom-call | flops 50000000 | bytes 125000 | tf_op jit(solution)/shard_map/chip_total/pallas_call | solution.py:547
  114.1 1.5 collective-permute-start.5
  115.6 2.5 %collective-permute-start.6 = (bf16[8,144,384]{2,1,0:T(8,128)(2,1)}, bf16[8,144,384]{2,1,0:T(8,128)(2,1)}, u32[]{:S(2)}, u32[]{:S(2)}) collective-permute-start(bf16[8,144,384]{2,1,0:T(8,128)(2,1)} %get-tuple-element.54), channel_id=1, source_target_pairs={{0,64},{16,80},{32,96},{48,112},{64,0},{80,16},{96,32},{112,48},{1... | collective-permute-start | bytes 2654216 | tf_op jit(solution)/shard_map/ppermute | solution.py:757
  118.1 1.2 collective-permute-start.7
  119.3 2.5 %gate.1.gate_in = bf16[4096,384]{1,0:T(8,128)(2,1)S(1)} custom-call(bf16[4096,192]{1,0:T(8,128)(2,1)S(1)} %copy-done.10, f32[1,192]{1,0:T(1,128)S(1)} %bitcast.126, bf16[192,384]{1,0:T(8,128)(2,1)S(1)} %copy-done.29), custom_call_target="tpu_custom_call" | custom-call | flops 60000000 | bytes 150000 | tf_op jit(solution)/shard_map/gate/pallas_call | solution.py:221
  121.8 7.9 %all-to-all-done.1.states = bf16[16,80,384]{2,1,0:T(8,128)(2,1)} async-done(((bf16[16,80,384]{2,1,0:T(8,128)(2,1)}), bf16[16,80,384]{2,1,0:T(8,128)(2,1)}, u32[]{:S(2)}, u32[]{:S(2)}) %all-to-all-start.1) | async-done | bytes 983072 | tf_op jit(solution)/shard_map/all_to_all | solution.py:754
  129.7 1.6 chain.1
  131.3 0.9 copy-done.16
  132.2 4.5 %all-to-all-start.2 = ((bf16[16,64,384]{2,1,0:T(8,128)(2,1)}), bf16[16,64,384]{2,1,0:T(8,128)(2,1)}, u32[]{:S(2)}, u32[]{:S(2)}) async-start(bf16[16,64,384]{2,1,0:T(8,128)(2,1)} %copy-done.16), calls=%async_computation.2 | async-start | bytes 1572864 | tf_op jit(solution)/shard_map/all_to_all | solution.py:764
  136.7 1.9 copy-done.3
  138.6 1.2 copy-done.6
  139.8 0.9 copy-done.17
  140.8 0.9 copy-done.20
  141.7 11.4 %inner_col.1.total_col = bf16[32,128,384]{2,1,0:T(8,128)(2,1)S(1)} custom-call(bf16[32,128,384]{2,1,0:T(8,128)(2,1)S(1)} %copy-done.3, bf16[32,128,128]{2,1,0:T(8,128)(2,1)S(1)} %copy-done.6, bf16[16,32,256]{2,1,0:T(8,128)(2,1)S(1)} %copy-done.20, bf16[16,32,256]{2,1,0:T(8,128)(2,1)S(1)} %copy-done.17, bf16[32,768]{1,0:T(8,128)(2,1)S(1)} %and_convert_fusion.heads_map), custom_call_target="tpu_custom_call" | custom-call | flops 160000000 | bytes 400000 | tf_op jit(solution)/shard_map/inner_col/pallas_call | solution.py:449
  153.1 1.7 copy-done
  154.8 1.9 copy-done.4
  156.7 1.2 copy-done.7
  157.9 0.9 copy-done.22
  158.8 0.9 copy-done.23
  159.8 16.0 %row_scan.1.total_row = bf16[32,128,384]{2,1,0:T(8,128)(2,1)S(1)} custom-call(bf16[32,128,384]{2,1,0:T(8,128)(2,1)S(1)} %copy-done.4, bf16[32,128,128]{2,1,0:T(8,128)(2,1)S(1)} %copy-done.7, bf16[32,2,16,384]{3,2,1,0:T(8,128)(2,1)} %bitcast.46.enter_row, bf16[32,32,128]{2,1,0:T(8,128)(2,1)S(1)} %bitcast.121, bf16[32,32,128]{2,1,0:T(8,128)(2,1)S(1)} %bitcast.122, ...), custom_call_target="tpu_custom_call" | custom-call | flops 200000000 | bytes 500000 | tf_op jit(solution)/shard_map/row_scan/pallas_call | solution.py:406
  176.0 3.9 %entering.1 = (bf16[8,2,128,384]{3,2,1,0:T(8,128)(2,1)S(1)}, bf16[8,2,128,384]{3,2,1,0:T(8,128)(2,1)S(1)}) custom-call(s32[2]{0:T(128)S(1)} %pad_add_fusion.spot, bf16[8,272,384]{2,1,0:T(8,128)(2,1)S(1)} %copy-done.13, bf16[8,272,384]{2,1,0:T(8,128)(2,1)S(1)} %copy-done.15, bf16[32,768]{1,0:T(8,128)(2,1)S(1)} %and_convert_fusion.heads_map, ...), custom_call_target="tpu_custom_call" | custom-call | flops 60000000 | bytes 150000 | tf_op jit(solution)/shard_map/entering/pallas_call | solution.py:607
  179.8 1.0 collective-permute-start.8
  180.9 3.0 %collective-permute-done.8.enter_other = bf16[8,2,128,384]{3,2,1,0:T(8,128)(2,1)S(1)} collective-permute-done((bf16[8,2,128,384]{3,2,1,0:T(8,128)(2,1)S(1)}, bf16[8,2,128,384]{3,2,1,0:T(8,128)(2,1)S(1)}, u32[]{:S(2)}, u32[]{:S(2)}) %collective-permute-start.8) | collective-permute-done | bytes 1572896 | tf_op jit(solution)/shard_map/ppermute | solution.py:772
  183.9 17.0 %finish.1 = bf16[32,192,128]{2,1,0:T(8,128)(2,1)} custom-call(s32[2]{0:T(128)S(1)} %pad_add_fusion.spot, bf16[32,128,384]{2,1,0:T(8,128)(2,1)S(1)} %row_scan.1.total_row, bf16[32,128,384]{2,1,0:T(8,128)(2,1)S(1)} %copy-done.1, bf16[32,128,128]{2,1,0:T(8,128)(2,1)S(1)} %copy-done.8, bf16[8,2,128,384]{3,2,1,0:T(8,128)(2,1)S(1)} %get-tuple-element.71.enter_own, ...), custom_call_target="tpu_custom_call" | custom-call | flops 250000000 | bytes 625000 | tf_op jit(solution)/shard_map/finish/pallas_call | solution.py:673
  (125 shorter events, 1.7 us)
Async XLA Ops:
  6.8 11.5 %copy-start.33 = (f32[4,6,32,128]{3,2,1,0:T(8,128)S(1)}, f32[4,6,32,128]{3,2,1,0:T(8,128)}, u32[]{:S(2)}) copy-start(f32[4,6,32,128]{3,2,1,0:T(8,128)} %param.30) | copy-start | bytes 1179652
  6.8 41.1 %all-to-all-start = ((bf16[128,32,256]{2,1,0:T(8,128)(2,1)}), bf16[128,32,256]{2,1,0:T(8,128)(2,1)S(1)}, u32[]{:S(2)}, u32[]{:S(2)}) async-start(bf16[128,32,256]{2,1,0:T(8,128)(2,1)} %copy.61), calls=%async_computation | async-start | bytes 4194304 | tf_op jit(solution)/shard_map/all_to_all | solution.py:708
  31.2 45.2 %copy-start.19 = (bf16[16,32,256]{2,1,0:T(8,128)(2,1)}, bf16[16,32,256]{2,1,0:T(8,128)(2,1)S(1)}, u32[]{:S(2)}) copy-start(bf16[16,32,256]{2,1,0:T(8,128)(2,1)S(1)} %copy.67.into_col) | copy-start | bytes 786436
  42.8 4.6 %copy-start.34 = (f32[3,3,384]{2,1,0:T(4,128)S(1)}, f32[3,3,384]{2,1,0:T(4,128)}, u32[]{:S(2)}) copy-start(f32[3,3,384]{2,1,0:T(4,128)} %param.26) | copy-start | bytes 41476
  42.9 4.6 %copy-start.35 = (f32[384]{0:T(512)S(1)}, f32[384]{0:T(512)}, u32[]{:S(2)}) copy-start(f32[384]{0:T(512)} %param.27) | copy-start | bytes 4612
  43.9 5.5 %copy-start.28 = (bf16[192,384]{1,0:T(8,128)(2,1)S(1)}, bf16[192,384]{1,0:T(8,128)(2,1)}, u32[]{:S(2)}) copy-start(bf16[192,384]{1,0:T(8,128)(2,1)} %in_x.1) | copy-start | bytes 442372
  43.9 5.5 %copy-start.31 = (f32[192]{0:T(256)S(1)}, f32[192]{0:T(256)}, u32[]{:S(2)}) copy-start(f32[192]{0:T(256)} %param.23) | copy-start | bytes 2308
  45.0 31.4 %copy-start.21 = (bf16[32,2,16,128]{3,2,1,0:T(8,128)(2,1)}, bf16[32,2,16,128]{3,2,1,0:T(8,128)(2,1)S(1)}, u32[]{:S(2)}) copy-start(bf16[32,2,16,128]{3,2,1,0:T(8,128)(2,1)S(1)} %copy.63) | copy-start | bytes 786436
  49.4 27.0 %copy-start.30 = (bf16[384,128]{1,0:T(8,128)(2,1)S(1)}, bf16[384,128]{1,0:T(8,128)(2,1)}, u32[]{:S(2)}) copy-start(bf16[384,128]{1,0:T(8,128)(2,1)} %x_proj.1) | copy-start | bytes 294916
  58.4 1.4 copy-start.9
  59.8 4.6 %collective-permute-start = (bf16[32,384]{1,0:T(8,128)(2,1)S(1)}, bf16[32,384]{1,0:T(8,128)(2,1)S(1)}, u32[]{:S(2)}, u32[]{:S(2)}) collective-permute-start(bf16[32,384]{1,0:T(8,128)(2,1)S(1)} %convert.19), channel_id=1, source_target_pairs={{0,1},{1,2},{2,3},{3,4},{4,5},{5,6},{6,7},{7,8},{8,9},{9,10},{10,1... | collective-permute-start | bytes 73736 | tf_op jit(solution)/shard_map/ppermute | solution.py:685
  63.1 4.6 %collective-permute-start.1 = (bf16[32,384]{1,0:T(8,128)(2,1)S(1)}, bf16[32,384]{1,0:T(8,128)(2,1)S(1)}, u32[]{:S(2)}, u32[]{:S(2)}) collective-permute-start(bf16[32,384]{1,0:T(8,128)(2,1)S(1)} %convert.18), channel_id=1, source_target_pairs={{1,0},{2,1},{3,2},{4,3},{5,4},{6,5},{7,6},{8,7},{9,8},{10,9},{11,1... | collective-permute-start | bytes 73736 | tf_op jit(solution)/shard_map/ppermute | solution.py:685
  67.7 7.1 %collective-permute-start.3 = (bf16[130,384]{1,0:T(8,128)(2,1)S(1)}, bf16[130,384]{1,0:T(8,128)(2,1)S(1)}, u32[]{:S(2)}, u32[]{:S(2)}) collective-permute-start(bf16[130,384]{1,0:T(8,128)(2,1)S(1)} %pad_maximum_fusion.2), channel_id=1, source_target_pairs={{16,0},{32,16},{48,32},{64,48},{80,64},{96,80},{112,96},{17,1},{33... | collective-permute-start | bytes 299528 | tf_op jit(solution)/shard_map/ppermute | solution.py:685
  71.5 4.7 %collective-permute-start.2 = (bf16[130,384]{1,0:T(8,128)(2,1)S(1)}, bf16[130,384]{1,0:T(8,128)(2,1)S(1)}, u32[]{:S(2)}, u32[]{:S(2)}) collective-permute-start(bf16[130,384]{1,0:T(8,128)(2,1)S(1)} %pad_maximum_fusion.1), channel_id=1, source_target_pairs={{0,16},{16,32},{32,48},{48,64},{64,80},{80,96},{96,112},{1,17},{17... | collective-permute-start | bytes 299528 | tf_op jit(solution)/shard_map/ppermute | solution.py:685
  98.5 1.6 copy-start.2
  100.1 1.0 copy-start.5
  101.1 1.0 copy-start.24
  101.1 13.0 %copy-start.12 = (bf16[8,272,384]{2,1,0:T(8,128)(2,1)}, bf16[8,272,384]{2,1,0:T(8,128)(2,1)S(1)}, u32[]{:S(2)}) copy-start(bf16[8,272,384]{2,1,0:T(8,128)(2,1)S(1)} %get-tuple-element.51.own) | copy-start | bytes 5013508
  101.1 9.7 %collective-permute-start.4 = (bf16[8,272,384]{2,1,0:T(8,128)(2,1)}, bf16[8,272,384]{2,1,0:T(8,128)(2,1)S(1)}, u32[]{:S(2)}, u32[]{:S(2)}) collective-permute-start(bf16[8,272,384]{2,1,0:T(8,128)(2,1)} %get-tuple-element.52), channel_id=1, source_target_pairs={{0,16},{16,0},{32,48},{48,32},{64,80},{80,64},{96,112},{112,96},{1... | collective-permute-start | bytes 5013512 | tf_op jit(solution)/shard_map/ppermute | solution.py:753
  102.1 27.6 %all-to-all-start.1 = ((bf16[16,80,384]{2,1,0:T(8,128)(2,1)}), bf16[16,80,384]{2,1,0:T(8,128)(2,1)}, u32[]{:S(2)}, u32[]{:S(2)}) async-start(bf16[16,80,384]{2,1,0:T(8,128)(2,1)} %copy-done.24), calls=%async_computation.1 | async-start | bytes 1966080 | tf_op jit(solution)/shard_map/all_to_all | solution.py:754
  110.8 8.5 %copy-start.10 = (bf16[4096,192]{1,0:T(8,128)(2,1)S(1)}, bf16[4096,192]{1,0:T(8,128)(2,1)}, u32[]{:S(2)}) copy-start(bf16[4096,192]{1,0:T(8,128)(2,1)} %copy-done.9) | copy-start | bytes 4718596
  110.8 8.4 %copy-start.29 = (bf16[192,384]{1,0:T(8,128)(2,1)S(1)}, bf16[192,384]{1,0:T(8,128)(2,1)}, u32[]{:S(2)}) copy-start(bf16[192,384]{1,0:T(8,128)(2,1)} %in_z.1) | copy-start | bytes 442372
  110.8 8.4 %copy-start.14 = (bf16[8,272,384]{2,1,0:T(8,128)(2,1)}, bf16[8,272,384]{2,1,0:T(8,128)(2,1)S(1)}, u32[]{:S(2)}) copy-start(bf16[8,272,384]{2,1,0:T(8,128)(2,1)S(1)} %collective-permute-done.4.got) | copy-start | bytes 5013508
  114.1 61.8 %collective-permute-start.5 = (bf16[8,144,384]{2,1,0:T(8,128)(2,1)}, bf16[8,144,384]{2,1,0:T(8,128)(2,1)}, u32[]{:S(2)}, u32[]{:S(2)}) collective-permute-start(bf16[8,144,384]{2,1,0:T(8,128)(2,1)} %get-tuple-element.53), channel_id=1, source_target_pairs={{0,32},{16,48},{32,64},{48,80},{64,96},{80,112},{96,0},{112,16},{1... | collective-permute-start | bytes 2654216 | tf_op jit(solution)/shard_map/ppermute | solution.py:757
  115.6 60.3 %collective-permute-start.6 = (bf16[8,144,384]{2,1,0:T(8,128)(2,1)}, bf16[8,144,384]{2,1,0:T(8,128)(2,1)}, u32[]{:S(2)}, u32[]{:S(2)}) collective-permute-start(bf16[8,144,384]{2,1,0:T(8,128)(2,1)} %get-tuple-element.54), channel_id=1, source_target_pairs={{0,64},{16,80},{32,96},{48,112},{64,0},{80,16},{96,32},{112,48},{1... | collective-permute-start | bytes 2654216 | tf_op jit(solution)/shard_map/ppermute | solution.py:757
  118.1 57.9 %collective-permute-start.7 = (bf16[8,144,384]{2,1,0:T(8,128)(2,1)}, bf16[8,144,384]{2,1,0:T(8,128)(2,1)}, u32[]{:S(2)}, u32[]{:S(2)}) collective-permute-start(bf16[8,144,384]{2,1,0:T(8,128)(2,1)} %get-tuple-element.55), channel_id=1, source_target_pairs={{0,96},{16,112},{32,0},{48,16},{64,32},{80,48},{96,64},{112,80},{1... | collective-permute-start | bytes 2654216 | tf_op jit(solution)/shard_map/ppermute | solution.py:757
  121.8 14.9 %copy-start.36 = (f32[384]{0:T(512)S(1)}, f32[384]{0:T(512)}, u32[]{:S(2)}) copy-start(f32[384]{0:T(512)} %param.29) | copy-start | bytes 4612
  131.3 0.9 copy-start.16
  132.2 22.6 %all-to-all-start.2 = ((bf16[16,64,384]{2,1,0:T(8,128)(2,1)}), bf16[16,64,384]{2,1,0:T(8,128)(2,1)}, u32[]{:S(2)}, u32[]{:S(2)}) async-start(bf16[16,64,384]{2,1,0:T(8,128)(2,1)} %copy-done.16), calls=%async_computation.2 | async-start | bytes 1572864 | tf_op jit(solution)/shard_map/all_to_all | solution.py:764
  136.7 1.9 copy-start.3
  138.6 1.2 copy-start.6
  139.8 0.9 copy-start.17
  140.8 0.9 copy-start.20
  153.1 1.7 copy-start
  154.8 1.9 copy-start.4
  156.7 1.2 copy-start.7
  157.9 0.9 copy-start.22
  158.8 0.9 copy-start.23
  159.8 16.2 %copy-start.13 = (bf16[8,272,384]{2,1,0:T(8,128)(2,1)S(1)}, bf16[8,272,384]{2,1,0:T(8,128)(2,1)}, u32[]{:S(2)}) copy-start(bf16[8,272,384]{2,1,0:T(8,128)(2,1)} %copy-done.12) | copy-start | bytes 5013508
  159.8 16.2 %copy-start.15 = (bf16[8,272,384]{2,1,0:T(8,128)(2,1)S(1)}, bf16[8,272,384]{2,1,0:T(8,128)(2,1)}, u32[]{:S(2)}) copy-start(bf16[8,272,384]{2,1,0:T(8,128)(2,1)} %copy-done.14) | copy-start | bytes 5013508
  159.8 24.1 %copy-start.11 = (bf16[4096,192]{1,0:T(8,128)(2,1)S(1)}, bf16[4096,192]{1,0:T(8,128)(2,1)}, u32[]{:S(2)}) copy-start(bf16[4096,192]{1,0:T(8,128)(2,1)} %copy-done.9) | copy-start | bytes 4718596
  175.8 5.0 %copy-start.37 = (f32[384]{0:T(512)S(1)}, f32[384]{0:T(512)}, u32[]{:S(2)}) copy-start(f32[384]{0:T(512)} %param.31) | copy-start | bytes 4612
  175.8 8.1 %copy-start.1 = (bf16[32,128,384]{2,1,0:T(8,128)(2,1)S(1)}, bf16[32,128,384]{2,1,0:T(8,128)(2,1)}, u32[]{:S(2)}) copy-start(bf16[32,128,384]{2,1,0:T(8,128)(2,1)} %copy-done) | copy-start | bytes 9437188
  175.8 8.1 %copy-start.8 = (bf16[32,128,128]{2,1,0:T(8,128)(2,1)S(1)}, bf16[32,128,128]{2,1,0:T(8,128)(2,1)}, u32[]{:S(2)}) copy-start(bf16[32,128,128]{2,1,0:T(8,128)(2,1)} %copy-done.5) | copy-start | bytes 3145732
  175.9 8.1 %copy-start.18 = (bf16[16,32,256]{2,1,0:T(8,128)(2,1)S(1)}, bf16[16,32,256]{2,1,0:T(8,128)(2,1)}, u32[]{:S(2)}) copy-start(bf16[16,32,256]{2,1,0:T(8,128)(2,1)} %copy.70.out_col) | copy-start | bytes 786436
  175.9 8.0 %copy-start.25 = (bf16[192,768]{1,0:T(8,128)(2,1)S(1)}, bf16[192,768]{1,0:T(8,128)(2,1)}, u32[]{:S(2)}) copy-start(bf16[192,768]{1,0:T(8,128)(2,1)} %ff_in.1) | copy-start | bytes 884740
  175.9 8.0 %copy-start.26 = (bf16[768,192]{0,1:T(8,128)(2,1)S(1)}, bf16[768,192]{0,1:T(8,128)(2,1)}, u32[]{:S(2)}) copy-start(bf16[768,192]{0,1:T(8,128)(2,1)} %param.35) | copy-start | bytes 884740
  175.9 8.0 %copy-start.27 = (bf16[384,192]{0,1:T(8,128)(2,1)S(1)}, bf16[384,192]{0,1:T(8,128)(2,1)}, u32[]{:S(2)}) copy-start(bf16[384,192]{0,1:T(8,128)(2,1)} %param.32) | copy-start | bytes 442372
  175.9 8.0 %copy-start.32 = (f32[192]{0:T(256)S(1)}, f32[192]{0:T(256)}, u32[]{:S(2)}) copy-start(f32[192]{0:T(256)} %param.33) | copy-start | bytes 2308
  179.8 4.0 %collective-permute-start.8 = (bf16[8,2,128,384]{3,2,1,0:T(8,128)(2,1)S(1)}, bf16[8,2,128,384]{3,2,1,0:T(8,128)(2,1)S(1)}, u32[]{:S(2)}, u32[]{:S(2)}) collective-permute-start(bf16[8,2,128,384]{3,2,1,0:T(8,128)(2,1)S(1)} %get-tuple-element.72), channel_id=1, source_target_pairs={{0,16},{16,0},{32,48},{48,32},{64,80},{80,64},{96,112},{112,96},{1... | collective-permute-start | bytes 4718600 | tf_op jit(solution)/shard_map/ppermute | solution.py:772

commit v9 on v8

--- a/solution.py
+++ b/solution.py
@@ -16,7 +16,7 @@
 LANES = 128
 SUB = 8
 KERNEL_MIB = dict(
-    place_norm_project=20, gate=10, conv_states=32, row_scan=16, inner_col=28, chain=8, chip_total=10, entering=13, finish=34
+    place_norm_project=20, gate=10, conv_states=32, row_scan=57, inner_col=57, chain=8, chip_total=10, entering=13, finish=34
 )
 
 
@@ -33,12 +33,22 @@
     return pl.BlockSpec(memory_space=pltpu.HBM)
 
 
-def call(body, outs, ins, scratch=(), name=None, out_specs=None):
+def block(shape, dim, size):
+    where = tuple(size if at == dim else length for at, length in enumerate(shape))
+    return pl.BlockSpec(where, lambda i: tuple(i if at == dim else 0 for at in range(len(shape))))
+
+
+def same(shape):
+    return pl.BlockSpec(shape, lambda i: (0,) * len(shape))
+
+
+def call(body, outs, ins, scratch=(), name=None, out_specs=None, grid=()):
     work = KERNEL_US[name] * 10**7
     return pl.pallas_call(
         body,
         cost_estimate=pl.CostEstimate(flops=work, bytes_accessed=work // 400, transcendentals=0),
         out_shape=outs,
+        grid=grid,
         in_specs=ins,
         out_specs=out_specs or jax.tree.map(lambda _: whole(), outs),
         scratch_shapes=list(scratch),
@@ -402,10 +412,16 @@
     loop(rows_n, row_step, UNROLL)
 
 
-def row_scan(x_in, *rest):
+def row_scan(x_in, coef, enter_row, into_row, out_row, heads_map, skip):
+    by_row = [block(array.shape, 0, UNROLL) for array in (x_in, coef, enter_row, into_row, out_row)]
     return call(
-        row_scan_body, jax.ShapeDtypeStruct(x_in.shape, BF16), [whole()] * 7, name="row_scan"
-    )(x_in, *rest)
+        row_scan_body,
+        jax.ShapeDtypeStruct(x_in.shape, BF16),
+        by_row + [same(heads_map.shape), same(skip.shape)],
+        name="row_scan",
+        out_specs=by_row[0],
+        grid=(x_in.shape[0] // UNROLL,),
+    )(x_in, coef, enter_row, into_row, out_row, heads_map, skip)
 
 
 def inner_col_body(x_in, coef_in, into_col, out_col, heads_map, total_out, x_wide, coef_wide, acc):
@@ -437,7 +453,7 @@
             total = total + dot(mixing, scaled) * out[k]
         acc[:, at, :] = total.reshape(rows_n, SUB, width)
 
-    loop(cols_n // SUB, col_step, UNROLL)
+    loop(cols_n // SUB, col_step, cols_n // SUB)
 
     def emit(r):
         total_out[r] = acc[r].astype(BF16)
@@ -445,18 +461,30 @@
     loop(rows_n, emit, UNROLL)
 
 
-def inner_col(x_in, coef_in, into_col, out_col, heads_map):
+def inner_col(x_in, coef, into_col, out_col, heads_map):
+    rows_n, cols_n, width = x_in.shape
+    groups = 4
+    wide = groups * SUB
+    cols = block(x_in.shape, 1, wide)
     return call(
         inner_col_body,
         jax.ShapeDtypeStruct(x_in.shape, BF16),
-        [whole()] * 5,
         [
-            pltpu.VMEM(x_in.shape, F32),
-            pltpu.VMEM(coef_in.shape, F32),
-            pltpu.VMEM(x_in.shape, F32),
+            cols,
+            block(coef.shape, 1, wide),
+            block(into_col.shape, 0, groups),
+            block(out_col.shape, 0, groups),
+            same(heads_map.shape),
+        ],
+        [
+            pltpu.VMEM((rows_n, wide, width), F32),
+            pltpu.VMEM((rows_n, wide, LANES), F32),
+            pltpu.VMEM((rows_n, wide, width), F32),
         ],
         name="inner_col",
-    )(x_in, coef_in, into_col, out_col, heads_map)
+        out_specs=cols,
+        grid=(cols_n // wide,),
+    )(x_in, coef, into_col, out_col, heads_map)
 
 
 def half_of(tile, k, heads_map):

time: 202 us -> 199 us (0.985)
  local copies, waits for them, and re-layouts: 47 us -> 41.3 us
  Pallas kernels: 86.7 us -> 90.4 us
    unnamed x76 -> x64, local copies, waits for them, and re-layouts: 17.6 us -> 11.5 us
    pallas_call x2, Pallas kernels: 27.4 us -> 31.2 us  [the longest x1 17.3 us: row_scan(): call(row_scan_body, jax.ShapeDtypeStruct(x_in.shape, BF16), by_row + [sam...]
  transfers between devices with their start and end apart: 12 -> 12, of which waited for: 5 -> 5; matrix products, arithmetic and copies ran while one was open for 15% -> 15% of each run, Pallas kernels for 17% -> 19%
where the time goes in v9:
time: 199 us; the launch traced here: 198 us
  Pallas kernels  90.4 us (45%)
  starting transfers between devices  42.1 us (21%)
  local copies, waits for them, and re-layouts  41.3 us (21%)
  waiting for transfers between devices  15.4 us (8%)
  other arithmetic  7.2 us (4%)
    pallas_call x1, Pallas kernels, conv_and_states(): call(conv_body, outs, [pl.BlockSpec(memory_space=pltpu.SMEM)] + [whole()]...  22 us
    pallas_call x1, Pallas kernels, row_scan(): call(row_scan_body, jax.ShapeDtypeStruct(x_in.shape, BF16), by_row + [sam...  17.3 us
    pallas_call x1, Pallas kernels, finish(): call(finish_body, jax.ShapeDtypeStruct((rows_n, channels, cols_n), BF16),...  17.1 us
    pallas_call x1, Pallas kernels, inner_col(): call(inner_col_body, jax.ShapeDtypeStruct(x_in.shape, BF16), [cols, block...  13.9 us
    all_to_all x1, starting transfers between devices, local(): lax.all_to_all(sent, ('row', 'col'), split_axis=0, concat_axis=0, tiled=T...  11.5 us
    unnamed x64, local copies, waits for them, and re-layouts  11.5 us
    ppermute x4, starting transfers between devices, shifted(): return lax.ppermute(block, axis, pairs)  11.5 us
    reshape x4, local copies, waits for them, and re-layouts, col_layout(): jnp.transpose(parts, (3, 0, 1, 2, 4)).reshape(c // SUB, k * m, r * SUB)  9.1 us
  transfers between devices with their start and end apart: 12, of which 5 were waited for; matrix products, arithmetic and copies ran while one was open for 15% of the time, Pallas kernels for 19%

profile of v9, /device:TPU:1, one launch (start us, length us, event | category | flops | bytes accessed | tf_op | source)
XLA Modules:
  0.0 198.5 jit_solution(5026005442222763901)
XLA Ops:
  0.0 0.7 fusion.56
  0.8 0.7 compare_bitcast_fusion
  1.6 1.6 bitcast_select_fusion
  3.2 0.6 maximum_maximum_fusion
  3.8 3.0 %copy.61 = bf16[128,32,256]{2,1,0:T(8,128)(2,1)} copy(bf16[128,32,256]{0,2,1:T(8,128)(2,1)S(1)} %bitcast.127) | data formatting | bytes 4194304 | tf_op jit(solution)/shard_map/transpose | solution.py:735
  6.8 11.5 %all-to-all-start = ((bf16[128,32,256]{2,1,0:T(8,128)(2,1)}), bf16[128,32,256]{2,1,0:T(8,128)(2,1)S(1)}, u32[]{:S(2)}, u32[]{:S(2)}) async-start(bf16[128,32,256]{2,1,0:T(8,128)(2,1)} %copy.61), calls=%async_computation | async-start | bytes 4194304 | tf_op jit(solution)/shard_map/all_to_all | solution.py:736
  18.3 0.1 slice_reduce_fusion.1
  18.5 0.3 convolution_bitcast_fusion
  18.8 0.4 convolution_bitcast_fusion.1
  19.1 0.3 convolution_bitcast_fusion.2
  19.5 0.3 convolution_bitcast_fusion.3
  19.8 0.1 broadcast_in_dim.89
  20.0 0.4 reduce-precision_convert_fusion
  20.4 0.9 fusion.4
  21.3 0.7 fusion.73
  22.1 0.5 copy.65
  22.6 4.3 %copy.66 = bf16[16,2,16,32,8]{2,1,4,3,0:T(2,128)(2,1)} copy(bf16[16,2,16,32,8]{3,4,0,2,1:T(8,128)(2,1)S(1)} %bitcast.128) | data formatting | bytes 524288 | tf_op jit(solution)/shard_map/transpose | solution.py:110
  26.9 3.9 %reshape.267 = bf16[16,32,256]{1,2,0:T(8,128)(2,1)S(1)} reshape(bf16[16,2,16,32,8]{2,1,4,3,0:T(2,128)(2,1)} %copy.66) | data formatting | bytes 524288 | tf_op jit(solution)/shard_map/reshape | solution.py:110
  30.8 0.3 copy.67.into_col
  31.1 2.0 %fusion.72 = (bf16[2,16,32,128]{3,2,1,0:T(8,128)(2,1)}, bf16[32,2,16,128]{3,0,2,1:T(8,128)(2,1)}) fusion(bf16[4,16,32,128]{3,2,1,0:T(8,128)(2,1)} %get-tuple-element.104), kind=kLoop, calls=%fused_computation.146 | loop fusion | bytes 1048576 | tf_op jit(solution)/shard_map/slice | solution.py:142
  33.1 1.4 copy.68
  34.5 4.3 %copy.69 = bf16[16,2,16,32,8]{2,1,4,3,0:T(2,128)(2,1)} copy(bf16[16,2,16,32,8]{3,4,0,2,1:T(8,128)(2,1)S(1)} %bitcast.129) | data formatting | bytes 524288 | tf_op jit(solution)/shard_map/transpose | solution.py:110
  38.8 3.9 %reshape.269 = bf16[16,32,256]{1,2,0:T(8,128)(2,1)S(1)} reshape(bf16[16,2,16,32,8]{2,1,4,3,0:T(2,128)(2,1)} %copy.69) | data formatting | bytes 524288 | tf_op jit(solution)/shard_map/reshape | solution.py:110
  42.8 1.0 copy.70.out_col
  43.8 1.1 copy.63
  44.9 1.8 copy.64
  46.8 0.1 copy.76
  46.9 0.1 reshape.271
  47.5 0.1 iota_compare_fusion.3
  47.8 1.4 add_reduce_fusion.cells
  49.3 9.0 %place_norm_project.1 = (bf16[4096,192]{1,0:T(8,128)(2,1)S(1)}, bf16[4096,384]{1,0:T(8,128)(2,1)S(1)}, f32[32,384]{1,0:T(8,128)S(1)}, f32[32,384]{1,0:T(8,128)S(1)}) custom-call(s32[4096]{0:T(1024)S(1)} %add_reduce_fusion.cells, bf16[4096,256]{1,0:T(8,128)(2,1)S(1)} %bitcast.118, f32[1,192]{1,0:T(1,128)S(1)} %bitcast.124, bf16[192,384]{1,0:T(8,128)(2,1)S(1)} %copy-done.22), custom_call_target="tpu_custom_call" | custom-call | flops 120000000 | bytes 300000 | tf_op jit(solution)/shard_map/place_norm_project/pallas_call | solution.py:205
  58.3 1.3 copy-done.5
  59.6 3.3 %collective-permute-start = (bf16[32,384]{1,0:T(8,128)(2,1)S(1)}, bf16[32,384]{1,0:T(8,128)(2,1)S(1)}, u32[]{:S(2)}, u32[]{:S(2)}) collective-permute-start(bf16[32,384]{1,0:T(8,128)(2,1)S(1)} %convert.19), channel_id=1, source_target_pairs={{0,1},{1,2},{2,3},{3,4},{4,5},{5,6},{6,7},{7,8},{8,9},{9,10},{10,1... | collective-permute-start | bytes 73736 | tf_op jit(solution)/shard_map/ppermute | solution.py:713
  62.9 1.3 collective-permute-start.1
  64.2 3.2 %collective-permute-done.1 = bf16[32,384]{1,0:T(8,128)(2,1)S(1)} collective-permute-done((bf16[32,384]{1,0:T(8,128)(2,1)S(1)}, bf16[32,384]{1,0:T(8,128)(2,1)S(1)}, u32[]{:S(2)}, u32[]{:S(2)}) %collective-permute-start.1) | collective-permute-done | bytes 24608 | tf_op jit(solution)/shard_map/ppermute | solution.py:713
  67.5 3.7 %collective-permute-start.3 = (bf16[130,384]{1,0:T(8,128)(2,1)S(1)}, bf16[130,384]{1,0:T(8,128)(2,1)S(1)}, u32[]{:S(2)}, u32[]{:S(2)}) collective-permute-start(bf16[130,384]{1,0:T(8,128)(2,1)S(1)} %pad_maximum_fusion.2), channel_id=1, source_target_pairs={{16,0},{32,16},{48,32},{64,48},{80,64},{96,80},{112,96},{17,1},{33... | collective-permute-start | bytes 299528 | tf_op jit(solution)/shard_map/ppermute | solution.py:713
  71.2 3.2 %collective-permute-start.2 = (bf16[130,384]{1,0:T(8,128)(2,1)S(1)}, bf16[130,384]{1,0:T(8,128)(2,1)S(1)}, u32[]{:S(2)}, u32[]{:S(2)}) collective-permute-start(bf16[130,384]{1,0:T(8,128)(2,1)S(1)} %pad_maximum_fusion.1), channel_id=1, source_target_pairs={{0,16},{16,32},{32,48},{48,64},{64,80},{80,96},{96,112},{1,17},{17... | collective-permute-start | bytes 299528 | tf_op jit(solution)/shard_map/ppermute | solution.py:713
  74.5 0.1 collective-permute-done.3
  74.6 1.3 collective-permute-done.2
  76.2 22.0 %conv_states.1 = (bf16[32,128,384]{2,1,0:T(8,128)(2,1)S(1)}, bf16[32,128,128]{2,1,0:T(8,128)(2,1)S(1)}, bf16[16,80,384]{2,1,0:T(8,128)(2,1)S(1)}, bf16[8,272,384]{2,1,0:T(8,128)(2,1)S(1)}, bf16[8,272,384]{2,1,0:T(8,128)(2,1)}) custom-call(s32[2]{0:T(128)S(1)} %pad_add_fusion.spot, bf16[32,128,384]{2,1,0:T(8,128)(2,1)S(1)} %bitcast.119, ...), custom_call_target="tpu_custom_call" | custom-call | flops 310000000 | bytes 775000 | tf_op jit(solution)/shard_map/conv_states/pallas_call | solution.py:357
  98.2 1.6 copy-done.2
  99.8 1.0 copy-done.3
  100.8 0.9 copy-done.18
  101.7 8.7 %all-to-all-start.1 = ((bf16[16,80,384]{2,1,0:T(8,128)(2,1)}), bf16[16,80,384]{2,1,0:T(8,128)(2,1)}, u32[]{:S(2)}, u32[]{:S(2)}) async-start(bf16[16,80,384]{2,1,0:T(8,128)(2,1)} %copy-done.18), calls=%async_computation.1 | async-start | bytes 1966080 | tf_op jit(solution)/shard_map/all_to_all | solution.py:782
  110.5 3.3 %chip_total.1 = (bf16[8,144,384]{2,1,0:T(8,128)(2,1)}, bf16[8,144,384]{2,1,0:T(8,128)(2,1)}, bf16[8,144,384]{2,1,0:T(8,128)(2,1)}) custom-call(s32[2]{0:T(128)S(1)} %pad_add_fusion.spot, bf16[8,272,384]{2,1,0:T(8,128)(2,1)S(1)} %get-tuple-element.51.own, bf16[8,272,384]{2,1,0:T(8,128)(2,1)S(1)} %collective-permute-done.4.got, ...), custom_call_target="tpu_custom_call" | custom-call | flops 50000000 | bytes 125000 | tf_op jit(solution)/shard_map/chip_total/pallas_call | solution.py:575
  113.7 1.6 collective-permute-start.5
  115.3 2.4 %collective-permute-start.6 = (bf16[8,144,384]{2,1,0:T(8,128)(2,1)}, bf16[8,144,384]{2,1,0:T(8,128)(2,1)}, u32[]{:S(2)}, u32[]{:S(2)}) collective-permute-start(bf16[8,144,384]{2,1,0:T(8,128)(2,1)} %get-tuple-element.54), channel_id=1, source_target_pairs={{0,64},{16,80},{32,96},{48,112},{64,0},{80,16},{96,32},{112,48},{1... | collective-permute-start | bytes 2654216 | tf_op jit(solution)/shard_map/ppermute | solution.py:785
  117.7 1.2 collective-permute-start.7
  118.9 2.5 %gate.1.gate_in = bf16[4096,384]{1,0:T(8,128)(2,1)S(1)} custom-call(bf16[4096,192]{1,0:T(8,128)(2,1)S(1)} %copy-done.6, f32[1,192]{1,0:T(1,128)S(1)} %bitcast.125, bf16[192,384]{1,0:T(8,128)(2,1)S(1)} %copy-done.23), custom_call_target="tpu_custom_call" | custom-call | flops 60000000 | bytes 150000 | tf_op jit(solution)/shard_map/gate/pallas_call | solution.py:231
  121.4 7.7 %all-to-all-done.1.states = bf16[16,80,384]{2,1,0:T(8,128)(2,1)} async-done(((bf16[16,80,384]{2,1,0:T(8,128)(2,1)}), bf16[16,80,384]{2,1,0:T(8,128)(2,1)}, u32[]{:S(2)}, u32[]{:S(2)}) %all-to-all-start.1) | async-done | bytes 983072 | tf_op jit(solution)/shard_map/all_to_all | solution.py:782
  129.2 1.6 chain.1
  130.8 0.9 copy-done.14
  131.6 4.5 %all-to-all-start.2 = ((bf16[16,64,384]{2,1,0:T(8,128)(2,1)}), bf16[16,64,384]{2,1,0:T(8,128)(2,1)}, u32[]{:S(2)}, u32[]{:S(2)}) async-start(bf16[16,64,384]{2,1,0:T(8,128)(2,1)} %copy-done.14), calls=%async_computation.2 | async-start | bytes 1572864 | tf_op jit(solution)/shard_map/all_to_all | solution.py:792
  136.2 0.6 broadcast_in_dim.93.skip
  136.7 13.9 %inner_col.1.total_col = bf16[32,128,384]{2,1,0:T(8,128)(2,1)} custom-call(bf16[32,128,384]{2,1,0:T(8,128)(2,1)} %copy-done.2, bf16[32,128,128]{2,1,0:T(8,128)(2,1)} %copy-done.3, bf16[16,32,256]{2,1,0:T(8,128)(2,1)} %copy-done.16, bf16[16,32,256]{2,1,0:T(8,128)(2,1)} %copy.70.out_col, bf16[32,768]{1,0:T(8,128)(2,1)} %copy-done.12), custom_call_target="tpu_custom_call" | custom-call | flops 160000000 | bytes 400000 | tf_op jit(solution)/shard_map/inner_col/pallas_call | solution.py:469
  150.8 17.3 %row_scan.1.total_row = bf16[32,128,384]{2,1,0:T(8,128)(2,1)} custom-call(bf16[32,128,384]{2,1,0:T(8,128)(2,1)} %copy-done.2, bf16[32,128,128]{2,1,0:T(8,128)(2,1)} %copy-done.3, bf16[32,2,16,384]{3,2,1,0:T(8,128)(2,1)} %bitcast.46.enter_row, bf16[32,32,128]{2,1,0:T(8,128)(2,1)} %bitcast.121, bf16[32,32,128]{2,1,0:T(8,128)(2,1)} %bitcast.130, ...), custom_call_target="tpu_custom_call" | custom-call | flops 200000000 | bytes 500000 | tf_op jit(solution)/shard_map/row_scan/pallas_call | solution.py:417
  168.1 1.6 copy-done.9
  169.7 1.6 copy-done.11
  171.3 3.7 %entering.1 = (bf16[8,2,128,384]{3,2,1,0:T(8,128)(2,1)S(1)}, bf16[8,2,128,384]{3,2,1,0:T(8,128)(2,1)S(1)}) custom-call(s32[2]{0:T(128)S(1)} %pad_add_fusion.spot, bf16[8,272,384]{2,1,0:T(8,128)(2,1)S(1)} %copy-done.9, bf16[8,272,384]{2,1,0:T(8,128)(2,1)S(1)} %copy-done.11, bf16[32,768]{1,0:T(8,128)(2,1)S(1)} %copy-done.13, ...), custom_call_target="tpu_custom_call" | custom-call | flops 60000000 | bytes 150000 | tf_op jit(solution)/shard_map/entering/pallas_call | solution.py:635
  175.0 0.8 collective-permute-start.8
  175.8 3.0 %collective-permute-done.8.enter_other = bf16[8,2,128,384]{3,2,1,0:T(8,128)(2,1)S(1)} collective-permute-done((bf16[8,2,128,384]{3,2,1,0:T(8,128)(2,1)S(1)}, bf16[8,2,128,384]{3,2,1,0:T(8,128)(2,1)S(1)}, u32[]{:S(2)}, u32[]{:S(2)}) %collective-permute-start.8) | collective-permute-done | bytes 1572896 | tf_op jit(solution)/shard_map/ppermute | solution.py:800
  178.8 1.6 copy-done.7
  180.4 1.0 copy-done.20
  181.4 17.1 %finish.1 = bf16[32,192,128]{2,1,0:T(8,128)(2,1)} custom-call(s32[2]{0:T(128)S(1)} %pad_add_fusion.spot, bf16[32,128,384]{2,1,0:T(8,128)(2,1)S(1)} %copy-done, bf16[32,128,384]{2,1,0:T(8,128)(2,1)S(1)} %copy-done.1, bf16[32,128,128]{2,1,0:T(8,128)(2,1)S(1)} %copy-done.4, bf16[8,2,128,384]{3,2,1,0:T(8,128)(2,1)S(1)} %get-tuple-element.71.enter_own, ...), custom_call_target="tpu_custom_call" | custom-call | flops 250000000 | bytes 625000 | tf_op jit(solution)/shard_map/finish/pallas_call | solution.py:701
  (113 shorter events, 1.3 us)
Async XLA Ops:
  6.8 11.5 %copy-start.27 = (f32[4,6,32,128]{3,2,1,0:T(8,128)S(1)}, f32[4,6,32,128]{3,2,1,0:T(8,128)}, u32[]{:S(2)}) copy-start(f32[4,6,32,128]{3,2,1,0:T(8,128)} %param.30) | copy-start | bytes 1179652
  6.8 41.0 %all-to-all-start = ((bf16[128,32,256]{2,1,0:T(8,128)(2,1)}), bf16[128,32,256]{2,1,0:T(8,128)(2,1)S(1)}, u32[]{:S(2)}, u32[]{:S(2)}) async-start(bf16[128,32,256]{2,1,0:T(8,128)(2,1)} %copy.61), calls=%async_computation | async-start | bytes 4194304 | tf_op jit(solution)/shard_map/all_to_all | solution.py:736
  31.1 45.0 %copy-start.16 = (bf16[16,32,256]{2,1,0:T(8,128)(2,1)}, bf16[16,32,256]{2,1,0:T(8,128)(2,1)S(1)}, u32[]{:S(2)}) copy-start(bf16[16,32,256]{2,1,0:T(8,128)(2,1)S(1)} %copy.67.into_col) | copy-start | bytes 786436
  42.7 4.6 %copy-start.28 = (f32[3,3,384]{2,1,0:T(4,128)S(1)}, f32[3,3,384]{2,1,0:T(4,128)}, u32[]{:S(2)}) copy-start(f32[3,3,384]{2,1,0:T(4,128)} %param.26) | copy-start | bytes 41476
  42.7 4.6 %copy-start.29 = (f32[384]{0:T(512)S(1)}, f32[384]{0:T(512)}, u32[]{:S(2)}) copy-start(f32[384]{0:T(512)} %param.27) | copy-start | bytes 4612
  43.8 5.5 %copy-start.22 = (bf16[192,384]{1,0:T(8,128)(2,1)S(1)}, bf16[192,384]{1,0:T(8,128)(2,1)}, u32[]{:S(2)}) copy-start(bf16[192,384]{1,0:T(8,128)(2,1)} %in_x.1) | copy-start | bytes 442372
  43.8 5.5 %copy-start.25 = (f32[192]{0:T(256)S(1)}, f32[192]{0:T(256)}, u32[]{:S(2)}) copy-start(f32[192]{0:T(256)} %param.23) | copy-start | bytes 2308
  44.9 31.3 %copy-start.17 = (bf16[32,2,16,128]{3,2,1,0:T(8,128)(2,1)}, bf16[32,2,16,128]{3,2,1,0:T(8,128)(2,1)S(1)}, u32[]{:S(2)}) copy-start(bf16[32,2,16,128]{3,2,1,0:T(8,128)(2,1)S(1)} %copy.63) | copy-start | bytes 786436
  47.8 81.4 %copy-start.12 = (bf16[32,768]{1,0:T(8,128)(2,1)}, bf16[32,768]{1,0:T(8,128)(2,1)S(1)}, u32[]{:S(2)}) copy-start(bf16[32,768]{1,0:T(8,128)(2,1)S(1)} %and_convert_fusion.heads_map) | copy-start | bytes 147460
  49.3 26.9 %copy-start.24 = (bf16[384,128]{1,0:T(8,128)(2,1)S(1)}, bf16[384,128]{1,0:T(8,128)(2,1)}, u32[]{:S(2)}) copy-start(bf16[384,128]{1,0:T(8,128)(2,1)} %x_proj.1) | copy-start | bytes 294916
  58.3 1.3 copy-start.5
  59.6 4.6 %collective-permute-start = (bf16[32,384]{1,0:T(8,128)(2,1)S(1)}, bf16[32,384]{1,0:T(8,128)(2,1)S(1)}, u32[]{:S(2)}, u32[]{:S(2)}) collective-permute-start(bf16[32,384]{1,0:T(8,128)(2,1)S(1)} %convert.19), channel_id=1, source_target_pairs={{0,1},{1,2},{2,3},{3,4},{4,5},{5,6},{6,7},{7,8},{8,9},{9,10},{10,1... | collective-permute-start | bytes 73736 | tf_op jit(solution)/shard_map/ppermute | solution.py:713
  62.9 4.6 %collective-permute-start.1 = (bf16[32,384]{1,0:T(8,128)(2,1)S(1)}, bf16[32,384]{1,0:T(8,128)(2,1)S(1)}, u32[]{:S(2)}, u32[]{:S(2)}) collective-permute-start(bf16[32,384]{1,0:T(8,128)(2,1)S(1)} %convert.18), channel_id=1, source_target_pairs={{1,0},{2,1},{3,2},{4,3},{5,4},{6,5},{7,6},{8,7},{9,8},{10,9},{11,1... | collective-permute-start | bytes 73736 | tf_op jit(solution)/shard_map/ppermute | solution.py:713
  67.5 7.2 %collective-permute-start.3 = (bf16[130,384]{1,0:T(8,128)(2,1)S(1)}, bf16[130,384]{1,0:T(8,128)(2,1)S(1)}, u32[]{:S(2)}, u32[]{:S(2)}) collective-permute-start(bf16[130,384]{1,0:T(8,128)(2,1)S(1)} %pad_maximum_fusion.2), channel_id=1, source_target_pairs={{16,0},{32,16},{48,32},{64,48},{80,64},{96,80},{112,96},{17,1},{33... | collective-permute-start | bytes 299528 | tf_op jit(solution)/shard_map/ppermute | solution.py:713
  71.2 4.7 %collective-permute-start.2 = (bf16[130,384]{1,0:T(8,128)(2,1)S(1)}, bf16[130,384]{1,0:T(8,128)(2,1)S(1)}, u32[]{:S(2)}, u32[]{:S(2)}) collective-permute-start(bf16[130,384]{1,0:T(8,128)(2,1)S(1)} %pad_maximum_fusion.1), channel_id=1, source_target_pairs={{0,16},{16,32},{32,48},{48,64},{64,80},{80,96},{96,112},{1,17},{17... | collective-permute-start | bytes 299528 | tf_op jit(solution)/shard_map/ppermute | solution.py:713
  98.2 1.6 copy-start.2
  99.8 1.0 copy-start.3
  100.8 1.0 copy-start.18
  100.8 13.0 %copy-start.8 = (bf16[8,272,384]{2,1,0:T(8,128)(2,1)}, bf16[8,272,384]{2,1,0:T(8,128)(2,1)S(1)}, u32[]{:S(2)}) copy-start(bf16[8,272,384]{2,1,0:T(8,128)(2,1)S(1)} %get-tuple-element.51.own) | copy-start | bytes 5013508
  100.8 9.7 %collective-permute-start.4 = (bf16[8,272,384]{2,1,0:T(8,128)(2,1)}, bf16[8,272,384]{2,1,0:T(8,128)(2,1)S(1)}, u32[]{:S(2)}, u32[]{:S(2)}) collective-permute-start(bf16[8,272,384]{2,1,0:T(8,128)(2,1)} %get-tuple-element.52), channel_id=1, source_target_pairs={{0,16},{16,0},{32,48},{48,32},{64,80},{80,64},{96,112},{112,96},{1... | collective-permute-start | bytes 5013512 | tf_op jit(solution)/shard_map/ppermute | solution.py:781
  101.7 27.4 %all-to-all-start.1 = ((bf16[16,80,384]{2,1,0:T(8,128)(2,1)}), bf16[16,80,384]{2,1,0:T(8,128)(2,1)}, u32[]{:S(2)}, u32[]{:S(2)}) async-start(bf16[16,80,384]{2,1,0:T(8,128)(2,1)} %copy-done.18), calls=%async_computation.1 | async-start | bytes 1966080 | tf_op jit(solution)/shard_map/all_to_all | solution.py:782
  110.4 8.5 %copy-start.6 = (bf16[4096,192]{1,0:T(8,128)(2,1)S(1)}, bf16[4096,192]{1,0:T(8,128)(2,1)}, u32[]{:S(2)}) copy-start(bf16[4096,192]{1,0:T(8,128)(2,1)} %copy-done.5) | copy-start | bytes 4718596
  110.4 8.5 %copy-start.23 = (bf16[192,384]{1,0:T(8,128)(2,1)S(1)}, bf16[192,384]{1,0:T(8,128)(2,1)}, u32[]{:S(2)}) copy-start(bf16[192,384]{1,0:T(8,128)(2,1)} %in_z.1) | copy-start | bytes 442372
  110.4 8.5 %copy-start.10 = (bf16[8,272,384]{2,1,0:T(8,128)(2,1)}, bf16[8,272,384]{2,1,0:T(8,128)(2,1)S(1)}, u32[]{:S(2)}) copy-start(bf16[8,272,384]{2,1,0:T(8,128)(2,1)S(1)} %collective-permute-done.4.got) | copy-start | bytes 5013508
  113.7 54.3 %collective-permute-start.5 = (bf16[8,144,384]{2,1,0:T(8,128)(2,1)}, bf16[8,144,384]{2,1,0:T(8,128)(2,1)}, u32[]{:S(2)}, u32[]{:S(2)}) collective-permute-start(bf16[8,144,384]{2,1,0:T(8,128)(2,1)} %get-tuple-element.53), channel_id=1, source_target_pairs={{0,32},{16,48},{32,64},{48,80},{64,96},{80,112},{96,0},{112,16},{1... | collective-permute-start | bytes 2654216 | tf_op jit(solution)/shard_map/ppermute | solution.py:785
  115.3 52.8 %collective-permute-start.6 = (bf16[8,144,384]{2,1,0:T(8,128)(2,1)}, bf16[8,144,384]{2,1,0:T(8,128)(2,1)}, u32[]{:S(2)}, u32[]{:S(2)}) collective-permute-start(bf16[8,144,384]{2,1,0:T(8,128)(2,1)} %get-tuple-element.54), channel_id=1, source_target_pairs={{0,64},{16,80},{32,96},{48,112},{64,0},{80,16},{96,32},{112,48},{1... | collective-permute-start | bytes 2654216 | tf_op jit(solution)/shard_map/ppermute | solution.py:785
  117.7 50.3 %collective-permute-start.7 = (bf16[8,144,384]{2,1,0:T(8,128)(2,1)}, bf16[8,144,384]{2,1,0:T(8,128)(2,1)}, u32[]{:S(2)}, u32[]{:S(2)}) collective-permute-start(bf16[8,144,384]{2,1,0:T(8,128)(2,1)} %get-tuple-element.55), channel_id=1, source_target_pairs={{0,96},{16,112},{32,0},{48,16},{64,32},{80,48},{96,64},{112,80},{1... | collective-permute-start | bytes 2654216 | tf_op jit(solution)/shard_map/ppermute | solution.py:785
  121.4 14.7 %copy-start.30 = (f32[384]{0:T(512)S(1)}, f32[384]{0:T(512)}, u32[]{:S(2)}) copy-start(f32[384]{0:T(512)} %param.29) | copy-start | bytes 4612
  130.8 0.9 copy-start.14
  131.6 19.0 %all-to-all-start.2 = ((bf16[16,64,384]{2,1,0:T(8,128)(2,1)}), bf16[16,64,384]{2,1,0:T(8,128)(2,1)}, u32[]{:S(2)}, u32[]{:S(2)}) async-start(bf16[16,64,384]{2,1,0:T(8,128)(2,1)} %copy-done.14), calls=%async_computation.2 | async-start | bytes 1572864 | tf_op jit(solution)/shard_map/all_to_all | solution.py:792
  150.7 17.4 %copy-start.13 = (bf16[32,768]{1,0:T(8,128)(2,1)S(1)}, bf16[32,768]{1,0:T(8,128)(2,1)}, u32[]{:S(2)}) copy-start(bf16[32,768]{1,0:T(8,128)(2,1)} %copy-done.12) | copy-start | bytes 147460
  150.7 25.1 %copy-start.31 = (f32[384]{0:T(512)S(1)}, f32[384]{0:T(512)}, u32[]{:S(2)}) copy-start(f32[384]{0:T(512)} %param.31) | copy-start | bytes 4612
  150.7 28.1 %copy-start.1 = (bf16[32,128,384]{2,1,0:T(8,128)(2,1)S(1)}, bf16[32,128,384]{2,1,0:T(8,128)(2,1)}, u32[]{:S(2)}) copy-start(bf16[32,128,384]{2,1,0:T(8,128)(2,1)} %inner_col.1.total_col) | copy-start | bytes 9437188
  150.7 28.1 %copy-start.15 = (bf16[16,32,256]{2,1,0:T(8,128)(2,1)S(1)}, bf16[16,32,256]{2,1,0:T(8,128)(2,1)}, u32[]{:S(2)}) copy-start(bf16[16,32,256]{2,1,0:T(8,128)(2,1)} %copy.70.out_col) | copy-start | bytes 786436
  150.7 28.1 %copy-start.19 = (bf16[192,768]{1,0:T(8,128)(2,1)S(1)}, bf16[192,768]{1,0:T(8,128)(2,1)}, u32[]{:S(2)}) copy-start(bf16[192,768]{1,0:T(8,128)(2,1)} %ff_in.1) | copy-start | bytes 884740
  150.7 28.1 %copy-start.21 = (bf16[384,192]{0,1:T(8,128)(2,1)S(1)}, bf16[384,192]{0,1:T(8,128)(2,1)}, u32[]{:S(2)}) copy-start(bf16[384,192]{0,1:T(8,128)(2,1)} %param.32) | copy-start | bytes 442372
  150.7 28.1 %copy-start.26 = (f32[192]{0:T(256)S(1)}, f32[192]{0:T(256)}, u32[]{:S(2)}) copy-start(f32[192]{0:T(256)} %param.33) | copy-start | bytes 2308
  168.0 10.8 %copy-start = (bf16[32,128,384]{2,1,0:T(8,128)(2,1)S(1)}, bf16[32,128,384]{2,1,0:T(8,128)(2,1)}, u32[]{:S(2)}) copy-start(bf16[32,128,384]{2,1,0:T(8,128)(2,1)} %row_scan.1.total_row) | copy-start | bytes 9437188
  168.0 10.8 %copy-start.4 = (bf16[32,128,128]{2,1,0:T(8,128)(2,1)S(1)}, bf16[32,128,128]{2,1,0:T(8,128)(2,1)}, u32[]{:S(2)}) copy-start(bf16[32,128,128]{2,1,0:T(8,128)(2,1)} %copy-done.3) | copy-start | bytes 3145732
  168.1 1.6 copy-start.9
  169.7 1.6 copy-start.11
  175.0 3.8 %collective-permute-start.8 = (bf16[8,2,128,384]{3,2,1,0:T(8,128)(2,1)S(1)}, bf16[8,2,128,384]{3,2,1,0:T(8,128)(2,1)S(1)}, u32[]{:S(2)}, u32[]{:S(2)}) collective-permute-start(bf16[8,2,128,384]{3,2,1,0:T(8,128)(2,1)S(1)} %get-tuple-element.72), channel_id=1, source_target_pairs={{0,16},{16,0},{32,48},{48,32},{64,80},{80,64},{96,112},{112,96},{1... | collective-permute-start | bytes 4718600 | tf_op jit(solution)/shard_map/ppermute | solution.py:800
  178.8 1.6 copy-start.7
  180.4 1.0 copy-start.20

commit v10 on v9

--- a/solution.py
+++ b/solution.py
@@ -16,7 +16,7 @@
 LANES = 128
 SUB = 8
 KERNEL_MIB = dict(
-    place_norm_project=20, gate=10, conv_states=32, row_scan=57, inner_col=57, chain=8, chip_total=10, entering=13, finish=34
+    place_norm_project=20, gate=10, conv_states=57, row_scan=57, inner_col=57, chain=8, chip_total=10, entering=13, finish=34
 )
 
 

time: 199 us -> 204 us (1.025)
  waiting for transfers between devices: 15.4 us -> 11.6 us
  other arithmetic: 7.2 us -> 10.1 us
  Pallas kernels: 90.4 us -> 93.3 us
  starting transfers between devices: 42.1 us -> 44.4 us
    all_to_all x1, waiting for transfers between devices: 7.71 us -> 3.87 us  [local(): lax.all_to_all(state_row, 'col', split_axis=0, concat_axis=0, tiled=True)]
    unnamed x64 -> x56, local copies, waits for them, and re-layouts: 11.5 us -> 7.94 us
    pallas_call x1, Pallas kernels: 22 us -> 24.9 us  [conv_and_states(): call(conv_body, outs, [pl.BlockSpec(memory_space=pltpu.SMEM)] + [whole()]...]
  transfers between devices with their start and end apart: 12 -> 12, of which waited for: 5 -> 5; matrix products, arithmetic and copies ran while one was open for 15% -> 17% of each run, Pallas kernels for 19% -> 19%
where the time goes in v10:
time: 204 us; the launch traced here: 203 us
  Pallas kernels  93.3 us (46%)
  starting transfers between devices  44.4 us (22%)
  local copies, waits for them, and re-layouts  41.7 us (20%)
  waiting for transfers between devices  11.6 us (6%)
  other arithmetic  10.1 us (5%)
    pallas_call x1, Pallas kernels, conv_and_states(): call(conv_body, outs, [pl.BlockSpec(memory_space=pltpu.SMEM)] + [whole()]...  24.9 us
    pallas_call x1, Pallas kernels, row_scan(): call(row_scan_body, jax.ShapeDtypeStruct(x_in.shape, BF16), by_row + [sam...  17.3 us
    pallas_call x1, Pallas kernels, finish(): call(finish_body, jax.ShapeDtypeStruct((rows_n, channels, cols_n), BF16),...  17.1 us
    pallas_call x1, Pallas kernels, inner_col(): call(inner_col_body, jax.ShapeDtypeStruct(x_in.shape, BF16), [cols, block...  13.9 us
    all_to_all x1, starting transfers between devices, local(): lax.all_to_all(sent, ('row', 'col'), split_axis=0, concat_axis=0, tiled=T...  11.5 us
    ppermute x4, starting transfers between devices, shifted(): return lax.ppermute(block, axis, pairs)  11.5 us
    reshape x4, local copies, waits for them, and re-layouts, col_layout(): jnp.transpose(parts, (3, 0, 1, 2, 4)).reshape(c // SUB, k * m, r * SUB)  9.83 us
    pallas_call x1, Pallas kernels, place(): call(place_body, outs, [pl.BlockSpec(memory_space=pltpu.SMEM), whole(), w...  8.99 us
  transfers between devices with their start and end apart: 12, of which 5 were waited for; matrix products, arithmetic and copies ran while one was open for 17% of the time, Pallas kernels for 19%

profile of v10, /device:TPU:1, one launch (start us, length us, event | category | flops | bytes accessed | tf_op | source)
XLA Modules:
  0.0 203.1 jit_solution(739748838479026135)
XLA Ops:
  0.0 0.7 fusion.56
  0.8 0.7 compare_bitcast_fusion
  1.6 1.6 bitcast_select_fusion
  3.2 0.6 maximum_maximum_fusion
  3.8 3.0 %copy.61 = bf16[128,32,256]{2,1,0:T(8,128)(2,1)} copy(bf16[128,32,256]{0,2,1:T(8,128)(2,1)S(1)} %bitcast.125) | data formatting | bytes 4194304 | tf_op jit(solution)/shard_map/transpose | solution.py:735
  6.8 11.5 %all-to-all-start = ((bf16[128,32,256]{2,1,0:T(8,128)(2,1)}), bf16[128,32,256]{2,1,0:T(8,128)(2,1)S(1)}, u32[]{:S(2)}, u32[]{:S(2)}) async-start(bf16[128,32,256]{2,1,0:T(8,128)(2,1)} %copy.61), calls=%async_computation | async-start | bytes 4194304 | tf_op jit(solution)/shard_map/all_to_all | solution.py:736
  18.8 0.4 convolution_bitcast_fusion.1
  19.2 0.3 convolution_bitcast_fusion.2
  20.0 0.4 reduce-precision_convert_fusion
  20.4 0.9 fusion.4
  21.3 0.8 fusion.73
  22.1 0.5 copy.65
  22.6 4.3 %copy.66 = bf16[16,2,16,32,8]{2,1,4,3,0:T(2,128)(2,1)} copy(bf16[16,2,16,32,8]{3,4,0,2,1:T(8,128)(2,1)S(1)} %bitcast.126) | data formatting | bytes 524288 | tf_op jit(solution)/shard_map/transpose | solution.py:110
  26.9 3.9 %reshape.267 = bf16[16,32,256]{1,2,0:T(8,128)(2,1)S(1)} reshape(bf16[16,2,16,32,8]{2,1,4,3,0:T(2,128)(2,1)} %copy.66) | data formatting | bytes 524288 | tf_op jit(solution)/shard_map/reshape | solution.py:110
  30.8 1.0 copy.67.into_col
  31.8 1.8 fusion.72
  33.6 0.5 copy.68
  34.1 4.3 %copy.69 = bf16[16,2,16,32,8]{2,1,4,3,0:T(2,128)(2,1)} copy(bf16[16,2,16,32,8]{3,4,0,2,1:T(8,128)(2,1)S(1)} %bitcast.127) | data formatting | bytes 524288 | tf_op jit(solution)/shard_map/transpose | solution.py:110
  38.4 3.9 %reshape.269 = bf16[16,32,256]{1,2,0:T(8,128)(2,1)S(1)} reshape(bf16[16,2,16,32,8]{2,1,4,3,0:T(2,128)(2,1)} %copy.69) | data formatting | bytes 524288 | tf_op jit(solution)/shard_map/reshape | solution.py:110
  42.3 1.0 copy.70.out_col
  43.3 1.8 copy.63
  45.1 1.8 copy.64
  47.1 0.7 pad.83.half_col
  48.1 0.7 pad.80.half_row
  48.8 0.6 reshape.273.conv_w
  49.4 0.6 broadcast_in_dim.92.conv_bias
  50.0 0.6 pad_add_fusion.spot
  50.7 0.6 add_convert_fusion.pick_b
  51.4 0.7 and_convert_fusion.heads_map
  52.1 1.4 add_reduce_fusion.cells
  53.6 9.0 %place_norm_project.1 = (bf16[4096,192]{1,0:T(8,128)(2,1)S(1)}, bf16[4096,384]{1,0:T(8,128)(2,1)S(1)}, f32[32,384]{1,0:T(8,128)S(1)}, f32[32,384]{1,0:T(8,128)S(1)}) custom-call(s32[4096]{0:T(1024)S(1)} %add_reduce_fusion.cells, bf16[4096,256]{1,0:T(8,128)(2,1)S(1)} %bitcast.118, f32[1,192]{1,0:T(1,128)S(1)} %bitcast.122, bf16[192,384]{1,0:T(8,128)(2,1)S(1)} %copy-done.18), custom_call_target="tpu_custom_call" | custom-call | flops 120000000 | bytes 300000 | tf_op jit(solution)/shard_map/place_norm_project/pallas_call | solution.py:205
  62.6 1.3 copy-done.3
  63.9 3.3 %collective-permute-start = (bf16[32,384]{1,0:T(8,128)(2,1)S(1)}, bf16[32,384]{1,0:T(8,128)(2,1)S(1)}, u32[]{:S(2)}, u32[]{:S(2)}) collective-permute-start(bf16[32,384]{1,0:T(8,128)(2,1)S(1)} %convert.19), channel_id=1, source_target_pairs={{0,1},{1,2},{2,3},{3,4},{4,5},{5,6},{6,7},{7,8},{8,9},{9,10},{10,1... | collective-permute-start | bytes 73736 | tf_op jit(solution)/shard_map/ppermute | solution.py:713
  67.2 1.3 collective-permute-start.1
  68.5 3.2 %collective-permute-done.1 = bf16[32,384]{1,0:T(8,128)(2,1)S(1)} collective-permute-done((bf16[32,384]{1,0:T(8,128)(2,1)S(1)}, bf16[32,384]{1,0:T(8,128)(2,1)S(1)}, u32[]{:S(2)}, u32[]{:S(2)}) %collective-permute-start.1) | collective-permute-done | bytes 24608 | tf_op jit(solution)/shard_map/ppermute | solution.py:713
  71.8 3.7 %collective-permute-start.3 = (bf16[130,384]{1,0:T(8,128)(2,1)S(1)}, bf16[130,384]{1,0:T(8,128)(2,1)S(1)}, u32[]{:S(2)}, u32[]{:S(2)}) collective-permute-start(bf16[130,384]{1,0:T(8,128)(2,1)S(1)} %pad_maximum_fusion.2), channel_id=1, source_target_pairs={{16,0},{32,16},{48,32},{64,48},{80,64},{96,80},{112,96},{17,1},{33... | collective-permute-start | bytes 299528 | tf_op jit(solution)/shard_map/ppermute | solution.py:713
  75.5 3.2 %collective-permute-start.2 = (bf16[130,384]{1,0:T(8,128)(2,1)S(1)}, bf16[130,384]{1,0:T(8,128)(2,1)S(1)}, u32[]{:S(2)}, u32[]{:S(2)}) collective-permute-start(bf16[130,384]{1,0:T(8,128)(2,1)S(1)} %pad_maximum_fusion.1), channel_id=1, source_target_pairs={{0,16},{16,32},{32,48},{48,64},{64,80},{80,96},{96,112},{1,17},{17... | collective-permute-start | bytes 299528 | tf_op jit(solution)/shard_map/ppermute | solution.py:713
  78.9 1.3 collective-permute-done.2
  80.2 0.7 maximum_convert_fusion.1.right
  80.9 0.7 maximum_convert_fusion.left
  81.6 0.7 slice.105.below
  82.3 0.6 slice.102.above
  82.9 24.9 %conv_states.1 = (bf16[32,128,384]{2,1,0:T(8,128)(2,1)}, bf16[32,128,128]{2,1,0:T(8,128)(2,1)}, bf16[16,80,384]{2,1,0:T(8,128)(2,1)}, bf16[8,272,384]{2,1,0:T(8,128)(2,1)}, bf16[8,272,384]{2,1,0:T(8,128)(2,1)}) custom-call(s32[2]{0:T(128)} %pad_add_fusion.spot, bf16[32,128,384]{2,1,0:T(8,128)(2,1)} %bitcast.119, bf16[128,384]{1,0:T(8,128)(2,1)} %slice.102.above, ...), custom_call_target="tpu_custom_call" | custom-call | flops 310000000 | bytes 775000 | tf_op jit(solution)/shard_map/conv_states/pallas_call | solution.py:357
  107.9 8.9 %all-to-all-start.1 = ((bf16[16,80,384]{2,1,0:T(8,128)(2,1)}), bf16[16,80,384]{2,1,0:T(8,128)(2,1)}, u32[]{:S(2)}, u32[]{:S(2)}) async-start(bf16[16,80,384]{2,1,0:T(8,128)(2,1)} %get-tuple-element.57), calls=%async_computation.1 | async-start | bytes 1966080 | tf_op jit(solution)/shard_map/all_to_all | solution.py:782
  116.8 3.3 %chip_total.1 = (bf16[8,144,384]{2,1,0:T(8,128)(2,1)}, bf16[8,144,384]{2,1,0:T(8,128)(2,1)}, bf16[8,144,384]{2,1,0:T(8,128)(2,1)}) custom-call(s32[2]{0:T(128)S(1)} %copy-done.20, bf16[8,272,384]{2,1,0:T(8,128)(2,1)S(1)} %copy-done.6, bf16[8,272,384]{2,1,0:T(8,128)(2,1)S(1)} %collective-permute-done.4.got, bf16[32,768]{1,0:T(8,128)(2,1)S(1)} %copy-done.11), custom_call_target="tpu_custom_call" | custom-call | flops 50000000 | bytes 125000 | tf_op jit(solution)/shard_map/chip_total/pallas_call | solution.py:575
  120.1 2.4 %collective-permute-start.5 = (bf16[8,144,384]{2,1,0:T(8,128)(2,1)}, bf16[8,144,384]{2,1,0:T(8,128)(2,1)}, u32[]{:S(2)}, u32[]{:S(2)}) collective-permute-start(bf16[8,144,384]{2,1,0:T(8,128)(2,1)} %get-tuple-element.53), channel_id=1, source_target_pairs={{0,32},{16,48},{32,64},{48,80},{64,96},{80,112},{96,0},{112,16},{1... | collective-permute-start | bytes 2654216 | tf_op jit(solution)/shard_map/ppermute | solution.py:785
  122.5 2.4 %collective-permute-start.6 = (bf16[8,144,384]{2,1,0:T(8,128)(2,1)}, bf16[8,144,384]{2,1,0:T(8,128)(2,1)}, u32[]{:S(2)}, u32[]{:S(2)}) collective-permute-start(bf16[8,144,384]{2,1,0:T(8,128)(2,1)} %get-tuple-element.54), channel_id=1, source_target_pairs={{0,64},{16,80},{32,96},{48,112},{64,0},{80,16},{96,32},{112,48},{1... | collective-permute-start | bytes 2654216 | tf_op jit(solution)/shard_map/ppermute | solution.py:785
  124.9 1.2 collective-permute-start.7
  126.1 2.5 %gate.1.gate_in = bf16[4096,384]{1,0:T(8,128)(2,1)S(1)} custom-call(bf16[4096,192]{1,0:T(8,128)(2,1)S(1)} %copy-done.4, f32[1,192]{1,0:T(1,128)S(1)} %bitcast.123, bf16[192,384]{1,0:T(8,128)(2,1)S(1)} %copy-done.19), custom_call_target="tpu_custom_call" | custom-call | flops 60000000 | bytes 150000 | tf_op jit(solution)/shard_map/gate/pallas_call | solution.py:231
  128.6 3.9 %all-to-all-done.1.states = bf16[16,80,384]{2,1,0:T(8,128)(2,1)} async-done(((bf16[16,80,384]{2,1,0:T(8,128)(2,1)}), bf16[16,80,384]{2,1,0:T(8,128)(2,1)}, u32[]{:S(2)}, u32[]{:S(2)}) %all-to-all-start.1) | async-done | bytes 983072 | tf_op jit(solution)/shard_map/all_to_all | solution.py:782
  132.5 1.6 chain.1
  134.1 0.9 copy-done.13
  134.9 4.5 %all-to-all-start.2 = ((bf16[16,64,384]{2,1,0:T(8,128)(2,1)}), bf16[16,64,384]{2,1,0:T(8,128)(2,1)}, u32[]{:S(2)}, u32[]{:S(2)}) async-start(bf16[16,64,384]{2,1,0:T(8,128)(2,1)} %copy-done.13), calls=%async_computation.2 | async-start | bytes 1572864 | tf_op jit(solution)/shard_map/all_to_all | solution.py:792
  139.5 0.6 broadcast_in_dim.93.skip
  140.1 13.9 %inner_col.1.total_col = bf16[32,128,384]{2,1,0:T(8,128)(2,1)} custom-call(bf16[32,128,384]{2,1,0:T(8,128)(2,1)} %get-tuple-element.64.x_in, bf16[32,128,128]{2,1,0:T(8,128)(2,1)} %get-tuple-element.62.coef_in, bf16[16,32,256]{2,1,0:T(8,128)(2,1)} %copy.67.into_col, bf16[16,32,256]{2,1,0:T(8,128)(2,1)} %copy.70.out_col, ...), custom_call_target="tpu_custom_call" | custom-call | flops 160000000 | bytes 400000 | tf_op jit(solution)/shard_map/inner_col/pallas_call | solution.py:469
  154.1 17.3 %row_scan.1.total_row = bf16[32,128,384]{2,1,0:T(8,128)(2,1)} custom-call(bf16[32,128,384]{2,1,0:T(8,128)(2,1)} %get-tuple-element.64.x_in, bf16[32,128,128]{2,1,0:T(8,128)(2,1)} %get-tuple-element.62.coef_in, bf16[32,2,16,384]{3,2,1,0:T(8,128)(2,1)} %bitcast.46.enter_row, bf16[32,32,128]{2,1,0:T(8,128)(2,1)} %bitcast.129, bf16[32,32,128]{2,1,0:T(8,128)(2,1)} %bitcast.130, ...), custom_call_target="tpu_custom_call" | custom-call | flops 200000000 | bytes 500000 | tf_op jit(solution)/shard_map/row_scan/pallas_call | solution.py:417
  171.4 1.6 copy-done.7
  173.0 1.6 copy-done.9
  174.6 3.7 %entering.1 = (bf16[8,2,128,384]{3,2,1,0:T(8,128)(2,1)S(1)}, bf16[8,2,128,384]{3,2,1,0:T(8,128)(2,1)S(1)}) custom-call(s32[2]{0:T(128)S(1)} %copy-done.20, bf16[8,272,384]{2,1,0:T(8,128)(2,1)S(1)} %copy-done.7, bf16[8,272,384]{2,1,0:T(8,128)(2,1)S(1)} %copy-done.9, bf16[32,768]{1,0:T(8,128)(2,1)S(1)} %copy-done.12, ...), custom_call_target="tpu_custom_call" | custom-call | flops 60000000 | bytes 150000 | tf_op jit(solution)/shard_map/entering/pallas_call | solution.py:635
  178.3 2.0 %collective-permute-start.8 = (bf16[8,2,128,384]{3,2,1,0:T(8,128)(2,1)S(1)}, bf16[8,2,128,384]{3,2,1,0:T(8,128)(2,1)S(1)}, u32[]{:S(2)}, u32[]{:S(2)}) collective-permute-start(bf16[8,2,128,384]{3,2,1,0:T(8,128)(2,1)S(1)} %get-tuple-element.72), channel_id=1, source_target_pairs={{0,16},{16,0},{32,48},{48,32},{64,80},{80,64},{96,112},{112,96},{1... | collective-permute-start | bytes 4718600 | tf_op jit(solution)/shard_map/ppermute | solution.py:800
  180.3 3.0 %collective-permute-done.8.enter_other = bf16[8,2,128,384]{3,2,1,0:T(8,128)(2,1)S(1)} collective-permute-done((bf16[8,2,128,384]{3,2,1,0:T(8,128)(2,1)S(1)}, bf16[8,2,128,384]{3,2,1,0:T(8,128)(2,1)S(1)}, u32[]{:S(2)}, u32[]{:S(2)}) %collective-permute-start.8) | collective-permute-done | bytes 1572896 | tf_op jit(solution)/shard_map/ppermute | solution.py:800
  183.4 1.6 copy-done.5
  185.0 1.0 copy-done.16
  186.0 17.1 %finish.1 = bf16[32,192,128]{2,1,0:T(8,128)(2,1)} custom-call(s32[2]{0:T(128)S(1)} %copy-done.20, bf16[32,128,384]{2,1,0:T(8,128)(2,1)S(1)} %copy-done, bf16[32,128,384]{2,1,0:T(8,128)(2,1)S(1)} %copy-done.1, bf16[32,128,128]{2,1,0:T(8,128)(2,1)S(1)} %copy-done.2, bf16[8,2,128,384]{3,2,1,0:T(8,128)(2,1)S(1)} %get-tuple-element.71.enter_own, ...), custom_call_target="tpu_custom_call" | custom-call | flops 250000000 | bytes 625000 | tf_op jit(solution)/shard_map/finish/pallas_call | solution.py:701
  (105 shorter events, 2.2 us)
Async XLA Ops:
  6.8 11.5 %copy-start.23 = (f32[4,6,32,128]{3,2,1,0:T(8,128)S(1)}, f32[4,6,32,128]{3,2,1,0:T(8,128)}, u32[]{:S(2)}) copy-start(f32[4,6,32,128]{3,2,1,0:T(8,128)} %param.30) | copy-start | bytes 1179652
  6.8 45.3 %all-to-all-start = ((bf16[128,32,256]{2,1,0:T(8,128)(2,1)}), bf16[128,32,256]{2,1,0:T(8,128)(2,1)S(1)}, u32[]{:S(2)}, u32[]{:S(2)}) async-start(bf16[128,32,256]{2,1,0:T(8,128)(2,1)} %copy.61), calls=%async_computation | async-start | bytes 4194304 | tf_op jit(solution)/shard_map/all_to_all | solution.py:736
  42.3 6.5 %copy-start.24 = (f32[3,3,384]{2,1,0:T(4,128)S(1)}, f32[3,3,384]{2,1,0:T(4,128)}, u32[]{:S(2)}) copy-start(f32[3,3,384]{2,1,0:T(4,128)} %param.26) | copy-start | bytes 41476
  42.3 7.1 %copy-start.25 = (f32[384]{0:T(512)S(1)}, f32[384]{0:T(512)}, u32[]{:S(2)}) copy-start(f32[384]{0:T(512)} %param.27) | copy-start | bytes 4612
  43.3 10.2 %copy-start.18 = (bf16[192,384]{1,0:T(8,128)(2,1)S(1)}, bf16[192,384]{1,0:T(8,128)(2,1)}, u32[]{:S(2)}) copy-start(bf16[192,384]{1,0:T(8,128)(2,1)} %in_x.1) | copy-start | bytes 442372
  43.3 10.2 %copy-start.21 = (f32[192]{0:T(256)S(1)}, f32[192]{0:T(256)}, u32[]{:S(2)}) copy-start(f32[192]{0:T(256)} %param.23) | copy-start | bytes 2308
  62.6 1.3 copy-start.3
  63.8 19.1 %copy-start.10 = (bf16[4096,384]{1,0:T(8,128)(2,1)}, bf16[4096,384]{1,0:T(8,128)(2,1)S(1)}, u32[]{:S(2)}) copy-start(bf16[4096,384]{1,0:T(8,128)(2,1)S(1)} %get-tuple-element.42) | copy-start | bytes 9437188
  63.9 4.6 %collective-permute-start = (bf16[32,384]{1,0:T(8,128)(2,1)S(1)}, bf16[32,384]{1,0:T(8,128)(2,1)S(1)}, u32[]{:S(2)}, u32[]{:S(2)}) collective-permute-start(bf16[32,384]{1,0:T(8,128)(2,1)S(1)} %convert.19), channel_id=1, source_target_pairs={{0,1},{1,2},{2,3},{3,4},{4,5},{5,6},{6,7},{7,8},{8,9},{9,10},{10,1... | collective-permute-start | bytes 73736 | tf_op jit(solution)/shard_map/ppermute | solution.py:713
  67.2 4.6 %collective-permute-start.1 = (bf16[32,384]{1,0:T(8,128)(2,1)S(1)}, bf16[32,384]{1,0:T(8,128)(2,1)S(1)}, u32[]{:S(2)}, u32[]{:S(2)}) collective-permute-start(bf16[32,384]{1,0:T(8,128)(2,1)S(1)} %convert.18), channel_id=1, source_target_pairs={{1,0},{2,1},{3,2},{4,3},{5,4},{6,5},{7,6},{8,7},{9,8},{10,9},{11,1... | collective-permute-start | bytes 73736 | tf_op jit(solution)/shard_map/ppermute | solution.py:713
  71.8 7.1 %collective-permute-start.3 = (bf16[130,384]{1,0:T(8,128)(2,1)S(1)}, bf16[130,384]{1,0:T(8,128)(2,1)S(1)}, u32[]{:S(2)}, u32[]{:S(2)}) collective-permute-start(bf16[130,384]{1,0:T(8,128)(2,1)S(1)} %pad_maximum_fusion.2), channel_id=1, source_target_pairs={{16,0},{32,16},{48,32},{64,48},{80,64},{96,80},{112,96},{17,1},{33... | collective-permute-start | bytes 299528 | tf_op jit(solution)/shard_map/ppermute | solution.py:713
  75.5 4.7 %collective-permute-start.2 = (bf16[130,384]{1,0:T(8,128)(2,1)S(1)}, bf16[130,384]{1,0:T(8,128)(2,1)S(1)}, u32[]{:S(2)}, u32[]{:S(2)}) collective-permute-start(bf16[130,384]{1,0:T(8,128)(2,1)S(1)} %pad_maximum_fusion.1), channel_id=1, source_target_pairs={{0,16},{16,32},{32,48},{48,64},{64,80},{80,96},{96,112},{1,17},{17... | collective-permute-start | bytes 299528 | tf_op jit(solution)/shard_map/ppermute | solution.py:713
  82.9 33.9 %copy-start.11 = (bf16[32,768]{1,0:T(8,128)(2,1)S(1)}, bf16[32,768]{1,0:T(8,128)(2,1)}, u32[]{:S(2)}) copy-start(bf16[32,768]{1,0:T(8,128)(2,1)} %and_convert_fusion.heads_map) | copy-start | bytes 147460
  82.9 33.9 %copy-start.20 = (s32[2]{0:T(128)S(1)}, s32[2]{0:T(128)}, u32[]{:S(2)}) copy-start(s32[2]{0:T(128)} %pad_add_fusion.spot) | copy-start | bytes 28
  107.8 9.0 %copy-start.6 = (bf16[8,272,384]{2,1,0:T(8,128)(2,1)S(1)}, bf16[8,272,384]{2,1,0:T(8,128)(2,1)}, u32[]{:S(2)}) copy-start(bf16[8,272,384]{2,1,0:T(8,128)(2,1)} %get-tuple-element.51.own) | copy-start | bytes 5013508
  107.8 9.0 %collective-permute-start.4 = (bf16[8,272,384]{2,1,0:T(8,128)(2,1)}, bf16[8,272,384]{2,1,0:T(8,128)(2,1)S(1)}, u32[]{:S(2)}, u32[]{:S(2)}) collective-permute-start(bf16[8,272,384]{2,1,0:T(8,128)(2,1)} %get-tuple-element.52), channel_id=1, source_target_pairs={{0,16},{16,0},{32,48},{48,32},{64,80},{80,64},{96,112},{112,96},{1... | collective-permute-start | bytes 5013512 | tf_op jit(solution)/shard_map/ppermute | solution.py:781
  107.9 24.6 %all-to-all-start.1 = ((bf16[16,80,384]{2,1,0:T(8,128)(2,1)}), bf16[16,80,384]{2,1,0:T(8,128)(2,1)}, u32[]{:S(2)}, u32[]{:S(2)}) async-start(bf16[16,80,384]{2,1,0:T(8,128)(2,1)} %get-tuple-element.57), calls=%async_computation.1 | async-start | bytes 1966080 | tf_op jit(solution)/shard_map/all_to_all | solution.py:782
  116.8 9.3 %copy-start.4 = (bf16[4096,192]{1,0:T(8,128)(2,1)S(1)}, bf16[4096,192]{1,0:T(8,128)(2,1)}, u32[]{:S(2)}) copy-start(bf16[4096,192]{1,0:T(8,128)(2,1)} %copy-done.3) | copy-start | bytes 4718596
  116.8 9.3 %copy-start.19 = (bf16[192,384]{1,0:T(8,128)(2,1)S(1)}, bf16[192,384]{1,0:T(8,128)(2,1)}, u32[]{:S(2)}) copy-start(bf16[192,384]{1,0:T(8,128)(2,1)} %in_z.1) | copy-start | bytes 442372
  116.8 9.3 %copy-start.8 = (bf16[8,272,384]{2,1,0:T(8,128)(2,1)}, bf16[8,272,384]{2,1,0:T(8,128)(2,1)S(1)}, u32[]{:S(2)}) copy-start(bf16[8,272,384]{2,1,0:T(8,128)(2,1)S(1)} %collective-permute-done.4.got) | copy-start | bytes 5013508
  120.1 51.3 %collective-permute-start.5 = (bf16[8,144,384]{2,1,0:T(8,128)(2,1)}, bf16[8,144,384]{2,1,0:T(8,128)(2,1)}, u32[]{:S(2)}, u32[]{:S(2)}) collective-permute-start(bf16[8,144,384]{2,1,0:T(8,128)(2,1)} %get-tuple-element.53), channel_id=1, source_target_pairs={{0,32},{16,48},{32,64},{48,80},{64,96},{80,112},{96,0},{112,16},{1... | collective-permute-start | bytes 2654216 | tf_op jit(solution)/shard_map/ppermute | solution.py:785
  122.5 48.9 %collective-permute-start.6 = (bf16[8,144,384]{2,1,0:T(8,128)(2,1)}, bf16[8,144,384]{2,1,0:T(8,128)(2,1)}, u32[]{:S(2)}, u32[]{:S(2)}) collective-permute-start(bf16[8,144,384]{2,1,0:T(8,128)(2,1)} %get-tuple-element.54), channel_id=1, source_target_pairs={{0,64},{16,80},{32,96},{48,112},{64,0},{80,16},{96,32},{112,48},{1... | collective-permute-start | bytes 2654216 | tf_op jit(solution)/shard_map/ppermute | solution.py:785
  124.9 46.5 %collective-permute-start.7 = (bf16[8,144,384]{2,1,0:T(8,128)(2,1)}, bf16[8,144,384]{2,1,0:T(8,128)(2,1)}, u32[]{:S(2)}, u32[]{:S(2)}) collective-permute-start(bf16[8,144,384]{2,1,0:T(8,128)(2,1)} %get-tuple-element.55), channel_id=1, source_target_pairs={{0,96},{16,112},{32,0},{48,16},{64,32},{80,48},{96,64},{112,80},{1... | collective-permute-start | bytes 2654216 | tf_op jit(solution)/shard_map/ppermute | solution.py:785
  128.6 10.9 %copy-start.26 = (f32[384]{0:T(512)S(1)}, f32[384]{0:T(512)}, u32[]{:S(2)}) copy-start(f32[384]{0:T(512)} %param.29) | copy-start | bytes 4612
  134.1 0.9 copy-start.13
  134.9 19.1 %all-to-all-start.2 = ((bf16[16,64,384]{2,1,0:T(8,128)(2,1)}), bf16[16,64,384]{2,1,0:T(8,128)(2,1)}, u32[]{:S(2)}, u32[]{:S(2)}) async-start(bf16[16,64,384]{2,1,0:T(8,128)(2,1)} %copy-done.13), calls=%async_computation.2 | async-start | bytes 1572864 | tf_op jit(solution)/shard_map/all_to_all | solution.py:792
  154.0 17.4 %copy-start.12 = (bf16[32,768]{1,0:T(8,128)(2,1)S(1)}, bf16[32,768]{1,0:T(8,128)(2,1)}, u32[]{:S(2)}) copy-start(bf16[32,768]{1,0:T(8,128)(2,1)} %and_convert_fusion.heads_map) | copy-start | bytes 147460
  154.0 26.3 %copy-start.27 = (f32[384]{0:T(512)S(1)}, f32[384]{0:T(512)}, u32[]{:S(2)}) copy-start(f32[384]{0:T(512)} %param.31) | copy-start | bytes 4612
  154.0 29.4 %copy-start.1 = (bf16[32,128,384]{2,1,0:T(8,128)(2,1)S(1)}, bf16[32,128,384]{2,1,0:T(8,128)(2,1)}, u32[]{:S(2)}) copy-start(bf16[32,128,384]{2,1,0:T(8,128)(2,1)} %inner_col.1.total_col) | copy-start | bytes 9437188
  154.0 29.4 %copy-start.14 = (bf16[16,32,256]{2,1,0:T(8,128)(2,1)S(1)}, bf16[16,32,256]{2,1,0:T(8,128)(2,1)}, u32[]{:S(2)}) copy-start(bf16[16,32,256]{2,1,0:T(8,128)(2,1)} %copy.70.out_col) | copy-start | bytes 786436
  154.0 29.3 %copy-start.15 = (bf16[192,768]{1,0:T(8,128)(2,1)S(1)}, bf16[192,768]{1,0:T(8,128)(2,1)}, u32[]{:S(2)}) copy-start(bf16[192,768]{1,0:T(8,128)(2,1)} %ff_in.1) | copy-start | bytes 884740
  154.0 29.3 %copy-start.17 = (bf16[384,192]{0,1:T(8,128)(2,1)S(1)}, bf16[384,192]{0,1:T(8,128)(2,1)}, u32[]{:S(2)}) copy-start(bf16[384,192]{0,1:T(8,128)(2,1)} %param.32) | copy-start | bytes 442372
  154.1 29.3 %copy-start.22 = (f32[192]{0:T(256)S(1)}, f32[192]{0:T(256)}, u32[]{:S(2)}) copy-start(f32[192]{0:T(256)} %param.33) | copy-start | bytes 2308
  171.4 12.0 %copy-start = (bf16[32,128,384]{2,1,0:T(8,128)(2,1)S(1)}, bf16[32,128,384]{2,1,0:T(8,128)(2,1)}, u32[]{:S(2)}) copy-start(bf16[32,128,384]{2,1,0:T(8,128)(2,1)} %row_scan.1.total_row) | copy-start | bytes 9437188
  171.4 12.1 %copy-start.2 = (bf16[32,128,128]{2,1,0:T(8,128)(2,1)S(1)}, bf16[32,128,128]{2,1,0:T(8,128)(2,1)}, u32[]{:S(2)}) copy-start(bf16[32,128,128]{2,1,0:T(8,128)(2,1)} %get-tuple-element.62.coef_in) | copy-start | bytes 3145732
  171.4 1.6 copy-start.7
  173.0 1.6 copy-start.9
  178.3 5.1 %collective-permute-start.8 = (bf16[8,2,128,384]{3,2,1,0:T(8,128)(2,1)S(1)}, bf16[8,2,128,384]{3,2,1,0:T(8,128)(2,1)S(1)}, u32[]{:S(2)}, u32[]{:S(2)}) collective-permute-start(bf16[8,2,128,384]{3,2,1,0:T(8,128)(2,1)S(1)} %get-tuple-element.72), channel_id=1, source_target_pairs={{0,16},{16,0},{32,48},{48,32},{64,80},{80,64},{96,112},{112,96},{1... | collective-permute-start | bytes 4718600 | tf_op jit(solution)/shard_map/ppermute | solution.py:800
  183.4 1.6 copy-start.5
  185.0 1.0 copy-start.16
